TPU v7x, 32 devices: a whole 2x2x4 slice. The times are simulated.
32 devices in a mesh: dp: 16 (over z, y, x), mp: 2 (over core).
Axes of the slice: x: 2, y: 2, z: 4, core: 2. Of those that a mesh axis runs over, the one named last changes fastest.
Arguments:
- residual: bfloat16 [256, 4608], P(None, 'dp'), may hold values from -60 to 60
- norm_gain: float32 [4608], P('dp'), may hold values from 0.25 to 1.75
- query_weight: bfloat16 [4608, 2048], P('dp', 'mp'), may hold values from -2 to 2
- key_weight: bfloat16 [4608, 1024], P('dp', 'mp'), may hold values from -2 to 2
- value_weight: bfloat16 [4608, 1024], P('dp', 'mp'), may hold values from -0.09375 to 0.09375
- out_weight: bfloat16 [2048, 4608], P('mp', 'dp'), may hold values from -1 to 1
- post_gain: float32 [4608], P('dp'), may hold values from 0.25 to 1.75
- encoder_weight: bfloat16 [4608, 8192], P(None, ('dp', 'mp')), may hold values from -0.09375 to 0.09375
- encoder_bias: float32 [8192], P(('dp', 'mp')), may hold values from -3 to 3
- decoder_weight: bfloat16 [8192, 4608], P(('dp', 'mp')), may hold values from -0.125 to 0.125
- decoder_bias: float32 [4608], replicated, may hold values from -3 to 3
Outputs:
- encoder_grad: bfloat16 [4608, 8192], P(None, ('dp', 'mp'))
- encoder_bias_grad: float32 [8192], P(('dp', 'mp'))
- decoder_grad: bfloat16 [8192, 4608], P(('dp', 'mp'))
All inputs are finite; a program needn't handle non-finite values.
Results may differ from a plain program's by a relative error of at most 0.015.
Values may be sent and summed in bfloat16 or wider, within the bound.
No kernel may reach another device: no remote copies, remote signals or barrier semaphores. Data moves between devices by JAX's collectives and lax.ppermute only.
A program may use at most 128 MiB of HBM per device.

v0:
```python
import jax
import jax.numpy as jnp
from jax import lax
from jax.sharding import PartitionSpec as P

HEAD_DIM = 128


epsilon = 1e-06
softcap = 50.0
query_scale = 1.0 / 12.0
rope_base = 10000.0
smoothing = 0.1
penalty = 1.0
loss_weight = 0.0625


def rotate(matrix, positions):
    half_dim = matrix.shape[-1] // 2
    frequency = rope_base ** (-2.0 * jnp.arange(half_dim, dtype=jnp.float32) / matrix.shape[-1])
    angles = positions.astype(jnp.float32)[:, None] * frequency[None, :]
    cosine = jnp.cos(angles)[:, None, :]
    sine_part = jnp.sin(angles)[:, None, :]
    front_half = matrix[..., :half_dim]
    back_half = matrix[..., half_dim:]
    return jnp.concatenate(
        [front_half * cosine - back_half * sine_part, back_half * cosine + front_half * sine_part],
        axis=-1,
    )


def project(summed, square_sum, positions, model_width, query_width, key_width, head_dim):
    inverse = lax.rsqrt(square_sum / model_width + epsilon)
    scaled = summed * inverse[:, None]
    row_count = scaled.shape[0]
    queries = rotate(scaled[:, :query_width].reshape(row_count, -1, head_dim), positions).astype(
        jnp.bfloat16
    )
    keys = rotate(
        scaled[:, query_width : query_width + key_width].reshape(row_count, -1, head_dim), positions
    ).astype(jnp.bfloat16)
    values = (
        scaled[:, query_width + key_width :].reshape(row_count, -1, head_dim).astype(jnp.bfloat16)
    )
    return (queries, keys, values)


def partial_attention(queries, keys, values, query_positions, key_positions):
    row_count, query_heads, head_dim = queries.shape
    key_heads = keys.shape[1]
    grouped = queries.reshape(row_count, key_heads, query_heads // key_heads, head_dim)
    scores = (
        jnp.einsum("rkgd,skd->kgrs", grouped, keys, preferred_element_type=jnp.float32)
        * query_scale
    )
    capped = softcap * jnp.tanh(scores / softcap)
    allowed = query_positions[:, None] >= key_positions[None, :]
    weights = jnp.where(allowed, jnp.exp(capped), 0.0)
    denominator = jnp.sum(weights, axis=3)
    numerator = jnp.einsum(
        "kgrs,skd->rkgd", weights.astype(jnp.bfloat16), values, preferred_element_type=jnp.float32
    )
    return (
        numerator.reshape(row_count, query_heads, head_dim),
        jnp.transpose(denominator, (2, 0, 1)).reshape(row_count, query_heads),
    )


def on_device(
    residual,
    norm_gain,
    query_weight,
    key_weight,
    value_weight,
    out_weight,
    post_gain,
    encoder_weight,
    encoder_bias,
    decoder_weight,
    decoder_bias,
):
    token_count = residual.shape[0]
    model_width = decoder_weight.shape[1]
    head_dim = HEAD_DIM
    query_width = query_weight.shape[1]
    key_width = key_weight.shape[1]
    residual_float = residual.astype(jnp.float32)
    scaled = (residual_float * norm_gain).astype(jnp.bfloat16)
    stacked = jnp.concatenate([query_weight, key_weight, value_weight], axis=1)
    projected_part = jnp.dot(scaled, stacked, preferred_element_type=jnp.float32)
    partial_squares = jnp.sum(residual_float * residual_float, axis=1)
    summed, square_sum = lax.psum((projected_part, partial_squares), "dp")
    positions = jnp.arange(token_count)
    queries, keys, values = project(
        summed, square_sum, positions, model_width, query_width, key_width, head_dim
    )
    numerator, denominator = partial_attention(queries, keys, values, positions, positions)
    attended = (
        (numerator / denominator[:, :, None]).astype(jnp.bfloat16).reshape(token_count, query_width)
    )
    heads_part = jnp.dot(attended, out_weight, preferred_element_type=jnp.float32)
    head_out = lax.psum(heads_part, "mp")
    out_squares = lax.psum(jnp.sum(head_out * head_out, axis=1), "dp")
    normed = head_out * lax.rsqrt(out_squares / model_width + epsilon)[:, None] * post_gain
    hidden_columns = (residual_float + normed).astype(jnp.bfloat16)
    portion = lax.all_gather(hidden_columns, "dp", axis=1, tiled=True)
    preact_sum = jnp.dot(portion, encoder_weight, preferred_element_type=jnp.float32)
    preact_sum, hidden = (preact_sum, portion)
    preact = preact_sum + encoder_bias
    active = smoothing * jax.nn.softplus(preact / smoothing)
    active_low = active.astype(jnp.bfloat16)
    gate_slope = jax.nn.sigmoid(preact / smoothing)
    decoder_norms = jnp.sqrt(
        jnp.sum(jnp.square(decoder_weight.astype(jnp.float32)), axis=1) + epsilon
    )
    activity = jnp.sum(active, axis=0)
    rebuilt_part = jnp.dot(active_low, decoder_weight, preferred_element_type=jnp.float32)
    rebuilt = lax.psum(rebuilt_part, ("dp", "mp"))
    error_low = (rebuilt + decoder_bias - hidden.astype(jnp.float32)).astype(jnp.bfloat16)
    feedback = lax.dot_general(
        error_low, decoder_weight, (((1,), (1,)), ((), ())), preferred_element_type=jnp.float32
    )
    outer_sum = lax.dot_general(
        active_low, error_low, (((0,), (0,)), ((), ())), preferred_element_type=jnp.float32
    )
    grad_active = loss_weight * (2.0 * feedback + penalty * decoder_norms)
    grad_preact = grad_active * gate_slope
    encoder_grad = lax.dot_general(
        hidden,
        grad_preact.astype(jnp.bfloat16),
        (((0,), (0,)), ((), ())),
        preferred_element_type=jnp.float32,
    ).astype(jnp.bfloat16)
    encoder_bias_grad = jnp.sum(grad_preact, axis=0)
    decoder_grad = (
        loss_weight
        * (
            2.0 * outer_sum
            + penalty * (activity / decoder_norms)[:, None] * decoder_weight.astype(jnp.float32)
        )
    ).astype(jnp.bfloat16)
    return (encoder_grad, encoder_bias_grad, decoder_grad)


def solution(mesh):
    placed = (
        P(None, "dp"),
        P("dp"),
        P("dp", "mp"),
        P("dp", "mp"),
        P("dp", "mp"),
        P("mp", "dp"),
        P("dp"),
        P(None, ("dp", "mp")),
        P(("dp", "mp")),
        P(("dp", "mp"), None),
        P(),
    )
    return jax.shard_map(
        on_device,
        mesh=mesh,
        in_specs=placed,
        out_specs=(P(None, ("dp", "mp")), P(("dp", "mp")), P(("dp", "mp"), None)),
        check_vma=False,
    )
```

profile of v0, /device:TPU:0, one launch (start us, length us, event | category | flops | bytes accessed | tf_op | source)
XLA Modules:
  0.0 448.3 jit_solution(4388165543059884381)
XLA Ops:
  7.2 0.0 copy-start
  7.2 0.0 copy-start.6
  7.2 0.0 all-reduce.4.cloned.1.call-start
  7.2 3.6 fusion.4
  10.9 0.0 all-reduce.4.cloned.1.call-update
  10.9 0.0 all-reduce.6.cloned.1.call-start
  10.9 0.0 copy-done.6
  10.9 0.1 fusion.21
  11.0 44.4 %psum.36 = f32[256]{0:T(256)S(1)} all-reduce(f32[256]{0:T(256)S(1)} %fusion.21), channel_id=1, replica_groups=mesh['dp'=16,'mp'=2] {'dp'}, use_global_device_ids=true, to_apply=%region_2.0 | all-reduce | flops 256 | bytes 2048 | tf_op jit(solution)/shard_map/psum | solution.py:92
  55.4 0.7 iota_compare_fusion
  56.1 1.3 multiply_cosine_fusion
  57.4 85.9 %all-reduce.4.cloned.1.call-done = f32[256,2048]{1,0:T(8,128)} async-done(((f32[256,2048]{1,0:T(8,128)}), f32[256,2048]{1,0:T(8,128)}) %all-reduce.4.cloned.1.call-update) | async-done | bytes 2097168 | tf_op jit(solution)/shard_map/psum | solution.py:92
  143.2 1.8 broadcast_multiply_fusion
  145.1 1.0 slice_bitcast_fusion
  146.1 0.8 slice.42
  146.9 0.2 reshape.99
  147.1 0.0 copy-start.4
  147.1 0.0 copy-start.7
  147.1 0.0 copy-start.8
  147.1 1.1 fusion.36
  148.2 0.1 copy-done.4
  148.3 0.2 copy.28
  148.5 0.0 copy-done.7
  148.5 0.0 copy-done.8
  148.5 0.0 copy-start.5
  148.5 0.5 subtract_convert_fusion.1
  149.0 0.9 copy.16
  149.9 0.9 copy.17
  150.8 1.8 copy.25
  152.6 0.0 copy-done.5
  152.6 1.1 subtract_convert_fusion.2
  153.7 0.0 copy-start.9
  153.7 3.3 fusion.37
  157.0 0.0 copy-done.9
  157.0 1.6 fusion.15
  158.6 0.0 copy-start.12
  158.6 0.0 copy-start.13
  158.6 0.1 fusion.14
  158.7 0.0 copy-done.10
  158.7 1.0 fusion.39
  159.8 0.0 all-reduce.6.cloned.1.call-update
  159.8 0.0 all-gather.2.cloned.1.call-start
  159.8 17.8 %all-reduce.6.cloned.1.call-done = f32[256,288]{0,1:T(8,128)} async-done(((f32[256,288]{0,1:T(8,128)}), f32[256,288]{0,1:T(8,128)}) %all-reduce.6.cloned.1.call-update) | async-done | bytes 294928 | tf_op jit(solution)/shard_map/psum | solution.py:102
  177.6 1.0 multiply_reduce_fusion
  178.6 42.0 %psum.38 = f32[256]{0:T(256)S(1)} all-reduce(f32[256]{0:T(256)S(1)} %multiply_reduce_fusion), channel_id=1, replica_groups=mesh['dp'=16,'mp'=2] {'dp'}, use_global_device_ids=true, to_apply=%region_6.7 | all-reduce | flops 256 | bytes 2048 | tf_op jit(solution)/shard_map/psum | solution.py:103
  220.6 0.0 copy-done.12
  220.6 1.7 fusion.22
  222.3 0.0 all-gather.2.cloned.1.call-update
  222.4 0.2 all-reduce.8.cloned.1.call-start
  222.6 58.1 %all-gather.2.cloned.1.call-done = bf16[256,4608]{0,1:T(8,128)(2,1)} async-done(((bf16[256,288]{0,1:T(8,128)(2,1)}), bf16[256,4608]{0,1:T(8,128)(2,1)}) %all-gather.2.cloned.1.call-update) | async-done | bytes 2359312 | tf_op jit(solution)/shard_map/all_gather | solution.py:106
  280.7 0.0 copy-done
  280.7 0.0 copy-done.13
  280.7 2.8 fusion.29
  283.4 0.0 copy-done.2
  283.5 3.3 fusion.34
  286.8 0.0 all-reduce.8.cloned.1.call-update
  286.8 0.0 copy-start.11
  286.8 2.2 fusion.3
  289.0 141.6 %all-reduce.8.cloned.1.call-done = f32[256,4608]{0,1:T(8,128)} async-done(((f32[256,4608]{0,1:T(8,128)}), f32[256,4608]{0,1:T(8,128)}) %all-reduce.8.cloned.1.call-update) | async-done | bytes 4718608 | tf_op jit(solution)/shard_map/psum | solution.py:118
  430.6 4.2 subtract_convert_fusion
  434.9 3.1 fusion.2
  438.0 1.4 fusion.38
  439.4 0.3 copy-done.1
  439.6 2.2 convolution_convert_fusion
  (13 shorter events, 0.1 us)
Async XLA Ops:
  7.2 273.5 %copy-start = (bf16[4608,256]{1,0:T(8,128)(2,1)S(1)}, bf16[4608,256]{1,0:T(8,128)(2,1)}, u32[]{:S(2)}) copy-start(bf16[4608,256]{1,0:T(8,128)(2,1)} %param.18) | copy-start | bytes 7077892
  7.2 3.8 copy-start.6
  7.2 136.0 %all-reduce.4.cloned.1.call-start = ((), (), s32[]{:S(2)}) async-start(), calls=%async_computation | async-start | bytes 4194304 | tf_op jit(solution)/shard_map/psum | solution.py:92
  10.9 166.7 %all-reduce.6.cloned.1.call-start = ((), (), s32[]{:S(2)}) async-start(), calls=%async_computation.1 | async-start | bytes 589824 | tf_op jit(solution)/shard_map/psum | solution.py:102
  147.1 1.2 copy-start.4
  147.1 1.4 copy-start.7
  147.1 1.4 copy-start.8
  148.5 4.1 copy-start.5
  153.7 3.3 copy-start.9
  157.0 1.7 copy-start.10
  158.6 62.0 %copy-start.12 = (f32[288]{0:T(512)S(1)}, f32[288]{0:T(512)}, u32[]{:S(2)}) copy-start(f32[288]{0:T(512)} %param.17) | copy-start | bytes 3460
  158.6 122.1 %copy-start.13 = (f32[256]{0:T(256)S(1)}, f32[256]{0:T(256)}, u32[]{:S(2)}) copy-start(f32[256]{0:T(256)} %param.19) | copy-start | bytes 3076
  159.8 120.9 %all-gather.2.cloned.1.call-start = ((), (), s32[]{:S(2)}) async-start(), calls=%async_computation.2 | async-start | bytes 2506752 | tf_op jit(solution)/shard_map/all_gather | solution.py:106
  222.4 208.3 %all-reduce.8.cloned.1.call-start = ((), (), s32[]{:S(2)}) async-start(), calls=%async_computation.3 | async-start | bytes 9437184 | tf_op jit(solution)/shard_map/psum | solution.py:118
  280.7 2.8 copy-start.2
  286.8 143.8 %copy-start.11 = (f32[4608]{0:T(1024)S(1)}, f32[4608]{0:T(1024)}, u32[]{:S(2)}) copy-start(f32[4608]{0:T(1024)} %param.21) | copy-start | bytes 55300
  430.6 4.3 copy-start.3
  438.0 1.7 copy-start.1
Sparse Core Ops, SparseCore 0:
  14.1 129.1 all-reduce.3
  159.9 17.6 all-reduce.5
  222.5 58.1 all-gather.1
  287.1 143.4 all-reduce.7
where the time goes:
time: 449 us; the launch traced here: 448 us
  waiting for transfers between devices  303 us (67%)
  blocking collectives  86.3 us (19%)
  matrix products  22.3 us (5%)
  other arithmetic  14.7 us (3%)
  between operations  14 us (3%)
  local copies, waits for them, and re-layouts  7.29 us (2%)
    psum x1, waiting for transfers between devices, on_device(): rebuilt = lax.psum(rebuilt_part, ('dp', 'mp'))  142 us
    psum x1, waiting for transfers between devices, on_device(): summed, square_sum = lax.psum((projected_part, partial_squares), 'dp')  85.9 us
    all_gather x1, waiting for transfers between devices, on_device(): portion = lax.all_gather(hidden_columns, 'dp', axis=1, tiled=True)  58.1 us
    psum x1, blocking collectives, on_device(): summed, square_sum = lax.psum((projected_part, partial_squares), 'dp')  44.4 us
    psum x1, blocking collectives, on_device(): out_squares = lax.psum(jnp.sum(head_out * head_out, axis=1), 'dp')  42 us
    psum x1, waiting for transfers between devices, on_device(): head_out = lax.psum(heads_part, 'mp')  17.8 us
  transfers between devices with their start and end apart: 4, of which 4 were waited for; matrix products, arithmetic and copies ran while one was open for 1% of the time, Pallas kernels for 0%

commit v1 on v0

v1 whole, which is shorter than its diff:
```python
import functools

import jax
import jax.numpy as jnp
from jax import lax
from jax.experimental import pallas as pl
from jax.experimental.pallas import tpu as pltpu
from jax.sharding import PartitionSpec as P

HEAD_DIM = 128
CHUNKS = 2

epsilon = 1e-06
softcap = 50.0
query_scale = 1.0 / 12.0
rope_base = 10000.0
smoothing = 0.1
penalty = 1.0
loss_weight = 0.0625

bf16 = jnp.bfloat16
f32 = jnp.float32
AXES = ("dp", "mp")


class Ladder:
    def __init__(self, dp, mp):
        self.dp, self.mp = dp, mp
        dp_bits, mp_bits = dp.bit_length() - 1, mp.bit_length() - 1
        assert dp == 1 << dp_bits and mp == 1 << mp_bits
        self.near = [("dp", k) for k in range(min(2, dp_bits))]
        self.far = [("dp", k) for k in range(dp_bits - 1, len(self.near) - 1, -1)]
        self.cores = [("mp", k) for k in range(mp_bits - 1, -1, -1)]

    def place(self, step, m):
        axis, k = step
        if axis == "dp" and k < 2 and len(self.near) == 2 and m & 1:
            k = 1 - k
        return axis, k

    def pairs(self, step):
        result = []
        for d in range(self.dp):
            for m in range(self.mp):
                axis, k = self.place(step, m)
                peer = (d ^ (1 << k), m) if axis == "dp" else (d, m ^ (1 << k))
                result.append((d * self.mp + m, peer[0] * self.mp + peer[1]))
        return result

    def static_bit(self, step, d, m):
        axis, k = self.place(step, m)
        return ((d if axis == "dp" else m) >> k) & 1

    def bit(self, step):
        d, m = lax.axis_index("dp"), lax.axis_index("mp")
        axis, k = step
        if axis == "mp":
            return (m >> k) & 1
        if k < 2 and len(self.near) == 2:
            k = jnp.where(m & 1 == 1, 1 - k, k)
        return (d >> k) & 1

    def swap(self, value, step):
        return lax.ppermute(value, AXES, self.pairs(step))

    def scatter(self, value, steps, wire):
        for step in steps:
            half = value.shape[0] // 2
            up = self.bit(step) == 1
            low, high = value[:half], value[half:]
            got = self.swap(jnp.where(up, low, high).astype(wire), step)
            value = jnp.where(up, high, low) + got.astype(f32)
        return value

    def gather(self, value, steps):
        for step in reversed(steps):
            got = self.swap(value, step)
            up = self.bit(step) == 1
            value = jnp.concatenate([jnp.where(up, got, value), jnp.where(up, value, got)], axis=0)
        return value

    def order(self, steps):
        where = {}
        for d in range(self.dp):
            for m in range(self.mp):
                p = 0
                for step in steps:
                    p = 2 * p + self.static_bit(step, d, m)
                where[p] = d * self.mp + m
        return [where[p] for p in range(self.dp * self.mp)]

    def position(self, steps):
        p = 0
        for step in steps:
            p = 2 * p + self.bit(step)
        return p


def attention_kernel(start, heads, own_ref, got_ref, inv_ref, cos_ref, sin_ref, oldk_ref, oldv_ref, out_ref, k_ref, v_ref):
    width = own_ref.shape[1]
    half = HEAD_DIM // 2
    inverse = inv_ref[...]
    cosine, sine = cos_ref[...], sin_ref[...]

    def rows(first, count):
        return (own_ref[pl.ds(first, count), :] + got_ref[pl.ds(first, count), :].astype(f32)) * inverse

    def rotated(first):
        front, back = rows(first, half), rows(first + half, half)
        return jnp.concatenate([front * cosine - back * sine, back * cosine + front * sine], axis=0).astype(bf16)

    base = heads * HEAD_DIM
    k_ref[pl.ds(0, HEAD_DIM), pl.ds(start, width)] = rotated(base)
    v_ref[pl.ds(0, HEAD_DIM), pl.ds(start, width)] = rows(base + HEAD_DIM, HEAD_DIM).astype(bf16)
    if start:
        k_ref[:, pl.ds(0, start)] = oldk_ref[...]
        v_ref[:, pl.ds(0, start)] = oldv_ref[...]
    keys, values = k_ref[...], v_ref[...]
    span = start + width
    allowed = lax.broadcasted_iota(jnp.int32, (span, width), 0) <= lax.broadcasted_iota(jnp.int32, (span, width), 1) + start
    for h in range(heads):
        query = rotated(h * HEAD_DIM)
        score = lax.dot_general(keys, query, (((0,), (0,)), ((), ())), preferred_element_type=f32) * query_scale
        capped = softcap * jnp.tanh(score / softcap)
        weights = jnp.where(allowed, jnp.exp(capped), 0.0)
        total = jnp.sum(weights, axis=0, keepdims=True)
        mixed = jnp.dot(values, weights.astype(bf16), preferred_element_type=f32)
        out_ref[pl.ds(h * HEAD_DIM, HEAD_DIM), :] = (mixed / total).astype(bf16)


def attend(start, heads, own, got, inverse, cosine, sine, oldk, oldv):
    width = own.shape[1]
    span = start + width
    return pl.pallas_call(
        functools.partial(attention_kernel, start, heads),
        out_shape=(
            jax.ShapeDtypeStruct((heads * HEAD_DIM, width), bf16),
            jax.ShapeDtypeStruct((HEAD_DIM, span), bf16),
            jax.ShapeDtypeStruct((HEAD_DIM, span), bf16),
        ),
        cost_estimate=pl.CostEstimate(
            flops=4 * heads * HEAD_DIM * span * width, bytes_accessed=8 * own.size, transcendentals=2 * heads * span * width
        ),
    )(own, got, inverse, cosine, sine, oldk, oldv)


def on_device(ladder, residual, norm_gain, query_weight, key_weight, value_weight, out_weight, post_gain,
              encoder_weight, encoder_bias, decoder_weight, decoder_bias):
    tokens = residual.shape[0]
    model_width = decoder_weight.shape[1]
    latents = decoder_weight.shape[0]
    groups = key_weight.shape[1] // HEAD_DIM
    heads = query_weight.shape[1] // key_weight.shape[1]
    width = tokens // CHUNKS
    cuts = [slice(c * width, (c + 1) * width) for c in range(CHUNKS)]

    near, far, cores = ladder.near, ladder.far, ladder.cores
    dp_steps = near + far
    all_steps = cores + dp_steps
    group_bits = groups.bit_length() - 1
    assert groups == 1 << group_bits and group_bits <= len(dp_steps)
    group_steps, copy_steps = dp_steps[:group_bits], dp_steps[group_bits:]

    residual_t = residual.T
    residual_float = residual_t.astype(f32)
    scaled = (residual_float * norm_gain[:, None]).astype(bf16)
    pieces = []
    for g in range(groups):
        pieces += [
            query_weight[:, g * heads * HEAD_DIM : (g + 1) * heads * HEAD_DIM],
            key_weight[:, g * HEAD_DIM : (g + 1) * HEAD_DIM],
            value_weight[:, g * HEAD_DIM : (g + 1) * HEAD_DIM],
        ]
    stacked = jnp.concatenate(pieces, axis=1)
    projected = lax.dot_general(stacked, scaled, (((0,), (0,)), ((), ())), preferred_element_type=f32)

    mine = residual_t
    for step in cores:
        half = mine.shape[0] // 2
        mine = jnp.where(ladder.bit(step) == 1, mine[half:], mine[:half])
    order = ladder.order(all_steps)
    block = model_width // len(order)
    back = [order.index(i) for i in range(len(order))]

    def reordered(value, places):
        return jnp.concatenate([value[p * block : (p + 1) * block] for p in places], axis=0)

    encoder_g = reordered(encoder_weight, order)
    gain_all = lax.all_gather(post_gain, "dp", axis=0, tiled=True)
    gain_g = reordered(gain_all, order)

    half_dim = HEAD_DIM // 2
    frequency = rope_base ** (-2.0 * jnp.arange(half_dim, dtype=f32) / HEAD_DIM)
    angles = frequency[:, None] * jnp.arange(tokens).astype(f32)[None, :]
    cosine, sine = jnp.cos(angles), jnp.sin(angles)

    norms = jnp.sqrt(jnp.sum(jnp.square(decoder_weight.astype(f32)), axis=1) + epsilon)
    slot = ladder.position(all_steps) * block

    oldk = oldv = jnp.zeros((HEAD_DIM, width), bf16)
    hiddens, actives, slopes, errors = [], [], [], []
    activity = 0.0
    for c, cut in enumerate(cuts):
        residual_g = ladder.gather(mine[:, cut], all_steps)
        square_sum = jnp.sum(jnp.square(residual_g.astype(f32)), axis=0, keepdims=True)
        inverse = lax.rsqrt(square_sum / model_width + epsilon)

        part = ladder.scatter(projected[:, cut], group_steps, bf16)
        for step in copy_steps[:-1]:
            part = part + ladder.swap(part.astype(bf16), step).astype(f32)
        got = ladder.swap(part.astype(bf16), copy_steps[-1])
        attended, oldk, oldv = attend(
            c * width, heads, part, got, inverse, cosine[:, cut], sine[:, cut], oldk, oldv
        )
        attended = ladder.gather(attended, group_steps)
        head_part = lax.dot_general(out_weight, attended, (((0,), (0,)), ((), ())), preferred_element_type=f32)
        head_mine = ladder.scatter(head_part, cores, f32)
        head_g = ladder.gather(head_mine.astype(bf16), all_steps).astype(f32)
        head_squares = jnp.sum(jnp.square(head_g), axis=0, keepdims=True)
        head_inverse = lax.rsqrt(head_squares / model_width + epsilon)
        hidden_g = (residual_g.astype(f32) + head_g * head_inverse * gain_g[:, None]).astype(bf16)
        preact = (
            lax.dot_general(encoder_g, hidden_g, (((0,), (0,)), ((), ())), preferred_element_type=f32)
            + encoder_bias[:, None]
        )
        active = smoothing * jax.nn.softplus(preact / smoothing)
        active_low = active.astype(bf16)
        slopes.append(jax.nn.sigmoid(preact / smoothing))
        activity = activity + jnp.sum(active, axis=1)
        rebuilt_part = lax.dot_general(
            decoder_weight, active_low, (((0,), (0,)), ((), ())), preferred_element_type=f32
        )
        rebuilt = ladder.scatter(rebuilt_part, all_steps, bf16)
        hidden = reordered(hidden_g, back)
        error = (
            rebuilt
            + lax.dynamic_slice_in_dim(decoder_bias, slot, block)[:, None]
            - lax.dynamic_slice_in_dim(hidden, slot, block, axis=0).astype(f32)
        ).astype(bf16)
        errors.append(ladder.gather(error, all_steps))
        hiddens.append(hidden)
        actives.append(active_low)

    hidden = jnp.concatenate(hiddens, axis=1)
    active_low = jnp.concatenate(actives, axis=1)
    slope = jnp.concatenate(slopes, axis=1)
    error_low = jnp.concatenate(errors, axis=1)
    feedback = jnp.dot(decoder_weight, error_low, preferred_element_type=f32)
    grad_preact = loss_weight * (2.0 * feedback + penalty * norms[:, None]) * slope
    encoder_grad = lax.dot_general(
        hidden, grad_preact.astype(bf16), (((1,), (1,)), ((), ())), preferred_element_type=f32
    ).astype(bf16)
    encoder_bias_grad = jnp.sum(grad_preact, axis=1)
    outer_sum = lax.dot_general(active_low, error_low, (((1,), (1,)), ((), ())), preferred_element_type=f32)
    decoder_grad = (
        loss_weight * (2.0 * outer_sum + penalty * (activity / norms)[:, None] * decoder_weight.astype(f32))
    ).astype(bf16)
    return encoder_grad, encoder_bias_grad, decoder_grad


def solution(mesh):
    ladder = Ladder(mesh.shape["dp"], mesh.shape["mp"])
    placed = (
        P(None, "dp"),
        P("dp"),
        P("dp", "mp"),
        P("dp", "mp"),
        P("dp", "mp"),
        P("mp", "dp"),
        P("dp"),
        P(None, ("dp", "mp")),
        P(("dp", "mp")),
        P(("dp", "mp"), None),
        P(),
    )
    return jax.shard_map(
        functools.partial(on_device, ladder),
        mesh=mesh,
        in_specs=placed,
        out_specs=(P(None, ("dp", "mp")), P(("dp", "mp")), P(("dp", "mp"), None)),
        check_vma=False,
    )
```

time: 449 us -> 283 us (0.63)
  waiting for transfers between devices: 303 us -> 78.2 us
  starting transfers between devices: 0.34 us -> 52.1 us
  local copies, waits for them, and re-layouts: 7.29 us -> 31.2 us
  between operations: 14 us -> 2.79 us
  blocking collectives: 86.3 us -> 75.9 us
  other arithmetic: 14.7 us -> 22.9 us
  matrix products: 22.3 us -> 14.7 us
    psum x3 -> x0, waiting for transfers between devices: 245 us -> none  [the longest x1 142 us: on_device(): rebuilt = lax.psum(rebuilt_part, ('dp', 'mp'))]
    psum x2 -> x0, blocking collectives: 86.3 us -> none  [the longest x1 44.4 us: on_device(): summed, square_sum = lax.psum((projected_part, partial_squares), 'dp')]
    ppermute x0 -> x54, waiting for transfers between devices: none -> 78.2 us  [swap(): return lax.ppermute(value, AXES, self.pairs(step))]
    unnamed x0 -> x1, blocking collectives: none -> 75.9 us
    all_gather x1 -> x0, waiting for transfers between devices: 58.1 us -> none  [on_device(): portion = lax.all_gather(hidden_columns, 'dp', axis=1, tiled=True)]
    ppermute x0 -> x54, starting transfers between devices: none -> 52.1 us  [swap(): return lax.ppermute(value, AXES, self.pairs(step))]
    unnamed x30 -> x141, local copies, waits for them, and re-layouts: 1.63 us -> 24 us
    dot_general x9 -> x10, matrix products: 22.3 us -> 14.7 us  [the longest x1 6.15 us: on_device(): lax.dot_general(active_low, error_low, (((1,), (1,)), ((), ())), preferre...]
  transfers between devices with their start and end apart: 4 -> 54, of which waited for: 4 -> 33; matrix products, arithmetic and copies ran while one was open for 1% -> 16% of each run, Pallas kernels for 0% -> 1%
where the time goes in v1:
time: 283 us; the launch traced here: 282 us
  waiting for transfers between devices  78.2 us (28%)
  blocking collectives  75.9 us (27%)
  starting transfers between devices  52.1 us (18%)
  local copies, waits for them, and re-layouts  31.2 us (11%)
  other arithmetic  22.9 us (8%)
  matrix products  14.7 us (5%)
  Pallas kernels  4.22 us (1%)
    ppermute x54, waiting for transfers between devices, swap(): return lax.ppermute(value, AXES, self.pairs(step))  78.2 us
    unnamed x1, blocking collectives  75.9 us
    ppermute x54, starting transfers between devices, swap(): return lax.ppermute(value, AXES, self.pairs(step))  52.1 us
    unnamed x141, local copies, waits for them, and re-layouts  24 us
    select_n x33, other arithmetic, gather(): jnp.where(up, got, value)  6.44 us
    convert_element_type x1, other arithmetic, on_device(): (residual_g.astype(f32) + head_g * head_inverse * gain_g[:, None]).astype...  6.29 us
    dot_general x1, matrix products, on_device(): lax.dot_general(active_low, error_low, (((1,), (1,)), ((), ())), preferre...  6.15 us
  transfers between devices with their start and end apart: 54, of which 33 were waited for; matrix products, arithmetic and copies ran while one was open for 16% of the time, Pallas kernels for 1%

profile of v1, /device:TPU:0, one launch (start us, length us, event | category | flops | bytes accessed | tf_op | source)
XLA Modules:
  0.0 282.0 jit_solution(14168003005692049463)
XLA Ops:
  2.4 3.0 %collective-permute-start = (bf16[144,128]{1,0:T(8,128)(2,1)}, bf16[144,128]{1,0:T(8,128)(2,1)}, u32[]{:S(2)}, u32[]{:S(2)}) collective-permute-start(bf16[144,128]{1,0:T(8,128)(2,1)} %slice.728), channel_id=1, source_target_pairs={{0,8},{1,9},{2,10},{3,11},{4,12},{5,13},{6,14},{7,15},{8,0},{9,1},... | collective-permute-start | bytes 110600 | tf_op jit(solution)/shard_map/ppermute | solution.py:64
  10.3 1.6 collective-permute-start.22
  15.9 1.4 dynamic-update-slice
  17.3 75.9 %all-reduce = f32[4608]{0:T(1024)} all-reduce(f32[4608]{0:T(1024)} %dynamic-update-slice), channel_id=1, replica_groups=mesh['dp'=16,'mp'=2] {'dp'}, use_global_device_ids=true, to_apply=%add | all-reduce | flops 4608 | bytes 36864
  93.2 1.7 fusion.51
  109.4 1.4 copy-done.11
  112.3 1.5 concatenate.142
  114.7 3.9 %collective-permute-done.17 = bf16[144,128]{1,0:T(8,128)(2,1)S(1)} collective-permute-done((bf16[144,128]{1,0:T(8,128)(2,1)S(1)}, bf16[144,128]{1,0:T(8,128)(2,1)S(1)}, u32[]{:S(2)}, u32[]{:S(2)}) %collective-permute-start.17) | collective-permute-done | bytes 36896 | tf_op jit(solution)/shard_map/ppermute | solution.py:64
  118.7 4.3 %collective-permute-done.1 = bf16[288,128]{1,0:T(8,128)(2,1)S(1)} collective-permute-done((bf16[288,128]{1,0:T(8,128)(2,1)S(1)}, bf16[288,128]{1,0:T(8,128)(2,1)S(1)}, u32[]{:S(2)}, u32[]{:S(2)}) %collective-permute-start.1) | collective-permute-done | bytes 73760 | tf_op jit(solution)/shard_map/ppermute | solution.py:64
  123.2 2.2 collective-permute-done.18
  125.5 2.8 collective-permute-done.2
  128.5 1.1 convert_add_fusion.7
  129.7 2.1 collective-permute-start.23
  131.9 2.1 collective-permute-start.20
  134.8 1.3 collective-permute-done.23
  136.1 1.7 collective-permute-start.24
  137.8 3.5 %collective-permute-done.7 = bf16[512,128]{1,0:T(8,128)(2,1)S(1)} collective-permute-done((bf16[512,128]{1,0:T(8,128)(2,1)S(1)}, bf16[512,128]{1,0:T(8,128)(2,1)S(1)}, u32[]{:S(2)}, u32[]{:S(2)}) %collective-permute-start.7) | collective-permute-done | bytes 131104 | tf_op jit(solution)/shard_map/ppermute | solution.py:64
  142.1 2.0 collective-permute-done.24
  145.9 1.3 collective-permute-done.4
  149.2 2.1 shard_map.130
  151.4 1.3 broadcast_select_fusion.7
  153.9 2.1 shard_map.131
  156.1 1.9 collective-permute-start.26
  158.8 2.1 collective-permute-start.10
  161.8 1.8 collective-permute-start.27
  164.3 2.4 collective-permute-done.27
  167.2 2.1 collective-permute-start.12
  169.4 1.8 collective-permute-done.12
  171.3 2.1 collective-permute-start.29
  173.7 2.3 collective-permute-done.29
  176.0 1.6 collective-permute-start.30
  177.6 2.8 %collective-permute-done.13 = bf16[288,128]{1,0:T(8,128)(2,1)S(1)} collective-permute-done((bf16[288,128]{1,0:T(8,128)(2,1)S(1)}, bf16[288,128]{1,0:T(8,128)(2,1)S(1)}, u32[]{:S(2)}, u32[]{:S(2)}) %collective-permute-start.13) | collective-permute-done | bytes 73760 | tf_op jit(solution)/shard_map/ppermute | solution.py:64
  180.5 2.0 collective-permute-start.14
  183.4 2.9 %collective-permute-done.14 = bf16[576,128]{1,0:T(8,128)(2,1)S(1)} collective-permute-done((bf16[576,128]{1,0:T(8,128)(2,1)S(1)}, bf16[576,128]{1,0:T(8,128)(2,1)S(1)}, u32[]{:S(2)}, u32[]{:S(2)}) %collective-permute-start.14) | collective-permute-done | bytes 147488 | tf_op jit(solution)/shard_map/ppermute | solution.py:64
  186.3 2.9 %collective-permute-start.15 = (bf16[1152,128]{1,0:T(8,128)(2,1)S(1)}, bf16[1152,128]{1,0:T(8,128)(2,1)S(1)}, u32[]{:S(2)}, u32[]{:S(2)}) collective-permute-start(bf16[1152,128]{1,0:T(8,128)(2,1)S(1)} %pad_maximum_fusion.11), channel_id=1, source_target_pairs={{0,2},{1,5},{2,0},{3,7},{4,6},{5,1},{6,4},{7,3},{8,10},{9,13},{10,... | collective-permute-start | bytes 884744 | tf_op jit(solution)/shard_map/ppermute | solution.py:64
  189.5 2.9 %collective-permute-start.32 = (bf16[1152,128]{1,0:T(8,128)(2,1)S(1)}, bf16[1152,128]{1,0:T(8,128)(2,1)S(1)}, u32[]{:S(2)}, u32[]{:S(2)}) collective-permute-start(bf16[1152,128]{1,0:T(8,128)(2,1)S(1)} %pad_maximum_fusion.13), channel_id=1, source_target_pairs={{0,2},{1,5},{2,0},{3,7},{4,6},{5,1},{6,4},{7,3},{8,10},{9,13},{10,... | collective-permute-start | bytes 884744 | tf_op jit(solution)/shard_map/ppermute | solution.py:64
  192.4 1.6 collective-permute-done.15
  194.2 2.9 %collective-permute-done.32 = bf16[1152,128]{1,0:T(8,128)(2,1)S(1)} collective-permute-done((bf16[1152,128]{1,0:T(8,128)(2,1)S(1)}, bf16[1152,128]{1,0:T(8,128)(2,1)S(1)}, u32[]{:S(2)}, u32[]{:S(2)}) %collective-permute-start.32) | collective-permute-done | bytes 294944 | tf_op jit(solution)/shard_map/ppermute | solution.py:64
  198.2 1.1 collective-permute-done.33
  200.3 6.3 %fusion.5 = (bf16[4608,128]{1,0:T(8,128)(2,1)S(1)}, bf16[4608,128]{1,0:T(8,128)(2,1)S(1)}) fusion(f32[4608]{0:T(1024)S(1)} %copy-done.9, f32[128]{0:T(128)S(1)} %add_rsqrt_fusion.1, bf16[2304,128]{1,0:T(8,128)(2,1)S(1)} %get-tuple-element.24, bf16[2304,128]{1,0:T(8,128)(2,1)S(1)} %get-tuple-element.23, bf16[2304,128]{1,0:T(8,128)(2,1)S(1)} %get-tuple-element.28, ...), kind=kLoop, calls=%fused_computation.19 | loop fusion | flops 14155776 | bytes 7097344 | tf_op jit(solution)/shard_map/convert_element_type | solution.py:221
  213.2 2.1 collective-permute-start.45
  215.9 4.1 %collective-permute-done.45 = bf16[1152,128]{1,0:T(8,128)(2,1)S(1)} collective-permute-done((bf16[1152,128]{1,0:T(8,128)(2,1)S(1)}, bf16[1152,128]{1,0:T(8,128)(2,1)S(1)}, u32[]{:S(2)}, u32[]{:S(2)}) %collective-permute-start.45) | collective-permute-done | bytes 294944 | tf_op jit(solution)/shard_map/ppermute | solution.py:64
  220.1 2.1 collective-permute-start.46
  222.3 1.4 collective-permute-done.35
  223.8 2.4 collective-permute-start.36
  226.3 3.0 %collective-permute-done.36 = bf16[576,128]{1,0:T(8,128)(2,1)S(1)} collective-permute-done((bf16[576,128]{1,0:T(8,128)(2,1)S(1)}, bf16[576,128]{1,0:T(8,128)(2,1)S(1)}, u32[]{:S(2)}, u32[]{:S(2)}) %collective-permute-start.36) | collective-permute-done | bytes 147488 | tf_op jit(solution)/shard_map/ppermute | solution.py:64
  229.5 4.0 %collective-permute-done.47 = bf16[288,128]{1,0:T(8,128)(2,1)S(1)} collective-permute-done((bf16[288,128]{1,0:T(8,128)(2,1)S(1)}, bf16[288,128]{1,0:T(8,128)(2,1)S(1)}, u32[]{:S(2)}, u32[]{:S(2)}) %collective-permute-start.47) | collective-permute-done | bytes 73760 | tf_op jit(solution)/shard_map/ppermute | solution.py:64
  233.6 1.4 collective-permute-done.37
  235.7 1.8 collective-permute-done.48
  237.5 1.6 collective-permute-done.38
  240.1 1.2 collective-permute-start.49
  241.3 2.2 collective-permute-done.39
  244.6 2.0 collective-permute-start.50
  246.6 3.0 %collective-permute-done.40 = bf16[288,128]{1,0:T(8,128)(2,1)S(1)} collective-permute-done((bf16[288,128]{1,0:T(8,128)(2,1)S(1)}, bf16[288,128]{1,0:T(8,128)(2,1)S(1)}, u32[]{:S(2)}, u32[]{:S(2)}) %collective-permute-start.40) | collective-permute-done | bytes 73760 | tf_op jit(solution)/shard_map/ppermute | solution.py:64
  249.6 2.3 collective-permute-start.41
  253.2 3.3 %collective-permute-done.41 = bf16[576,128]{1,0:T(8,128)(2,1)S(1)} collective-permute-done((bf16[576,128]{1,0:T(8,128)(2,1)S(1)}, bf16[576,128]{1,0:T(8,128)(2,1)S(1)}, u32[]{:S(2)}, u32[]{:S(2)}) %collective-permute-start.41) | collective-permute-done | bytes 147488 | tf_op jit(solution)/shard_map/ppermute | solution.py:64
  256.5 3.2 %collective-permute-done.51 = bf16[576,128]{1,0:T(8,128)(2,1)S(1)} collective-permute-done((bf16[576,128]{1,0:T(8,128)(2,1)S(1)}, bf16[576,128]{1,0:T(8,128)(2,1)S(1)}, u32[]{:S(2)}, u32[]{:S(2)}) %collective-permute-start.51) | collective-permute-done | bytes 147488 | tf_op jit(solution)/shard_map/ppermute | solution.py:64
  259.8 2.1 collective-permute-start.42
  262.1 4.6 %collective-permute-done.42 = bf16[1152,128]{1,0:T(8,128)(2,1)S(1)} collective-permute-done((bf16[1152,128]{1,0:T(8,128)(2,1)S(1)}, bf16[1152,128]{1,0:T(8,128)(2,1)S(1)}, u32[]{:S(2)}, u32[]{:S(2)}) %collective-permute-start.42) | collective-permute-done | bytes 294944 | tf_op jit(solution)/shard_map/ppermute | solution.py:64
  266.9 2.9 %collective-permute-done.52 = bf16[1152,128]{1,0:T(8,128)(2,1)S(1)} collective-permute-done((bf16[1152,128]{1,0:T(8,128)(2,1)S(1)}, bf16[1152,128]{1,0:T(8,128)(2,1)S(1)}, u32[]{:S(2)}, u32[]{:S(2)}) %collective-permute-start.52) | collective-permute-done | bytes 294944 | tf_op jit(solution)/shard_map/ppermute | solution.py:64
  270.3 1.7 collective-permute-done.53
  272.3 6.1 %fusion.2 = bf16[256,4608]{1,0:T(8,128)(2,1)} fusion(bf16[256,4608]{1,0:T(8,128)(2,1)S(1)} %copy-done.2, f32[256]{0:T(256)S(1)} %get-tuple-element.134, bf16[2304,128]{1,0:T(8,128)(2,1)S(1)} %get-tuple-element.22, bf16[2304,128]{1,0:T(8,128)(2,1)S(1)} %get-tuple-element.21, bf16[2304,128]{1,0:T(8,128)(2,1)S(1)} %get-tuple-element.20, ...), kind=kOutput, calls=%fused_computation.3 | convolution fusion | flops 620756992 | bytes 7209984 | tf_op jit(solution)/shard_map/dot_general | solution.py:254
  278.4 1.4 fusion.53
  279.8 2.2 convolution_convert_fusion
  (315 shorter events, 53.6 us)
Async XLA Ops:
  0.6 163.3 %copy-start = (bf16[1024,288]{0,1:T(8,128)(2,1)S(1)}, bf16[1024,288]{0,1:T(8,128)(2,1)}, u32[]{:S(2)}) copy-start(bf16[1024,288]{0,1:T(8,128)(2,1)} %param.16) | copy-start | bytes 1769476
  0.6 8.5 %copy-start.5 = (bf16[288,1024]{1,0:T(8,128)(2,1)S(1)}, bf16[288,1024]{1,0:T(8,128)(2,1)}, u32[]{:S(2)}) copy-start(bf16[288,1024]{1,0:T(8,128)(2,1)} %param.13) | copy-start | bytes 1769476
  0.7 8.4 %copy-start.6 = (bf16[288,512]{1,0:T(8,128)(2,1)S(1)}, bf16[288,512]{1,0:T(8,128)(2,1)}, u32[]{:S(2)}) copy-start(bf16[288,512]{1,0:T(8,128)(2,1)} %param.14) | copy-start | bytes 884740
  0.7 8.5 %copy-start.7 = (bf16[288,512]{1,0:T(8,128)(2,1)S(1)}, bf16[288,512]{1,0:T(8,128)(2,1)}, u32[]{:S(2)}) copy-start(bf16[288,512]{1,0:T(8,128)(2,1)} %param.15) | copy-start | bytes 884740
  2.4 111.4 %collective-permute-start = (bf16[144,128]{1,0:T(8,128)(2,1)}, bf16[144,128]{1,0:T(8,128)(2,1)}, u32[]{:S(2)}, u32[]{:S(2)}) collective-permute-start(bf16[144,128]{1,0:T(8,128)(2,1)} %slice.728), channel_id=1, source_target_pairs={{0,8},{1,9},{2,10},{3,11},{4,12},{5,13},{6,14},{7,15},{8,0},{9,1},... | collective-permute-start | bytes 110600 | tf_op jit(solution)/shard_map/ppermute | solution.py:64
  5.4 4.0 %copy-start.13 = (f32[288]{0:T(512)S(1)}, f32[288]{0:T(512)}, u32[]{:S(2)}) copy-start(f32[288]{0:T(512)} %param.12) | copy-start | bytes 3460
  10.2 5.7 %copy-start.14 = (f32[288]{0:T(512)S(1)}, f32[288]{0:T(512)}, u32[]{:S(2)}) copy-start(f32[288]{0:T(512)} %param.17) | copy-start | bytes 3460
  10.3 118.1 %collective-permute-start.22 = (bf16[1024,128]{1,0:T(8,128)(2,1)S(1)}, bf16[1024,128]{1,0:T(8,128)(2,1)S(1)}, u32[]{:S(2)}, u32[]{:S(2)}) collective-permute-start(bf16[1024,128]{1,0:T(8,128)(2,1)S(1)} %get-tuple-element.18), channel_id=1, source_target_pairs={{0,2},{1,5},{2,0},{3,7},{4,6},{5,1},{6,4},{7,3},{8,10},{9,13},{10,... | collective-permute-start | bytes 786440 | tf_op jit(solution)/shard_map/ppermute | solution.py:64
  11.9 116.6 %collective-permute-start.5 = (bf16[1024,128]{1,0:T(8,128)(2,1)S(1)}, bf16[1024,128]{1,0:T(8,128)(2,1)}, u32[]{:S(2)}, u32[]{:S(2)}) collective-permute-start(bf16[1024,128]{1,0:T(8,128)(2,1)S(1)} %get-tuple-element.17), channel_id=1, source_target_pairs={{0,2},{1,5},{2,0},{3,7},{4,6},{5,1},{6,4},{7,3},{8,10},{9,13},{10,... | collective-permute-start | bytes 786440 | tf_op jit(solution)/shard_map/ppermute | solution.py:64
  93.2 15.9 %copy-start.3 = (bf16[4608,256]{1,0:T(8,128)(2,1)S(1)}, bf16[4608,256]{1,0:T(8,128)(2,1)}, u32[]{:S(2)}) copy-start(bf16[4608,256]{1,0:T(8,128)(2,1)} %param.18) | copy-start | bytes 7077892
  114.5 4.0 %collective-permute-start.17 = (bf16[144,128]{1,0:T(8,128)(2,1)S(1)}, bf16[144,128]{1,0:T(8,128)(2,1)S(1)}, u32[]{:S(2)}, u32[]{:S(2)}) collective-permute-start(bf16[144,128]{1,0:T(8,128)(2,1)S(1)} %get-tuple-element.93), channel_id=1, source_target_pairs={{0,8},{1,9},{2,10},{3,11},{4,12},{5,13},{6,14},{7,15},{8,0},{9,1},... | collective-permute-start | bytes 110600 | tf_op jit(solution)/shard_map/ppermute | solution.py:64
  114.6 8.4 %collective-permute-start.1 = (bf16[288,128]{1,0:T(8,128)(2,1)S(1)}, bf16[288,128]{1,0:T(8,128)(2,1)S(1)}, u32[]{:S(2)}, u32[]{:S(2)}) collective-permute-start(bf16[288,128]{1,0:T(8,128)(2,1)S(1)} %pad_maximum_fusion.24), channel_id=1, source_target_pairs={{0,16},{1,17},{2,18},{3,19},{4,20},{5,21},{6,22},{7,23},{8,24},{9,... | collective-permute-start | bytes 221192 | tf_op jit(solution)/shard_map/ppermute | solution.py:64
  118.6 6.8 %collective-permute-start.18 = (bf16[288,128]{1,0:T(8,128)(2,1)S(1)}, bf16[288,128]{1,0:T(8,128)(2,1)S(1)}, u32[]{:S(2)}, u32[]{:S(2)}) collective-permute-start(bf16[288,128]{1,0:T(8,128)(2,1)S(1)} %pad_maximum_fusion.26), channel_id=1, source_target_pairs={{0,16},{1,17},{2,18},{3,19},{4,20},{5,21},{6,22},{7,23},{8,24},{9,... | collective-permute-start | bytes 221192 | tf_op jit(solution)/shard_map/ppermute | solution.py:64
  123.1 5.2 %collective-permute-start.2 = (bf16[576,128]{1,0:T(8,128)(2,1)S(1)}, bf16[576,128]{1,0:T(8,128)(2,1)S(1)}, u32[]{:S(2)}, u32[]{:S(2)}) collective-permute-start(bf16[576,128]{1,0:T(8,128)(2,1)S(1)} %pad_maximum_fusion.16), channel_id=1, source_target_pairs={{0,4},{1,3},{2,6},{3,1},{4,0},{5,7},{6,2},{7,5},{8,12},{9,11},{10,... | collective-permute-start | bytes 442376 | tf_op jit(solution)/shard_map/ppermute | solution.py:64
  125.4 6.4 %collective-permute-start.19 = (bf16[576,128]{1,0:T(8,128)(2,1)S(1)}, bf16[576,128]{1,0:T(8,128)(2,1)S(1)}, u32[]{:S(2)}, u32[]{:S(2)}) collective-permute-start(bf16[576,128]{1,0:T(8,128)(2,1)S(1)} %pad_maximum_fusion.18), channel_id=1, source_target_pairs={{0,4},{1,3},{2,6},{3,1},{4,0},{5,7},{6,2},{7,5},{8,12},{9,11},{10,... | collective-permute-start | bytes 442376 | tf_op jit(solution)/shard_map/ppermute | solution.py:64
  128.4 16.6 %collective-permute-start.3 = (bf16[1152,128]{1,0:T(8,128)(2,1)S(1)}, bf16[1152,128]{1,0:T(8,128)(2,1)S(1)}, u32[]{:S(2)}, u32[]{:S(2)}) collective-permute-start(bf16[1152,128]{1,0:T(8,128)(2,1)S(1)} %pad_maximum_fusion.10), channel_id=1, source_target_pairs={{0,2},{1,5},{2,0},{3,7},{4,6},{5,1},{6,4},{7,3},{8,10},{9,13},{10,... | collective-permute-start | bytes 884744 | tf_op jit(solution)/shard_map/ppermute | solution.py:64
  129.6 5.0 %collective-permute-start.6 = (bf16[512,128]{1,0:T(8,128)(2,1)S(1)}, bf16[512,128]{1,0:T(8,128)(2,1)S(1)}, u32[]{:S(2)}, u32[]{:S(2)}) collective-permute-start(bf16[512,128]{1,0:T(8,128)(2,1)S(1)} %select_convert_fusion.9), channel_id=1, source_target_pairs={{0,4},{1,3},{2,6},{3,1},{4,0},{5,7},{6,2},{7,5},{8,12},{9,11},{10,... | collective-permute-start | bytes 393224 | tf_op jit(solution)/shard_map/ppermute | solution.py:64
  129.7 6.3 %collective-permute-start.23 = (bf16[512,128]{1,0:T(8,128)(2,1)S(1)}, bf16[512,128]{1,0:T(8,128)(2,1)S(1)}, u32[]{:S(2)}, u32[]{:S(2)}) collective-permute-start(bf16[512,128]{1,0:T(8,128)(2,1)S(1)} %select_convert_fusion.8), channel_id=1, source_target_pairs={{0,4},{1,3},{2,6},{3,1},{4,0},{5,7},{6,2},{7,5},{8,12},{9,11},{10,... | collective-permute-start | bytes 393224 | tf_op jit(solution)/shard_map/ppermute | solution.py:64
  131.9 13.3 %collective-permute-start.20 = (bf16[1152,128]{1,0:T(8,128)(2,1)S(1)}, bf16[1152,128]{1,0:T(8,128)(2,1)S(1)}, u32[]{:S(2)}, u32[]{:S(2)}) collective-permute-start(bf16[1152,128]{1,0:T(8,128)(2,1)S(1)} %pad_maximum_fusion.12), channel_id=1, source_target_pairs={{0,2},{1,5},{2,0},{3,7},{4,6},{5,1},{6,4},{7,3},{8,10},{9,13},{10,... | collective-permute-start | bytes 884744 | tf_op jit(solution)/shard_map/ppermute | solution.py:64
  134.7 6.6 %collective-permute-start.7 = (bf16[512,128]{1,0:T(8,128)(2,1)S(1)}, bf16[512,128]{1,0:T(8,128)(2,1)S(1)}, u32[]{:S(2)}, u32[]{:S(2)}) collective-permute-start(bf16[512,128]{1,0:T(8,128)(2,1)S(1)} %fusion.39), channel_id=1, source_target_pairs={{0,16},{1,17},{2,18},{3,19},{4,20},{5,21},{6,22},{7,23},{8,24},{9,... | collective-permute-start | bytes 393224 | tf_op jit(solution)/shard_map/ppermute | solution.py:64
  136.1 8.0 %collective-permute-start.24 = (bf16[512,128]{1,0:T(8,128)(2,1)S(1)}, bf16[512,128]{1,0:T(8,128)(2,1)S(1)}, u32[]{:S(2)}, u32[]{:S(2)}) collective-permute-start(bf16[512,128]{1,0:T(8,128)(2,1)S(1)} %fusion.40), channel_id=1, source_target_pairs={{0,16},{1,17},{2,18},{3,19},{4,20},{5,21},{6,22},{7,23},{8,24},{9,... | collective-permute-start | bytes 393224 | tf_op jit(solution)/shard_map/ppermute | solution.py:64
  142.1 6.5 %collective-permute-start.8 = (bf16[512,128]{1,0:T(8,128)(2,1)S(1)}, bf16[512,128]{1,0:T(8,128)(2,1)}, u32[]{:S(2)}, u32[]{:S(2)}) collective-permute-start(bf16[512,128]{1,0:T(8,128)(2,1)S(1)} %get-tuple-element.11), channel_id=1, source_target_pairs={{0,8},{1,9},{2,10},{3,11},{4,12},{5,13},{6,14},{7,15},{8,0},{9,1},... | collective-permute-start | bytes 393224 | tf_op jit(solution)/shard_map/ppermute | solution.py:64
  144.9 9.0 %collective-permute-start.25 = (bf16[512,128]{1,0:T(8,128)(2,1)}, bf16[512,128]{1,0:T(8,128)(2,1)}, u32[]{:S(2)}, u32[]{:S(2)}) collective-permute-start(bf16[512,128]{1,0:T(8,128)(2,1)} %get-tuple-element.13), channel_id=1, source_target_pairs={{0,8},{1,9},{2,10},{3,11},{4,12},{5,13},{6,14},{7,15},{8,0},{9,1},... | collective-permute-start | bytes 393224 | tf_op jit(solution)/shard_map/ppermute | solution.py:64
  145.1 2.1 collective-permute-start.4
  145.4 6.1 %collective-permute-start.21 = (bf16[2304,128]{1,0:T(8,128)(2,1)S(1)}, bf16[2304,128]{1,0:T(8,128)(2,1)}, u32[]{:S(2)}, u32[]{:S(2)}) collective-permute-start(bf16[2304,128]{1,0:T(8,128)(2,1)S(1)} %pad_maximum_fusion.6), channel_id=1, source_target_pairs={{0,1},{1,0},{2,3},{3,2},{4,5},{5,4},{6,7},{7,6},{8,9},{9,8},{10,11... | collective-permute-start | bytes 1769480 | tf_op jit(solution)/shard_map/ppermute | solution.py:64
  151.3 6.7 %collective-permute-start.9 = (bf16[256,128]{1,0:T(8,128)(2,1)}, bf16[256,128]{1,0:T(8,128)(2,1)}, u32[]{:S(2)}, u32[]{:S(2)}) collective-permute-start(bf16[256,128]{1,0:T(8,128)(2,1)} %get-tuple-element.7), channel_id=1, source_target_pairs={{0,4},{1,3},{2,6},{3,1},{4,0},{5,7},{6,2},{7,5},{8,12},{9,11},{10,... | collective-permute-start | bytes 196616 | tf_op jit(solution)/shard_map/ppermute | solution.py:64
  152.8 5.2 %copy-start.10 = (bf16[256,128]{1,0:T(8,128)(2,1)S(1)}, bf16[256,128]{1,0:T(8,128)(2,1)}, u32[]{:S(2)}) copy-start(bf16[256,128]{1,0:T(8,128)(2,1)} %get-tuple-element.7) | copy-start | bytes 196612
  156.1 4.8 %collective-permute-start.26 = (bf16[256,128]{1,0:T(8,128)(2,1)}, bf16[256,128]{1,0:T(8,128)(2,1)S(1)}, u32[]{:S(2)}, u32[]{:S(2)}) collective-permute-start(bf16[256,128]{1,0:T(8,128)(2,1)} %get-tuple-element.10), channel_id=1, source_target_pairs={{0,4},{1,3},{2,6},{3,1},{4,0},{5,7},{6,2},{7,5},{8,12},{9,11},{10,... | collective-permute-start | bytes 196616 | tf_op jit(solution)/shard_map/ppermute | solution.py:64
  158.8 5.0 %collective-permute-start.10 = (bf16[512,128]{1,0:T(8,128)(2,1)S(1)}, bf16[512,128]{1,0:T(8,128)(2,1)S(1)}, u32[]{:S(2)}, u32[]{:S(2)}) collective-permute-start(bf16[512,128]{1,0:T(8,128)(2,1)S(1)} %pad_maximum_fusion.22), channel_id=1, source_target_pairs={{0,2},{1,5},{2,0},{3,7},{4,6},{5,1},{6,4},{7,3},{8,10},{9,13},{10,... | collective-permute-start | bytes 393224 | tf_op jit(solution)/shard_map/ppermute | solution.py:64
  161.8 5.0 %collective-permute-start.27 = (bf16[512,128]{1,0:T(8,128)(2,1)S(1)}, bf16[512,128]{1,0:T(8,128)(2,1)S(1)}, u32[]{:S(2)}, u32[]{:S(2)}) collective-permute-start(bf16[512,128]{1,0:T(8,128)(2,1)S(1)} %pad_maximum_fusion.23), channel_id=1, source_target_pairs={{0,2},{1,5},{2,0},{3,7},{4,6},{5,1},{6,4},{7,3},{8,10},{9,13},{10,... | collective-permute-start | bytes 393224 | tf_op jit(solution)/shard_map/ppermute | solution.py:64
  164.3 2.9 %collective-permute-start.11 = (f32[144,128]{1,0:T(8,128)S(1)}, f32[144,128]{1,0:T(8,128)S(1)}, u32[]{:S(2)}, u32[]{:S(2)}) collective-permute-start(f32[144,128]{1,0:T(8,128)S(1)} %slice_select_fusion.2), channel_id=1, source_target_pairs={{0,1},{1,0},{2,3},{3,2},{4,5},{5,4},{6,7},{7,6},{8,9},{9,8},{10,11... | collective-permute-start | bytes 221192 | tf_op jit(solution)/shard_map/ppermute | solution.py:64
  167.2 4.0 %collective-permute-start.12 = (bf16[144,128]{1,0:T(8,128)(2,1)S(1)}, bf16[144,128]{1,0:T(8,128)(2,1)S(1)}, u32[]{:S(2)}, u32[]{:S(2)}) collective-permute-start(bf16[144,128]{1,0:T(8,128)(2,1)S(1)} %add_convert_fusion.1), channel_id=1, source_target_pairs={{0,8},{1,9},{2,10},{3,11},{4,12},{5,13},{6,14},{7,15},{8,0},{9,1},... | collective-permute-start | bytes 110600 | tf_op jit(solution)/shard_map/ppermute | solution.py:64
  169.3 1.9 collective-permute-start.28
  171.3 4.7 %collective-permute-start.29 = (bf16[144,128]{1,0:T(8,128)(2,1)S(1)}, bf16[144,128]{1,0:T(8,128)(2,1)S(1)}, u32[]{:S(2)}, u32[]{:S(2)}) collective-permute-start(bf16[144,128]{1,0:T(8,128)(2,1)S(1)} %add_convert_fusion), channel_id=1, source_target_pairs={{0,8},{1,9},{2,10},{3,11},{4,12},{5,13},{6,14},{7,15},{8,0},{9,1},... | collective-permute-start | bytes 110600 | tf_op jit(solution)/shard_map/ppermute | solution.py:64
  173.4 7.1 %collective-permute-start.13 = (bf16[288,128]{1,0:T(8,128)(2,1)S(1)}, bf16[288,128]{1,0:T(8,128)(2,1)S(1)}, u32[]{:S(2)}, u32[]{:S(2)}) collective-permute-start(bf16[288,128]{1,0:T(8,128)(2,1)S(1)} %pad_maximum_fusion.25), channel_id=1, source_target_pairs={{0,16},{1,17},{2,18},{3,19},{4,20},{5,21},{6,22},{7,23},{8,24},{9,... | collective-permute-start | bytes 221192 | tf_op jit(solution)/shard_map/ppermute | solution.py:64
  176.0 6.5 %collective-permute-start.30 = (bf16[288,128]{1,0:T(8,128)(2,1)S(1)}, bf16[288,128]{1,0:T(8,128)(2,1)S(1)}, u32[]{:S(2)}, u32[]{:S(2)}) collective-permute-start(bf16[288,128]{1,0:T(8,128)(2,1)S(1)} %pad_maximum_fusion.27), channel_id=1, source_target_pairs={{0,16},{1,17},{2,18},{3,19},{4,20},{5,21},{6,22},{7,23},{8,24},{9,... | collective-permute-start | bytes 221192 | tf_op jit(solution)/shard_map/ppermute | solution.py:64
  180.5 5.7 %collective-permute-start.14 = (bf16[576,128]{1,0:T(8,128)(2,1)S(1)}, bf16[576,128]{1,0:T(8,128)(2,1)S(1)}, u32[]{:S(2)}, u32[]{:S(2)}) collective-permute-start(bf16[576,128]{1,0:T(8,128)(2,1)S(1)} %pad_maximum_fusion.17), channel_id=1, source_target_pairs={{0,4},{1,3},{2,6},{3,1},{4,0},{5,7},{6,2},{7,5},{8,12},{9,11},{10,... | collective-permute-start | bytes 442376 | tf_op jit(solution)/shard_map/ppermute | solution.py:64
  182.6 6.8 %collective-permute-start.31 = (bf16[576,128]{1,0:T(8,128)(2,1)S(1)}, bf16[576,128]{1,0:T(8,128)(2,1)S(1)}, u32[]{:S(2)}, u32[]{:S(2)}) collective-permute-start(bf16[576,128]{1,0:T(8,128)(2,1)S(1)} %pad_maximum_fusion.19), channel_id=1, source_target_pairs={{0,4},{1,3},{2,6},{3,1},{4,0},{5,7},{6,2},{7,5},{8,12},{9,11},{10,... | collective-permute-start | bytes 442376 | tf_op jit(solution)/shard_map/ppermute | solution.py:64
  186.3 7.6 %collective-permute-start.15 = (bf16[1152,128]{1,0:T(8,128)(2,1)S(1)}, bf16[1152,128]{1,0:T(8,128)(2,1)S(1)}, u32[]{:S(2)}, u32[]{:S(2)}) collective-permute-start(bf16[1152,128]{1,0:T(8,128)(2,1)S(1)} %pad_maximum_fusion.11), channel_id=1, source_target_pairs={{0,2},{1,5},{2,0},{3,7},{4,6},{5,1},{6,4},{7,3},{8,10},{9,13},{10,... | collective-permute-start | bytes 884744 | tf_op jit(solution)/shard_map/ppermute | solution.py:64
  189.5 7.6 %collective-permute-start.32 = (bf16[1152,128]{1,0:T(8,128)(2,1)S(1)}, bf16[1152,128]{1,0:T(8,128)(2,1)S(1)}, u32[]{:S(2)}, u32[]{:S(2)}) collective-permute-start(bf16[1152,128]{1,0:T(8,128)(2,1)S(1)} %pad_maximum_fusion.13), channel_id=1, source_target_pairs={{0,2},{1,5},{2,0},{3,7},{4,6},{5,1},{6,4},{7,3},{8,10},{9,13},{10,... | collective-permute-start | bytes 884744 | tf_op jit(solution)/shard_map/ppermute | solution.py:64
  194.1 3.2 %collective-permute-start.16 = (bf16[2304,128]{1,0:T(8,128)(2,1)S(1)}, bf16[2304,128]{1,0:T(8,128)(2,1)S(1)}, u32[]{:S(2)}, u32[]{:S(2)}) collective-permute-start(bf16[2304,128]{1,0:T(8,128)(2,1)S(1)} %pad_maximum_fusion.5), channel_id=1, source_target_pairs={{0,1},{1,0},{2,3},{3,2},{4,5},{5,4},{6,7},{7,6},{8,9},{9,8},{10,11... | collective-permute-start | bytes 1769480 | tf_op jit(solution)/shard_map/ppermute | solution.py:64
  197.2 2.1 collective-permute-start.33
  200.3 6.3 %copy-start.12 = (bf16[4608,256]{1,0:T(8,128)(2,1)S(1)}, bf16[4608,256]{1,0:T(8,128)(2,1)}, u32[]{:S(2)}) copy-start(bf16[4608,256]{1,0:T(8,128)(2,1)} %copy-done.11) | copy-start | bytes 7077892
  200.3 6.3 %copy-start.15 = (f32[256]{0:T(256)S(1)}, f32[256]{0:T(256)}, u32[]{:S(2)}) copy-start(f32[256]{0:T(256)} %param.19) | copy-start | bytes 3076
  210.2 2.8 collective-permute-start.44
  211.6 3.7 %collective-permute-start.34 = (bf16[2304,128]{1,0:T(8,128)(2,1)S(1)}, bf16[2304,128]{1,0:T(8,128)(2,1)S(1)}, u32[]{:S(2)}, u32[]{:S(2)}) collective-permute-start(bf16[2304,128]{1,0:T(8,128)(2,1)S(1)} %select_convert_fusion.1), channel_id=1, source_target_pairs={{0,1},{1,0},{2,3},{3,2},{4,5},{5,4},{6,7},{7,6},{8,9},{9,8},{10,11... | collective-permute-start | bytes 1769480 | tf_op jit(solution)/shard_map/ppermute | solution.py:64
  213.2 6.8 %collective-permute-start.45 = (bf16[1152,128]{1,0:T(8,128)(2,1)S(1)}, bf16[1152,128]{1,0:T(8,128)(2,1)S(1)}, u32[]{:S(2)}, u32[]{:S(2)}) collective-permute-start(bf16[1152,128]{1,0:T(8,128)(2,1)S(1)} %select_convert_fusion.2), channel_id=1, source_target_pairs={{0,2},{1,5},{2,0},{3,7},{4,6},{5,1},{6,4},{7,3},{8,10},{9,13},{10,... | collective-permute-start | bytes 884744 | tf_op jit(solution)/shard_map/ppermute | solution.py:64
  215.5 8.1 %collective-permute-start.35 = (bf16[1152,128]{1,0:T(8,128)(2,1)S(1)}, bf16[1152,128]{1,0:T(8,128)(2,1)S(1)}, u32[]{:S(2)}, u32[]{:S(2)}) collective-permute-start(bf16[1152,128]{1,0:T(8,128)(2,1)S(1)} %select_convert_fusion.3), channel_id=1, source_target_pairs={{0,2},{1,5},{2,0},{3,7},{4,6},{5,1},{6,4},{7,3},{8,10},{9,13},{10,... | collective-permute-start | bytes 884744 | tf_op jit(solution)/shard_map/ppermute | solution.py:64
  220.1 6.1 %collective-permute-start.46 = (bf16[576,128]{1,0:T(8,128)(2,1)S(1)}, bf16[576,128]{1,0:T(8,128)(2,1)S(1)}, u32[]{:S(2)}, u32[]{:S(2)}) collective-permute-start(bf16[576,128]{1,0:T(8,128)(2,1)S(1)} %select_convert_fusion.6), channel_id=1, source_target_pairs={{0,4},{1,3},{2,6},{3,1},{4,0},{5,7},{6,2},{7,5},{8,12},{9,11},{10,... | collective-permute-start | bytes 442376 | tf_op jit(solution)/shard_map/ppermute | solution.py:64
  223.8 5.6 %collective-permute-start.36 = (bf16[576,128]{1,0:T(8,128)(2,1)S(1)}, bf16[576,128]{1,0:T(8,128)(2,1)S(1)}, u32[]{:S(2)}, u32[]{:S(2)}) collective-permute-start(bf16[576,128]{1,0:T(8,128)(2,1)S(1)} %select_convert_fusion.7), channel_id=1, source_target_pairs={{0,4},{1,3},{2,6},{3,1},{4,0},{5,7},{6,2},{7,5},{8,12},{9,11},{10,... | collective-permute-start | bytes 442376 | tf_op jit(solution)/shard_map/ppermute | solution.py:64
  226.3 7.2 %collective-permute-start.47 = (bf16[288,128]{1,0:T(8,128)(2,1)S(1)}, bf16[288,128]{1,0:T(8,128)(2,1)S(1)}, u32[]{:S(2)}, u32[]{:S(2)}) collective-permute-start(bf16[288,128]{1,0:T(8,128)(2,1)S(1)} %select_convert_fusion.10), channel_id=1, source_target_pairs={{0,16},{1,17},{2,18},{3,19},{4,20},{5,21},{6,22},{7,23},{8,24},{9,... | collective-permute-start | bytes 221192 | tf_op jit(solution)/shard_map/ppermute | solution.py:64
  229.4 5.6 %collective-permute-start.37 = (bf16[288,128]{1,0:T(8,128)(2,1)S(1)}, bf16[288,128]{1,0:T(8,128)(2,1)S(1)}, u32[]{:S(2)}, u32[]{:S(2)}) collective-permute-start(bf16[288,128]{1,0:T(8,128)(2,1)S(1)} %select_convert_fusion.11), channel_id=1, source_target_pairs={{0,16},{1,17},{2,18},{3,19},{4,20},{5,21},{6,22},{7,23},{8,24},{9,... | collective-permute-start | bytes 221192 | tf_op jit(solution)/shard_map/ppermute | solution.py:64
  233.5 4.0 %collective-permute-start.48 = (bf16[144,128]{1,0:T(8,128)(2,1)S(1)}, bf16[144,128]{1,0:T(8,128)(2,1)S(1)}, u32[]{:S(2)}, u32[]{:S(2)}) collective-permute-start(bf16[144,128]{1,0:T(8,128)(2,1)S(1)} %select_convert_fusion.12), channel_id=1, source_target_pairs={{0,8},{1,9},{2,10},{3,11},{4,12},{5,13},{6,14},{7,15},{8,0},{9,1},... | collective-permute-start | bytes 110600 | tf_op jit(solution)/shard_map/ppermute | solution.py:64
  235.0 4.0 %collective-permute-start.38 = (bf16[144,128]{1,0:T(8,128)(2,1)S(1)}, bf16[144,128]{1,0:T(8,128)(2,1)S(1)}, u32[]{:S(2)}, u32[]{:S(2)}) collective-permute-start(bf16[144,128]{1,0:T(8,128)(2,1)S(1)} %select_convert_fusion.13), channel_id=1, source_target_pairs={{0,8},{1,9},{2,10},{3,11},{4,12},{5,13},{6,14},{7,15},{8,0},{9,1},... | collective-permute-start | bytes 110600 | tf_op jit(solution)/shard_map/ppermute | solution.py:64
  239.2 4.3 %collective-permute-start.39 = (bf16[144,128]{1,0:T(8,128)(2,1)S(1)}, bf16[144,128]{1,0:T(8,128)(2,1)S(1)}, u32[]{:S(2)}, u32[]{:S(2)}) collective-permute-start(bf16[144,128]{1,0:T(8,128)(2,1)S(1)} %get-tuple-element.136), channel_id=1, source_target_pairs={{0,8},{1,9},{2,10},{3,11},{4,12},{5,13},{6,14},{7,15},{8,0},{9,1},... | collective-permute-start | bytes 110600 | tf_op jit(solution)/shard_map/ppermute | solution.py:64
  240.1 4.5 %collective-permute-start.49 = (bf16[144,128]{1,0:T(8,128)(2,1)S(1)}, bf16[144,128]{1,0:T(8,128)(2,1)S(1)}, u32[]{:S(2)}, u32[]{:S(2)}) collective-permute-start(bf16[144,128]{1,0:T(8,128)(2,1)S(1)} %get-tuple-element.137), channel_id=1, source_target_pairs={{0,8},{1,9},{2,10},{3,11},{4,12},{5,13},{6,14},{7,15},{8,0},{9,1},... | collective-permute-start | bytes 110600 | tf_op jit(solution)/shard_map/ppermute | solution.py:64
  243.5 6.1 %collective-permute-start.40 = (bf16[288,128]{1,0:T(8,128)(2,1)S(1)}, bf16[288,128]{1,0:T(8,128)(2,1)S(1)}, u32[]{:S(2)}, u32[]{:S(2)}) collective-permute-start(bf16[288,128]{1,0:T(8,128)(2,1)S(1)} %pad_maximum_fusion.28), channel_id=1, source_target_pairs={{0,16},{1,17},{2,18},{3,19},{4,20},{5,21},{6,22},{7,23},{8,24},{9,... | collective-permute-start | bytes 221192 | tf_op jit(solution)/shard_map/ppermute | solution.py:64
  244.6 7.3 %collective-permute-start.50 = (bf16[288,128]{1,0:T(8,128)(2,1)S(1)}, bf16[288,128]{1,0:T(8,128)(2,1)S(1)}, u32[]{:S(2)}, u32[]{:S(2)}) collective-permute-start(bf16[288,128]{1,0:T(8,128)(2,1)S(1)} %pad_maximum_fusion.29), channel_id=1, source_target_pairs={{0,16},{1,17},{2,18},{3,19},{4,20},{5,21},{6,22},{7,23},{8,24},{9,... | collective-permute-start | bytes 221192 | tf_op jit(solution)/shard_map/ppermute | solution.py:64
  249.6 6.9 %collective-permute-start.41 = (bf16[576,128]{1,0:T(8,128)(2,1)S(1)}, bf16[576,128]{1,0:T(8,128)(2,1)S(1)}, u32[]{:S(2)}, u32[]{:S(2)}) collective-permute-start(bf16[576,128]{1,0:T(8,128)(2,1)S(1)} %pad_maximum_fusion.20), channel_id=1, source_target_pairs={{0,4},{1,3},{2,6},{3,1},{4,0},{5,7},{6,2},{7,5},{8,12},{9,11},{10,... | collective-permute-start | bytes 442376 | tf_op jit(solution)/shard_map/ppermute | solution.py:64
  252.0 7.7 %collective-permute-start.51 = (bf16[576,128]{1,0:T(8,128)(2,1)S(1)}, bf16[576,128]{1,0:T(8,128)(2,1)S(1)}, u32[]{:S(2)}, u32[]{:S(2)}) collective-permute-start(bf16[576,128]{1,0:T(8,128)(2,1)S(1)} %pad_maximum_fusion.21), channel_id=1, source_target_pairs={{0,4},{1,3},{2,6},{3,1},{4,0},{5,7},{6,2},{7,5},{8,12},{9,11},{10,... | collective-permute-start | bytes 442376 | tf_op jit(solution)/shard_map/ppermute | solution.py:64
  259.8 6.8 %collective-permute-start.42 = (bf16[1152,128]{1,0:T(8,128)(2,1)S(1)}, bf16[1152,128]{1,0:T(8,128)(2,1)S(1)}, u32[]{:S(2)}, u32[]{:S(2)}) collective-permute-start(bf16[1152,128]{1,0:T(8,128)(2,1)S(1)} %pad_maximum_fusion.14), channel_id=1, source_target_pairs={{0,2},{1,5},{2,0},{3,7},{4,6},{5,1},{6,4},{7,3},{8,10},{9,13},{10,... | collective-permute-start | bytes 884744 | tf_op jit(solution)/shard_map/ppermute | solution.py:64
  262.0 7.8 %collective-permute-start.52 = (bf16[1152,128]{1,0:T(8,128)(2,1)S(1)}, bf16[1152,128]{1,0:T(8,128)(2,1)S(1)}, u32[]{:S(2)}, u32[]{:S(2)}) collective-permute-start(bf16[1152,128]{1,0:T(8,128)(2,1)S(1)} %pad_maximum_fusion.15), channel_id=1, source_target_pairs={{0,2},{1,5},{2,0},{3,7},{4,6},{5,1},{6,4},{7,3},{8,10},{9,13},{10,... | collective-permute-start | bytes 884744 | tf_op jit(solution)/shard_map/ppermute | solution.py:64
  266.8 3.2 %collective-permute-start.43 = (bf16[2304,128]{1,0:T(8,128)(2,1)S(1)}, bf16[2304,128]{1,0:T(8,128)(2,1)S(1)}, u32[]{:S(2)}, u32[]{:S(2)}) collective-permute-start(bf16[2304,128]{1,0:T(8,128)(2,1)S(1)} %pad_maximum_fusion.8), channel_id=1, source_target_pairs={{0,1},{1,0},{2,3},{3,2},{4,5},{5,4},{6,7},{7,6},{8,9},{9,8},{10,11... | collective-permute-start | bytes 1769480 | tf_op jit(solution)/shard_map/ppermute | solution.py:64
  270.0 2.1 collective-permute-start.53
  (7 other events, 15.5 us)

commit v2 on v1

v2 whole, which is shorter than its diff:
```python
import functools

import jax
import jax.numpy as jnp
from jax import lax
from jax.experimental import pallas as pl
from jax.experimental.pallas import tpu as pltpu
from jax.sharding import PartitionSpec as P

HEAD_DIM = 128
CHUNKS = 2
EXTRA = 16

epsilon = 1e-06
softcap = 50.0
query_scale = 1.0 / 12.0
rope_base = 10000.0
smoothing = 0.1
penalty = 1.0
loss_weight = 0.0625

bf16 = jnp.bfloat16
f32 = jnp.float32
AXES = ("dp", "mp")


class Ladder:
    def __init__(self, dp, mp):
        self.dp, self.mp = dp, mp
        dp_bits, mp_bits = dp.bit_length() - 1, mp.bit_length() - 1
        assert dp == 1 << dp_bits and mp == 1 << mp_bits
        self.dp_bits = dp_bits
        self.cores = [(("mp", k), ("mp", k)) for k in range(mp_bits - 1, -1, -1)]

    def route(self, even, odd):
        if self.dp_bits < len(even):
            even = odd = tuple(range(self.dp_bits))
        rest = tuple(range(len(even), self.dp_bits))
        return [(("dp", j), ("dp", k)) for j, k in zip(even + rest, odd + rest)]

    def pairs(self, step):
        result = []
        for d in range(self.dp):
            for m in range(self.mp):
                axis, k = step[m & 1]
                peer = (d ^ (1 << k), m) if axis == "dp" else (d, m ^ (1 << k))
                result.append((d * self.mp + m, peer[0] * self.mp + peer[1]))
        return result

    def static_bit(self, step, d, m):
        axis, k = step[m & 1]
        return ((d if axis == "dp" else m) >> k) & 1

    def bit(self, step):
        d, m = lax.axis_index("dp"), lax.axis_index("mp")
        (axis, even), (_, odd) = step
        value = d if axis == "dp" else m
        if even == odd:
            return (value >> even) & 1
        return jnp.where(m & 1 == 0, (value >> even) & 1, (value >> odd) & 1)

    def swap(self, value, step):
        return lax.ppermute(value, AXES, self.pairs(step))

    def scatter(self, value, steps, wire):
        for step in steps:
            half = value.shape[0] // 2
            up = self.bit(step) == 1
            low, high = value[:half], value[half:]
            got = self.swap(jnp.where(up, low, high).astype(wire), step)
            value = jnp.where(up, high, low) + got.astype(f32)
        return value

    def gather(self, value, steps):
        for step in reversed(steps):
            got = self.swap(value, step)
            up = self.bit(step) == 1
            value = jnp.concatenate([jnp.where(up, got, value), jnp.where(up, value, got)], axis=0)
        return value

    def quarters(self, value, core, steps):
        own = self.gather(value, steps[1:])
        far = self.swap(own, steps[0])
        return own, far, self.swap(own, core), self.swap(far, core)

    def order(self, steps):
        where = {}
        for d in range(self.dp):
            for m in range(self.mp):
                p = 0
                for step in steps:
                    p = 2 * p + self.static_bit(step, d, m)
                where[p] = d * self.mp + m
        return [where[p] for p in range(self.dp * self.mp)]

    def position(self, steps):
        p = 0
        for step in steps:
            p = 2 * p + self.bit(step)
        return p

    def piece(self, core, step, k):
        up = self.bit(core)
        if k < 2:
            near = self.bit(step)
            return up, near if k == 0 else 1 - near
        d, m = lax.axis_index("dp"), lax.axis_index("mp") ^ (1 << core[0][1])
        (axis, even), (_, odd) = step
        value = d if axis == "dp" else m
        near = jnp.where(m & 1 == 0, (value >> even) & 1, (value >> odd) & 1)
        return 1 - up, near if k == 2 else 1 - near


VMEM = pl.BlockSpec(memory_space=pltpu.VMEM)
SMALL = pltpu.CompilerParams(vmem_limit_bytes=6 << 20)


def aligned(index, size):
    return pl.ds(pl.multiple_of(index * size, size), size)


def square_rows(total, ref, first):
    high = total.astype(bf16).astype(f32)
    place = lax.broadcasted_iota(jnp.int32, (EXTRA, total.shape[1]), 0)
    rows = jnp.where(place == 0, high, jnp.where(place == 1, total - high, 0.0))
    ref[pl.ds(first, EXTRA), :] = rows.astype(bf16)


def column(ref, width):
    return jnp.broadcast_to(ref[...][None, :], (width, ref.shape[0])).T


def project_kernel(ladder, step, groups, heads, chunks, residual_ref, gain_ref, *refs):
    weights, outs = refs[:3], refs[3 : 3 + 3 * chunks]
    query_ref, key_ref, value_ref = refs[-4:-1]
    copies = [pltpu.make_async_copy(w, r, refs[-1].at[i]) for i, (w, r) in enumerate(zip(weights, refs[-4:-1]))]
    for copy in copies:
        copy.start()
    up = ladder.bit(step)
    tokens = residual_ref.shape[1]
    width = tokens // chunks
    wide = heads * HEAD_DIM
    residual = residual_ref[...].astype(f32)
    scaled = (residual * column(gain_ref, tokens)).astype(bf16)
    square = jnp.sum(residual * residual, axis=0, keepdims=True)
    for copy in copies:
        copy.wait()
    sends, keeps, squares = outs[:chunks], outs[chunks : 2 * chunks], outs[2 * chunks :]
    half = groups // 2

    def times(weight):
        return lax.dot_general(weight, scaled, (((0,), (0,)), ((), ())), preferred_element_type=f32)

    for refs, side in ((sends, 1 - up), (keeps, up)):
        for j in range(half):
            g = side * half + j
            first = j * (wide + 2 * HEAD_DIM)
            for weight, size in ((query_ref, wide), (key_ref, HEAD_DIM), (value_ref, HEAD_DIM)):
                value = times(weight[:, aligned(g, size)])
                for c, ref in enumerate(refs):
                    ref[pl.ds(first, size), :] = value[:, c * width : (c + 1) * width].astype(ref.dtype)
                first += size
    for c in range(chunks):
        part = square[:, c * width : (c + 1) * width]
        squares[c][...] = part
        square_rows(part, sends[c], half * (wide + 2 * HEAD_DIM))


def project(ladder, step, groups, heads, residual, gain, query, key, value):
    width = residual.shape[1] // CHUNKS
    rows = groups // 2 * (heads + 2) * HEAD_DIM
    shapes = (
        [jax.ShapeDtypeStruct((rows + EXTRA, width), bf16)] * CHUNKS
        + [jax.ShapeDtypeStruct((rows, width), f32)] * CHUNKS
        + [jax.ShapeDtypeStruct((1, width), f32)] * CHUNKS
    )
    outs = pl.pallas_call(
        functools.partial(project_kernel, ladder, step, groups, heads, CHUNKS),
        out_shape=shapes,
        in_specs=[VMEM] * 2 + [pl.BlockSpec(memory_space=pltpu.HBM)] * 3,
        scratch_shapes=[
            pltpu.VMEM(query.shape, bf16),
            pltpu.VMEM(key.shape, bf16),
            pltpu.VMEM(value.shape, bf16),
            pltpu.SemaphoreType.DMA((3,)),
        ],
        compiler_params=pltpu.CompilerParams(vmem_limit_bytes=10 << 20),
        cost_estimate=pl.CostEstimate(
            flops=4 * rows * residual.size, bytes_accessed=2 * (query.size + key.size + value.size), transcendentals=0
        ),
    )(residual, gain, query, key, value)
    return outs[:CHUNKS], outs[CHUNKS : 2 * CHUNKS], outs[2 * CHUNKS :]


def step_kernel(ladder, step, halve, own_ref, got_ref, square_ref, send_ref, keep_ref, total_ref):
    rows, kept = own_ref.shape[0], keep_ref.shape[0]
    total = square_ref[...] + jnp.sum(got_ref[pl.ds(rows, EXTRA), :].astype(f32), axis=0, keepdims=True)
    total_ref[...] = total
    square_rows(total, send_ref, kept)
    if halve:
        up = ladder.bit(step)
        here, there = aligned(up, kept), aligned(1 - up, kept)
        send_ref[pl.ds(0, kept), :] = (own_ref[there, :] + got_ref[there, :].astype(f32)).astype(bf16)
        keep_ref[...] = own_ref[here, :] + got_ref[here, :].astype(f32)
    else:
        value = own_ref[...] + got_ref[pl.ds(0, rows), :].astype(f32)
        send_ref[pl.ds(0, kept), :] = value.astype(bf16)
        keep_ref[...] = value


def advance(ladder, step, halve, own, got, square):
    rows, width = own.shape
    kept = rows // 2 if halve else rows
    return pl.pallas_call(
        functools.partial(step_kernel, ladder, step, halve),
        out_shape=(
            jax.ShapeDtypeStruct((kept + EXTRA, width), bf16),
            jax.ShapeDtypeStruct((kept, width), f32),
            jax.ShapeDtypeStruct((1, width), f32),
        ),
        in_specs=[VMEM] * 3,
        compiler_params=SMALL,
        cost_estimate=pl.CostEstimate(flops=2 * own.size, bytes_accessed=12 * own.size, transcendentals=0),
    )(own, got, square)


def attention_kernel(start, heads, model_width, own_ref, got_ref, square_ref, cos_ref, sin_ref, *refs):
    oldk_ref, oldv_ref = refs[:2] if start else (None, None)
    out_ref, k_ref, v_ref = refs[-3:]
    width = own_ref.shape[1]
    half = HEAD_DIM // 2
    body = own_ref.shape[0]
    tail = jnp.sum(got_ref[pl.ds(body, EXTRA), :].astype(f32), axis=0, keepdims=True)
    inverse = lax.rsqrt((square_ref[...] + tail) / model_width + epsilon)
    lanes = pl.ds(start, width)
    cosine, sine = cos_ref[:, lanes], sin_ref[:, lanes]

    def rows(first, count):
        return (own_ref[pl.ds(first, count), :] + got_ref[pl.ds(first, count), :].astype(f32)) * inverse

    def rotated(first):
        front, back = rows(first, half), rows(first + half, half)
        return jnp.concatenate([front * cosine - back * sine, back * cosine + front * sine], axis=0).astype(bf16)

    base = heads * HEAD_DIM
    k_ref[:, pl.ds(start, width)] = rotated(base)
    v_ref[:, pl.ds(start, width)] = rows(base + HEAD_DIM, HEAD_DIM).astype(bf16)
    if start:
        k_ref[:, pl.ds(0, start)] = oldk_ref[...]
        v_ref[:, pl.ds(0, start)] = oldv_ref[...]
    keys, values = k_ref[...], v_ref[...]
    span = start + width
    allowed = lax.broadcasted_iota(jnp.int32, (span, width), 0) <= lax.broadcasted_iota(jnp.int32, (span, width), 1) + start
    for h in range(heads):
        query = rotated(h * HEAD_DIM)
        score = lax.dot_general(keys, query, (((0,), (0,)), ((), ())), preferred_element_type=f32) * query_scale
        capped = softcap * jnp.tanh(score / softcap)
        weights = jnp.where(allowed, jnp.exp(capped), 0.0)
        total = jnp.sum(weights, axis=0, keepdims=True)
        mixed = jnp.dot(values, weights.astype(bf16), preferred_element_type=f32)
        out_ref[pl.ds(h * HEAD_DIM, HEAD_DIM), :] = (mixed / total).astype(bf16)


def attend(start, heads, model_width, own, got, square, cosine, sine, *old):
    width = own.shape[1]
    span = start + width
    return pl.pallas_call(
        functools.partial(attention_kernel, start, heads, model_width),
        out_shape=(
            jax.ShapeDtypeStruct((heads * HEAD_DIM, width), bf16),
            jax.ShapeDtypeStruct((HEAD_DIM, span), bf16),
            jax.ShapeDtypeStruct((HEAD_DIM, span), bf16),
        ),
        compiler_params=SMALL,
        cost_estimate=pl.CostEstimate(
            flops=4 * heads * HEAD_DIM * span * width, bytes_accessed=8 * own.size, transcendentals=2 * heads * span * width
        ),
    )(own, got, square, cosine, sine, *old)


def out_kernel(ladder, near, core, own_ref, got_ref, weight_ref, send_ref, keep_ref):
    rows, columns = send_ref.shape[0], own_ref.shape[0]
    order, up = ladder.bit(near), ladder.bit(core)
    here, there = aligned(order, columns), aligned(1 - order, columns)
    for ref, half in ((send_ref, 1 - up), (keep_ref, up)):
        part = aligned(half, rows)
        ref[...] = jnp.dot(weight_ref[part, here], own_ref[...], preferred_element_type=f32) + jnp.dot(
            weight_ref[part, there], got_ref[...], preferred_element_type=f32
        )


def project_out(ladder, near, core, own, got, weight):
    shape = jax.ShapeDtypeStruct((weight.shape[0] // 2, own.shape[1]), f32)
    return pl.pallas_call(
        functools.partial(out_kernel, ladder, near, core),
        out_shape=(shape, shape),
        in_specs=[VMEM] * 3,
        compiler_params=SMALL,
        cost_estimate=pl.CostEstimate(
            flops=2 * weight.size * own.shape[1], bytes_accessed=2 * weight.size, transcendentals=0
        ),
    )(own, got, weight)


def pack_kernel(ladder, core, keep_ref, got_ref, gain_ref, packed_ref):
    head = keep_ref[...] + got_ref[...]
    rows, width = head.shape
    gain = column(gain_ref, width)
    gain = jnp.where(ladder.bit(core) == 1, gain[rows:], gain[:rows])
    packed_ref[pl.ds(0, rows), :] = (head * gain).astype(bf16)
    square_rows(jnp.sum(head * head, axis=0, keepdims=True), packed_ref, rows)


def pack(ladder, core, keep, got, gain):
    return pl.pallas_call(
        functools.partial(pack_kernel, ladder, core),
        out_shape=jax.ShapeDtypeStruct((keep.shape[0] + EXTRA, keep.shape[1]), bf16),
        in_specs=[VMEM] * 3,
        compiler_params=SMALL,
        cost_estimate=pl.CostEstimate(flops=4 * keep.size, bytes_accessed=10 * keep.size, transcendentals=0),
    )(keep, got, gain)


def targets(ladder, core, step, places, block, count, k):
    if not places:
        return [pl.ds((k * count + p) * block, block) for p in range(count)]
    side, near = ladder.piece(core, step, k)
    result = []
    for p in range(count):
        a, b, c, d = (places[q * count + p] for q in range(4))
        place = jnp.where(side == 0, jnp.where(near == 0, a, b), jnp.where(near == 0, c, d))
        result.append(aligned(place, block))
    return result


def assemble_kernel(ladder, core, step, places, block, *refs):
    out_ref = refs[4]
    count = refs[0].shape[0] // block
    for k in range(4):
        for p, target in enumerate(targets(ladder, core, step, places, block, count, k)):
            out_ref[target, :] = refs[k][pl.ds(p * block, block), :]


def assemble(ladder, core, step, places, block, pieces):
    rows, width = pieces[0].shape
    return pl.pallas_call(
        functools.partial(assemble_kernel, ladder, core, step, places, block),
        out_shape=jax.ShapeDtypeStruct((4 * rows, width), bf16),
        in_specs=[VMEM] * 4,
        compiler_params=pltpu.CompilerParams(vmem_limit_bytes=8 << 20),
        cost_estimate=pl.CostEstimate(flops=0, bytes_accessed=16 * rows * width, transcendentals=0),
    )(*pieces)


def hidden_kernel(ladder, core, step, places, first, block, model_width, *refs):
    pieces = refs[:4]
    residual_ref, enc_any, bias_ref, dec_any = refs[4:8]
    hidden_ref, low_ref, slope_ref, activity_ref, send_ref, keep_ref = refs[8:14]
    enc_ref, dec_ref, sems = refs[14:]
    load_enc = pltpu.make_async_copy(enc_any, enc_ref, sems.at[0])
    load_dec = pltpu.make_async_copy(dec_any, dec_ref, sems.at[1])
    load_enc.start()
    load_dec.start()
    width = pieces[0].shape[1]
    stride = block + EXTRA
    count = pieces[0].shape[0] // stride
    lanes = pl.ds(first, width)
    tail = jnp.zeros((EXTRA, width), f32)
    for ref in pieces:
        for p in range(count):
            tail = tail + ref[pl.ds(p * stride + block, EXTRA), :].astype(f32)
    inverse = lax.rsqrt(jnp.sum(tail, axis=0, keepdims=True) / model_width + epsilon)
    for k, ref in enumerate(pieces):
        for p, target in enumerate(targets(ladder, core, step, places, block, count, k)):
            value = residual_ref[target, lanes].astype(f32) + ref[pl.ds(p * stride, block), :].astype(f32) * inverse
            hidden_ref[target, :] = value.astype(bf16)
    load_enc.wait()
    preact = lax.dot_general(enc_ref[...], hidden_ref[...], (((0,), (0,)), ((), ())), preferred_element_type=f32)
    scaled = (preact + column(bias_ref, width)) / smoothing
    active = smoothing * (jnp.maximum(scaled, 0.0) + jnp.log1p(jnp.exp(-jnp.abs(scaled))))
    low = active.astype(bf16)
    low_ref[...] = low
    slope_ref[...] = jax.nn.sigmoid(scaled)
    activity_ref[...] = jnp.sum(active, axis=1, keepdims=True)
    half = send_ref.shape[0]
    up = ladder.bit(core)
    tile = half // 9
    load_dec.wait()
    for ref, side in ((send_ref, 1 - up), (keep_ref, up)):
        for t in range(9):
            rows = pl.ds(pl.multiple_of(side * half + t * tile, tile), tile)
            value = lax.dot_general(dec_ref[:, rows], low, (((0,), (0,)), ((), ())), preferred_element_type=f32)
            ref[pl.ds(t * tile, tile), :] = value.astype(ref.dtype)


def encode(ladder, core, step, places, first, block, pieces, residual, encoder, bias, decoder):
    width = pieces[0].shape[1]
    model_width, latents = encoder.shape
    any_space = pl.BlockSpec(memory_space=pltpu.HBM)
    return pl.pallas_call(
        functools.partial(hidden_kernel, ladder, core, step, places, first, block, model_width),
        out_shape=(
            jax.ShapeDtypeStruct((model_width, width), bf16),
            jax.ShapeDtypeStruct((latents, width), bf16),
            jax.ShapeDtypeStruct((latents, width), f32),
            jax.ShapeDtypeStruct((latents, 1), f32),
            jax.ShapeDtypeStruct((model_width // 2, width), bf16),
            jax.ShapeDtypeStruct((model_width // 2, width), f32),
        ),
        in_specs=[VMEM] * 5 + [any_space, VMEM, any_space],
        scratch_shapes=[
            pltpu.VMEM(encoder.shape, bf16),
            pltpu.VMEM(decoder.shape, bf16),
            pltpu.SemaphoreType.DMA((2,)),
        ],
        compiler_params=pltpu.CompilerParams(vmem_limit_bytes=(5 * encoder.size + (8 << 20))),
        cost_estimate=pl.CostEstimate(
            flops=4 * encoder.size * width, bytes_accessed=4 * encoder.size, transcendentals=4 * latents * width
        ),
    )(*pieces, residual, encoder, bias, decoder)


def final_kernel(ladder, core, steps, *refs):
    chunks = CHUNKS
    errors = [refs[4 * c : 4 * c + 4] for c in range(chunks)]
    refs = refs[4 * chunks :]
    hidden_any, low, slope, activity = (refs[i * chunks : (i + 1) * chunks] for i in range(4))
    dec_any, norm_ref, enc_out, bias_ref, dec_out = refs[4 * chunks : 4 * chunks + 5]
    hidden, dec_ref, error, enc_buf, dec_buf, in_sem, enc_sem, dec_sem = refs[4 * chunks + 5 :]
    width = hidden_any[0].shape[1]
    load_dec = pltpu.make_async_copy(dec_any, dec_ref, in_sem.at[0])
    load_dec.start()
    loads = []
    for c in range(chunks):
        place = hidden.at[:, pl.ds(c * width, width)]
        loads.append(pltpu.make_async_copy(hidden_any[c], place, in_sem.at[c + 1]))
        loads[-1].start()
    quarter = errors[0][0].shape[0]
    for c in range(chunks):
        for k in range(4):
            side, near = ladder.piece(core, steps[c], k)
            error[aligned(2 * side + near, quarter), pl.ds(c * width, width)] = errors[c][k][...]
    lows = jnp.concatenate([ref[...] for ref in low], axis=1)
    slopes = jnp.concatenate([ref[...] for ref in slope], axis=1)
    norms = column(norm_ref, 128)[:, :1]
    load_dec.wait()
    feedback = jnp.dot(dec_ref[...], error[...], preferred_element_type=f32)
    turned = (loss_weight * (2.0 * feedback + penalty * norms) * slopes).T
    bias_ref[...] = jnp.sum(turned, axis=0, keepdims=True)
    turned = turned.astype(bf16)
    copies = []

    def send(buf, out, index, sem):
        copies.append(pltpu.make_async_copy(buf.at[index], out.at[index], sem))
        copies[-1].start()

    for load in loads:
        load.wait()
    tile = hidden.shape[0] // 9
    for t in range(9):
        rows = pl.ds(t * tile, tile)
        enc_buf[rows, :] = jnp.dot(hidden[rows, :], turned, preferred_element_type=f32).astype(bf16)
        send(enc_buf, enc_out, (rows, slice(None)), enc_sem.at[t])
    ratio = loss_weight * penalty * sum(ref[...] for ref in activity) / norms
    for t in range(9):
        columns = pl.ds(t * tile, tile)
        outer = lax.dot_general(lows, error[columns, :], (((1,), (1,)), ((), ())), preferred_element_type=f32)
        dec_buf[:, columns] = (2.0 * loss_weight * outer + ratio * dec_ref[:, columns].astype(f32)).astype(bf16)
        send(dec_buf, dec_out, (slice(None), columns), dec_sem.at[t])
    for copy in copies:
        copy.wait()


def gradients(ladder, core, steps, errors, hidden, low, slope, activity, decoder, norms):
    latents, model_width = decoder.shape
    tokens = CHUNKS * hidden[0].shape[1]
    hbm = pl.BlockSpec(memory_space=pltpu.HBM)
    flat = [piece for pieces in errors for piece in pieces]
    return pl.pallas_call(
        functools.partial(final_kernel, ladder, core, steps),
        out_shape=(
            jax.ShapeDtypeStruct((model_width, latents), bf16),
            jax.ShapeDtypeStruct((1, latents), f32),
            jax.ShapeDtypeStruct((latents, model_width), bf16),
        ),
        in_specs=[VMEM] * len(flat) + [hbm] * CHUNKS + [VMEM] * (3 * CHUNKS) + [hbm, VMEM],
        out_specs=(hbm, VMEM, hbm),
        scratch_shapes=[
            pltpu.VMEM((model_width, tokens), bf16),
            pltpu.VMEM((latents, model_width), bf16),
            pltpu.VMEM((model_width, tokens), bf16),
            pltpu.VMEM((model_width, latents), bf16),
            pltpu.VMEM((latents, model_width), bf16),
            pltpu.SemaphoreType.DMA((1 + CHUNKS,)),
            pltpu.SemaphoreType.DMA((9,)),
            pltpu.SemaphoreType.DMA((9,)),
        ],
        compiler_params=pltpu.CompilerParams(
            vmem_limit_bytes=6 * decoder.size + 8 * model_width * tokens + (6 << 20)
        ),
        cost_estimate=pl.CostEstimate(
            flops=6 * decoder.size * tokens, bytes_accessed=12 * decoder.size, transcendentals=0
        ),
    )(*flat, *hidden, *low, *slope, *activity, decoder, norms)


def split_rows(value):
    high = lax.reduce_precision(value, 8, 7)
    rows = jnp.concatenate([high, value - high], axis=0).astype(bf16)
    return jnp.concatenate([rows, jnp.zeros((EXTRA - 2, value.shape[1]), bf16)], axis=0)


def on_device(ladder, residual, norm_gain, query_weight, key_weight, value_weight, out_weight, post_gain,
              encoder_weight, encoder_bias, decoder_weight, decoder_bias):
    tokens = residual.shape[0]
    model_width = decoder_weight.shape[1]
    groups = key_weight.shape[1] // HEAD_DIM
    heads = query_weight.shape[1] // key_weight.shape[1]
    width = tokens // CHUNKS
    cuts = [slice(c * width, (c + 1) * width) for c in range(CHUNKS)]

    cores = ladder.cores
    dp_steps = ladder.route((0, 1, 2), (1, 0, 2))
    routes = [ladder.route((0, 1, 2), (1, 2, 0)), ladder.route((2, 0, 1), (1, 0, 2))]
    group_bits = groups.bit_length() - 1
    assert groups == 1 << group_bits and group_bits <= len(dp_steps)
    group_steps, copy_steps = dp_steps[:group_bits], dp_steps[group_bits:]

    residual_t = residual.T
    core = cores[0]
    core_bit = ladder.bit(core)
    paired = len(cores) == 1 and residual_t.shape[0] % 32 == 0 and group_bits >= 1

    mine, gain = residual_t, post_gain[:, None]
    for step in cores:
        half = mine.shape[0] // 2
        up = ladder.bit(step) == 1
        mine = jnp.where(up, mine[half:], mine[:half])
        gain = jnp.where(up, gain[half:], gain[:half])
    block = mine.shape[0]

    def canonical(pieces, steps, stride):
        own, far, own_peer, far_peer = pieces
        value = []
        for k, (a, b) in ((0, (own, far)), (2, (own_peer, far_peer))):
            _, near = ladder.piece(core, steps[0], k)
            value.append(jnp.concatenate([jnp.where(near == 1, b, a), jnp.where(near == 1, a, b)], axis=0))
        own, got = value
        value = jnp.concatenate([jnp.where(core_bit == 1, got, own), jnp.where(core_bit == 1, own, got)], axis=0)
        order = ladder.order(cores[:1] + steps)
        return jnp.concatenate(
            [value[p * stride : p * stride + block] for p in (order.index(i) for i in range(len(order)))], axis=0
        )

    def cut_four(value):
        quarter = value.shape[0] // 4
        return [value[k * quarter : (k + 1) * quarter] for k in range(4)]

    steps = cores[1:] + routes[0]
    residual_own = ladder.gather(mine, steps[1:])
    residual_far = ladder.swap(residual_own, steps[0])
    half_dim = HEAD_DIM // 2
    frequency = rope_base ** (-2.0 * jnp.arange(half_dim, dtype=f32) / HEAD_DIM)
    angles = frequency[:, None] * jnp.arange(tokens).astype(f32)[None, :]
    cosine, sine = jnp.cos(angles), jnp.sin(angles)

    out_t = out_weight.T
    norms = jnp.sqrt(jnp.sum(jnp.square(decoder_weight.astype(f32)), axis=1) + epsilon)

    if paired:
        sends, keeps, squares = project(
            ladder, dp_steps[0], groups, heads, residual_t, norm_gain, query_weight, key_weight, value_weight
        )
    else:
        residual_float = residual_t.astype(f32)
        scaled = (residual_float * norm_gain[:, None]).astype(bf16)
        square = jnp.sum(residual_float * residual_float, axis=0, keepdims=True)
        pieces = []
        for g in range(groups):
            pieces += [
                query_weight[:, g * heads * HEAD_DIM : (g + 1) * heads * HEAD_DIM],
                key_weight[:, g * HEAD_DIM : (g + 1) * HEAD_DIM],
                value_weight[:, g * HEAD_DIM : (g + 1) * HEAD_DIM],
            ]
        stacked = jnp.concatenate(pieces, axis=1)
        projected = lax.dot_general(stacked, scaled, (((0,), (0,)), ((), ())), preferred_element_type=f32)
        sends, keeps, squares = [], [], []
        for cut in cuts:
            send = keep = projected[:, cut]
            if group_bits:
                half = send.shape[0] // 2
                up = ladder.bit(dp_steps[0]) == 1
                send, keep = jnp.where(up, keep[:half], keep[half:]), jnp.where(up, keep[half:], keep[:half])
            sends.append(jnp.concatenate([send.astype(bf16), split_rows(square[:, cut])], axis=0))
            keeps.append(keep)
            squares.append(square[:, cut])

    old = ()
    attendeds = []
    errors, nears, hiddens, lows, slopes, activities = [], [], [], [], [], []
    for c in range(CHUNKS):
        send, part, square = sends[c], keeps[c], squares[c]
        for i, step in enumerate(dp_steps):
            got = ladder.swap(send, step)
            if i < len(dp_steps) - 1:
                send, part, square = advance(ladder, dp_steps[i + 1], i + 1 < group_bits, part, got, square)
        attended, *old = attend(c * width, heads, model_width, part, got, square, cosine, sine, *old)
        attendeds.append(attended)

    residuals = (residual_own, residual_far, ladder.swap(residual_own, core), ladder.swap(residual_far, core))
    if paired:
        residual_all = assemble(ladder, core, steps[0], ladder.order(cores + routes[0]), block, residuals)
    else:
        residual_all = canonical(residuals, steps, block)

    for c, attended in enumerate(attendeds):
        if paired:
            attended = ladder.gather(attended, group_steps[1:])
            got = ladder.swap(attended, group_steps[0])
            send, keep = project_out(ladder, group_steps[0], core, attended, got, out_t)
            packed = pack(ladder, core, keep, ladder.swap(send, core), post_gain)
        else:
            attended = ladder.gather(attended, group_steps)
            head = ladder.scatter(jnp.dot(out_t, attended, preferred_element_type=f32), cores, f32)
            packed = jnp.concatenate(
                [(head * gain).astype(bf16), split_rows(jnp.sum(head * head, axis=0, keepdims=True))], axis=0
            )
        steps = routes[c % len(routes)]
        pieces = ladder.quarters(packed, core, cores[1:] + steps)
        near = (cores[1:] + steps)[0]
        kernel_block, places = block, ladder.order(cores + steps)
        if not paired:
            stride = block + EXTRA
            tails = sum(
                v[p * stride + block : (p + 1) * stride].astype(f32)
                for v in pieces
                for p in range(v.shape[0] // stride)
            )
            tails = split_rows(jnp.sum(tails, axis=0, keepdims=True))
            whole = cut_four(canonical(pieces, cores[1:] + steps, stride))
            pieces = [
                jnp.concatenate([v, tails if k == 0 else jnp.zeros_like(tails)], axis=0) for k, v in enumerate(whole)
            ]
            kernel_block, places = model_width // 4, ()
        if c == CHUNKS - 1:
            last, norms = lax.optimization_barrier((pieces[-1], norms))
            pieces = (*pieces[:-1], last)
        hidden, low, slope, activity, send, part = encode(
            ladder, core, near, places, c * width, kernel_block, pieces, residual_all,
            encoder_weight, encoder_bias, decoder_weight,
        )
        part = part + ladder.swap(send, core).astype(f32)
        rebuilt = ladder.scatter(part, cores[1:] + steps, bf16)
        slot = ladder.position(cores + steps) * block
        bias_mine = lax.dynamic_slice_in_dim(decoder_bias, slot, block)[:, None]
        error = (rebuilt + bias_mine - lax.dynamic_slice_in_dim(hidden, slot, block, axis=0).astype(f32)).astype(bf16)
        errors.append(ladder.quarters(error, core, cores[1:] + steps))
        nears.append(near)
        hiddens.append(hidden)
        lows.append(low)
        slopes.append(slope)
        activities.append(activity)

    encoder_grad, encoder_bias_grad, decoder_grad = gradients(
        ladder, core, nears, errors, hiddens, lows, slopes, activities, decoder_weight, norms
    )
    return encoder_grad, encoder_bias_grad[0], decoder_grad


def solution(mesh):
    ladder = Ladder(mesh.shape["dp"], mesh.shape["mp"])
    placed = (
        P(None, "dp"),
        P("dp"),
        P("dp", "mp"),
        P("dp", "mp"),
        P("dp", "mp"),
        P("mp", "dp"),
        P("dp"),
        P(None, ("dp", "mp")),
        P(("dp", "mp")),
        P(("dp", "mp"), None),
        P(),
    )
    return jax.shard_map(
        functools.partial(on_device, ladder),
        mesh=mesh,
        in_specs=placed,
        out_specs=(P(None, ("dp", "mp")), P(("dp", "mp")), P(("dp", "mp"), None)),
        check_vma=False,
    )
```

time: 283 us -> 156 us (0.55)
  blocking collectives: 75.9 us -> 0 us
  other arithmetic: 22.9 us -> 3.77 us
  local copies, waits for them, and re-layouts: 31.2 us -> 13.8 us
  waiting for transfers between devices: 78.2 us -> 62.1 us
  matrix products: 14.7 us -> 0 us
  Pallas kernels: 4.22 us -> 16.9 us
  starting transfers between devices: 52.1 us -> 57.8 us
    unnamed x1 -> x0, blocking collectives: 75.9 us -> none
    ppermute x54, waiting for transfers between devices: 78.2 us -> 62.1 us  [swap(): return lax.ppermute(value, AXES, self.pairs(step))]
    dot_general x10 -> x0, matrix products: 14.7 us -> none  [the longest x1 6.15 us: on_device(): lax.dot_general(active_low, error_low, (((1,), (1,)), ((), ())), preferre...]
    pallas_call x2 -> x17, Pallas kernels: 4.22 us -> 16.9 us  [the longest x2 6.92 us: encode(): pl.pallas_call(functools.partial(hidden_kernel, ladder, core, step, place...]
    unnamed x141 -> x40, local copies, waits for them, and re-layouts: 24 us -> 12.9 us
    convert_element_type x8 -> x2, other arithmetic: 8.13 us -> 0.17 us  [on_device(): (rebuilt + bias_mine - lax.dynamic_slice_in_dim(hidden, slot, block, axis...]
    select_n x33 -> x17, other arithmetic: 6.44 us -> 0.66 us  [gather(): jnp.where(up, got, value)]
    ppermute x54, starting transfers between devices: 52.1 us -> 57.8 us  [swap(): return lax.ppermute(value, AXES, self.pairs(step))]
  transfers between devices with their start and end apart: 54 -> 54, of which waited for: 33 -> 34; matrix products, arithmetic and copies ran while one was open for 16% -> 3% of each run, Pallas kernels for 1% -> 6%
where the time goes in v2:
time: 156 us
  waiting for transfers between devices  62.1 us (40%)
  starting transfers between devices  57.8 us (37%)
  Pallas kernels  16.9 us (11%)
  local copies, waits for them, and re-layouts  13.8 us (9%)
  other arithmetic  3.77 us (2%)
    ppermute x54, waiting for transfers between devices, swap(): return lax.ppermute(value, AXES, self.pairs(step))  62.1 us
    ppermute x54, starting transfers between devices, swap(): return lax.ppermute(value, AXES, self.pairs(step))  57.8 us
    unnamed x40, local copies, waits for them, and re-layouts  12.9 us
    pallas_call x2, Pallas kernels, encode(): pl.pallas_call(functools.partial(hidden_kernel, ladder, core, step, place...  6.92 us
    pallas_call x1, Pallas kernels, gradients(): pl.pallas_call(functools.partial(final_kernel, ladder, core, steps), out_...  6.25 us
  transfers between devices with their start and end apart: 54, of which 34 were waited for; matrix products, arithmetic and copies ran while one was open for 3% of the time, Pallas kernels for 6%

profile of v2, /device:TPU:0, one launch (start us, length us, event | category | flops | bytes accessed | tf_op | source)
XLA Modules:
  0.0 155.7 jit_solution(15874394778784286327)
XLA Ops:
  1.5 1.1 copy-done.12
  2.6 1.0 copy-done.13
  5.2 1.2 shard_map.130
  6.4 3.0 %collective-permute-start = (bf16[1040,128]{1,0:T(8,128)(2,1)S(1)}, bf16[1040,128]{1,0:T(8,128)(2,1)S(1)}, u32[]{:S(2)}, u32[]{:S(2)}) collective-permute-start(bf16[1040,128]{1,0:T(8,128)(2,1)S(1)} %get-tuple-element.53), channel_id=1, source_target_pairs={{0,2},{1,5},{2,0},{3,7},{4,6},{5,1},{6,4},{7,3},{8,10},{9,13},{10,... | collective-permute-start | bytes 798728 | tf_op jit(solution)/shard_map/ppermute | solution.py:63
  9.5 3.1 %collective-permute-start.13 = (bf16[144,256]{1,0:T(8,128)(2,1)S(1)}, bf16[144,256]{1,0:T(8,128)(2,1)S(1)}, u32[]{:S(2)}, u32[]{:S(2)}) collective-permute-start(bf16[144,256]{1,0:T(8,128)(2,1)S(1)} %slice_select_fusion), channel_id=1, source_target_pairs={{0,16},{1,17},{2,18},{3,19},{4,20},{5,21},{6,22},{7,23},{8,24},{9,... | collective-permute-start | bytes 221192 | tf_op jit(solution)/shard_map/ppermute | solution.py:63
  12.6 1.2 collective-permute-done.got_ref
  13.8 2.1 %collective-permute-start.1 = (bf16[528,128]{1,0:T(8,128)(2,1)S(1)}, bf16[528,128]{1,0:T(8,128)(2,1)S(1)}, u32[]{:S(2)}, u32[]{:S(2)}) collective-permute-start(bf16[528,128]{1,0:T(8,128)(2,1)S(1)} %get-tuple-element.56), channel_id=1, source_target_pairs={{0,4},{1,3},{2,6},{3,1},{4,0},{5,7},{6,2},{7,5},{8,12},{9,11},{10,... | collective-permute-start | bytes 405512 | tf_op jit(solution)/shard_map/ppermute | solution.py:63
  16.0 1.4 collective-permute-done.30.got_ref
  17.5 2.4 %collective-permute-start.31 = (bf16[528,128]{1,0:T(8,128)(2,1)S(1)}, bf16[528,128]{1,0:T(8,128)(2,1)S(1)}, u32[]{:S(2)}, u32[]{:S(2)}) collective-permute-start(bf16[528,128]{1,0:T(8,128)(2,1)S(1)} %get-tuple-element.74), channel_id=1, source_target_pairs={{0,4},{1,3},{2,6},{3,1},{4,0},{5,7},{6,2},{7,5},{8,12},{9,11},{10,... | collective-permute-start | bytes 405512 | tf_op jit(solution)/shard_map/ppermute | solution.py:63
  19.9 1.6 %collective-permute-start.14 = (bf16[288,256]{1,0:T(8,128)(2,1)S(1)}, bf16[288,256]{1,0:T(8,128)(2,1)S(1)}, u32[]{:S(2)}, u32[]{:S(2)}) collective-permute-start(bf16[288,256]{1,0:T(8,128)(2,1)S(1)} %pad_maximum_fusion.8), channel_id=1, source_target_pairs={{0,8},{1,3},{2,10},{3,1},{4,12},{5,7},{6,14},{7,5},{8,0},{9,11},{1... | collective-permute-start | bytes 442376 | tf_op jit(solution)/shard_map/ppermute | solution.py:63
  22.9 2.1 %collective-permute-start.32 = (bf16[528,128]{1,0:T(8,128)(2,1)S(1)}, bf16[528,128]{1,0:T(8,128)(2,1)S(1)}, u32[]{:S(2)}, u32[]{:S(2)}) collective-permute-start(bf16[528,128]{1,0:T(8,128)(2,1)S(1)} %get-tuple-element.77), channel_id=1, source_target_pairs={{0,8},{1,9},{2,10},{3,11},{4,12},{5,13},{6,14},{7,15},{8,0},{9,1},... | collective-permute-start | bytes 405512 | tf_op jit(solution)/shard_map/ppermute | solution.py:63
  25.4 3.4 %collective-permute-done.2.got_ref = bf16[528,128]{1,0:T(8,128)(2,1)S(1)} collective-permute-done((bf16[528,128]{1,0:T(8,128)(2,1)S(1)}, bf16[528,128]{1,0:T(8,128)(2,1)S(1)}, u32[]{:S(2)}, u32[]{:S(2)}) %collective-permute-start.2) | collective-permute-done | bytes 135200 | tf_op jit(solution)/shard_map/ppermute | solution.py:63
  28.8 3.0 %collective-permute-start.3 = (bf16[528,128]{1,0:T(8,128)(2,1)S(1)}, bf16[528,128]{1,0:T(8,128)(2,1)S(1)}, u32[]{:S(2)}, u32[]{:S(2)}) collective-permute-start(bf16[528,128]{1,0:T(8,128)(2,1)S(1)} %get-tuple-element.62), channel_id=1, source_target_pairs={{0,16},{1,17},{2,18},{3,19},{4,20},{5,21},{6,22},{7,23},{8,24},{9,... | collective-permute-start | bytes 405512 | tf_op jit(solution)/shard_map/ppermute | solution.py:63
  31.8 2.6 %collective-permute-start.33 = (bf16[528,128]{1,0:T(8,128)(2,1)S(1)}, bf16[528,128]{1,0:T(8,128)(2,1)S(1)}, u32[]{:S(2)}, u32[]{:S(2)}) collective-permute-start(bf16[528,128]{1,0:T(8,128)(2,1)S(1)} %get-tuple-element.80), channel_id=1, source_target_pairs={{0,16},{1,17},{2,18},{3,19},{4,20},{5,21},{6,22},{7,23},{8,24},{9,... | collective-permute-start | bytes 405512 | tf_op jit(solution)/shard_map/ppermute | solution.py:63
  34.4 1.8 %collective-permute-done.3.got_ref = bf16[528,128]{1,0:T(8,128)(2,1)S(1)} collective-permute-done((bf16[528,128]{1,0:T(8,128)(2,1)S(1)}, bf16[528,128]{1,0:T(8,128)(2,1)S(1)}, u32[]{:S(2)}, u32[]{:S(2)}) %collective-permute-start.3) | collective-permute-done | bytes 135200 | tf_op jit(solution)/shard_map/ppermute | solution.py:63
  36.7 2.6 %collective-permute-done.33.got_ref = bf16[528,128]{1,0:T(8,128)(2,1)S(1)} collective-permute-done((bf16[528,128]{1,0:T(8,128)(2,1)S(1)}, bf16[528,128]{1,0:T(8,128)(2,1)S(1)}, u32[]{:S(2)}, u32[]{:S(2)}) %collective-permute-start.33) | collective-permute-done | bytes 135200 | tf_op jit(solution)/shard_map/ppermute | solution.py:63
  40.2 1.6 %collective-permute-start.34 = (bf16[256,128]{1,0:T(8,128)(2,1)S(1)}, bf16[256,128]{1,0:T(8,128)(2,1)S(1)}, u32[]{:S(2)}, u32[]{:S(2)}) collective-permute-start(bf16[256,128]{1,0:T(8,128)(2,1)S(1)} %get-tuple-element.84), channel_id=1, source_target_pairs={{0,4},{1,3},{2,6},{3,1},{4,0},{5,7},{6,2},{7,5},{8,12},{9,11},{10,... | collective-permute-start | bytes 196616 | tf_op jit(solution)/shard_map/ppermute | solution.py:63
  42.3 1.6 %collective-permute-start.4 = (bf16[256,128]{1,0:T(8,128)(2,1)S(1)}, bf16[256,128]{1,0:T(8,128)(2,1)S(1)}, u32[]{:S(2)}, u32[]{:S(2)}) collective-permute-start(bf16[256,128]{1,0:T(8,128)(2,1)S(1)} %get-tuple-element.64), channel_id=1, source_target_pairs={{0,4},{1,3},{2,6},{3,1},{4,0},{5,7},{6,2},{7,5},{8,12},{9,11},{10,... | collective-permute-start | bytes 196616 | tf_op jit(solution)/shard_map/ppermute | solution.py:63
  44.5 1.6 %collective-permute-start.35 = (bf16[512,128]{1,0:T(8,128)(2,1)S(1)}, bf16[512,128]{1,0:T(8,128)(2,1)S(1)}, u32[]{:S(2)}, u32[]{:S(2)}) collective-permute-start(bf16[512,128]{1,0:T(8,128)(2,1)S(1)} %pad_maximum_fusion.12.own_ref), channel_id=1, source_target_pairs={{0,2},{1,5},{2,0},{3,7},{4,6},{5,1},{6,4},{7,3},{8,10},{9,13},{10,... | collective-permute-start | bytes 393224 | tf_op jit(solution)/shard_map/ppermute | solution.py:63
  46.1 3.3 %collective-permute-done.4 = bf16[256,128]{1,0:T(8,128)(2,1)S(1)} collective-permute-done((bf16[256,128]{1,0:T(8,128)(2,1)S(1)}, bf16[256,128]{1,0:T(8,128)(2,1)S(1)}, u32[]{:S(2)}, u32[]{:S(2)}) %collective-permute-start.4) | collective-permute-done | bytes 65568 | tf_op jit(solution)/shard_map/ppermute | solution.py:63
  49.4 1.6 %collective-permute-start.5 = (bf16[512,128]{1,0:T(8,128)(2,1)S(1)}, bf16[512,128]{1,0:T(8,128)(2,1)S(1)}, u32[]{:S(2)}, u32[]{:S(2)}) collective-permute-start(bf16[512,128]{1,0:T(8,128)(2,1)S(1)} %pad_maximum_fusion.11.own_ref), channel_id=1, source_target_pairs={{0,2},{1,5},{2,0},{3,7},{4,6},{5,1},{6,4},{7,3},{8,10},{9,13},{10,... | collective-permute-start | bytes 393224 | tf_op jit(solution)/shard_map/ppermute | solution.py:63
  51.6 2.9 %collective-permute-done.5.got_ref = bf16[512,128]{1,0:T(8,128)(2,1)S(1)} collective-permute-done((bf16[512,128]{1,0:T(8,128)(2,1)S(1)}, bf16[512,128]{1,0:T(8,128)(2,1)S(1)}, u32[]{:S(2)}, u32[]{:S(2)}) %collective-permute-start.5) | collective-permute-done | bytes 131104 | tf_op jit(solution)/shard_map/ppermute | solution.py:63
  54.9 1.3 collective-permute-start.37
  56.3 2.0 %collective-permute-start.16 = (bf16[1152,256]{1,0:T(8,128)(2,1)S(1)}, bf16[1152,256]{1,0:T(8,128)(2,1)S(1)}, u32[]{:S(2)}, u32[]{:S(2)}) collective-permute-start(bf16[1152,256]{1,0:T(8,128)(2,1)S(1)} %pad_maximum_fusion.refs_0_), channel_id=1, source_target_pairs={{0,2},{1,5},{2,0},{3,7},{4,6},{5,1},{6,4},{7,3},{8,10},{9,13},{10,... | collective-permute-start | bytes 1769480 | tf_op jit(solution)/shard_map/ppermute | solution.py:63
  58.3 1.5 collective-permute-start.7
  61.4 1.9 %collective-permute-done.7 = bf16[160,128]{1,0:T(8,128)(2,1)S(1)} collective-permute-done((bf16[160,128]{1,0:T(8,128)(2,1)S(1)}, bf16[160,128]{1,0:T(8,128)(2,1)S(1)}, u32[]{:S(2)}, u32[]{:S(2)}) %collective-permute-start.7) | collective-permute-done | bytes 40992 | tf_op jit(solution)/shard_map/ppermute | solution.py:63
  63.3 2.1 %collective-permute-start.8 = (bf16[320,128]{1,0:T(8,128)(2,1)S(1)}, bf16[320,128]{1,0:T(8,128)(2,1)S(1)}, u32[]{:S(2)}, u32[]{:S(2)}) collective-permute-start(bf16[320,128]{1,0:T(8,128)(2,1)S(1)} %pad_maximum_fusion.13), channel_id=1, source_target_pairs={{0,8},{1,3},{2,10},{3,1},{4,12},{5,7},{6,14},{7,5},{8,0},{9,11},{1... | collective-permute-start | bytes 245768 | tf_op jit(solution)/shard_map/ppermute | solution.py:63
  66.3 1.6 %collective-permute-start.39 = (bf16[640,128]{1,0:T(8,128)(2,1)S(1)}, bf16[640,128]{1,0:T(8,128)(2,1)S(1)}, u32[]{:S(2)}, u32[]{:S(2)}) collective-permute-start(bf16[640,128]{1,0:T(8,128)(2,1)S(1)} %pad_maximum_fusion.7), channel_id=1, source_target_pairs={{0,2},{1,3},{2,0},{3,1},{4,6},{5,7},{6,4},{7,5},{8,10},{9,11},{10,... | collective-permute-start | bytes 491528 | tf_op jit(solution)/shard_map/ppermute | solution.py:63
  68.0 1.3 collective-permute-start.9
  69.3 2.4 %collective-permute-done.39 = bf16[640,128]{1,0:T(8,128)(2,1)S(1)} collective-permute-done((bf16[640,128]{1,0:T(8,128)(2,1)S(1)}, bf16[640,128]{1,0:T(8,128)(2,1)S(1)}, u32[]{:S(2)}, u32[]{:S(2)}) %collective-permute-start.39) | collective-permute-done | bytes 163872 | tf_op jit(solution)/shard_map/ppermute | solution.py:63
  71.8 1.0 collective-permute-start.40
  74.0 1.1 collective-permute-done.9
  75.2 3.7 %collective-permute-done.40.refs_1_ = bf16[1280,128]{1,0:T(8,128)(2,1)S(1)} collective-permute-done((bf16[1280,128]{1,0:T(8,128)(2,1)S(1)}, bf16[1280,128]{1,0:T(8,128)(2,1)S(1)}, u32[]{:S(2)}, u32[]{:S(2)}) %collective-permute-start.40) | collective-permute-done | bytes 327712 | tf_op jit(solution)/shard_map/ppermute | solution.py:63
  78.9 1.6 %collective-permute-start.10 = (bf16[1280,128]{1,0:T(8,128)(2,1)S(1)}, bf16[1280,128]{1,0:T(8,128)(2,1)S(1)}, u32[]{:S(2)}, u32[]{:S(2)}) collective-permute-start(bf16[1280,128]{1,0:T(8,128)(2,1)S(1)} %pad_maximum_fusion.1.refs_0_), channel_id=1, source_target_pairs={{0,2},{1,5},{2,0},{3,7},{4,6},{5,1},{6,4},{7,3},{8,10},{9,13},{10,... | collective-permute-start | bytes 983048 | tf_op jit(solution)/shard_map/ppermute | solution.py:63
  80.8 2.3 %copy-done.3 = bf16[4608,256]{1,0:T(8,128)(2,1)S(1)} copy-done((bf16[4608,256]{1,0:T(8,128)(2,1)S(1)}, bf16[4608,256]{1,0:T(8,128)(2,1)}, u32[]{:S(2)}) %copy-start.3) | copy-done | bytes 2359320
  83.1 3.1 %shard_map.145 = (bf16[4608,128]{1,0:T(8,128)(2,1)S(1)}, bf16[256,128]{1,0:T(8,128)(2,1)S(1)}, f32[256,128]{1,0:T(8,128)S(1)}, f32[256,1]{1,0:T(8,128)S(1)}, bf1...) custom-call(bf16[1280,128]{1,0:T(8,128)(2,1)S(1)} %pad_maximum_fusion.2.refs_0_, ...), custom_call_target="tpu_custom_call" | custom-call | flops 603979776 | bytes 4718592 | tf_op jit(solution)/shard_map/pallas_call | solution.py:400
  86.2 1.0 copy-done.8
  87.3 1.0 copy-done.10
  90.3 1.2 collective-permute-done.11.refs_2_
  92.0 1.7 %copy-done.2 = bf16[4608,256]{1,0:T(8,128)(2,1)S(1)} copy-done((bf16[4608,256]{1,0:T(8,128)(2,1)S(1)}, bf16[4608,256]{1,0:T(8,128)(2,1)}, u32[]{:S(2)}) %copy-start.2) | copy-done | bytes 2359320
  93.7 1.7 %copy-done.4 = bf16[4608,256]{1,0:T(8,128)(2,1)S(1)} copy-done((bf16[4608,256]{1,0:T(8,128)(2,1)S(1)}, bf16[4608,256]{1,0:T(8,128)(2,1)}, u32[]{:S(2)}) %copy-start.4) | copy-done | bytes 2359320
  95.3 3.8 %shard_map.138 = (bf16[4608,128]{1,0:T(8,128)(2,1)S(1)}, bf16[256,128]{1,0:T(8,128)(2,1)S(1)}, f32[256,128]{1,0:T(8,128)S(1)}, f32[256,1]{1,0:T(8,128)S(1)}, bf1...) custom-call(bf16[1280,128]{1,0:T(8,128)(2,1)S(1)} %pad_maximum_fusion.1.refs_0_, ...), custom_call_target="tpu_custom_call" | custom-call | flops 603979776 | bytes 4718592 | tf_op jit(solution)/shard_map/pallas_call | solution.py:400
  99.4 1.2 convert_add_fusion
  100.6 1.0 collective-permute-start.44
  102.5 4.9 %collective-permute-done.44 = bf16[1152,128]{1,0:T(8,128)(2,1)S(1)} collective-permute-done((bf16[1152,128]{1,0:T(8,128)(2,1)S(1)}, bf16[1152,128]{1,0:T(8,128)(2,1)S(1)}, u32[]{:S(2)}, u32[]{:S(2)}) %collective-permute-start.44) | collective-permute-done | bytes 294944 | tf_op jit(solution)/shard_map/ppermute | solution.py:63
  108.7 1.2 collective-permute-start.21
  109.8 3.0 %collective-permute-done.45 = bf16[576,128]{1,0:T(8,128)(2,1)S(1)} collective-permute-done((bf16[576,128]{1,0:T(8,128)(2,1)S(1)}, bf16[576,128]{1,0:T(8,128)(2,1)S(1)}, u32[]{:S(2)}, u32[]{:S(2)}) %collective-permute-start.45) | collective-permute-done | bytes 147488 | tf_op jit(solution)/shard_map/ppermute | solution.py:63
  113.9 1.2 collective-permute-start.22
  115.1 2.2 %collective-permute-done.46 = bf16[288,128]{1,0:T(8,128)(2,1)S(1)} collective-permute-done((bf16[288,128]{1,0:T(8,128)(2,1)S(1)}, bf16[288,128]{1,0:T(8,128)(2,1)S(1)}, u32[]{:S(2)}, u32[]{:S(2)}) %collective-permute-start.46) | collective-permute-done | bytes 73760 | tf_op jit(solution)/shard_map/ppermute | solution.py:63
  118.4 2.1 %collective-permute-start.23 = (bf16[144,128]{1,0:T(8,128)(2,1)S(1)}, bf16[144,128]{1,0:T(8,128)(2,1)S(1)}, u32[]{:S(2)}, u32[]{:S(2)}) collective-permute-start(bf16[144,128]{1,0:T(8,128)(2,1)S(1)} %select_convert_fusion.7), channel_id=1, source_target_pairs={{0,16},{1,17},{2,18},{3,19},{4,20},{5,21},{6,22},{7,23},{8,24},{9,... | collective-permute-start | bytes 110600 | tf_op jit(solution)/shard_map/ppermute | solution.py:63
  120.5 2.3 %collective-permute-done.47 = bf16[144,128]{1,0:T(8,128)(2,1)S(1)} collective-permute-done((bf16[144,128]{1,0:T(8,128)(2,1)S(1)}, bf16[144,128]{1,0:T(8,128)(2,1)S(1)}, u32[]{:S(2)}, u32[]{:S(2)}) %collective-permute-start.47) | collective-permute-done | bytes 36896 | tf_op jit(solution)/shard_map/ppermute | solution.py:63
  124.0 2.1 %collective-permute-start.24 = (bf16[144,128]{1,0:T(8,128)(2,1)S(1)}, bf16[144,128]{1,0:T(8,128)(2,1)S(1)}, u32[]{:S(2)}, u32[]{:S(2)}) collective-permute-start(bf16[144,128]{1,0:T(8,128)(2,1)S(1)} %subtract_convert_fusion.1), channel_id=1, source_target_pairs={{0,16},{1,17},{2,18},{3,19},{4,20},{5,21},{6,22},{7,23},{8,24},{9,... | collective-permute-start | bytes 110600 | tf_op jit(solution)/shard_map/ppermute | solution.py:63
  126.1 2.1 %collective-permute-done.48 = bf16[144,128]{1,0:T(8,128)(2,1)S(1)} collective-permute-done((bf16[144,128]{1,0:T(8,128)(2,1)S(1)}, bf16[144,128]{1,0:T(8,128)(2,1)S(1)}, u32[]{:S(2)}, u32[]{:S(2)}) %collective-permute-start.48) | collective-permute-done | bytes 36896 | tf_op jit(solution)/shard_map/ppermute | solution.py:63
  129.0 1.4 collective-permute-start.25
  130.3 2.3 %collective-permute-done.49 = bf16[288,128]{1,0:T(8,128)(2,1)S(1)} collective-permute-done((bf16[288,128]{1,0:T(8,128)(2,1)S(1)}, bf16[288,128]{1,0:T(8,128)(2,1)S(1)}, u32[]{:S(2)}, u32[]{:S(2)}) %collective-permute-start.49) | collective-permute-done | bytes 73760 | tf_op jit(solution)/shard_map/ppermute | solution.py:63
  132.8 1.1 collective-permute-done.25
  133.9 1.0 collective-permute-start.26
  134.9 3.0 %collective-permute-done.50 = bf16[576,128]{1,0:T(8,128)(2,1)S(1)} collective-permute-done((bf16[576,128]{1,0:T(8,128)(2,1)S(1)}, bf16[576,128]{1,0:T(8,128)(2,1)S(1)}, u32[]{:S(2)}, u32[]{:S(2)}) %collective-permute-start.50) | collective-permute-done | bytes 147488 | tf_op jit(solution)/shard_map/ppermute | solution.py:63
  138.3 2.5 %collective-permute-done.26 = bf16[576,128]{1,0:T(8,128)(2,1)S(1)} collective-permute-done((bf16[576,128]{1,0:T(8,128)(2,1)S(1)}, bf16[576,128]{1,0:T(8,128)(2,1)S(1)}, u32[]{:S(2)}, u32[]{:S(2)}) %collective-permute-start.26) | collective-permute-done | bytes 147488 | tf_op jit(solution)/shard_map/ppermute | solution.py:63
  140.9 1.0 collective-permute-start.27
  142.4 2.4 %collective-permute-done.51.refs_5_ = bf16[1152,128]{1,0:T(8,128)(2,1)S(1)} collective-permute-done((bf16[1152,128]{1,0:T(8,128)(2,1)S(1)}, bf16[1152,128]{1,0:T(8,128)(2,1)S(1)}, u32[]{:S(2)}, u32[]{:S(2)}) %collective-permute-start.51) | collective-permute-done | bytes 294944 | tf_op jit(solution)/shard_map/ppermute | solution.py:63
  144.8 2.8 %collective-permute-done.27.refs_1_ = bf16[1152,128]{1,0:T(8,128)(2,1)S(1)} collective-permute-done((bf16[1152,128]{1,0:T(8,128)(2,1)S(1)}, bf16[1152,128]{1,0:T(8,128)(2,1)S(1)}, u32[]{:S(2)}, u32[]{:S(2)}) %collective-permute-start.27) | collective-permute-done | bytes 294944 | tf_op jit(solution)/shard_map/ppermute | solution.py:63
  147.7 1.6 %collective-permute-done.29.refs_3_ = bf16[1152,128]{1,0:T(8,128)(2,1)S(1)} collective-permute-done((bf16[1152,128]{1,0:T(8,128)(2,1)S(1)}, bf16[1152,128]{1,0:T(8,128)(2,1)S(1)}, u32[]{:S(2)}, u32[]{:S(2)}) %collective-permute-start.29) | collective-permute-done | bytes 294944 | tf_op jit(solution)/shard_map/ppermute | solution.py:63
  149.2 6.3 %shard_map.146 = (bf16[4608,256]{1,0:T(8,128)(2,1)}, f32[1,256]{1,0:T(1,128)}, bf16[256,4608]{1,0:T(8,128)(2,1)}) custom-call(bf16[1152,128]{1,0:T(8,128)(2,1)S(1)} %pad_maximum_fusion.4.refs_0_, bf16[1152,128]{1,0:T(8,128)(2,1)S(1)} %collective-permute-done.27.refs_1_, bf16[1152,128]{1,0:T(8,128)(2,1)S(1)} %collective-permute-done.28.refs_2_, ...), custom_call_target="tpu_custom_call" | custom-call | flops 1811939328 | bytes 14155776 | tf_op jit(solution)/shard_map/pallas_call | solution.py:479
  (160 shorter events, 22.2 us)
Async XLA Ops:
  5.2 4.3 %copy-start.7 = (bf16[256,288]{0,1:T(8,128)(2,1)S(1)}, bf16[256,288]{0,1:T(8,128)(2,1)}, u32[]{:S(2)}) copy-start(bf16[256,288]{0,1:T(8,128)(2,1)} %param.11) | copy-start | bytes 442372
  6.4 7.4 %collective-permute-start = (bf16[1040,128]{1,0:T(8,128)(2,1)S(1)}, bf16[1040,128]{1,0:T(8,128)(2,1)S(1)}, u32[]{:S(2)}, u32[]{:S(2)}) collective-permute-start(bf16[1040,128]{1,0:T(8,128)(2,1)S(1)} %get-tuple-element.53), channel_id=1, source_target_pairs={{0,2},{1,5},{2,0},{3,7},{4,6},{5,1},{6,4},{7,3},{8,10},{9,13},{10,... | collective-permute-start | bytes 798728 | tf_op jit(solution)/shard_map/ppermute | solution.py:63
  9.4 8.0 %collective-permute-start.30 = (bf16[1040,128]{1,0:T(8,128)(2,1)S(1)}, bf16[1040,128]{1,0:T(8,128)(2,1)S(1)}, u32[]{:S(2)}, u32[]{:S(2)}) collective-permute-start(bf16[1040,128]{1,0:T(8,128)(2,1)S(1)} %get-tuple-element.71), channel_id=1, source_target_pairs={{0,2},{1,5},{2,0},{3,7},{4,6},{5,1},{6,4},{7,3},{8,10},{9,13},{10,... | collective-permute-start | bytes 798728 | tf_op jit(solution)/shard_map/ppermute | solution.py:63
  9.5 10.4 %collective-permute-start.13 = (bf16[144,256]{1,0:T(8,128)(2,1)S(1)}, bf16[144,256]{1,0:T(8,128)(2,1)S(1)}, u32[]{:S(2)}, u32[]{:S(2)}) collective-permute-start(bf16[144,256]{1,0:T(8,128)(2,1)S(1)} %slice_select_fusion), channel_id=1, source_target_pairs={{0,16},{1,17},{2,18},{3,19},{4,20},{5,21},{6,22},{7,23},{8,24},{9,... | collective-permute-start | bytes 221192 | tf_op jit(solution)/shard_map/ppermute | solution.py:63
  13.8 7.7 %collective-permute-start.1 = (bf16[528,128]{1,0:T(8,128)(2,1)S(1)}, bf16[528,128]{1,0:T(8,128)(2,1)S(1)}, u32[]{:S(2)}, u32[]{:S(2)}) collective-permute-start(bf16[528,128]{1,0:T(8,128)(2,1)S(1)} %get-tuple-element.56), channel_id=1, source_target_pairs={{0,4},{1,3},{2,6},{3,1},{4,0},{5,7},{6,2},{7,5},{8,12},{9,11},{10,... | collective-permute-start | bytes 405512 | tf_op jit(solution)/shard_map/ppermute | solution.py:63
  17.5 5.4 %collective-permute-start.31 = (bf16[528,128]{1,0:T(8,128)(2,1)S(1)}, bf16[528,128]{1,0:T(8,128)(2,1)S(1)}, u32[]{:S(2)}, u32[]{:S(2)}) collective-permute-start(bf16[528,128]{1,0:T(8,128)(2,1)S(1)} %get-tuple-element.74), channel_id=1, source_target_pairs={{0,4},{1,3},{2,6},{3,1},{4,0},{5,7},{6,2},{7,5},{8,12},{9,11},{10,... | collective-permute-start | bytes 405512 | tf_op jit(solution)/shard_map/ppermute | solution.py:63
  19.9 14.4 %collective-permute-start.14 = (bf16[288,256]{1,0:T(8,128)(2,1)S(1)}, bf16[288,256]{1,0:T(8,128)(2,1)S(1)}, u32[]{:S(2)}, u32[]{:S(2)}) collective-permute-start(bf16[288,256]{1,0:T(8,128)(2,1)S(1)} %pad_maximum_fusion.8), channel_id=1, source_target_pairs={{0,8},{1,3},{2,10},{3,1},{4,12},{5,7},{6,14},{7,5},{8,0},{9,11},{1... | collective-permute-start | bytes 442376 | tf_op jit(solution)/shard_map/ppermute | solution.py:63
  21.6 7.1 %collective-permute-start.2 = (bf16[528,128]{1,0:T(8,128)(2,1)S(1)}, bf16[528,128]{1,0:T(8,128)(2,1)S(1)}, u32[]{:S(2)}, u32[]{:S(2)}) collective-permute-start(bf16[528,128]{1,0:T(8,128)(2,1)S(1)} %get-tuple-element.59), channel_id=1, source_target_pairs={{0,8},{1,9},{2,10},{3,11},{4,12},{5,13},{6,14},{7,15},{8,0},{9,1},... | collective-permute-start | bytes 405512 | tf_op jit(solution)/shard_map/ppermute | solution.py:63
  22.9 8.8 %collective-permute-start.32 = (bf16[528,128]{1,0:T(8,128)(2,1)S(1)}, bf16[528,128]{1,0:T(8,128)(2,1)S(1)}, u32[]{:S(2)}, u32[]{:S(2)}) collective-permute-start(bf16[528,128]{1,0:T(8,128)(2,1)S(1)} %get-tuple-element.77), channel_id=1, source_target_pairs={{0,8},{1,9},{2,10},{3,11},{4,12},{5,13},{6,14},{7,15},{8,0},{9,1},... | collective-permute-start | bytes 405512 | tf_op jit(solution)/shard_map/ppermute | solution.py:63
  28.8 7.5 %collective-permute-start.3 = (bf16[528,128]{1,0:T(8,128)(2,1)S(1)}, bf16[528,128]{1,0:T(8,128)(2,1)S(1)}, u32[]{:S(2)}, u32[]{:S(2)}) collective-permute-start(bf16[528,128]{1,0:T(8,128)(2,1)S(1)} %get-tuple-element.62), channel_id=1, source_target_pairs={{0,16},{1,17},{2,18},{3,19},{4,20},{5,21},{6,22},{7,23},{8,24},{9,... | collective-permute-start | bytes 405512 | tf_op jit(solution)/shard_map/ppermute | solution.py:63
  31.8 7.5 %collective-permute-start.33 = (bf16[528,128]{1,0:T(8,128)(2,1)S(1)}, bf16[528,128]{1,0:T(8,128)(2,1)S(1)}, u32[]{:S(2)}, u32[]{:S(2)}) collective-permute-start(bf16[528,128]{1,0:T(8,128)(2,1)S(1)} %get-tuple-element.80), channel_id=1, source_target_pairs={{0,16},{1,17},{2,18},{3,19},{4,20},{5,21},{6,22},{7,23},{8,24},{9,... | collective-permute-start | bytes 405512 | tf_op jit(solution)/shard_map/ppermute | solution.py:63
  36.7 14.4 %copy-start.5 = (bf16[1024,288]{0,1:T(8,128)(2,1)S(1)}, bf16[1024,288]{0,1:T(8,128)(2,1)}, u32[]{:S(2)}) copy-start(bf16[1024,288]{0,1:T(8,128)(2,1)} %param.16) | copy-start | bytes 1769476
  40.2 4.3 %collective-permute-start.34 = (bf16[256,128]{1,0:T(8,128)(2,1)S(1)}, bf16[256,128]{1,0:T(8,128)(2,1)S(1)}, u32[]{:S(2)}, u32[]{:S(2)}) collective-permute-start(bf16[256,128]{1,0:T(8,128)(2,1)S(1)} %get-tuple-element.84), channel_id=1, source_target_pairs={{0,4},{1,3},{2,6},{3,1},{4,0},{5,7},{6,2},{7,5},{8,12},{9,11},{10,... | collective-permute-start | bytes 196616 | tf_op jit(solution)/shard_map/ppermute | solution.py:63
  41.9 9.6 %collective-permute-start.15 = (bf16[576,256]{1,0:T(8,128)(2,1)S(1)}, bf16[576,256]{1,0:T(8,128)(2,1)S(1)}, u32[]{:S(2)}, u32[]{:S(2)}) collective-permute-start(bf16[576,256]{1,0:T(8,128)(2,1)S(1)} %pad_maximum_fusion.3), channel_id=1, source_target_pairs={{0,4},{1,9},{2,6},{3,11},{4,0},{5,13},{6,2},{7,15},{8,12},{9,1},{1... | collective-permute-start | bytes 884744 | tf_op jit(solution)/shard_map/ppermute | solution.py:63
  42.3 7.0 %collective-permute-start.4 = (bf16[256,128]{1,0:T(8,128)(2,1)S(1)}, bf16[256,128]{1,0:T(8,128)(2,1)S(1)}, u32[]{:S(2)}, u32[]{:S(2)}) collective-permute-start(bf16[256,128]{1,0:T(8,128)(2,1)S(1)} %get-tuple-element.64), channel_id=1, source_target_pairs={{0,4},{1,3},{2,6},{3,1},{4,0},{5,7},{6,2},{7,5},{8,12},{9,11},{10,... | collective-permute-start | bytes 196616 | tf_op jit(solution)/shard_map/ppermute | solution.py:63
  44.5 6.5 %collective-permute-start.35 = (bf16[512,128]{1,0:T(8,128)(2,1)S(1)}, bf16[512,128]{1,0:T(8,128)(2,1)S(1)}, u32[]{:S(2)}, u32[]{:S(2)}) collective-permute-start(bf16[512,128]{1,0:T(8,128)(2,1)S(1)} %pad_maximum_fusion.12.own_ref), channel_id=1, source_target_pairs={{0,2},{1,5},{2,0},{3,7},{4,6},{5,1},{6,4},{7,3},{8,10},{9,13},{10,... | collective-permute-start | bytes 393224 | tf_op jit(solution)/shard_map/ppermute | solution.py:63
  49.4 5.0 %collective-permute-start.5 = (bf16[512,128]{1,0:T(8,128)(2,1)S(1)}, bf16[512,128]{1,0:T(8,128)(2,1)S(1)}, u32[]{:S(2)}, u32[]{:S(2)}) collective-permute-start(bf16[512,128]{1,0:T(8,128)(2,1)S(1)} %pad_maximum_fusion.11.own_ref), channel_id=1, source_target_pairs={{0,2},{1,5},{2,0},{3,7},{4,6},{5,1},{6,4},{7,3},{8,10},{9,13},{10,... | collective-permute-start | bytes 393224 | tf_op jit(solution)/shard_map/ppermute | solution.py:63
  51.3 3.5 %copy-start.17 = (f32[288]{0:T(512)S(1)}, f32[288]{0:T(512)}, u32[]{:S(2)}) copy-start(f32[288]{0:T(512)} %gain_ref.5) | copy-start | bytes 3460
  51.4 3.4 %collective-permute-start.36 = (f32[144,128]{1,0:T(8,128)S(1)}, f32[144,128]{1,0:T(8,128)S(1)}, u32[]{:S(2)}, u32[]{:S(2)}) collective-permute-start(f32[144,128]{1,0:T(8,128)S(1)} %get-tuple-element.86), channel_id=1, source_target_pairs={{0,1},{1,0},{2,3},{3,2},{4,5},{5,4},{6,7},{7,6},{8,9},{9,8},{10,11... | collective-permute-start | bytes 221192 | tf_op jit(solution)/shard_map/ppermute | solution.py:63
  54.7 3.5 %collective-permute-start.6 = (f32[144,128]{1,0:T(8,128)S(1)}, f32[144,128]{1,0:T(8,128)S(1)}, u32[]{:S(2)}, u32[]{:S(2)}) collective-permute-start(f32[144,128]{1,0:T(8,128)S(1)} %get-tuple-element.66), channel_id=1, source_target_pairs={{0,1},{1,0},{2,3},{3,2},{4,5},{5,4},{6,7},{7,6},{8,9},{9,8},{10,11... | collective-permute-start | bytes 221192 | tf_op jit(solution)/shard_map/ppermute | solution.py:63
  54.9 5.8 %collective-permute-start.37 = (bf16[160,128]{1,0:T(8,128)(2,1)S(1)}, bf16[160,128]{1,0:T(8,128)(2,1)S(1)}, u32[]{:S(2)}, u32[]{:S(2)}) collective-permute-start(bf16[160,128]{1,0:T(8,128)(2,1)S(1)} %shard_map.144), channel_id=1, source_target_pairs={{0,16},{1,17},{2,18},{3,19},{4,20},{5,21},{6,22},{7,23},{8,24},{9,... | collective-permute-start | bytes 122888 | tf_op jit(solution)/shard_map/ppermute | solution.py:63
  56.3 17.2 %collective-permute-start.16 = (bf16[1152,256]{1,0:T(8,128)(2,1)S(1)}, bf16[1152,256]{1,0:T(8,128)(2,1)S(1)}, u32[]{:S(2)}, u32[]{:S(2)}) collective-permute-start(bf16[1152,256]{1,0:T(8,128)(2,1)S(1)} %pad_maximum_fusion.refs_0_), channel_id=1, source_target_pairs={{0,2},{1,5},{2,0},{3,7},{4,6},{5,1},{6,4},{7,3},{8,10},{9,13},{10,... | collective-permute-start | bytes 1769480 | tf_op jit(solution)/shard_map/ppermute | solution.py:63
  58.3 5.0 %collective-permute-start.7 = (bf16[160,128]{1,0:T(8,128)(2,1)S(1)}, bf16[160,128]{1,0:T(8,128)(2,1)S(1)}, u32[]{:S(2)}, u32[]{:S(2)}) collective-permute-start(bf16[160,128]{1,0:T(8,128)(2,1)S(1)} %shard_map.136), channel_id=1, source_target_pairs={{0,16},{1,17},{2,18},{3,19},{4,20},{5,21},{6,22},{7,23},{8,24},{9,... | collective-permute-start | bytes 122888 | tf_op jit(solution)/shard_map/ppermute | solution.py:63
  60.8 5.5 %collective-permute-start.38 = (bf16[320,128]{1,0:T(8,128)(2,1)S(1)}, bf16[320,128]{1,0:T(8,128)(2,1)S(1)}, u32[]{:S(2)}, u32[]{:S(2)}) collective-permute-start(bf16[320,128]{1,0:T(8,128)(2,1)S(1)} %pad_maximum_fusion.14), channel_id=1, source_target_pairs={{0,4},{1,9},{2,6},{3,11},{4,0},{5,13},{6,2},{7,15},{8,12},{9,1},{1... | collective-permute-start | bytes 245768 | tf_op jit(solution)/shard_map/ppermute | solution.py:63
  63.3 4.6 %collective-permute-start.8 = (bf16[320,128]{1,0:T(8,128)(2,1)S(1)}, bf16[320,128]{1,0:T(8,128)(2,1)S(1)}, u32[]{:S(2)}, u32[]{:S(2)}) collective-permute-start(bf16[320,128]{1,0:T(8,128)(2,1)S(1)} %pad_maximum_fusion.13), channel_id=1, source_target_pairs={{0,8},{1,3},{2,10},{3,1},{4,12},{5,7},{6,14},{7,5},{8,0},{9,11},{1... | collective-permute-start | bytes 245768 | tf_op jit(solution)/shard_map/ppermute | solution.py:63
  66.2 6.6 %copy-start = (bf16[256,4608]{1,0:T(8,128)(2,1)S(1)}, bf16[256,4608]{1,0:T(8,128)(2,1)}, u32[]{:S(2)}) copy-start(bf16[256,4608]{1,0:T(8,128)(2,1)} %refs_16_.1) | copy-start | bytes 7077892
  66.3 5.4 %collective-permute-start.39 = (bf16[640,128]{1,0:T(8,128)(2,1)S(1)}, bf16[640,128]{1,0:T(8,128)(2,1)S(1)}, u32[]{:S(2)}, u32[]{:S(2)}) collective-permute-start(bf16[640,128]{1,0:T(8,128)(2,1)S(1)} %pad_maximum_fusion.7), channel_id=1, source_target_pairs={{0,2},{1,3},{2,0},{3,1},{4,6},{5,7},{6,4},{7,5},{8,10},{9,11},{10,... | collective-permute-start | bytes 491528 | tf_op jit(solution)/shard_map/ppermute | solution.py:63
  68.0 7.1 %collective-permute-start.9 = (bf16[640,128]{1,0:T(8,128)(2,1)S(1)}, bf16[640,128]{1,0:T(8,128)(2,1)S(1)}, u32[]{:S(2)}, u32[]{:S(2)}) collective-permute-start(bf16[640,128]{1,0:T(8,128)(2,1)S(1)} %pad_maximum_fusion.6), channel_id=1, source_target_pairs={{0,4},{1,9},{2,6},{3,11},{4,0},{5,13},{6,2},{7,15},{8,12},{9,1},{1... | collective-permute-start | bytes 491528 | tf_op jit(solution)/shard_map/ppermute | solution.py:63
  71.8 7.1 %collective-permute-start.40 = (bf16[1280,128]{1,0:T(8,128)(2,1)S(1)}, bf16[1280,128]{1,0:T(8,128)(2,1)S(1)}, u32[]{:S(2)}, u32[]{:S(2)}) collective-permute-start(bf16[1280,128]{1,0:T(8,128)(2,1)S(1)} %pad_maximum_fusion.2.refs_0_), channel_id=1, source_target_pairs={{0,8},{1,5},{2,10},{3,7},{4,12},{5,1},{6,14},{7,3},{8,0},{9,13},{1... | collective-permute-start | bytes 983048 | tf_op jit(solution)/shard_map/ppermute | solution.py:63
  73.3 7.2 %collective-permute-start.17 = (bf16[1152,256]{1,0:T(8,128)(2,1)S(1)}, bf16[1152,256]{1,0:T(8,128)(2,1)S(1)}, u32[]{:S(2)}, u32[]{:S(2)}) collective-permute-start(bf16[1152,256]{1,0:T(8,128)(2,1)S(1)} %pad_maximum_fusion.refs_0_), channel_id=1, source_target_pairs={{0,1},{1,0},{2,3},{3,2},{4,5},{5,4},{6,7},{7,6},{8,9},{9,8},{10,11... | collective-permute-start | bytes 1769480 | tf_op jit(solution)/shard_map/ppermute | solution.py:63
  73.4 7.2 %collective-permute-start.18 = (bf16[1152,256]{1,0:T(8,128)(2,1)S(1)}, bf16[1152,256]{1,0:T(8,128)(2,1)S(1)}, u32[]{:S(2)}, u32[]{:S(2)}) collective-permute-start(bf16[1152,256]{1,0:T(8,128)(2,1)S(1)} %collective-permute-done.16.refs_1_), channel_id=1, source_target_pairs={{0,1},{1,0},{2,3},{3,2},{4,5},{5,4},{6,7},{7,6},{8,9},{9,8},{10,11... | collective-permute-start | bytes 1769480 | tf_op jit(solution)/shard_map/ppermute | solution.py:63
  73.9 6.9 %collective-permute-start.41 = (bf16[1280,128]{1,0:T(8,128)(2,1)S(1)}, bf16[1280,128]{1,0:T(8,128)(2,1)S(1)}, u32[]{:S(2)}, u32[]{:S(2)}) collective-permute-start(bf16[1280,128]{1,0:T(8,128)(2,1)S(1)} %pad_maximum_fusion.2.refs_0_), channel_id=1, source_target_pairs={{0,1},{1,0},{2,3},{3,2},{4,5},{5,4},{6,7},{7,6},{8,9},{9,8},{10,11... | collective-permute-start | bytes 983048 | tf_op jit(solution)/shard_map/ppermute | solution.py:63
  78.9 1.9 %collective-permute-start.42 = (bf16[1280,128]{1,0:T(8,128)(2,1)S(1)}, bf16[1280,128]{1,0:T(8,128)(2,1)S(1)}, u32[]{:S(2)}, u32[]{:S(2)}) collective-permute-start(bf16[1280,128]{1,0:T(8,128)(2,1)S(1)} %collective-permute-done.40.refs_1_), channel_id=1, source_target_pairs={{0,1},{1,0},{2,3},{3,2},{4,5},{5,4},{6,7},{7,6},{8,9},{9,8},{10,11... | collective-permute-start | bytes 983048 | tf_op jit(solution)/shard_map/ppermute | solution.py:63
  78.9 10.5 %collective-permute-start.10 = (bf16[1280,128]{1,0:T(8,128)(2,1)S(1)}, bf16[1280,128]{1,0:T(8,128)(2,1)S(1)}, u32[]{:S(2)}, u32[]{:S(2)}) collective-permute-start(bf16[1280,128]{1,0:T(8,128)(2,1)S(1)} %pad_maximum_fusion.1.refs_0_), channel_id=1, source_target_pairs={{0,2},{1,5},{2,0},{3,7},{4,6},{5,1},{6,4},{7,3},{8,10},{9,13},{10,... | collective-permute-start | bytes 983048 | tf_op jit(solution)/shard_map/ppermute | solution.py:63
  80.6 2.5 %copy-start.3 = (bf16[4608,256]{1,0:T(8,128)(2,1)S(1)}, bf16[4608,256]{1,0:T(8,128)(2,1)}, u32[]{:S(2)}) copy-start(bf16[4608,256]{1,0:T(8,128)(2,1)} %refs_5_.3) | copy-start | bytes 7077892
  80.6 2.5 %copy-start.18 = (f32[256]{0:T(256)S(1)}, f32[256]{0:T(256)}, u32[]{:S(2)}) copy-start(f32[256]{0:T(256)} %refs_6_.3) | copy-start | bytes 3076
  80.8 5.4 %copy-start.1 = (bf16[4608,256]{1,0:T(8,128)(2,1)}, bf16[4608,256]{1,0:T(8,128)(2,1)S(1)}, u32[]{:S(2)}) copy-start(bf16[4608,256]{1,0:T(8,128)(2,1)S(1)} %shard_map.137.refs_4_) | copy-start | bytes 7077892
  88.9 10.4 %collective-permute-start.43 = (bf16[2304,128]{1,0:T(8,128)(2,1)}, bf16[2304,128]{1,0:T(8,128)(2,1)}, u32[]{:S(2)}, u32[]{:S(2)}) collective-permute-start(bf16[2304,128]{1,0:T(8,128)(2,1)} %get-tuple-element.89), channel_id=1, source_target_pairs={{0,1},{1,0},{2,3},{3,2},{4,5},{5,4},{6,7},{7,6},{8,9},{9,8},{10,11... | collective-permute-start | bytes 1769480 | tf_op jit(solution)/shard_map/ppermute | solution.py:63
  88.9 2.6 %collective-permute-start.11 = (bf16[1280,128]{1,0:T(8,128)(2,1)S(1)}, bf16[1280,128]{1,0:T(8,128)(2,1)S(1)}, u32[]{:S(2)}, u32[]{:S(2)}) collective-permute-start(bf16[1280,128]{1,0:T(8,128)(2,1)S(1)} %pad_maximum_fusion.1.refs_0_), channel_id=1, source_target_pairs={{0,1},{1,0},{2,3},{3,2},{4,5},{5,4},{6,7},{7,6},{8,9},{9,8},{10,11... | collective-permute-start | bytes 983048 | tf_op jit(solution)/shard_map/ppermute | solution.py:63
  89.4 2.6 %collective-permute-start.12 = (bf16[1280,128]{1,0:T(8,128)(2,1)S(1)}, bf16[1280,128]{1,0:T(8,128)(2,1)}, u32[]{:S(2)}, u32[]{:S(2)}) collective-permute-start(bf16[1280,128]{1,0:T(8,128)(2,1)S(1)} %collective-permute-done.10.refs_1_), channel_id=1, source_target_pairs={{0,1},{1,0},{2,3},{3,2},{4,5},{5,4},{6,7},{7,6},{8,9},{9,8},{10,11... | collective-permute-start | bytes 983048 | tf_op jit(solution)/shard_map/ppermute | solution.py:63
  95.3 4.0 %copy-start.11 = (f32[2304,128]{1,0:T(8,128)S(1)}, f32[2304,128]{1,0:T(8,128)}, u32[]{:S(2)}) copy-start(f32[2304,128]{1,0:T(8,128)} %copy-done.10) | copy-start | bytes 3538948
  99.1 2.5 %collective-permute-start.19 = (bf16[2304,128]{1,0:T(8,128)(2,1)S(1)}, bf16[2304,128]{1,0:T(8,128)(2,1)S(1)}, u32[]{:S(2)}, u32[]{:S(2)}) collective-permute-start(bf16[2304,128]{1,0:T(8,128)(2,1)S(1)} %get-tuple-element.68), channel_id=1, source_target_pairs={{0,1},{1,0},{2,3},{3,2},{4,5},{5,4},{6,7},{7,6},{8,9},{9,8},{10,11... | collective-permute-start | bytes 1769480 | tf_op jit(solution)/shard_map/ppermute | solution.py:63
  100.6 6.8 %collective-permute-start.44 = (bf16[1152,128]{1,0:T(8,128)(2,1)S(1)}, bf16[1152,128]{1,0:T(8,128)(2,1)S(1)}, u32[]{:S(2)}, u32[]{:S(2)}) collective-permute-start(bf16[1152,128]{1,0:T(8,128)(2,1)S(1)} %select_convert_fusion), channel_id=1, source_target_pairs={{0,8},{1,5},{2,10},{3,7},{4,12},{5,1},{6,14},{7,3},{8,0},{9,13},{1... | collective-permute-start | bytes 884744 | tf_op jit(solution)/shard_map/ppermute | solution.py:63
  101.8 6.8 %collective-permute-start.20 = (bf16[1152,128]{1,0:T(8,128)(2,1)S(1)}, bf16[1152,128]{1,0:T(8,128)(2,1)S(1)}, u32[]{:S(2)}, u32[]{:S(2)}) collective-permute-start(bf16[1152,128]{1,0:T(8,128)(2,1)S(1)} %select_convert_fusion.1), channel_id=1, source_target_pairs={{0,2},{1,5},{2,0},{3,7},{4,6},{5,1},{6,4},{7,3},{8,10},{9,13},{10,... | collective-permute-start | bytes 884744 | tf_op jit(solution)/shard_map/ppermute | solution.py:63
  107.5 5.3 %collective-permute-start.45 = (bf16[576,128]{1,0:T(8,128)(2,1)S(1)}, bf16[576,128]{1,0:T(8,128)(2,1)S(1)}, u32[]{:S(2)}, u32[]{:S(2)}) collective-permute-start(bf16[576,128]{1,0:T(8,128)(2,1)S(1)} %select_convert_fusion.2), channel_id=1, source_target_pairs={{0,2},{1,3},{2,0},{3,1},{4,6},{5,7},{6,4},{7,5},{8,10},{9,11},{10,... | collective-permute-start | bytes 442376 | tf_op jit(solution)/shard_map/ppermute | solution.py:63
  108.7 5.2 %collective-permute-start.21 = (bf16[576,128]{1,0:T(8,128)(2,1)S(1)}, bf16[576,128]{1,0:T(8,128)(2,1)S(1)}, u32[]{:S(2)}, u32[]{:S(2)}) collective-permute-start(bf16[576,128]{1,0:T(8,128)(2,1)S(1)} %select_convert_fusion.3), channel_id=1, source_target_pairs={{0,4},{1,9},{2,6},{3,11},{4,0},{5,13},{6,2},{7,15},{8,12},{9,1},{1... | collective-permute-start | bytes 442376 | tf_op jit(solution)/shard_map/ppermute | solution.py:63
  112.9 9.9 %copy-start.9 = (bf16[4608,128]{1,0:T(8,128)(2,1)S(1)}, bf16[4608,128]{1,0:T(8,128)(2,1)}, u32[]{:S(2)}) copy-start(bf16[4608,128]{1,0:T(8,128)(2,1)} %copy-done.8) | copy-start | bytes 3538948
  112.9 4.4 %collective-permute-start.46 = (bf16[288,128]{1,0:T(8,128)(2,1)S(1)}, bf16[288,128]{1,0:T(8,128)(2,1)S(1)}, u32[]{:S(2)}, u32[]{:S(2)}) collective-permute-start(bf16[288,128]{1,0:T(8,128)(2,1)S(1)} %select_convert_fusion.4), channel_id=1, source_target_pairs={{0,4},{1,9},{2,6},{3,11},{4,0},{5,13},{6,2},{7,15},{8,12},{9,1},{1... | collective-permute-start | bytes 221192 | tf_op jit(solution)/shard_map/ppermute | solution.py:63
  113.9 4.4 %collective-permute-start.22 = (bf16[288,128]{1,0:T(8,128)(2,1)S(1)}, bf16[288,128]{1,0:T(8,128)(2,1)S(1)}, u32[]{:S(2)}, u32[]{:S(2)}) collective-permute-start(bf16[288,128]{1,0:T(8,128)(2,1)S(1)} %select_convert_fusion.5), channel_id=1, source_target_pairs={{0,8},{1,3},{2,10},{3,1},{4,12},{5,7},{6,14},{7,5},{8,0},{9,11},{1... | collective-permute-start | bytes 221192 | tf_op jit(solution)/shard_map/ppermute | solution.py:63
  117.4 5.4 %collective-permute-start.47 = (bf16[144,128]{1,0:T(8,128)(2,1)S(1)}, bf16[144,128]{1,0:T(8,128)(2,1)S(1)}, u32[]{:S(2)}, u32[]{:S(2)}) collective-permute-start(bf16[144,128]{1,0:T(8,128)(2,1)S(1)} %select_convert_fusion.6), channel_id=1, source_target_pairs={{0,16},{1,17},{2,18},{3,19},{4,20},{5,21},{6,22},{7,23},{8,24},{9,... | collective-permute-start | bytes 110600 | tf_op jit(solution)/shard_map/ppermute | solution.py:63
  118.4 5.5 %collective-permute-start.23 = (bf16[144,128]{1,0:T(8,128)(2,1)S(1)}, bf16[144,128]{1,0:T(8,128)(2,1)S(1)}, u32[]{:S(2)}, u32[]{:S(2)}) collective-permute-start(bf16[144,128]{1,0:T(8,128)(2,1)S(1)} %select_convert_fusion.7), channel_id=1, source_target_pairs={{0,16},{1,17},{2,18},{3,19},{4,20},{5,21},{6,22},{7,23},{8,24},{9,... | collective-permute-start | bytes 110600 | tf_op jit(solution)/shard_map/ppermute | solution.py:63
  122.9 5.3 %collective-permute-start.48 = (bf16[144,128]{1,0:T(8,128)(2,1)S(1)}, bf16[144,128]{1,0:T(8,128)(2,1)S(1)}, u32[]{:S(2)}, u32[]{:S(2)}) collective-permute-start(bf16[144,128]{1,0:T(8,128)(2,1)S(1)} %subtract_convert_fusion), channel_id=1, source_target_pairs={{0,16},{1,17},{2,18},{3,19},{4,20},{5,21},{6,22},{7,23},{8,24},{9,... | collective-permute-start | bytes 110600 | tf_op jit(solution)/shard_map/ppermute | solution.py:63
  124.0 4.9 %collective-permute-start.24 = (bf16[144,128]{1,0:T(8,128)(2,1)S(1)}, bf16[144,128]{1,0:T(8,128)(2,1)S(1)}, u32[]{:S(2)}, u32[]{:S(2)}) collective-permute-start(bf16[144,128]{1,0:T(8,128)(2,1)S(1)} %subtract_convert_fusion.1), channel_id=1, source_target_pairs={{0,16},{1,17},{2,18},{3,19},{4,20},{5,21},{6,22},{7,23},{8,24},{9,... | collective-permute-start | bytes 110600 | tf_op jit(solution)/shard_map/ppermute | solution.py:63
  128.2 4.4 %collective-permute-start.49 = (bf16[288,128]{1,0:T(8,128)(2,1)S(1)}, bf16[288,128]{1,0:T(8,128)(2,1)S(1)}, u32[]{:S(2)}, u32[]{:S(2)}) collective-permute-start(bf16[288,128]{1,0:T(8,128)(2,1)S(1)} %pad_maximum_fusion.16), channel_id=1, source_target_pairs={{0,4},{1,9},{2,6},{3,11},{4,0},{5,13},{6,2},{7,15},{8,12},{9,1},{1... | collective-permute-start | bytes 221192 | tf_op jit(solution)/shard_map/ppermute | solution.py:63
  129.0 4.9 %collective-permute-start.25 = (bf16[288,128]{1,0:T(8,128)(2,1)S(1)}, bf16[288,128]{1,0:T(8,128)(2,1)S(1)}, u32[]{:S(2)}, u32[]{:S(2)}) collective-permute-start(bf16[288,128]{1,0:T(8,128)(2,1)S(1)} %pad_maximum_fusion.15), channel_id=1, source_target_pairs={{0,8},{1,3},{2,10},{3,1},{4,12},{5,7},{6,14},{7,5},{8,0},{9,11},{1... | collective-permute-start | bytes 221192 | tf_op jit(solution)/shard_map/ppermute | solution.py:63
  132.7 5.2 %collective-permute-start.50 = (bf16[576,128]{1,0:T(8,128)(2,1)S(1)}, bf16[576,128]{1,0:T(8,128)(2,1)S(1)}, u32[]{:S(2)}, u32[]{:S(2)}) collective-permute-start(bf16[576,128]{1,0:T(8,128)(2,1)S(1)} %pad_maximum_fusion.10), channel_id=1, source_target_pairs={{0,2},{1,3},{2,0},{3,1},{4,6},{5,7},{6,4},{7,5},{8,10},{9,11},{10,... | collective-permute-start | bytes 442376 | tf_op jit(solution)/shard_map/ppermute | solution.py:63
  133.9 15.3 %copy-start.16 = (f32[256,1]{1,0:T(8,128)S(1)}, f32[256,1]{1,0:T(8,128)}, u32[]{:S(2)}) copy-start(f32[256,1]{1,0:T(8,128)} %copy-done.15) | copy-start | bytes 3076
  133.9 6.9 %collective-permute-start.26 = (bf16[576,128]{1,0:T(8,128)(2,1)S(1)}, bf16[576,128]{1,0:T(8,128)(2,1)S(1)}, u32[]{:S(2)}, u32[]{:S(2)}) collective-permute-start(bf16[576,128]{1,0:T(8,128)(2,1)S(1)} %pad_maximum_fusion.9), channel_id=1, source_target_pairs={{0,4},{1,9},{2,6},{3,11},{4,0},{5,13},{6,2},{7,15},{8,12},{9,1},{1... | collective-permute-start | bytes 442376 | tf_op jit(solution)/shard_map/ppermute | solution.py:63
  138.0 6.8 %collective-permute-start.51 = (bf16[1152,128]{1,0:T(8,128)(2,1)S(1)}, bf16[1152,128]{1,0:T(8,128)(2,1)S(1)}, u32[]{:S(2)}, u32[]{:S(2)}) collective-permute-start(bf16[1152,128]{1,0:T(8,128)(2,1)S(1)} %pad_maximum_fusion.5.refs_4_), channel_id=1, source_target_pairs={{0,8},{1,5},{2,10},{3,7},{4,12},{5,1},{6,14},{7,3},{8,0},{9,13},{1... | collective-permute-start | bytes 884744 | tf_op jit(solution)/shard_map/ppermute | solution.py:63
  140.9 6.8 %collective-permute-start.27 = (bf16[1152,128]{1,0:T(8,128)(2,1)S(1)}, bf16[1152,128]{1,0:T(8,128)(2,1)S(1)}, u32[]{:S(2)}, u32[]{:S(2)}) collective-permute-start(bf16[1152,128]{1,0:T(8,128)(2,1)S(1)} %pad_maximum_fusion.4.refs_0_), channel_id=1, source_target_pairs={{0,2},{1,5},{2,0},{3,7},{4,6},{5,1},{6,4},{7,3},{8,10},{9,13},{10,... | collective-permute-start | bytes 884744 | tf_op jit(solution)/shard_map/ppermute | solution.py:63
  141.9 5.8 %collective-permute-start.52 = (bf16[1152,128]{1,0:T(8,128)(2,1)S(1)}, bf16[1152,128]{1,0:T(8,128)(2,1)S(1)}, u32[]{:S(2)}, u32[]{:S(2)}) collective-permute-start(bf16[1152,128]{1,0:T(8,128)(2,1)S(1)} %pad_maximum_fusion.5.refs_4_), channel_id=1, source_target_pairs={{0,1},{1,0},{2,3},{3,2},{4,5},{5,4},{6,7},{7,6},{8,9},{9,8},{10,11... | collective-permute-start | bytes 884744 | tf_op jit(solution)/shard_map/ppermute | solution.py:63
  141.9 5.8 %collective-permute-start.28 = (bf16[1152,128]{1,0:T(8,128)(2,1)S(1)}, bf16[1152,128]{1,0:T(8,128)(2,1)S(1)}, u32[]{:S(2)}, u32[]{:S(2)}) collective-permute-start(bf16[1152,128]{1,0:T(8,128)(2,1)S(1)} %pad_maximum_fusion.4.refs_0_), channel_id=1, source_target_pairs={{0,1},{1,0},{2,3},{3,2},{4,5},{5,4},{6,7},{7,6},{8,9},{9,8},{10,11... | collective-permute-start | bytes 884744 | tf_op jit(solution)/shard_map/ppermute | solution.py:63
  144.8 2.9 %collective-permute-start.53 = (bf16[1152,128]{1,0:T(8,128)(2,1)S(1)}, bf16[1152,128]{1,0:T(8,128)(2,1)S(1)}, u32[]{:S(2)}, u32[]{:S(2)}) collective-permute-start(bf16[1152,128]{1,0:T(8,128)(2,1)S(1)} %collective-permute-done.51.refs_5_), channel_id=1, source_target_pairs={{0,1},{1,0},{2,3},{3,2},{4,5},{5,4},{6,7},{7,6},{8,9},{9,8},{10,11... | collective-permute-start | bytes 884744 | tf_op jit(solution)/shard_map/ppermute | solution.py:63
  147.7 1.6 %collective-permute-start.29 = (bf16[1152,128]{1,0:T(8,128)(2,1)S(1)}, bf16[1152,128]{1,0:T(8,128)(2,1)S(1)}, u32[]{:S(2)}, u32[]{:S(2)}) collective-permute-start(bf16[1152,128]{1,0:T(8,128)(2,1)S(1)} %collective-permute-done.27.refs_1_), channel_id=1, source_target_pairs={{0,1},{1,0},{2,3},{3,2},{4,5},{5,4},{6,7},{7,6},{8,9},{9,8},{10,11... | collective-permute-start | bytes 884744 | tf_op jit(solution)/shard_map/ppermute | solution.py:63
  (10 other events, 10.6 us)

commit v3 on v2

--- a/solution.py
+++ b/solution.py
@@ -112,6 +112,12 @@
 
 
 VMEM = pl.BlockSpec(memory_space=pltpu.VMEM)
+
+
+def in_hbm(value):
+    return pltpu.with_memory_space_constraint(value, pltpu.HBM)
+
+
 SMALL = pltpu.CompilerParams(vmem_limit_bytes=6 << 20)
 
 
@@ -188,8 +194,8 @@
         cost_estimate=pl.CostEstimate(
             flops=4 * rows * residual.size, bytes_accessed=2 * (query.size + key.size + value.size), transcendentals=0
         ),
-    )(residual, gain, query, key, value)
-    return outs[:CHUNKS], outs[CHUNKS : 2 * CHUNKS], outs[2 * CHUNKS :]
+    )(residual, gain, in_hbm(query), in_hbm(key), in_hbm(value))
+    return list(outs[:CHUNKS]), outs[CHUNKS : 2 * CHUNKS], outs[2 * CHUNKS :]
 
 
 def step_kernel(ladder, step, halve, own_ref, got_ref, square_ref, send_ref, keep_ref, total_ref):
@@ -334,90 +340,125 @@
 
 
 def assemble_kernel(ladder, core, step, places, block, *refs):
-    out_ref = refs[4]
     count = refs[0].shape[0] // block
+    width = refs[4].shape[1]
     for k in range(4):
         for p, target in enumerate(targets(ladder, core, step, places, block, count, k)):
-            out_ref[target, :] = refs[k][pl.ds(p * block, block), :]
+            value = refs[k][pl.ds(p * block, block), :]
+            for c, out_ref in enumerate(refs[4:]):
+                out_ref[target, :] = value[:, c * width : (c + 1) * width]
 
 
 def assemble(ladder, core, step, places, block, pieces):
     rows, width = pieces[0].shape
     return pl.pallas_call(
         functools.partial(assemble_kernel, ladder, core, step, places, block),
-        out_shape=jax.ShapeDtypeStruct((4 * rows, width), bf16),
+        out_shape=[jax.ShapeDtypeStruct((4 * rows, width // CHUNKS), bf16)] * CHUNKS,
         in_specs=[VMEM] * 4,
         compiler_params=pltpu.CompilerParams(vmem_limit_bytes=8 << 20),
         cost_estimate=pl.CostEstimate(flops=0, bytes_accessed=16 * rows * width, transcendentals=0),
     )(*pieces)
 
 
-def hidden_kernel(ladder, core, step, places, first, block, model_width, *refs):
+def encode_kernel(ladder, core, steps, places, block, model_width, *refs):
     pieces = refs[:4]
-    residual_ref, enc_any, bias_ref, dec_any = refs[4:8]
-    hidden_ref, low_ref, slope_ref, activity_ref, send_ref, keep_ref = refs[8:14]
-    enc_ref, dec_ref, sems = refs[14:]
-    load_enc = pltpu.make_async_copy(enc_any, enc_ref, sems.at[0])
-    load_dec = pltpu.make_async_copy(dec_any, dec_ref, sems.at[1])
-    load_enc.start()
-    load_dec.start()
+    residual_ref, enc_any, bias_ref, offset_ref = refs[4:8]
+    hidden_ref, low_ref, slope_ref, activity_ref, base_ref, hidden_buf, enc_ref, sems = refs[8:]
+    load = pltpu.make_async_copy(enc_any, enc_ref, sems.at[1])
+    load.start()
     width = pieces[0].shape[1]
     stride = block + EXTRA
     count = pieces[0].shape[0] // stride
-    lanes = pl.ds(first, width)
     tail = jnp.zeros((EXTRA, width), f32)
     for ref in pieces:
         for p in range(count):
             tail = tail + ref[pl.ds(p * stride + block, EXTRA), :].astype(f32)
     inverse = lax.rsqrt(jnp.sum(tail, axis=0, keepdims=True) / model_width + epsilon)
     for k, ref in enumerate(pieces):
-        for p, target in enumerate(targets(ladder, core, step, places, block, count, k)):
-            value = residual_ref[target, lanes].astype(f32) + ref[pl.ds(p * stride, block), :].astype(f32) * inverse
-            hidden_ref[target, :] = value.astype(bf16)
-    load_enc.wait()
-    preact = lax.dot_general(enc_ref[...], hidden_ref[...], (((0,), (0,)), ((), ())), preferred_element_type=f32)
+        for p, target in enumerate(targets(ladder, core, steps[1], places, block, count, k)):
+            value = residual_ref[target, :].astype(f32) + ref[pl.ds(p * stride, block), :].astype(f32) * inverse
+            hidden_buf[target, :] = value.astype(bf16)
+    store = pltpu.make_async_copy(hidden_buf, hidden_ref, sems.at[0])
+    store.start()
+    if places:
+        mine = hidden_buf[aligned(ladder.position(steps), block), :].astype(f32)
+        base_ref[...] = column(offset_ref, width) - mine
+    else:
+        base_ref[...] = column(offset_ref, width)
+    load.wait()
+    preact = lax.dot_general(enc_ref[...], hidden_buf[...], (((0,), (0,)), ((), ())), preferred_element_type=f32)
     scaled = (preact + column(bias_ref, width)) / smoothing
     active = smoothing * (jnp.maximum(scaled, 0.0) + jnp.log1p(jnp.exp(-jnp.abs(scaled))))
-    low = active.astype(bf16)
-    low_ref[...] = low
+    low_ref[...] = active.astype(bf16)
     slope_ref[...] = jax.nn.sigmoid(scaled)
     activity_ref[...] = jnp.sum(active, axis=1, keepdims=True)
-    half = send_ref.shape[0]
-    up = ladder.bit(core)
-    tile = half // 9
-    load_dec.wait()
-    for ref, side in ((send_ref, 1 - up), (keep_ref, up)):
-        for t in range(9):
-            rows = pl.ds(pl.multiple_of(side * half + t * tile, tile), tile)
-            value = lax.dot_general(dec_ref[:, rows], low, (((0,), (0,)), ((), ())), preferred_element_type=f32)
-            ref[pl.ds(t * tile, tile), :] = value.astype(ref.dtype)
-
-
-def encode(ladder, core, step, places, first, block, pieces, residual, encoder, bias, decoder):
+    store.wait()
+
+
+def encode(ladder, core, steps, places, block, pieces, residual, encoder, bias, offset):
     width = pieces[0].shape[1]
     model_width, latents = encoder.shape
-    any_space = pl.BlockSpec(memory_space=pltpu.HBM)
+    hbm = pl.BlockSpec(memory_space=pltpu.HBM)
     return pl.pallas_call(
-        functools.partial(hidden_kernel, ladder, core, step, places, first, block, model_width),
+        functools.partial(encode_kernel, ladder, core, steps, places, block, model_width),
         out_shape=(
             jax.ShapeDtypeStruct((model_width, width), bf16),
             jax.ShapeDtypeStruct((latents, width), bf16),
             jax.ShapeDtypeStruct((latents, width), f32),
             jax.ShapeDtypeStruct((latents, 1), f32),
-            jax.ShapeDtypeStruct((model_width // 2, width), bf16),
-            jax.ShapeDtypeStruct((model_width // 2, width), f32),
-        ),
-        in_specs=[VMEM] * 5 + [any_space, VMEM, any_space],
+            jax.ShapeDtypeStruct((offset.shape[0], width), f32),
+        ),
+        in_specs=[VMEM] * 5 + [hbm] + [VMEM] * 2,
+        out_specs=[hbm] + [VMEM] * 4,
         scratch_shapes=[
+            pltpu.VMEM((model_width, width), bf16),
             pltpu.VMEM(encoder.shape, bf16),
-            pltpu.VMEM(decoder.shape, bf16),
             pltpu.SemaphoreType.DMA((2,)),
         ],
-        compiler_params=pltpu.CompilerParams(vmem_limit_bytes=(5 * encoder.size + (8 << 20))),
+        compiler_params=pltpu.CompilerParams(vmem_limit_bytes=2 * encoder.size + 8 * model_width * width + (4 << 20)),
         cost_estimate=pl.CostEstimate(
-            flops=4 * encoder.size * width, bytes_accessed=4 * encoder.size, transcendentals=4 * latents * width
-        ),
-    )(*pieces, residual, encoder, bias, decoder)
+            flops=2 * encoder.size * width, bytes_accessed=2 * encoder.size, transcendentals=4 * latents * width
+        ),
+    )(*pieces, residual, in_hbm(encoder), bias, offset)
+
+
+def decode_kernel(ladder, core, step, low_ref, peer_low_ref, dec_any, peer_dec_any, send_ref, keep_ref, buf, sems):
+    up = ladder.bit(step)
+    half = send_ref.shape[0]
+    first = 2 * ladder.bit(core)
+    loads = []
+    for i, side in enumerate((1 - up, up)):
+        for j, source in enumerate((dec_any, peer_dec_any)):
+            loads.append(pltpu.make_async_copy(source.at[:, aligned(first + side, half)], buf.at[i, j], sems.at[2 * i + j]))
+            loads[-1].start()
+    lows = (low_ref[...], peer_low_ref[...])
+    tile = half // 3
+    for i, ref in enumerate((send_ref, keep_ref)):
+        loads[2 * i].wait()
+        loads[2 * i + 1].wait()
+        for t in range(3):
+            rows = pl.ds(t * tile, tile)
+            value = sum(
+                lax.dot_general(buf[i, j, :, rows], lows[j], (((0,), (0,)), ((), ())), preferred_element_type=f32)
+                for j in range(2)
+            )
+            ref[rows, :] = value.astype(ref.dtype)
+
+
+def decode(ladder, core, step, low, peer_low, decoder, peer_decoder):
+    latents, width = low.shape
+    half = decoder.shape[1] // 4
+    hbm = pl.BlockSpec(memory_space=pltpu.HBM)
+    return pl.pallas_call(
+        functools.partial(decode_kernel, ladder, core, step),
+        out_shape=(jax.ShapeDtypeStruct((half, width), bf16), jax.ShapeDtypeStruct((half, width), f32)),
+        in_specs=[VMEM] * 2 + [hbm] * 2,
+        scratch_shapes=[pltpu.VMEM((2, 2, latents, half), bf16), pltpu.SemaphoreType.DMA((4,))],
+        compiler_params=pltpu.CompilerParams(vmem_limit_bytes=2 * decoder.size + 6 * half * width + (6 << 20)),
+        cost_estimate=pl.CostEstimate(
+            flops=4 * decoder.size * width, bytes_accessed=4 * decoder.size, transcendentals=0
+        ),
+    )(low, peer_low, in_hbm(decoder), in_hbm(peer_decoder))
 
 
 def final_kernel(ladder, core, steps, *refs):
@@ -556,15 +597,13 @@
         quarter = value.shape[0] // 4
         return [value[k * quarter : (k + 1) * quarter] for k in range(4)]
 
-    steps = cores[1:] + routes[0]
-    residual_own = ladder.gather(mine, steps[1:])
-    residual_far = ladder.swap(residual_own, steps[0])
     half_dim = HEAD_DIM // 2
     frequency = rope_base ** (-2.0 * jnp.arange(half_dim, dtype=f32) / HEAD_DIM)
     angles = frequency[:, None] * jnp.arange(tokens).astype(f32)[None, :]
     cosine, sine = jnp.cos(angles), jnp.sin(angles)
 
     out_t = out_weight.T
+    decoder_peer = ladder.swap(decoder_weight, core)
     norms = jnp.sqrt(jnp.sum(jnp.square(decoder_weight.astype(f32)), axis=1) + epsilon)
 
     if paired:
@@ -595,6 +634,10 @@
             keeps.append(keep)
             squares.append(square[:, cut])
 
+    sends[0], mine = lax.optimization_barrier((sends[0], mine))
+    steps = cores[1:] + routes[0]
+    residual_own = ladder.gather(mine, steps[1:])
+    residual_far = ladder.swap(residual_own, steps[0])
     old = ()
     attendeds = []
     errors, nears, hiddens, lows, slopes, activities = [], [], [], [], [], []
@@ -612,7 +655,10 @@
         residual_all = assemble(ladder, core, steps[0], ladder.order(cores + routes[0]), block, residuals)
     else:
         residual_all = canonical(residuals, steps, block)
-
+        residual_all = [residual_all[:, cut] for cut in cuts]
+
+    slots = [ladder.position(cores + routes[c % len(routes)]) * block for c in range(CHUNKS)]
+    offsets = [lax.dynamic_slice_in_dim(decoder_bias, slot, block) for slot in slots]
     for c, attended in enumerate(attendeds):
         if paired:
             attended = ladder.gather(attended, group_steps[1:])
@@ -626,7 +672,12 @@
                 [(head * gain).astype(bf16), split_rows(jnp.sum(head * head, axis=0, keepdims=True))], axis=0
             )
         steps = routes[c % len(routes)]
-        pieces = ladder.quarters(packed, core, cores[1:] + steps)
+        path = cores[1:] + steps
+        own = ladder.gather(packed, path[1:])
+        if c == 1:
+            own, norms, offsets, residual_all = lax.optimization_barrier((own, norms, offsets, residual_all))
+        far = ladder.swap(own, path[0])
+        pieces = own, far, ladder.swap(own, core), ladder.swap(far, core)
         near = (cores[1:] + steps)[0]
         kernel_block, places = block, ladder.order(cores + steps)
         if not paired:
@@ -642,18 +693,15 @@
                 jnp.concatenate([v, tails if k == 0 else jnp.zeros_like(tails)], axis=0) for k, v in enumerate(whole)
             ]
             kernel_block, places = model_width // 4, ()
-        if c == CHUNKS - 1:
-            last, norms = lax.optimization_barrier((pieces[-1], norms))
-            pieces = (*pieces[:-1], last)
-        hidden, low, slope, activity, send, part = encode(
-            ladder, core, near, places, c * width, kernel_block, pieces, residual_all,
-            encoder_weight, encoder_bias, decoder_weight,
+        slot, offset = slots[c], offsets[c]
+        hidden, low, slope, activity, base = encode(
+            ladder, core, cores + steps, places, kernel_block, pieces, residual_all[c], encoder_weight, encoder_bias, offset
         )
-        part = part + ladder.swap(send, core).astype(f32)
-        rebuilt = ladder.scatter(part, cores[1:] + steps, bf16)
-        slot = ladder.position(cores + steps) * block
-        bias_mine = lax.dynamic_slice_in_dim(decoder_bias, slot, block)[:, None]
-        error = (rebuilt + bias_mine - lax.dynamic_slice_in_dim(hidden, slot, block, axis=0).astype(f32)).astype(bf16)
+        if not paired:
+            base = base - lax.dynamic_slice_in_dim(hidden, slot, block, axis=0).astype(f32)
+        send, part = decode(ladder, core, path[0], low, ladder.swap(low, core), decoder_weight, decoder_peer)
+        part = part + ladder.swap(send, path[0]).astype(f32)
+        error = (ladder.scatter(part, path[1:], bf16) + base).astype(bf16)
         errors.append(ladder.quarters(error, core, cores[1:] + steps))
         nears.append(near)
         hiddens.append(hidden)

time: 156 us -> 151 us (0.968)
  local copies, waits for them, and re-layouts: 13.8 us -> 2.46 us
  starting transfers between devices: 57.8 us -> 62.8 us
  waiting for transfers between devices: 62.1 us -> 57.1 us
  Pallas kernels: 16.9 us -> 21.7 us
    unnamed x40 -> x12, local copies, waits for them, and re-layouts: 12.9 us -> 1.61 us
    ppermute x54 -> x55, starting transfers between devices: 57.8 us -> 62.8 us  [swap(): return lax.ppermute(value, AXES, self.pairs(step))]
    ppermute x54 -> x55, waiting for transfers between devices: 62.1 us -> 57.1 us  [swap(): return lax.ppermute(value, AXES, self.pairs(step))]
    pallas_call x2 -> x4, Pallas kernels: 6.92 us -> 10.7 us  [the longest x2 5.76 us: encode(): pl.pallas_call(functools.partial(encode_kernel, ladder, core, steps, plac...]
    reduce_sum x1, other arithmetic: 0.55 us -> 2.21 us  [on_device(): jnp.sum(jnp.square(decoder_weight.astype(f32)), axis=1) + epsilon]
  transfers between devices with their start and end apart: 54 -> 55, of which waited for: 34 -> 31; matrix products, arithmetic and copies ran while one was open for 3% -> 3% of each run, Pallas kernels for 6% -> 9%
where the time goes in v3:
time: 151 us; the launch traced here: 150 us
  starting transfers between devices  62.8 us (42%)
  waiting for transfers between devices  57.1 us (38%)
  Pallas kernels  21.7 us (14%)
  other arithmetic  4.82 us (3%)
  local copies, waits for them, and re-layouts  2.46 us (2%)
    ppermute x55, starting transfers between devices, swap(): return lax.ppermute(value, AXES, self.pairs(step))  62.8 us
    ppermute x55, waiting for transfers between devices, swap(): return lax.ppermute(value, AXES, self.pairs(step))  57.1 us
    pallas_call x1, Pallas kernels, gradients(): pl.pallas_call(functools.partial(final_kernel, ladder, core, steps), out_...  6.26 us
    pallas_call x2, Pallas kernels, encode(): pl.pallas_call(functools.partial(encode_kernel, ladder, core, steps, plac...  5.76 us
    pallas_call x2, Pallas kernels, decode(): pl.pallas_call(functools.partial(decode_kernel, ladder, core, step), out_...  4.92 us
  transfers between devices with their start and end apart: 55, of which 31 were waited for; matrix products, arithmetic and copies ran while one was open for 3% of the time, Pallas kernels for 9%

profile of v3, /device:TPU:0, one launch (start us, length us, event | category | flops | bytes accessed | tf_op | source)
XLA Modules:
  0.0 150.3 jit_solution(10434770351429957813)
XLA Ops:
  0.6 0.9 slice_select_fusion
  3.2 2.0 %shard_map.130 = (bf16[1040,128]{1,0:T(8,128)(2,1)S(1)}, bf16[1040,128]{1,0:T(8,128)(2,1)S(1)}, f32[1024,128]{1,0:T(8,128)S(1)}, f32[1024,128]{1,0:T(8,128)S(1)}...) custom-call(bf16[288,256]{1,0:T(8,128)(2,1)S(1)} %bitcast.6, f32[288]{0:T(512)S(1)} %copy-done.5, bf16[288,1024]{1,0:T(8,128)(2,1)} %refs_0_.1, ...), custom_call_target="tpu_custom_call" | custom-call | flops 301989888 | bytes 1179648 | tf_op jit(solution)/shard_map/pallas_call | solution.py:183
  5.2 4.1 %collective-permute-start.13 = (bf16[144,256]{1,0:T(8,128)(2,1)S(1)}, bf16[144,256]{1,0:T(8,128)(2,1)S(1)}, u32[]{:S(2)}, u32[]{:S(2)}) collective-permute-start(bf16[144,256]{1,0:T(8,128)(2,1)S(1)} %slice_select_fusion), channel_id=1, source_target_pairs={{0,16},{1,17},{2,18},{3,19},{4,20},{5,21},{6,22},{7,23},{8,24},{9,... | collective-permute-start | bytes 221192 | tf_op jit(solution)/shard_map/ppermute | solution.py:63
  9.3 1.5 collective-permute-start
  11.4 2.2 %multiply_reduce_fusion = f32[256]{0:T(256)S(1)} fusion(bf16[256,4608]{1,0:T(8,128)(2,1)} %refs_16_.1), kind=kLoop, calls=%fused_computation | loop fusion | flops 3538688 | bytes 2360320 | tf_op jit(solution)/shard_map/reduce_sum | solution.py:607
  13.9 1.8 %collective-permute-done.got_ref = bf16[1040,128]{1,0:T(8,128)(2,1)S(1)} collective-permute-done((bf16[1040,128]{1,0:T(8,128)(2,1)S(1)}, bf16[1040,128]{1,0:T(8,128)(2,1)S(1)}, u32[]{:S(2)}, u32[]{:S(2)}) %collective-permute-start) | collective-permute-done | bytes 266272 | tf_op jit(solution)/shard_map/ppermute | solution.py:63
  15.8 1.6 %collective-permute-start.1 = (bf16[528,128]{1,0:T(8,128)(2,1)S(1)}, bf16[528,128]{1,0:T(8,128)(2,1)S(1)}, u32[]{:S(2)}, u32[]{:S(2)}) collective-permute-start(bf16[528,128]{1,0:T(8,128)(2,1)S(1)} %get-tuple-element.65), channel_id=1, source_target_pairs={{0,4},{1,3},{2,6},{3,1},{4,0},{5,7},{6,2},{7,5},{8,12},{9,11},{10,... | collective-permute-start | bytes 405512 | tf_op jit(solution)/shard_map/ppermute | solution.py:63
  17.4 2.6 %collective-permute-done.31.got_ref = bf16[1040,128]{1,0:T(8,128)(2,1)S(1)} collective-permute-done((bf16[1040,128]{1,0:T(8,128)(2,1)S(1)}, bf16[1040,128]{1,0:T(8,128)(2,1)S(1)}, u32[]{:S(2)}, u32[]{:S(2)}) %collective-permute-start.31) | collective-permute-done | bytes 266272 | tf_op jit(solution)/shard_map/ppermute | solution.py:63
  20.0 1.6 %collective-permute-start.32 = (bf16[528,128]{1,0:T(8,128)(2,1)S(1)}, bf16[528,128]{1,0:T(8,128)(2,1)S(1)}, u32[]{:S(2)}, u32[]{:S(2)}) collective-permute-start(bf16[528,128]{1,0:T(8,128)(2,1)S(1)} %get-tuple-element.86), channel_id=1, source_target_pairs={{0,4},{1,3},{2,6},{3,1},{4,0},{5,7},{6,2},{7,5},{8,12},{9,11},{10,... | collective-permute-start | bytes 405512 | tf_op jit(solution)/shard_map/ppermute | solution.py:63
  21.6 1.6 %collective-permute-start.14 = (bf16[288,256]{1,0:T(8,128)(2,1)S(1)}, bf16[288,256]{1,0:T(8,128)(2,1)S(1)}, u32[]{:S(2)}, u32[]{:S(2)}) collective-permute-start(bf16[288,256]{1,0:T(8,128)(2,1)S(1)} %pad_maximum_fusion.8), channel_id=1, source_target_pairs={{0,8},{1,3},{2,10},{3,1},{4,12},{5,7},{6,14},{7,5},{8,0},{9,11},{1... | collective-permute-start | bytes 442376 | tf_op jit(solution)/shard_map/ppermute | solution.py:63
  23.8 1.2 collective-permute-done.32.got_ref
  25.1 1.6 %collective-permute-start.33 = (bf16[528,128]{1,0:T(8,128)(2,1)S(1)}, bf16[528,128]{1,0:T(8,128)(2,1)S(1)}, u32[]{:S(2)}, u32[]{:S(2)}) collective-permute-start(bf16[528,128]{1,0:T(8,128)(2,1)S(1)} %get-tuple-element.89), channel_id=1, source_target_pairs={{0,8},{1,9},{2,10},{3,11},{4,12},{5,13},{6,14},{7,15},{8,0},{9,1},... | collective-permute-start | bytes 405512 | tf_op jit(solution)/shard_map/ppermute | solution.py:63
  27.6 2.9 %collective-permute-done.2.got_ref = bf16[528,128]{1,0:T(8,128)(2,1)S(1)} collective-permute-done((bf16[528,128]{1,0:T(8,128)(2,1)S(1)}, bf16[528,128]{1,0:T(8,128)(2,1)S(1)}, u32[]{:S(2)}, u32[]{:S(2)}) %collective-permute-start.2) | collective-permute-done | bytes 135200 | tf_op jit(solution)/shard_map/ppermute | solution.py:63
  30.7 1.6 %collective-permute-done.33.got_ref = bf16[528,128]{1,0:T(8,128)(2,1)S(1)} collective-permute-done((bf16[528,128]{1,0:T(8,128)(2,1)S(1)}, bf16[528,128]{1,0:T(8,128)(2,1)S(1)}, u32[]{:S(2)}, u32[]{:S(2)}) %collective-permute-start.33) | collective-permute-done | bytes 135200 | tf_op jit(solution)/shard_map/ppermute | solution.py:63
  32.3 1.4 collective-permute-start.34
  33.7 2.9 %collective-permute-done.3.got_ref = bf16[528,128]{1,0:T(8,128)(2,1)S(1)} collective-permute-done((bf16[528,128]{1,0:T(8,128)(2,1)S(1)}, bf16[528,128]{1,0:T(8,128)(2,1)S(1)}, u32[]{:S(2)}, u32[]{:S(2)}) %collective-permute-start.3) | collective-permute-done | bytes 135200 | tf_op jit(solution)/shard_map/ppermute | solution.py:63
  37.1 1.8 %collective-permute-start.4 = (bf16[256,128]{1,0:T(8,128)(2,1)S(1)}, bf16[256,128]{1,0:T(8,128)(2,1)S(1)}, u32[]{:S(2)}, u32[]{:S(2)}) collective-permute-start(bf16[256,128]{1,0:T(8,128)(2,1)S(1)} %get-tuple-element.73), channel_id=1, source_target_pairs={{0,4},{1,3},{2,6},{3,1},{4,0},{5,7},{6,2},{7,5},{8,12},{9,11},{10,... | collective-permute-start | bytes 196616 | tf_op jit(solution)/shard_map/ppermute | solution.py:63
  40.3 1.6 %collective-permute-start.35 = (bf16[256,128]{1,0:T(8,128)(2,1)S(1)}, bf16[256,128]{1,0:T(8,128)(2,1)S(1)}, u32[]{:S(2)}, u32[]{:S(2)}) collective-permute-start(bf16[256,128]{1,0:T(8,128)(2,1)S(1)} %get-tuple-element.96), channel_id=1, source_target_pairs={{0,4},{1,3},{2,6},{3,1},{4,0},{5,7},{6,2},{7,5},{8,12},{9,11},{10,... | collective-permute-start | bytes 196616 | tf_op jit(solution)/shard_map/ppermute | solution.py:63
  42.0 1.7 %collective-permute-start.5 = (bf16[512,128]{1,0:T(8,128)(2,1)S(1)}, bf16[512,128]{1,0:T(8,128)(2,1)S(1)}, u32[]{:S(2)}, u32[]{:S(2)}) collective-permute-start(bf16[512,128]{1,0:T(8,128)(2,1)S(1)} %pad_maximum_fusion.11.own_ref), channel_id=1, source_target_pairs={{0,2},{1,5},{2,0},{3,7},{4,6},{5,1},{6,4},{7,3},{8,10},{9,13},{10,... | collective-permute-start | bytes 393224 | tf_op jit(solution)/shard_map/ppermute | solution.py:63
  43.7 3.0 %collective-permute-done.35 = bf16[256,128]{1,0:T(8,128)(2,1)S(1)} collective-permute-done((bf16[256,128]{1,0:T(8,128)(2,1)S(1)}, bf16[256,128]{1,0:T(8,128)(2,1)S(1)}, u32[]{:S(2)}, u32[]{:S(2)}) %collective-permute-start.35) | collective-permute-done | bytes 65568 | tf_op jit(solution)/shard_map/ppermute | solution.py:63
  46.7 1.6 %collective-permute-start.36 = (bf16[512,128]{1,0:T(8,128)(2,1)S(1)}, bf16[512,128]{1,0:T(8,128)(2,1)S(1)}, u32[]{:S(2)}, u32[]{:S(2)}) collective-permute-start(bf16[512,128]{1,0:T(8,128)(2,1)S(1)} %pad_maximum_fusion.12.own_ref), channel_id=1, source_target_pairs={{0,2},{1,5},{2,0},{3,7},{4,6},{5,1},{6,4},{7,3},{8,10},{9,13},{10,... | collective-permute-start | bytes 393224 | tf_op jit(solution)/shard_map/ppermute | solution.py:63
  48.8 3.0 %collective-permute-done.36.got_ref = bf16[512,128]{1,0:T(8,128)(2,1)S(1)} collective-permute-done((bf16[512,128]{1,0:T(8,128)(2,1)S(1)}, bf16[512,128]{1,0:T(8,128)(2,1)S(1)}, u32[]{:S(2)}, u32[]{:S(2)}) %collective-permute-start.36) | collective-permute-done | bytes 131104 | tf_op jit(solution)/shard_map/ppermute | solution.py:63
  53.3 2.0 %collective-permute-start.16 = (bf16[1152,256]{1,0:T(8,128)(2,1)S(1)}, bf16[1152,256]{1,0:T(8,128)(2,1)S(1)}, u32[]{:S(2)}, u32[]{:S(2)}) collective-permute-start(bf16[1152,256]{1,0:T(8,128)(2,1)S(1)} %pad_maximum_fusion.refs_0_), channel_id=1, source_target_pairs={{0,2},{1,5},{2,0},{3,7},{4,6},{5,1},{6,4},{7,3},{8,10},{9,13},{10,... | collective-permute-start | bytes 1769480 | tf_op jit(solution)/shard_map/ppermute | solution.py:63
  55.4 1.8 %collective-permute-start.38 = (bf16[160,128]{1,0:T(8,128)(2,1)S(1)}, bf16[160,128]{1,0:T(8,128)(2,1)S(1)}, u32[]{:S(2)}, u32[]{:S(2)}) collective-permute-start(bf16[160,128]{1,0:T(8,128)(2,1)S(1)} %shard_map.145), channel_id=1, source_target_pairs={{0,16},{1,17},{2,18},{3,19},{4,20},{5,21},{6,22},{7,23},{8,24},{9,... | collective-permute-start | bytes 122888 | tf_op jit(solution)/shard_map/ppermute | solution.py:63
  57.3 2.4 %collective-permute-start.8 = (bf16[320,128]{1,0:T(8,128)(2,1)S(1)}, bf16[320,128]{1,0:T(8,128)(2,1)S(1)}, u32[]{:S(2)}, u32[]{:S(2)}) collective-permute-start(bf16[320,128]{1,0:T(8,128)(2,1)S(1)} %pad_maximum_fusion.13), channel_id=1, source_target_pairs={{0,8},{1,3},{2,10},{3,1},{4,12},{5,7},{6,14},{7,5},{8,0},{9,11},{1... | collective-permute-start | bytes 245768 | tf_op jit(solution)/shard_map/ppermute | solution.py:63
  59.7 1.0 collective-permute-done.38
  60.7 1.3 collective-permute-start.39
  62.4 2.1 %collective-permute-start.9 = (bf16[640,128]{1,0:T(8,128)(2,1)S(1)}, bf16[640,128]{1,0:T(8,128)(2,1)S(1)}, u32[]{:S(2)}, u32[]{:S(2)}) collective-permute-start(bf16[640,128]{1,0:T(8,128)(2,1)S(1)} %pad_maximum_fusion.6), channel_id=1, source_target_pairs={{0,4},{1,9},{2,6},{3,11},{4,0},{5,13},{6,2},{7,15},{8,12},{9,1},{1... | collective-permute-start | bytes 491528 | tf_op jit(solution)/shard_map/ppermute | solution.py:63
  65.3 0.9 collective-permute-start.40
  66.2 1.6 %collective-permute-done.9 = bf16[640,128]{1,0:T(8,128)(2,1)S(1)} collective-permute-done((bf16[640,128]{1,0:T(8,128)(2,1)S(1)}, bf16[640,128]{1,0:T(8,128)(2,1)S(1)}, u32[]{:S(2)}, u32[]{:S(2)}) %collective-permute-start.9) | collective-permute-done | bytes 163872 | tf_op jit(solution)/shard_map/ppermute | solution.py:63
  67.9 1.6 %collective-permute-start.10 = (bf16[1280,128]{1,0:T(8,128)(2,1)S(1)}, bf16[1280,128]{1,0:T(8,128)(2,1)S(1)}, u32[]{:S(2)}, u32[]{:S(2)}) collective-permute-start(bf16[1280,128]{1,0:T(8,128)(2,1)S(1)} %pad_maximum_fusion.1.refs_0_), channel_id=1, source_target_pairs={{0,2},{1,5},{2,0},{3,7},{4,6},{5,1},{6,4},{7,3},{8,10},{9,13},{10,... | collective-permute-start | bytes 983048 | tf_op jit(solution)/shard_map/ppermute | solution.py:63
  69.5 1.2 collective-permute-done.40
  71.1 1.6 %collective-permute-start.41 = (bf16[1280,128]{1,0:T(8,128)(2,1)S(1)}, bf16[1280,128]{1,0:T(8,128)(2,1)S(1)}, u32[]{:S(2)}, u32[]{:S(2)}) collective-permute-start(bf16[1280,128]{1,0:T(8,128)(2,1)S(1)} %pad_maximum_fusion.2.refs_0_), channel_id=1, source_target_pairs={{0,8},{1,5},{2,10},{3,7},{4,12},{5,1},{6,14},{7,3},{8,0},{9,13},{1... | collective-permute-start | bytes 983048 | tf_op jit(solution)/shard_map/ppermute | solution.py:63
  72.7 2.4 %collective-permute-done.10.refs_1_ = bf16[1280,128]{1,0:T(8,128)(2,1)S(1)} collective-permute-done((bf16[1280,128]{1,0:T(8,128)(2,1)S(1)}, bf16[1280,128]{1,0:T(8,128)(2,1)S(1)}, u32[]{:S(2)}, u32[]{:S(2)}) %collective-permute-start.10) | collective-permute-done | bytes 327712 | tf_op jit(solution)/shard_map/ppermute | solution.py:63
  75.6 2.7 %collective-permute-done.41.refs_1_ = bf16[1280,128]{1,0:T(8,128)(2,1)S(1)} collective-permute-done((bf16[1280,128]{1,0:T(8,128)(2,1)S(1)}, bf16[1280,128]{1,0:T(8,128)(2,1)S(1)}, u32[]{:S(2)}, u32[]{:S(2)}) %collective-permute-start.41) | collective-permute-done | bytes 327712 | tf_op jit(solution)/shard_map/ppermute | solution.py:63
  78.3 2.9 %shard_map.138 = (bf16[4608,128]{1,0:T(8,128)(2,1)S(1)}, bf16[256,128]{1,0:T(8,128)(2,1)S(1)}, f32[256,128]{1,0:T(8,128)S(1)}, f32[256,1]{1,0:T(8,128)S(1)}, f32[144,128]{1,0:T(8,128)S(1)}) custom-call(bf16[1280,128]{1,0:T(8,128)(2,1)S(1)} %pad_maximum_fusion.1.refs_0_, bf16[1280,128]{1,0:T(8,128)(2,1)S(1)} %collective-permute-done.10.refs_1_, ...), custom_call_target="tpu_custom_call" | custom-call | flops 301989888 | bytes 2359296 | tf_op jit(solution)/shard_map/pallas_call | solution.py:402
  82.7 2.5 %shard_map.139 = (bf16[1152,128]{1,0:T(8,128)(2,1)S(1)}, f32[1152,128]{1,0:T(8,128)S(1)}) custom-call(bf16[256,128]{1,0:T(8,128)(2,1)S(1)} %get-tuple-element.78.low_ref.refs_10_, bf16[256,128]{1,0:T(8,128)(2,1)S(1)} %collective-permute-done.19.peer_low_ref, bf16[256,4608]{1,0:T(8,128)(2,1)} %refs_16_.1, bf16[256,4608]{1,0:T(8,128)(2,1)} %collective-permute-done.20.peer_dec_any), custom_call_target="tpu_custom_call" | custom-call | flops 603979776 | bytes 4718592 | tf_op jit(solution)/shard_map/pallas_call | solution.py:452
  85.1 1.0 collective-permute-start.21
  86.1 2.9 %shard_map.146 = (bf16[4608,128]{1,0:T(8,128)(2,1)S(1)}, bf16[256,128]{1,0:T(8,128)(2,1)S(1)}, f32[256,128]{1,0:T(8,128)S(1)}, f32[256,1]{1,0:T(8,128)S(1)}, f32[144,128]{1,0:T(8,128)S(1)}) custom-call(bf16[1280,128]{1,0:T(8,128)(2,1)S(1)} %pad_maximum_fusion.2.refs_0_, bf16[1280,128]{1,0:T(8,128)(2,1)S(1)} %collective-permute-done.41.refs_1_, ...), custom_call_target="tpu_custom_call" | custom-call | flops 301989888 | bytes 2359296 | tf_op jit(solution)/shard_map/pallas_call | solution.py:402
  90.3 2.5 %shard_map.147 = (bf16[1152,128]{1,0:T(8,128)(2,1)S(1)}, f32[1152,128]{1,0:T(8,128)S(1)}) custom-call(bf16[256,128]{1,0:T(8,128)(2,1)S(1)} %get-tuple-element.103.low_ref.refs_11_, bf16[256,128]{1,0:T(8,128)(2,1)S(1)} %collective-permute-done.44.peer_low_ref, bf16[256,4608]{1,0:T(8,128)(2,1)} %refs_16_.1, bf16[256,4608]{1,0:T(8,128)(2,1)} %collective-permute-done.20.peer_dec_any), custom_call_target="tpu_custom_call" | custom-call | flops 603979776 | bytes 4718592 | tf_op jit(solution)/shard_map/pallas_call | solution.py:452
  92.8 1.4 collective-permute-start.45
  94.3 1.2 collective-permute-start.22
  95.4 5.8 %collective-permute-done.45 = bf16[1152,128]{1,0:T(8,128)(2,1)S(1)} collective-permute-done((bf16[1152,128]{1,0:T(8,128)(2,1)S(1)}, bf16[1152,128]{1,0:T(8,128)(2,1)S(1)}, u32[]{:S(2)}, u32[]{:S(2)}) %collective-permute-start.45) | collective-permute-done | bytes 294944 | tf_op jit(solution)/shard_map/ppermute | solution.py:63
  101.3 1.2 collective-permute-start.46
  102.5 1.3 collective-permute-start.23
  103.8 3.0 %collective-permute-done.46 = bf16[576,128]{1,0:T(8,128)(2,1)S(1)} collective-permute-done((bf16[576,128]{1,0:T(8,128)(2,1)S(1)}, bf16[576,128]{1,0:T(8,128)(2,1)S(1)}, u32[]{:S(2)}, u32[]{:S(2)}) %collective-permute-start.46) | collective-permute-done | bytes 147488 | tf_op jit(solution)/shard_map/ppermute | solution.py:63
  107.0 1.7 %collective-permute-start.24 = (bf16[144,128]{1,0:T(8,128)(2,1)S(1)}, bf16[144,128]{1,0:T(8,128)(2,1)S(1)}, u32[]{:S(2)}, u32[]{:S(2)}) collective-permute-start(bf16[144,128]{1,0:T(8,128)(2,1)S(1)} %select_convert_fusion.5), channel_id=1, source_target_pairs={{0,16},{1,17},{2,18},{3,19},{4,20},{5,21},{6,22},{7,23},{8,24},{9,... | collective-permute-start | bytes 110600 | tf_op jit(solution)/shard_map/ppermute | solution.py:63
  108.7 1.4 collective-permute-start.47
  110.2 1.8 %collective-permute-done.24 = bf16[144,128]{1,0:T(8,128)(2,1)S(1)} collective-permute-done((bf16[144,128]{1,0:T(8,128)(2,1)S(1)}, bf16[144,128]{1,0:T(8,128)(2,1)S(1)}, u32[]{:S(2)}, u32[]{:S(2)}) %collective-permute-start.24) | collective-permute-done | bytes 36896 | tf_op jit(solution)/shard_map/ppermute | solution.py:63
  112.0 1.7 %collective-permute-start.25 = (bf16[144,128]{1,0:T(8,128)(2,1)S(1)}, bf16[144,128]{1,0:T(8,128)(2,1)S(1)}, u32[]{:S(2)}, u32[]{:S(2)}) collective-permute-start(bf16[144,128]{1,0:T(8,128)(2,1)S(1)} %add_convert_fusion.1), channel_id=1, source_target_pairs={{0,16},{1,17},{2,18},{3,19},{4,20},{5,21},{6,22},{7,23},{8,24},{9,... | collective-permute-start | bytes 110600 | tf_op jit(solution)/shard_map/ppermute | solution.py:63
  113.8 1.3 collective-permute-start.48
  115.2 2.2 %collective-permute-done.25 = bf16[144,128]{1,0:T(8,128)(2,1)S(1)} collective-permute-done((bf16[144,128]{1,0:T(8,128)(2,1)S(1)}, bf16[144,128]{1,0:T(8,128)(2,1)S(1)}, u32[]{:S(2)}, u32[]{:S(2)}) %collective-permute-start.25) | collective-permute-done | bytes 36896 | tf_op jit(solution)/shard_map/ppermute | solution.py:63
  117.4 1.4 collective-permute-done.48
  118.8 1.4 collective-permute-start.49
  120.2 2.8 %collective-permute-start.26 = (bf16[288,128]{1,0:T(8,128)(2,1)S(1)}, bf16[288,128]{1,0:T(8,128)(2,1)S(1)}, u32[]{:S(2)}, u32[]{:S(2)}) collective-permute-start(bf16[288,128]{1,0:T(8,128)(2,1)S(1)} %pad_maximum_fusion.15), channel_id=1, source_target_pairs={{0,8},{1,3},{2,10},{3,1},{4,12},{5,7},{6,14},{7,5},{8,0},{9,11},{1... | collective-permute-start | bytes 221192 | tf_op jit(solution)/shard_map/ppermute | solution.py:63
  123.8 1.6 %collective-permute-start.50 = (bf16[288,128]{1,0:T(8,128)(2,1)S(1)}, bf16[288,128]{1,0:T(8,128)(2,1)S(1)}, u32[]{:S(2)}, u32[]{:S(2)}) collective-permute-start(bf16[288,128]{1,0:T(8,128)(2,1)S(1)} %pad_maximum_fusion.16), channel_id=1, source_target_pairs={{0,4},{1,9},{2,6},{3,11},{4,0},{5,13},{6,2},{7,15},{8,12},{9,1},{1... | collective-permute-start | bytes 221192 | tf_op jit(solution)/shard_map/ppermute | solution.py:63
  127.0 1.2 collective-permute-done.50
  128.3 1.2 collective-permute-start.51
  129.5 3.4 %collective-permute-done.27 = bf16[576,128]{1,0:T(8,128)(2,1)S(1)} collective-permute-done((bf16[576,128]{1,0:T(8,128)(2,1)S(1)}, bf16[576,128]{1,0:T(8,128)(2,1)S(1)}, u32[]{:S(2)}, u32[]{:S(2)}) %collective-permute-start.27) | collective-permute-done | bytes 147488 | tf_op jit(solution)/shard_map/ppermute | solution.py:63
  133.7 3.8 %collective-permute-start.52 = (bf16[1152,128]{1,0:T(8,128)(2,1)S(1)}, bf16[1152,128]{1,0:T(8,128)(2,1)S(1)}, u32[]{:S(2)}, u32[]{:S(2)}) collective-permute-start(bf16[1152,128]{1,0:T(8,128)(2,1)S(1)} %pad_maximum_fusion.5.refs_4_), channel_id=1, source_target_pairs={{0,8},{1,5},{2,10},{3,7},{4,12},{5,1},{6,14},{7,3},{8,0},{9,13},{1... | collective-permute-start | bytes 884744 | tf_op jit(solution)/shard_map/ppermute | solution.py:63
  138.1 1.7 %collective-permute-done.28.refs_1_ = bf16[1152,128]{1,0:T(8,128)(2,1)S(1)} collective-permute-done((bf16[1152,128]{1,0:T(8,128)(2,1)S(1)}, bf16[1152,128]{1,0:T(8,128)(2,1)S(1)}, u32[]{:S(2)}, u32[]{:S(2)}) %collective-permute-start.28) | collective-permute-done | bytes 294944 | tf_op jit(solution)/shard_map/ppermute | solution.py:63
  139.8 2.5 %collective-permute-done.52.refs_5_ = bf16[1152,128]{1,0:T(8,128)(2,1)S(1)} collective-permute-done((bf16[1152,128]{1,0:T(8,128)(2,1)S(1)}, bf16[1152,128]{1,0:T(8,128)(2,1)S(1)}, u32[]{:S(2)}, u32[]{:S(2)}) %collective-permute-start.52) | collective-permute-done | bytes 294944 | tf_op jit(solution)/shard_map/ppermute | solution.py:63
  142.3 1.6 %collective-permute-done.54.refs_7_ = bf16[1152,128]{1,0:T(8,128)(2,1)S(1)} collective-permute-done((bf16[1152,128]{1,0:T(8,128)(2,1)S(1)}, bf16[1152,128]{1,0:T(8,128)(2,1)S(1)}, u32[]{:S(2)}, u32[]{:S(2)}) %collective-permute-start.54) | collective-permute-done | bytes 294944 | tf_op jit(solution)/shard_map/ppermute | solution.py:63
  143.9 6.3 %shard_map.148 = (bf16[4608,256]{1,0:T(8,128)(2,1)}, f32[1,256]{1,0:T(1,128)}, bf16[256,4608]{1,0:T(8,128)(2,1)}) custom-call(bf16[1152,128]{1,0:T(8,128)(2,1)S(1)} %pad_maximum_fusion.4.refs_0_, bf16[1152,128]{1,0:T(8,128)(2,1)S(1)} %collective-permute-done.28.refs_1_, bf16[1152,128]{1,0:T(8,128)(2,1)S(1)} %collective-permute-done.29.refs_2_, ...), custom_call_target="tpu_custom_call" | custom-call | flops 1811939328 | bytes 14155776 | tf_op jit(solution)/shard_map/pallas_call | solution.py:520
  (132 shorter events, 17.7 us)
Async XLA Ops:
  1.6 0.9 copy-start.2
  2.5 0.7 copy-start.5
  5.2 16.4 %collective-permute-start.13 = (bf16[144,256]{1,0:T(8,128)(2,1)S(1)}, bf16[144,256]{1,0:T(8,128)(2,1)S(1)}, u32[]{:S(2)}, u32[]{:S(2)}) collective-permute-start(bf16[144,256]{1,0:T(8,128)(2,1)S(1)} %slice_select_fusion), channel_id=1, source_target_pairs={{0,16},{1,17},{2,18},{3,19},{4,20},{5,21},{6,22},{7,23},{8,24},{9,... | collective-permute-start | bytes 221192 | tf_op jit(solution)/shard_map/ppermute | solution.py:63
  9.3 6.4 %collective-permute-start = (bf16[1040,128]{1,0:T(8,128)(2,1)S(1)}, bf16[1040,128]{1,0:T(8,128)(2,1)S(1)}, u32[]{:S(2)}, u32[]{:S(2)}) collective-permute-start(bf16[1040,128]{1,0:T(8,128)(2,1)S(1)} %get-tuple-element.62), channel_id=1, source_target_pairs={{0,2},{1,5},{2,0},{3,7},{4,6},{5,1},{6,4},{7,3},{8,10},{9,13},{10,... | collective-permute-start | bytes 798728 | tf_op jit(solution)/shard_map/ppermute | solution.py:63
  10.8 9.1 %collective-permute-start.31 = (bf16[1040,128]{1,0:T(8,128)(2,1)S(1)}, bf16[1040,128]{1,0:T(8,128)(2,1)S(1)}, u32[]{:S(2)}, u32[]{:S(2)}) collective-permute-start(bf16[1040,128]{1,0:T(8,128)(2,1)S(1)} %get-tuple-element.83), channel_id=1, source_target_pairs={{0,2},{1,5},{2,0},{3,7},{4,6},{5,1},{6,4},{7,3},{8,10},{9,13},{10,... | collective-permute-start | bytes 798728 | tf_op jit(solution)/shard_map/ppermute | solution.py:63
  11.3 71.3 %collective-permute-start.20 = (bf16[256,4608]{1,0:T(8,128)(2,1)}, bf16[256,4608]{1,0:T(8,128)(2,1)}, u32[]{:S(2)}, u32[]{:S(2)}) collective-permute-start(bf16[256,4608]{1,0:T(8,128)(2,1)} %refs_16_.1), channel_id=1, source_target_pairs={{0,1},{1,0},{2,3},{3,2},{4,5},{5,4},{6,7},{7,6},{8,9},{9,8},{10,11... | collective-permute-start | bytes 7077896 | tf_op jit(solution)/shard_map/ppermute | solution.py:63
  15.8 7.5 %collective-permute-start.1 = (bf16[528,128]{1,0:T(8,128)(2,1)S(1)}, bf16[528,128]{1,0:T(8,128)(2,1)S(1)}, u32[]{:S(2)}, u32[]{:S(2)}) collective-permute-start(bf16[528,128]{1,0:T(8,128)(2,1)S(1)} %get-tuple-element.65), channel_id=1, source_target_pairs={{0,4},{1,3},{2,6},{3,1},{4,0},{5,7},{6,2},{7,5},{8,12},{9,11},{10,... | collective-permute-start | bytes 405512 | tf_op jit(solution)/shard_map/ppermute | solution.py:63
  20.0 5.1 %collective-permute-start.32 = (bf16[528,128]{1,0:T(8,128)(2,1)S(1)}, bf16[528,128]{1,0:T(8,128)(2,1)S(1)}, u32[]{:S(2)}, u32[]{:S(2)}) collective-permute-start(bf16[528,128]{1,0:T(8,128)(2,1)S(1)} %get-tuple-element.86), channel_id=1, source_target_pairs={{0,4},{1,3},{2,6},{3,1},{4,0},{5,7},{6,2},{7,5},{8,12},{9,11},{10,... | collective-permute-start | bytes 405512 | tf_op jit(solution)/shard_map/ppermute | solution.py:63
  21.6 12.1 %collective-permute-start.14 = (bf16[288,256]{1,0:T(8,128)(2,1)S(1)}, bf16[288,256]{1,0:T(8,128)(2,1)S(1)}, u32[]{:S(2)}, u32[]{:S(2)}) collective-permute-start(bf16[288,256]{1,0:T(8,128)(2,1)S(1)} %pad_maximum_fusion.8), channel_id=1, source_target_pairs={{0,8},{1,3},{2,10},{3,1},{4,12},{5,7},{6,14},{7,5},{8,0},{9,11},{1... | collective-permute-start | bytes 442376 | tf_op jit(solution)/shard_map/ppermute | solution.py:63
  23.3 24.9 %copy-start.1 = (bf16[1024,288]{0,1:T(8,128)(2,1)S(1)}, bf16[1024,288]{0,1:T(8,128)(2,1)}, u32[]{:S(2)}) copy-start(bf16[1024,288]{0,1:T(8,128)(2,1)} %param.16) | copy-start | bytes 1769476
  23.3 7.2 %collective-permute-start.2 = (bf16[528,128]{1,0:T(8,128)(2,1)S(1)}, bf16[528,128]{1,0:T(8,128)(2,1)S(1)}, u32[]{:S(2)}, u32[]{:S(2)}) collective-permute-start(bf16[528,128]{1,0:T(8,128)(2,1)S(1)} %get-tuple-element.68), channel_id=1, source_target_pairs={{0,8},{1,9},{2,10},{3,11},{4,12},{5,13},{6,14},{7,15},{8,0},{9,1},... | collective-permute-start | bytes 405512 | tf_op jit(solution)/shard_map/ppermute | solution.py:63
  25.1 7.1 %collective-permute-start.33 = (bf16[528,128]{1,0:T(8,128)(2,1)S(1)}, bf16[528,128]{1,0:T(8,128)(2,1)S(1)}, u32[]{:S(2)}, u32[]{:S(2)}) collective-permute-start(bf16[528,128]{1,0:T(8,128)(2,1)S(1)} %get-tuple-element.89), channel_id=1, source_target_pairs={{0,8},{1,9},{2,10},{3,11},{4,12},{5,13},{6,14},{7,15},{8,0},{9,1},... | collective-permute-start | bytes 405512 | tf_op jit(solution)/shard_map/ppermute | solution.py:63
  30.6 6.1 %collective-permute-start.3 = (bf16[528,128]{1,0:T(8,128)(2,1)S(1)}, bf16[528,128]{1,0:T(8,128)(2,1)S(1)}, u32[]{:S(2)}, u32[]{:S(2)}) collective-permute-start(bf16[528,128]{1,0:T(8,128)(2,1)S(1)} %get-tuple-element.71), channel_id=1, source_target_pairs={{0,16},{1,17},{2,18},{3,19},{4,20},{5,21},{6,22},{7,23},{8,24},{9,... | collective-permute-start | bytes 405512 | tf_op jit(solution)/shard_map/ppermute | solution.py:63
  32.3 7.2 %collective-permute-start.34 = (bf16[528,128]{1,0:T(8,128)(2,1)S(1)}, bf16[528,128]{1,0:T(8,128)(2,1)S(1)}, u32[]{:S(2)}, u32[]{:S(2)}) collective-permute-start(bf16[528,128]{1,0:T(8,128)(2,1)S(1)} %get-tuple-element.92), channel_id=1, source_target_pairs={{0,16},{1,17},{2,18},{3,19},{4,20},{5,21},{6,22},{7,23},{8,24},{9,... | collective-permute-start | bytes 405512 | tf_op jit(solution)/shard_map/ppermute | solution.py:63
  37.1 4.9 %collective-permute-start.4 = (bf16[256,128]{1,0:T(8,128)(2,1)S(1)}, bf16[256,128]{1,0:T(8,128)(2,1)S(1)}, u32[]{:S(2)}, u32[]{:S(2)}) collective-permute-start(bf16[256,128]{1,0:T(8,128)(2,1)S(1)} %get-tuple-element.73), channel_id=1, source_target_pairs={{0,4},{1,3},{2,6},{3,1},{4,0},{5,7},{6,2},{7,5},{8,12},{9,11},{10,... | collective-permute-start | bytes 196616 | tf_op jit(solution)/shard_map/ppermute | solution.py:63
  38.9 13.2 %copy-start.3 = (f32[288]{0:T(512)S(1)}, f32[288]{0:T(512)}, u32[]{:S(2)}) copy-start(f32[288]{0:T(512)} %gain_ref.5) | copy-start | bytes 3460
  39.0 9.7 %collective-permute-start.15 = (bf16[576,256]{1,0:T(8,128)(2,1)S(1)}, bf16[576,256]{1,0:T(8,128)(2,1)S(1)}, u32[]{:S(2)}, u32[]{:S(2)}) collective-permute-start(bf16[576,256]{1,0:T(8,128)(2,1)S(1)} %pad_maximum_fusion.3), channel_id=1, source_target_pairs={{0,4},{1,9},{2,6},{3,11},{4,0},{5,13},{6,2},{7,15},{8,12},{9,1},{1... | collective-permute-start | bytes 884744 | tf_op jit(solution)/shard_map/ppermute | solution.py:63
  40.3 6.3 %collective-permute-start.35 = (bf16[256,128]{1,0:T(8,128)(2,1)S(1)}, bf16[256,128]{1,0:T(8,128)(2,1)S(1)}, u32[]{:S(2)}, u32[]{:S(2)}) collective-permute-start(bf16[256,128]{1,0:T(8,128)(2,1)S(1)} %get-tuple-element.96), channel_id=1, source_target_pairs={{0,4},{1,3},{2,6},{3,1},{4,0},{5,7},{6,2},{7,5},{8,12},{9,11},{10,... | collective-permute-start | bytes 196616 | tf_op jit(solution)/shard_map/ppermute | solution.py:63
  42.0 6.2 %collective-permute-start.5 = (bf16[512,128]{1,0:T(8,128)(2,1)S(1)}, bf16[512,128]{1,0:T(8,128)(2,1)S(1)}, u32[]{:S(2)}, u32[]{:S(2)}) collective-permute-start(bf16[512,128]{1,0:T(8,128)(2,1)S(1)} %pad_maximum_fusion.11.own_ref), channel_id=1, source_target_pairs={{0,2},{1,5},{2,0},{3,7},{4,6},{5,1},{6,4},{7,3},{8,10},{9,13},{10,... | collective-permute-start | bytes 393224 | tf_op jit(solution)/shard_map/ppermute | solution.py:63
  46.7 5.0 %collective-permute-start.36 = (bf16[512,128]{1,0:T(8,128)(2,1)S(1)}, bf16[512,128]{1,0:T(8,128)(2,1)S(1)}, u32[]{:S(2)}, u32[]{:S(2)}) collective-permute-start(bf16[512,128]{1,0:T(8,128)(2,1)S(1)} %pad_maximum_fusion.12.own_ref), channel_id=1, source_target_pairs={{0,2},{1,5},{2,0},{3,7},{4,6},{5,1},{6,4},{7,3},{8,10},{9,13},{10,... | collective-permute-start | bytes 393224 | tf_op jit(solution)/shard_map/ppermute | solution.py:63
  48.6 3.6 %collective-permute-start.6 = (f32[144,128]{1,0:T(8,128)S(1)}, f32[144,128]{1,0:T(8,128)S(1)}, u32[]{:S(2)}, u32[]{:S(2)}) collective-permute-start(f32[144,128]{1,0:T(8,128)S(1)} %get-tuple-element.75), channel_id=1, source_target_pairs={{0,1},{1,0},{2,3},{3,2},{4,5},{5,4},{6,7},{7,6},{8,9},{9,8},{10,11... | collective-permute-start | bytes 221192 | tf_op jit(solution)/shard_map/ppermute | solution.py:63
  52.0 3.3 %collective-permute-start.37 = (f32[144,128]{1,0:T(8,128)S(1)}, f32[144,128]{1,0:T(8,128)S(1)}, u32[]{:S(2)}, u32[]{:S(2)}) collective-permute-start(f32[144,128]{1,0:T(8,128)S(1)} %get-tuple-element.98), channel_id=1, source_target_pairs={{0,1},{1,0},{2,3},{3,2},{4,5},{5,4},{6,7},{7,6},{8,9},{9,8},{10,11... | collective-permute-start | bytes 221192 | tf_op jit(solution)/shard_map/ppermute | solution.py:63
  52.3 5.0 %collective-permute-start.7 = (bf16[160,128]{1,0:T(8,128)(2,1)S(1)}, bf16[160,128]{1,0:T(8,128)(2,1)S(1)}, u32[]{:S(2)}, u32[]{:S(2)}) collective-permute-start(bf16[160,128]{1,0:T(8,128)(2,1)S(1)} %shard_map.136), channel_id=1, source_target_pairs={{0,16},{1,17},{2,18},{3,19},{4,20},{5,21},{6,22},{7,23},{8,24},{9,... | collective-permute-start | bytes 122888 | tf_op jit(solution)/shard_map/ppermute | solution.py:63
  53.0 17.7 %collective-permute-start.17 = (bf16[1152,256]{1,0:T(8,128)(2,1)S(1)}, bf16[1152,256]{1,0:T(8,128)(2,1)S(1)}, u32[]{:S(2)}, u32[]{:S(2)}) collective-permute-start(bf16[1152,256]{1,0:T(8,128)(2,1)S(1)} %pad_maximum_fusion.refs_0_), channel_id=1, source_target_pairs={{0,1},{1,0},{2,3},{3,2},{4,5},{5,4},{6,7},{7,6},{8,9},{9,8},{10,11... | collective-permute-start | bytes 1769480 | tf_op jit(solution)/shard_map/ppermute | solution.py:63
  53.3 12.9 %collective-permute-start.16 = (bf16[1152,256]{1,0:T(8,128)(2,1)S(1)}, bf16[1152,256]{1,0:T(8,128)(2,1)S(1)}, u32[]{:S(2)}, u32[]{:S(2)}) collective-permute-start(bf16[1152,256]{1,0:T(8,128)(2,1)S(1)} %pad_maximum_fusion.refs_0_), channel_id=1, source_target_pairs={{0,2},{1,5},{2,0},{3,7},{4,6},{5,1},{6,4},{7,3},{8,10},{9,13},{10,... | collective-permute-start | bytes 1769480 | tf_op jit(solution)/shard_map/ppermute | solution.py:63
  55.4 5.2 %collective-permute-start.38 = (bf16[160,128]{1,0:T(8,128)(2,1)S(1)}, bf16[160,128]{1,0:T(8,128)(2,1)S(1)}, u32[]{:S(2)}, u32[]{:S(2)}) collective-permute-start(bf16[160,128]{1,0:T(8,128)(2,1)S(1)} %shard_map.145), channel_id=1, source_target_pairs={{0,16},{1,17},{2,18},{3,19},{4,20},{5,21},{6,22},{7,23},{8,24},{9,... | collective-permute-start | bytes 122888 | tf_op jit(solution)/shard_map/ppermute | solution.py:63
  57.3 5.1 %collective-permute-start.8 = (bf16[320,128]{1,0:T(8,128)(2,1)S(1)}, bf16[320,128]{1,0:T(8,128)(2,1)S(1)}, u32[]{:S(2)}, u32[]{:S(2)}) collective-permute-start(bf16[320,128]{1,0:T(8,128)(2,1)S(1)} %pad_maximum_fusion.13), channel_id=1, source_target_pairs={{0,8},{1,3},{2,10},{3,1},{4,12},{5,7},{6,14},{7,5},{8,0},{9,11},{1... | collective-permute-start | bytes 245768 | tf_op jit(solution)/shard_map/ppermute | solution.py:63
  60.7 4.5 %collective-permute-start.39 = (bf16[320,128]{1,0:T(8,128)(2,1)S(1)}, bf16[320,128]{1,0:T(8,128)(2,1)S(1)}, u32[]{:S(2)}, u32[]{:S(2)}) collective-permute-start(bf16[320,128]{1,0:T(8,128)(2,1)S(1)} %pad_maximum_fusion.14), channel_id=1, source_target_pairs={{0,4},{1,9},{2,6},{3,11},{4,0},{5,13},{6,2},{7,15},{8,12},{9,1},{1... | collective-permute-start | bytes 245768 | tf_op jit(solution)/shard_map/ppermute | solution.py:63
  62.4 5.4 %collective-permute-start.9 = (bf16[640,128]{1,0:T(8,128)(2,1)S(1)}, bf16[640,128]{1,0:T(8,128)(2,1)S(1)}, u32[]{:S(2)}, u32[]{:S(2)}) collective-permute-start(bf16[640,128]{1,0:T(8,128)(2,1)S(1)} %pad_maximum_fusion.6), channel_id=1, source_target_pairs={{0,4},{1,9},{2,6},{3,11},{4,0},{5,13},{6,2},{7,15},{8,12},{9,1},{1... | collective-permute-start | bytes 491528 | tf_op jit(solution)/shard_map/ppermute | solution.py:63
  65.3 13.0 %copy-start.4 = (f32[256]{0:T(256)S(1)}, f32[256]{0:T(256)}, u32[]{:S(2)}) copy-start(f32[256]{0:T(256)} %refs_6_.3) | copy-start | bytes 3076
  65.3 5.4 %collective-permute-start.40 = (bf16[640,128]{1,0:T(8,128)(2,1)S(1)}, bf16[640,128]{1,0:T(8,128)(2,1)S(1)}, u32[]{:S(2)}, u32[]{:S(2)}) collective-permute-start(bf16[640,128]{1,0:T(8,128)(2,1)S(1)} %pad_maximum_fusion.7), channel_id=1, source_target_pairs={{0,2},{1,3},{2,0},{3,1},{4,6},{5,7},{6,4},{7,5},{8,10},{9,11},{10,... | collective-permute-start | bytes 491528 | tf_op jit(solution)/shard_map/ppermute | solution.py:63
  66.2 4.6 %collective-permute-start.18 = (bf16[1152,256]{1,0:T(8,128)(2,1)S(1)}, bf16[1152,256]{1,0:T(8,128)(2,1)S(1)}, u32[]{:S(2)}, u32[]{:S(2)}) collective-permute-start(bf16[1152,256]{1,0:T(8,128)(2,1)S(1)} %collective-permute-done.16.refs_1_), channel_id=1, source_target_pairs={{0,1},{1,0},{2,3},{3,2},{4,5},{5,4},{6,7},{7,6},{8,9},{9,8},{10,11... | collective-permute-start | bytes 1769480 | tf_op jit(solution)/shard_map/ppermute | solution.py:63
  67.9 7.1 %collective-permute-start.10 = (bf16[1280,128]{1,0:T(8,128)(2,1)S(1)}, bf16[1280,128]{1,0:T(8,128)(2,1)S(1)}, u32[]{:S(2)}, u32[]{:S(2)}) collective-permute-start(bf16[1280,128]{1,0:T(8,128)(2,1)S(1)} %pad_maximum_fusion.1.refs_0_), channel_id=1, source_target_pairs={{0,2},{1,5},{2,0},{3,7},{4,6},{5,1},{6,4},{7,3},{8,10},{9,13},{10,... | collective-permute-start | bytes 983048 | tf_op jit(solution)/shard_map/ppermute | solution.py:63
  71.1 7.1 %collective-permute-start.41 = (bf16[1280,128]{1,0:T(8,128)(2,1)S(1)}, bf16[1280,128]{1,0:T(8,128)(2,1)S(1)}, u32[]{:S(2)}, u32[]{:S(2)}) collective-permute-start(bf16[1280,128]{1,0:T(8,128)(2,1)S(1)} %pad_maximum_fusion.2.refs_0_), channel_id=1, source_target_pairs={{0,8},{1,5},{2,10},{3,7},{4,12},{5,1},{6,14},{7,3},{8,0},{9,13},{1... | collective-permute-start | bytes 983048 | tf_op jit(solution)/shard_map/ppermute | solution.py:63
  72.7 5.6 %collective-permute-start.11 = (bf16[1280,128]{1,0:T(8,128)(2,1)S(1)}, bf16[1280,128]{1,0:T(8,128)(2,1)S(1)}, u32[]{:S(2)}, u32[]{:S(2)}) collective-permute-start(bf16[1280,128]{1,0:T(8,128)(2,1)S(1)} %pad_maximum_fusion.1.refs_0_), channel_id=1, source_target_pairs={{0,1},{1,0},{2,3},{3,2},{4,5},{5,4},{6,7},{7,6},{8,9},{9,8},{10,11... | collective-permute-start | bytes 983048 | tf_op jit(solution)/shard_map/ppermute | solution.py:63
  75.1 3.2 %collective-permute-start.12 = (bf16[1280,128]{1,0:T(8,128)(2,1)S(1)}, bf16[1280,128]{1,0:T(8,128)(2,1)S(1)}, u32[]{:S(2)}, u32[]{:S(2)}) collective-permute-start(bf16[1280,128]{1,0:T(8,128)(2,1)S(1)} %collective-permute-done.10.refs_1_), channel_id=1, source_target_pairs={{0,1},{1,0},{2,3},{3,2},{4,5},{5,4},{6,7},{7,6},{8,9},{9,8},{10,11... | collective-permute-start | bytes 983048 | tf_op jit(solution)/shard_map/ppermute | solution.py:63
  75.1 11.0 %collective-permute-start.42 = (bf16[1280,128]{1,0:T(8,128)(2,1)S(1)}, bf16[1280,128]{1,0:T(8,128)(2,1)S(1)}, u32[]{:S(2)}, u32[]{:S(2)}) collective-permute-start(bf16[1280,128]{1,0:T(8,128)(2,1)S(1)} %pad_maximum_fusion.2.refs_0_), channel_id=1, source_target_pairs={{0,1},{1,0},{2,3},{3,2},{4,5},{5,4},{6,7},{7,6},{8,9},{9,8},{10,11... | collective-permute-start | bytes 983048 | tf_op jit(solution)/shard_map/ppermute | solution.py:63
  78.3 7.8 %collective-permute-start.43 = (bf16[1280,128]{1,0:T(8,128)(2,1)S(1)}, bf16[1280,128]{1,0:T(8,128)(2,1)S(1)}, u32[]{:S(2)}, u32[]{:S(2)}) collective-permute-start(bf16[1280,128]{1,0:T(8,128)(2,1)S(1)} %collective-permute-done.41.refs_1_), channel_id=1, source_target_pairs={{0,1},{1,0},{2,3},{3,2},{4,5},{5,4},{6,7},{7,6},{8,9},{9,8},{10,11... | collective-permute-start | bytes 983048 | tf_op jit(solution)/shard_map/ppermute | solution.py:63
  81.2 1.5 collective-permute-start.19
  85.1 9.0 %collective-permute-start.21 = (bf16[1152,128]{1,0:T(8,128)(2,1)S(1)}, bf16[1152,128]{1,0:T(8,128)(2,1)S(1)}, u32[]{:S(2)}, u32[]{:S(2)}) collective-permute-start(bf16[1152,128]{1,0:T(8,128)(2,1)S(1)} %get-tuple-element.80), channel_id=1, source_target_pairs={{0,2},{1,5},{2,0},{3,7},{4,6},{5,1},{6,4},{7,3},{8,10},{9,13},{10,... | collective-permute-start | bytes 884744 | tf_op jit(solution)/shard_map/ppermute | solution.py:63
  89.0 1.3 collective-permute-start.44
  92.8 8.4 %collective-permute-start.45 = (bf16[1152,128]{1,0:T(8,128)(2,1)S(1)}, bf16[1152,128]{1,0:T(8,128)(2,1)S(1)}, u32[]{:S(2)}, u32[]{:S(2)}) collective-permute-start(bf16[1152,128]{1,0:T(8,128)(2,1)S(1)} %get-tuple-element.105), channel_id=1, source_target_pairs={{0,8},{1,5},{2,10},{3,7},{4,12},{5,1},{6,14},{7,3},{8,0},{9,13},{1... | collective-permute-start | bytes 884744 | tf_op jit(solution)/shard_map/ppermute | solution.py:63
  94.3 8.2 %collective-permute-start.22 = (bf16[576,128]{1,0:T(8,128)(2,1)S(1)}, bf16[576,128]{1,0:T(8,128)(2,1)S(1)}, u32[]{:S(2)}, u32[]{:S(2)}) collective-permute-start(bf16[576,128]{1,0:T(8,128)(2,1)S(1)} %select_convert_fusion.1), channel_id=1, source_target_pairs={{0,4},{1,9},{2,6},{3,11},{4,0},{5,13},{6,2},{7,15},{8,12},{9,1},{1... | collective-permute-start | bytes 442376 | tf_op jit(solution)/shard_map/ppermute | solution.py:63
  101.3 5.5 %collective-permute-start.46 = (bf16[576,128]{1,0:T(8,128)(2,1)S(1)}, bf16[576,128]{1,0:T(8,128)(2,1)S(1)}, u32[]{:S(2)}, u32[]{:S(2)}) collective-permute-start(bf16[576,128]{1,0:T(8,128)(2,1)S(1)} %select_convert_fusion), channel_id=1, source_target_pairs={{0,2},{1,3},{2,0},{3,1},{4,6},{5,7},{6,4},{7,5},{8,10},{9,11},{10,... | collective-permute-start | bytes 442376 | tf_op jit(solution)/shard_map/ppermute | solution.py:63
  102.5 4.4 %collective-permute-start.23 = (bf16[288,128]{1,0:T(8,128)(2,1)S(1)}, bf16[288,128]{1,0:T(8,128)(2,1)S(1)}, u32[]{:S(2)}, u32[]{:S(2)}) collective-permute-start(bf16[288,128]{1,0:T(8,128)(2,1)S(1)} %select_convert_fusion.3), channel_id=1, source_target_pairs={{0,8},{1,3},{2,10},{3,1},{4,12},{5,7},{6,14},{7,5},{8,0},{9,11},{1... | collective-permute-start | bytes 221192 | tf_op jit(solution)/shard_map/ppermute | solution.py:63
  107.0 5.0 %collective-permute-start.24 = (bf16[144,128]{1,0:T(8,128)(2,1)S(1)}, bf16[144,128]{1,0:T(8,128)(2,1)S(1)}, u32[]{:S(2)}, u32[]{:S(2)}) collective-permute-start(bf16[144,128]{1,0:T(8,128)(2,1)S(1)} %select_convert_fusion.5), channel_id=1, source_target_pairs={{0,16},{1,17},{2,18},{3,19},{4,20},{5,21},{6,22},{7,23},{8,24},{9,... | collective-permute-start | bytes 110600 | tf_op jit(solution)/shard_map/ppermute | solution.py:63
  108.7 5.0 %collective-permute-start.47 = (bf16[288,128]{1,0:T(8,128)(2,1)S(1)}, bf16[288,128]{1,0:T(8,128)(2,1)S(1)}, u32[]{:S(2)}, u32[]{:S(2)}) collective-permute-start(bf16[288,128]{1,0:T(8,128)(2,1)S(1)} %select_convert_fusion.2), channel_id=1, source_target_pairs={{0,4},{1,9},{2,6},{3,11},{4,0},{5,13},{6,2},{7,15},{8,12},{9,1},{1... | collective-permute-start | bytes 221192 | tf_op jit(solution)/shard_map/ppermute | solution.py:63
  112.0 5.3 %collective-permute-start.25 = (bf16[144,128]{1,0:T(8,128)(2,1)S(1)}, bf16[144,128]{1,0:T(8,128)(2,1)S(1)}, u32[]{:S(2)}, u32[]{:S(2)}) collective-permute-start(bf16[144,128]{1,0:T(8,128)(2,1)S(1)} %add_convert_fusion.1), channel_id=1, source_target_pairs={{0,16},{1,17},{2,18},{3,19},{4,20},{5,21},{6,22},{7,23},{8,24},{9,... | collective-permute-start | bytes 110600 | tf_op jit(solution)/shard_map/ppermute | solution.py:63
  113.8 30.0 %copy-start = (bf16[256,4608]{1,0:T(8,128)(2,1)S(1)}, bf16[256,4608]{1,0:T(8,128)(2,1)}, u32[]{:S(2)}) copy-start(bf16[256,4608]{1,0:T(8,128)(2,1)} %refs_16_.1) | copy-start | bytes 7077892
  113.8 4.9 %collective-permute-start.48 = (bf16[144,128]{1,0:T(8,128)(2,1)S(1)}, bf16[144,128]{1,0:T(8,128)(2,1)S(1)}, u32[]{:S(2)}, u32[]{:S(2)}) collective-permute-start(bf16[144,128]{1,0:T(8,128)(2,1)S(1)} %select_convert_fusion.4), channel_id=1, source_target_pairs={{0,16},{1,17},{2,18},{3,19},{4,20},{5,21},{6,22},{7,23},{8,24},{9,... | collective-permute-start | bytes 110600 | tf_op jit(solution)/shard_map/ppermute | solution.py:63
  118.8 5.0 %collective-permute-start.49 = (bf16[144,128]{1,0:T(8,128)(2,1)S(1)}, bf16[144,128]{1,0:T(8,128)(2,1)S(1)}, u32[]{:S(2)}, u32[]{:S(2)}) collective-permute-start(bf16[144,128]{1,0:T(8,128)(2,1)S(1)} %add_convert_fusion), channel_id=1, source_target_pairs={{0,16},{1,17},{2,18},{3,19},{4,20},{5,21},{6,22},{7,23},{8,24},{9,... | collective-permute-start | bytes 110600 | tf_op jit(solution)/shard_map/ppermute | solution.py:63
  120.2 5.9 %collective-permute-start.26 = (bf16[288,128]{1,0:T(8,128)(2,1)S(1)}, bf16[288,128]{1,0:T(8,128)(2,1)S(1)}, u32[]{:S(2)}, u32[]{:S(2)}) collective-permute-start(bf16[288,128]{1,0:T(8,128)(2,1)S(1)} %pad_maximum_fusion.15), channel_id=1, source_target_pairs={{0,8},{1,3},{2,10},{3,1},{4,12},{5,7},{6,14},{7,5},{8,0},{9,11},{1... | collective-permute-start | bytes 221192 | tf_op jit(solution)/shard_map/ppermute | solution.py:63
  123.8 4.4 %collective-permute-start.50 = (bf16[288,128]{1,0:T(8,128)(2,1)S(1)}, bf16[288,128]{1,0:T(8,128)(2,1)S(1)}, u32[]{:S(2)}, u32[]{:S(2)}) collective-permute-start(bf16[288,128]{1,0:T(8,128)(2,1)S(1)} %pad_maximum_fusion.16), channel_id=1, source_target_pairs={{0,4},{1,9},{2,6},{3,11},{4,0},{5,13},{6,2},{7,15},{8,12},{9,1},{1... | collective-permute-start | bytes 221192 | tf_op jit(solution)/shard_map/ppermute | solution.py:63
  126.2 6.7 %collective-permute-start.27 = (bf16[576,128]{1,0:T(8,128)(2,1)S(1)}, bf16[576,128]{1,0:T(8,128)(2,1)S(1)}, u32[]{:S(2)}, u32[]{:S(2)}) collective-permute-start(bf16[576,128]{1,0:T(8,128)(2,1)S(1)} %pad_maximum_fusion.9), channel_id=1, source_target_pairs={{0,4},{1,9},{2,6},{3,11},{4,0},{5,13},{6,2},{7,15},{8,12},{9,1},{1... | collective-permute-start | bytes 442376 | tf_op jit(solution)/shard_map/ppermute | solution.py:63
  128.3 5.3 %collective-permute-start.51 = (bf16[576,128]{1,0:T(8,128)(2,1)S(1)}, bf16[576,128]{1,0:T(8,128)(2,1)S(1)}, u32[]{:S(2)}, u32[]{:S(2)}) collective-permute-start(bf16[576,128]{1,0:T(8,128)(2,1)S(1)} %pad_maximum_fusion.10), channel_id=1, source_target_pairs={{0,2},{1,3},{2,0},{3,1},{4,6},{5,7},{6,4},{7,5},{8,10},{9,11},{10,... | collective-permute-start | bytes 442376 | tf_op jit(solution)/shard_map/ppermute | solution.py:63
  133.0 6.8 %collective-permute-start.28 = (bf16[1152,128]{1,0:T(8,128)(2,1)S(1)}, bf16[1152,128]{1,0:T(8,128)(2,1)S(1)}, u32[]{:S(2)}, u32[]{:S(2)}) collective-permute-start(bf16[1152,128]{1,0:T(8,128)(2,1)S(1)} %pad_maximum_fusion.4.refs_0_), channel_id=1, source_target_pairs={{0,2},{1,5},{2,0},{3,7},{4,6},{5,1},{6,4},{7,3},{8,10},{9,13},{10,... | collective-permute-start | bytes 884744 | tf_op jit(solution)/shard_map/ppermute | solution.py:63
  133.7 8.5 %collective-permute-start.52 = (bf16[1152,128]{1,0:T(8,128)(2,1)S(1)}, bf16[1152,128]{1,0:T(8,128)(2,1)S(1)}, u32[]{:S(2)}, u32[]{:S(2)}) collective-permute-start(bf16[1152,128]{1,0:T(8,128)(2,1)S(1)} %pad_maximum_fusion.5.refs_4_), channel_id=1, source_target_pairs={{0,8},{1,5},{2,10},{3,7},{4,12},{5,1},{6,14},{7,3},{8,0},{9,13},{1... | collective-permute-start | bytes 884744 | tf_op jit(solution)/shard_map/ppermute | solution.py:63
  137.6 4.7 %collective-permute-start.29 = (bf16[1152,128]{1,0:T(8,128)(2,1)S(1)}, bf16[1152,128]{1,0:T(8,128)(2,1)S(1)}, u32[]{:S(2)}, u32[]{:S(2)}) collective-permute-start(bf16[1152,128]{1,0:T(8,128)(2,1)S(1)} %pad_maximum_fusion.4.refs_0_), channel_id=1, source_target_pairs={{0,1},{1,0},{2,3},{3,2},{4,5},{5,4},{6,7},{7,6},{8,9},{9,8},{10,11... | collective-permute-start | bytes 884744 | tf_op jit(solution)/shard_map/ppermute | solution.py:63
  137.6 4.7 %collective-permute-start.53 = (bf16[1152,128]{1,0:T(8,128)(2,1)S(1)}, bf16[1152,128]{1,0:T(8,128)(2,1)S(1)}, u32[]{:S(2)}, u32[]{:S(2)}) collective-permute-start(bf16[1152,128]{1,0:T(8,128)(2,1)S(1)} %pad_maximum_fusion.5.refs_4_), channel_id=1, source_target_pairs={{0,1},{1,0},{2,3},{3,2},{4,5},{5,4},{6,7},{7,6},{8,9},{9,8},{10,11... | collective-permute-start | bytes 884744 | tf_op jit(solution)/shard_map/ppermute | solution.py:63
  139.8 2.5 %collective-permute-start.30 = (bf16[1152,128]{1,0:T(8,128)(2,1)S(1)}, bf16[1152,128]{1,0:T(8,128)(2,1)S(1)}, u32[]{:S(2)}, u32[]{:S(2)}) collective-permute-start(bf16[1152,128]{1,0:T(8,128)(2,1)S(1)} %collective-permute-done.28.refs_1_), channel_id=1, source_target_pairs={{0,1},{1,0},{2,3},{3,2},{4,5},{5,4},{6,7},{7,6},{8,9},{9,8},{10,11... | collective-permute-start | bytes 884744 | tf_op jit(solution)/shard_map/ppermute | solution.py:63
  142.3 1.6 %collective-permute-start.54 = (bf16[1152,128]{1,0:T(8,128)(2,1)S(1)}, bf16[1152,128]{1,0:T(8,128)(2,1)S(1)}, u32[]{:S(2)}, u32[]{:S(2)}) collective-permute-start(bf16[1152,128]{1,0:T(8,128)(2,1)S(1)} %collective-permute-done.52.refs_5_), channel_id=1, source_target_pairs={{0,1},{1,0},{2,3},{3,2},{4,5},{5,4},{6,7},{7,6},{8,9},{9,8},{10,11... | collective-permute-start | bytes 884744 | tf_op jit(solution)/shard_map/ppermute | solution.py:63

commit v4 on v3

--- a/solution.py
+++ b/solution.py
@@ -116,6 +116,10 @@
 
 def in_hbm(value):
     return pltpu.with_memory_space_constraint(value, pltpu.HBM)
+
+
+def in_vmem(value):
+    return pltpu.with_memory_space_constraint(value, pltpu.VMEM)
 
 
 SMALL = pltpu.CompilerParams(vmem_limit_bytes=6 << 20)
@@ -362,10 +366,8 @@
 
 def encode_kernel(ladder, core, steps, places, block, model_width, *refs):
     pieces = refs[:4]
-    residual_ref, enc_any, bias_ref, offset_ref = refs[4:8]
-    hidden_ref, low_ref, slope_ref, activity_ref, base_ref, hidden_buf, enc_ref, sems = refs[8:]
-    load = pltpu.make_async_copy(enc_any, enc_ref, sems.at[1])
-    load.start()
+    residual_ref, enc_ref, bias_ref, offset_ref = refs[4:8]
+    hidden_ref, low_ref, slope_ref, activity_ref, base_ref, hidden_buf, sems = refs[8:]
     width = pieces[0].shape[1]
     stride = block + EXTRA
     count = pieces[0].shape[0] // stride
@@ -385,7 +387,6 @@
         base_ref[...] = column(offset_ref, width) - mine
     else:
         base_ref[...] = column(offset_ref, width)
-    load.wait()
     preact = lax.dot_general(enc_ref[...], hidden_buf[...], (((0,), (0,)), ((), ())), preferred_element_type=f32)
     scaled = (preact + column(bias_ref, width)) / smoothing
     active = smoothing * (jnp.maximum(scaled, 0.0) + jnp.log1p(jnp.exp(-jnp.abs(scaled))))
@@ -408,39 +409,34 @@
             jax.ShapeDtypeStruct((latents, 1), f32),
             jax.ShapeDtypeStruct((offset.shape[0], width), f32),
         ),
-        in_specs=[VMEM] * 5 + [hbm] + [VMEM] * 2,
+        in_specs=[VMEM] * 8,
         out_specs=[hbm] + [VMEM] * 4,
-        scratch_shapes=[
-            pltpu.VMEM((model_width, width), bf16),
-            pltpu.VMEM(encoder.shape, bf16),
-            pltpu.SemaphoreType.DMA((2,)),
-        ],
+        scratch_shapes=[pltpu.VMEM((model_width, width), bf16), pltpu.SemaphoreType.DMA((1,))],
         compiler_params=pltpu.CompilerParams(vmem_limit_bytes=2 * encoder.size + 8 * model_width * width + (4 << 20)),
         cost_estimate=pl.CostEstimate(
             flops=2 * encoder.size * width, bytes_accessed=2 * encoder.size, transcendentals=4 * latents * width
         ),
-    )(*pieces, residual, in_hbm(encoder), bias, offset)
-
-
-def decode_kernel(ladder, core, step, low_ref, peer_low_ref, dec_any, peer_dec_any, send_ref, keep_ref, buf, sems):
+    )(*pieces, residual, encoder, bias, offset)
+
+
+def decode_kernel(ladder, core, step, low_ref, peer_low_ref, dec_ref, peer_dec_any, send_ref, keep_ref, buf, sems):
     up = ladder.bit(step)
     half = send_ref.shape[0]
     first = 2 * ladder.bit(core)
     loads = []
     for i, side in enumerate((1 - up, up)):
-        for j, source in enumerate((dec_any, peer_dec_any)):
-            loads.append(pltpu.make_async_copy(source.at[:, aligned(first + side, half)], buf.at[i, j], sems.at[2 * i + j]))
-            loads[-1].start()
-    lows = (low_ref[...], peer_low_ref[...])
+        loads.append(pltpu.make_async_copy(peer_dec_any.at[:, aligned(first + side, half)], buf.at[i], sems.at[i]))
+        loads[-1].start()
+    low, peer_low = low_ref[...], peer_low_ref[...]
     tile = half // 3
-    for i, ref in enumerate((send_ref, keep_ref)):
-        loads[2 * i].wait()
-        loads[2 * i + 1].wait()
+    for i, (ref, side) in enumerate(((send_ref, 1 - up), (keep_ref, up))):
+        loads[i].wait()
         for t in range(3):
             rows = pl.ds(t * tile, tile)
-            value = sum(
-                lax.dot_general(buf[i, j, :, rows], lows[j], (((0,), (0,)), ((), ())), preferred_element_type=f32)
-                for j in range(2)
+            columns = pl.ds(pl.multiple_of((first + side) * half + t * tile, tile), tile)
+            value = lax.dot_general(dec_ref[:, columns], low, (((0,), (0,)), ((), ())), preferred_element_type=f32)
+            value = value + lax.dot_general(
+                buf[i, :, rows], peer_low, (((0,), (0,)), ((), ())), preferred_element_type=f32
             )
             ref[rows, :] = value.astype(ref.dtype)
 
@@ -452,13 +448,13 @@
     return pl.pallas_call(
         functools.partial(decode_kernel, ladder, core, step),
         out_shape=(jax.ShapeDtypeStruct((half, width), bf16), jax.ShapeDtypeStruct((half, width), f32)),
-        in_specs=[VMEM] * 2 + [hbm] * 2,
-        scratch_shapes=[pltpu.VMEM((2, 2, latents, half), bf16), pltpu.SemaphoreType.DMA((4,))],
+        in_specs=[VMEM] * 3 + [hbm],
+        scratch_shapes=[pltpu.VMEM((2, latents, half), bf16), pltpu.SemaphoreType.DMA((2,))],
         compiler_params=pltpu.CompilerParams(vmem_limit_bytes=2 * decoder.size + 6 * half * width + (6 << 20)),
         cost_estimate=pl.CostEstimate(
             flops=4 * decoder.size * width, bytes_accessed=4 * decoder.size, transcendentals=0
         ),
-    )(low, peer_low, in_hbm(decoder), in_hbm(peer_decoder))
+    )(low, peer_low, decoder, in_hbm(peer_decoder))
 
 
 def final_kernel(ladder, core, steps, *refs):
@@ -466,15 +462,13 @@
     errors = [refs[4 * c : 4 * c + 4] for c in range(chunks)]
     refs = refs[4 * chunks :]
     hidden_any, low, slope, activity = (refs[i * chunks : (i + 1) * chunks] for i in range(4))
-    dec_any, norm_ref, enc_out, bias_ref, dec_out = refs[4 * chunks : 4 * chunks + 5]
-    hidden, dec_ref, error, enc_buf, dec_buf, in_sem, enc_sem, dec_sem = refs[4 * chunks + 5 :]
+    dec_ref, norm_ref, enc_out, bias_ref, dec_out = refs[4 * chunks : 4 * chunks + 5]
+    hidden, error, enc_buf, dec_buf, in_sem, enc_sem, dec_sem = refs[4 * chunks + 5 :]
     width = hidden_any[0].shape[1]
-    load_dec = pltpu.make_async_copy(dec_any, dec_ref, in_sem.at[0])
-    load_dec.start()
     loads = []
     for c in range(chunks):
         place = hidden.at[:, pl.ds(c * width, width)]
-        loads.append(pltpu.make_async_copy(hidden_any[c], place, in_sem.at[c + 1]))
+        loads.append(pltpu.make_async_copy(hidden_any[c], place, in_sem.at[c]))
         loads[-1].start()
     quarter = errors[0][0].shape[0]
     for c in range(chunks):
@@ -484,30 +478,29 @@
     lows = jnp.concatenate([ref[...] for ref in low], axis=1)
     slopes = jnp.concatenate([ref[...] for ref in slope], axis=1)
     norms = column(norm_ref, 128)[:, :1]
-    load_dec.wait()
-    feedback = jnp.dot(dec_ref[...], error[...], preferred_element_type=f32)
-    turned = (loss_weight * (2.0 * feedback + penalty * norms) * slopes).T
-    bias_ref[...] = jnp.sum(turned, axis=0, keepdims=True)
-    turned = turned.astype(bf16)
     copies = []
 
     def send(buf, out, index, sem):
         copies.append(pltpu.make_async_copy(buf.at[index], out.at[index], sem))
         copies[-1].start()
 
-    for load in loads:
-        load.wait()
     tile = hidden.shape[0] // 9
-    for t in range(9):
-        rows = pl.ds(t * tile, tile)
-        enc_buf[rows, :] = jnp.dot(hidden[rows, :], turned, preferred_element_type=f32).astype(bf16)
-        send(enc_buf, enc_out, (rows, slice(None)), enc_sem.at[t])
     ratio = loss_weight * penalty * sum(ref[...] for ref in activity) / norms
     for t in range(9):
         columns = pl.ds(t * tile, tile)
         outer = lax.dot_general(lows, error[columns, :], (((1,), (1,)), ((), ())), preferred_element_type=f32)
         dec_buf[:, columns] = (2.0 * loss_weight * outer + ratio * dec_ref[:, columns].astype(f32)).astype(bf16)
-        send(dec_buf, dec_out, (slice(None), columns), dec_sem.at[t])
+    send(dec_buf, dec_out, slice(None), dec_sem.at[0])
+    feedback = jnp.dot(dec_ref[...], error[...], preferred_element_type=f32)
+    turned = (loss_weight * (2.0 * feedback + penalty * norms) * slopes).T
+    bias_ref[...] = jnp.sum(turned, axis=0, keepdims=True)
+    turned = turned.astype(bf16)
+    for load in loads:
+        load.wait()
+    for t in range(9):
+        rows = pl.ds(t * tile, tile)
+        enc_buf[rows, :] = jnp.dot(hidden[rows, :], turned, preferred_element_type=f32).astype(bf16)
+        send(enc_buf, enc_out, (rows, slice(None)), enc_sem.at[t])
     for copy in copies:
         copy.wait()
 
@@ -524,20 +517,19 @@
             jax.ShapeDtypeStruct((1, latents), f32),
             jax.ShapeDtypeStruct((latents, model_width), bf16),
         ),
-        in_specs=[VMEM] * len(flat) + [hbm] * CHUNKS + [VMEM] * (3 * CHUNKS) + [hbm, VMEM],
+        in_specs=[VMEM] * len(flat) + [hbm] * CHUNKS + [VMEM] * (3 * CHUNKS + 2),
         out_specs=(hbm, VMEM, hbm),
         scratch_shapes=[
             pltpu.VMEM((model_width, tokens), bf16),
-            pltpu.VMEM((latents, model_width), bf16),
             pltpu.VMEM((model_width, tokens), bf16),
             pltpu.VMEM((model_width, latents), bf16),
             pltpu.VMEM((latents, model_width), bf16),
-            pltpu.SemaphoreType.DMA((1 + CHUNKS,)),
+            pltpu.SemaphoreType.DMA((CHUNKS,)),
             pltpu.SemaphoreType.DMA((9,)),
-            pltpu.SemaphoreType.DMA((9,)),
+            pltpu.SemaphoreType.DMA((1,)),
         ],
         compiler_params=pltpu.CompilerParams(
-            vmem_limit_bytes=6 * decoder.size + 8 * model_width * tokens + (6 << 20)
+            vmem_limit_bytes=4 * decoder.size + 4 * model_width * tokens + (6 << 20)
         ),
         cost_estimate=pl.CostEstimate(
             flops=6 * decoder.size * tokens, bytes_accessed=12 * decoder.size, transcendentals=0
@@ -604,6 +596,7 @@
 
     out_t = out_weight.T
     decoder_peer = ladder.swap(decoder_weight, core)
+    encoder_near, decoder_near = in_vmem(encoder_weight), in_vmem(decoder_weight)
     norms = jnp.sqrt(jnp.sum(jnp.square(decoder_weight.astype(f32)), axis=1) + epsilon)
 
     if paired:
@@ -695,11 +688,11 @@
             kernel_block, places = model_width // 4, ()
         slot, offset = slots[c], offsets[c]
         hidden, low, slope, activity, base = encode(
-            ladder, core, cores + steps, places, kernel_block, pieces, residual_all[c], encoder_weight, encoder_bias, offset
+            ladder, core, cores + steps, places, kernel_block, pieces, residual_all[c], encoder_near, encoder_bias, offset
         )
         if not paired:
             base = base - lax.dynamic_slice_in_dim(hidden, slot, block, axis=0).astype(f32)
-        send, part = decode(ladder, core, path[0], low, ladder.swap(low, core), decoder_weight, decoder_peer)
+        send, part = decode(ladder, core, path[0], low, ladder.swap(low, core), decoder_near, decoder_peer)
         part = part + ladder.swap(send, path[0]).astype(f32)
         error = (ladder.scatter(part, path[1:], bf16) + base).astype(bf16)
         errors.append(ladder.quarters(error, core, cores[1:] + steps))
@@ -710,7 +703,7 @@
         activities.append(activity)
 
     encoder_grad, encoder_bias_grad, decoder_grad = gradients(
-        ladder, core, nears, errors, hiddens, lows, slopes, activities, decoder_weight, norms
+        ladder, core, nears, errors, hiddens, lows, slopes, activities, decoder_near, norms
     )
     return encoder_grad, encoder_bias_grad[0], decoder_grad
 

time: 151 us -> 147 us (0.974)
  Pallas kernels: 21.7 us -> 18.4 us
    pallas_call x2, Pallas kernels: 5.76 us -> 3.45 us  [encode(): pl.pallas_call(functools.partial(encode_kernel, ladder, core, steps, plac...]
  transfers between devices with their start and end apart: 55 -> 55, of which waited for: 31 -> 30; matrix products, arithmetic and copies ran while one was open for 3% -> 3% of each run, Pallas kernels for 9% -> 7%
where the time goes in v4:
time: 147 us
  starting transfers between devices  62.9 us (43%)
  waiting for transfers between devices  57.1 us (39%)
  Pallas kernels  18.4 us (13%)
  other arithmetic  4.83 us (3%)
  local copies, waits for them, and re-layouts  2.47 us (2%)
    ppermute x55, starting transfers between devices, swap(): return lax.ppermute(value, AXES, self.pairs(step))  62.9 us
    ppermute x55, waiting for transfers between devices, swap(): return lax.ppermute(value, AXES, self.pairs(step))  57.1 us
    pallas_call x1, Pallas kernels, gradients(): pl.pallas_call(functools.partial(final_kernel, ladder, core, steps), out_...  5.7 us
    pallas_call x2, Pallas kernels, decode(): pl.pallas_call(functools.partial(decode_kernel, ladder, core, step), out_...  4.52 us
    pallas_call x2, Pallas kernels, encode(): pl.pallas_call(functools.partial(encode_kernel, ladder, core, steps, plac...  3.45 us
  transfers between devices with their start and end apart: 55, of which 30 were waited for; matrix products, arithmetic and copies ran while one was open for 3% of the time, Pallas kernels for 7%

profile of v4, /device:TPU:0, one launch (start us, length us, event | category | flops | bytes accessed | tf_op | source)
XLA Modules:
  0.0 147.0 jit_solution(9897614642011364771)
XLA Ops:
  0.6 0.9 slice_select_fusion
  3.2 2.0 %shard_map.130 = (bf16[1040,128]{1,0:T(8,128)(2,1)S(1)}, bf16[1040,128]{1,0:T(8,128)(2,1)S(1)}, f32[1024,128]{1,0:T(8,128)S(1)}, f32[1024,128]{1,0:T(8,128)S(1)}...) custom-call(bf16[288,256]{1,0:T(8,128)(2,1)S(1)} %bitcast.6, f32[288]{0:T(512)S(1)} %copy-done.6, bf16[288,1024]{1,0:T(8,128)(2,1)} %refs_0_.1, ...), custom_call_target="tpu_custom_call" | custom-call | flops 301989888 | bytes 1179648 | tf_op jit(solution)/shard_map/pallas_call | solution.py:187
  5.2 4.1 %collective-permute-start.13 = (bf16[144,256]{1,0:T(8,128)(2,1)S(1)}, bf16[144,256]{1,0:T(8,128)(2,1)S(1)}, u32[]{:S(2)}, u32[]{:S(2)}) collective-permute-start(bf16[144,256]{1,0:T(8,128)(2,1)S(1)} %slice_select_fusion), channel_id=1, source_target_pairs={{0,16},{1,17},{2,18},{3,19},{4,20},{5,21},{6,22},{7,23},{8,24},{9,... | collective-permute-start | bytes 221192 | tf_op jit(solution)/shard_map/ppermute | solution.py:63
  9.3 1.5 %collective-permute-start = (bf16[1040,128]{1,0:T(8,128)(2,1)S(1)}, bf16[1040,128]{1,0:T(8,128)(2,1)S(1)}, u32[]{:S(2)}, u32[]{:S(2)}) collective-permute-start(bf16[1040,128]{1,0:T(8,128)(2,1)S(1)} %get-tuple-element.62), channel_id=1, source_target_pairs={{0,2},{1,5},{2,0},{3,7},{4,6},{5,1},{6,4},{7,3},{8,10},{9,13},{10,... | collective-permute-start | bytes 798728 | tf_op jit(solution)/shard_map/ppermute | solution.py:63
  11.4 2.2 %multiply_reduce_fusion = f32[256]{0:T(256)S(1)} fusion(bf16[256,4608]{1,0:T(8,128)(2,1)} %refs_16_.1), kind=kLoop, calls=%fused_computation | loop fusion | flops 3538688 | bytes 2360320 | tf_op jit(solution)/shard_map/reduce_sum | solution.py:600
  13.9 1.8 %collective-permute-done.got_ref = bf16[1040,128]{1,0:T(8,128)(2,1)S(1)} collective-permute-done((bf16[1040,128]{1,0:T(8,128)(2,1)S(1)}, bf16[1040,128]{1,0:T(8,128)(2,1)S(1)}, u32[]{:S(2)}, u32[]{:S(2)}) %collective-permute-start) | collective-permute-done | bytes 266272 | tf_op jit(solution)/shard_map/ppermute | solution.py:63
  15.8 1.6 %collective-permute-start.1 = (bf16[528,128]{1,0:T(8,128)(2,1)S(1)}, bf16[528,128]{1,0:T(8,128)(2,1)S(1)}, u32[]{:S(2)}, u32[]{:S(2)}) collective-permute-start(bf16[528,128]{1,0:T(8,128)(2,1)S(1)} %get-tuple-element.65), channel_id=1, source_target_pairs={{0,4},{1,3},{2,6},{3,1},{4,0},{5,7},{6,2},{7,5},{8,12},{9,11},{10,... | collective-permute-start | bytes 405512 | tf_op jit(solution)/shard_map/ppermute | solution.py:63
  17.4 2.6 %collective-permute-done.31.got_ref = bf16[1040,128]{1,0:T(8,128)(2,1)S(1)} collective-permute-done((bf16[1040,128]{1,0:T(8,128)(2,1)S(1)}, bf16[1040,128]{1,0:T(8,128)(2,1)S(1)}, u32[]{:S(2)}, u32[]{:S(2)}) %collective-permute-start.31) | collective-permute-done | bytes 266272 | tf_op jit(solution)/shard_map/ppermute | solution.py:63
  20.0 1.6 %collective-permute-start.32 = (bf16[528,128]{1,0:T(8,128)(2,1)S(1)}, bf16[528,128]{1,0:T(8,128)(2,1)S(1)}, u32[]{:S(2)}, u32[]{:S(2)}) collective-permute-start(bf16[528,128]{1,0:T(8,128)(2,1)S(1)} %get-tuple-element.86), channel_id=1, source_target_pairs={{0,4},{1,3},{2,6},{3,1},{4,0},{5,7},{6,2},{7,5},{8,12},{9,11},{10,... | collective-permute-start | bytes 405512 | tf_op jit(solution)/shard_map/ppermute | solution.py:63
  21.6 1.6 %collective-permute-start.14 = (bf16[288,256]{1,0:T(8,128)(2,1)S(1)}, bf16[288,256]{1,0:T(8,128)(2,1)S(1)}, u32[]{:S(2)}, u32[]{:S(2)}) collective-permute-start(bf16[288,256]{1,0:T(8,128)(2,1)S(1)} %pad_maximum_fusion.8), channel_id=1, source_target_pairs={{0,8},{1,3},{2,10},{3,1},{4,12},{5,7},{6,14},{7,5},{8,0},{9,11},{1... | collective-permute-start | bytes 442376 | tf_op jit(solution)/shard_map/ppermute | solution.py:63
  23.8 1.2 collective-permute-done.32.got_ref
  25.1 1.6 %collective-permute-start.33 = (bf16[528,128]{1,0:T(8,128)(2,1)S(1)}, bf16[528,128]{1,0:T(8,128)(2,1)S(1)}, u32[]{:S(2)}, u32[]{:S(2)}) collective-permute-start(bf16[528,128]{1,0:T(8,128)(2,1)S(1)} %get-tuple-element.89), channel_id=1, source_target_pairs={{0,8},{1,9},{2,10},{3,11},{4,12},{5,13},{6,14},{7,15},{8,0},{9,1},... | collective-permute-start | bytes 405512 | tf_op jit(solution)/shard_map/ppermute | solution.py:63
  27.6 2.9 %collective-permute-done.2.got_ref = bf16[528,128]{1,0:T(8,128)(2,1)S(1)} collective-permute-done((bf16[528,128]{1,0:T(8,128)(2,1)S(1)}, bf16[528,128]{1,0:T(8,128)(2,1)S(1)}, u32[]{:S(2)}, u32[]{:S(2)}) %collective-permute-start.2) | collective-permute-done | bytes 135200 | tf_op jit(solution)/shard_map/ppermute | solution.py:63
  30.7 1.6 %collective-permute-done.33.got_ref = bf16[528,128]{1,0:T(8,128)(2,1)S(1)} collective-permute-done((bf16[528,128]{1,0:T(8,128)(2,1)S(1)}, bf16[528,128]{1,0:T(8,128)(2,1)S(1)}, u32[]{:S(2)}, u32[]{:S(2)}) %collective-permute-start.33) | collective-permute-done | bytes 135200 | tf_op jit(solution)/shard_map/ppermute | solution.py:63
  32.3 1.4 collective-permute-start.34
  33.7 2.9 %collective-permute-done.3.got_ref = bf16[528,128]{1,0:T(8,128)(2,1)S(1)} collective-permute-done((bf16[528,128]{1,0:T(8,128)(2,1)S(1)}, bf16[528,128]{1,0:T(8,128)(2,1)S(1)}, u32[]{:S(2)}, u32[]{:S(2)}) %collective-permute-start.3) | collective-permute-done | bytes 135200 | tf_op jit(solution)/shard_map/ppermute | solution.py:63
  37.1 1.8 %collective-permute-start.4 = (bf16[256,128]{1,0:T(8,128)(2,1)S(1)}, bf16[256,128]{1,0:T(8,128)(2,1)S(1)}, u32[]{:S(2)}, u32[]{:S(2)}) collective-permute-start(bf16[256,128]{1,0:T(8,128)(2,1)S(1)} %get-tuple-element.73), channel_id=1, source_target_pairs={{0,4},{1,3},{2,6},{3,1},{4,0},{5,7},{6,2},{7,5},{8,12},{9,11},{10,... | collective-permute-start | bytes 196616 | tf_op jit(solution)/shard_map/ppermute | solution.py:63
  40.4 1.6 %collective-permute-start.35 = (bf16[256,128]{1,0:T(8,128)(2,1)S(1)}, bf16[256,128]{1,0:T(8,128)(2,1)S(1)}, u32[]{:S(2)}, u32[]{:S(2)}) collective-permute-start(bf16[256,128]{1,0:T(8,128)(2,1)S(1)} %get-tuple-element.96), channel_id=1, source_target_pairs={{0,4},{1,3},{2,6},{3,1},{4,0},{5,7},{6,2},{7,5},{8,12},{9,11},{10,... | collective-permute-start | bytes 196616 | tf_op jit(solution)/shard_map/ppermute | solution.py:63
  42.0 1.7 %collective-permute-start.5 = (bf16[512,128]{1,0:T(8,128)(2,1)S(1)}, bf16[512,128]{1,0:T(8,128)(2,1)S(1)}, u32[]{:S(2)}, u32[]{:S(2)}) collective-permute-start(bf16[512,128]{1,0:T(8,128)(2,1)S(1)} %pad_maximum_fusion.11.own_ref), channel_id=1, source_target_pairs={{0,2},{1,5},{2,0},{3,7},{4,6},{5,1},{6,4},{7,3},{8,10},{9,13},{10,... | collective-permute-start | bytes 393224 | tf_op jit(solution)/shard_map/ppermute | solution.py:63
  43.7 3.0 %collective-permute-done.35 = bf16[256,128]{1,0:T(8,128)(2,1)S(1)} collective-permute-done((bf16[256,128]{1,0:T(8,128)(2,1)S(1)}, bf16[256,128]{1,0:T(8,128)(2,1)S(1)}, u32[]{:S(2)}, u32[]{:S(2)}) %collective-permute-start.35) | collective-permute-done | bytes 65568 | tf_op jit(solution)/shard_map/ppermute | solution.py:63
  46.7 1.6 %collective-permute-start.36 = (bf16[512,128]{1,0:T(8,128)(2,1)S(1)}, bf16[512,128]{1,0:T(8,128)(2,1)S(1)}, u32[]{:S(2)}, u32[]{:S(2)}) collective-permute-start(bf16[512,128]{1,0:T(8,128)(2,1)S(1)} %pad_maximum_fusion.12.own_ref), channel_id=1, source_target_pairs={{0,2},{1,5},{2,0},{3,7},{4,6},{5,1},{6,4},{7,3},{8,10},{9,13},{10,... | collective-permute-start | bytes 393224 | tf_op jit(solution)/shard_map/ppermute | solution.py:63
  48.8 2.9 %collective-permute-done.36.got_ref = bf16[512,128]{1,0:T(8,128)(2,1)S(1)} collective-permute-done((bf16[512,128]{1,0:T(8,128)(2,1)S(1)}, bf16[512,128]{1,0:T(8,128)(2,1)S(1)}, u32[]{:S(2)}, u32[]{:S(2)}) %collective-permute-start.36) | collective-permute-done | bytes 131104 | tf_op jit(solution)/shard_map/ppermute | solution.py:63
  53.3 2.0 %collective-permute-start.16 = (bf16[1152,256]{1,0:T(8,128)(2,1)S(1)}, bf16[1152,256]{1,0:T(8,128)(2,1)S(1)}, u32[]{:S(2)}, u32[]{:S(2)}) collective-permute-start(bf16[1152,256]{1,0:T(8,128)(2,1)S(1)} %pad_maximum_fusion.refs_0_), channel_id=1, source_target_pairs={{0,2},{1,5},{2,0},{3,7},{4,6},{5,1},{6,4},{7,3},{8,10},{9,13},{10,... | collective-permute-start | bytes 1769480 | tf_op jit(solution)/shard_map/ppermute | solution.py:63
  55.4 1.8 %collective-permute-start.38 = (bf16[160,128]{1,0:T(8,128)(2,1)S(1)}, bf16[160,128]{1,0:T(8,128)(2,1)S(1)}, u32[]{:S(2)}, u32[]{:S(2)}) collective-permute-start(bf16[160,128]{1,0:T(8,128)(2,1)S(1)} %shard_map.145), channel_id=1, source_target_pairs={{0,16},{1,17},{2,18},{3,19},{4,20},{5,21},{6,22},{7,23},{8,24},{9,... | collective-permute-start | bytes 122888 | tf_op jit(solution)/shard_map/ppermute | solution.py:63
  57.3 2.4 %collective-permute-start.8 = (bf16[320,128]{1,0:T(8,128)(2,1)S(1)}, bf16[320,128]{1,0:T(8,128)(2,1)S(1)}, u32[]{:S(2)}, u32[]{:S(2)}) collective-permute-start(bf16[320,128]{1,0:T(8,128)(2,1)S(1)} %pad_maximum_fusion.13), channel_id=1, source_target_pairs={{0,8},{1,3},{2,10},{3,1},{4,12},{5,7},{6,14},{7,5},{8,0},{9,11},{1... | collective-permute-start | bytes 245768 | tf_op jit(solution)/shard_map/ppermute | solution.py:63
  59.6 1.0 collective-permute-done.38
  60.7 1.3 collective-permute-start.39
  62.4 2.1 %collective-permute-start.9 = (bf16[640,128]{1,0:T(8,128)(2,1)S(1)}, bf16[640,128]{1,0:T(8,128)(2,1)S(1)}, u32[]{:S(2)}, u32[]{:S(2)}) collective-permute-start(bf16[640,128]{1,0:T(8,128)(2,1)S(1)} %pad_maximum_fusion.6), channel_id=1, source_target_pairs={{0,4},{1,9},{2,6},{3,11},{4,0},{5,13},{6,2},{7,15},{8,12},{9,1},{1... | collective-permute-start | bytes 491528 | tf_op jit(solution)/shard_map/ppermute | solution.py:63
  65.3 0.9 collective-permute-start.40
  66.2 1.6 %collective-permute-done.9 = bf16[640,128]{1,0:T(8,128)(2,1)S(1)} collective-permute-done((bf16[640,128]{1,0:T(8,128)(2,1)S(1)}, bf16[640,128]{1,0:T(8,128)(2,1)S(1)}, u32[]{:S(2)}, u32[]{:S(2)}) %collective-permute-start.9) | collective-permute-done | bytes 163872 | tf_op jit(solution)/shard_map/ppermute | solution.py:63
  67.9 1.6 %collective-permute-start.10 = (bf16[1280,128]{1,0:T(8,128)(2,1)S(1)}, bf16[1280,128]{1,0:T(8,128)(2,1)S(1)}, u32[]{:S(2)}, u32[]{:S(2)}) collective-permute-start(bf16[1280,128]{1,0:T(8,128)(2,1)S(1)} %pad_maximum_fusion.1.refs_0_), channel_id=1, source_target_pairs={{0,2},{1,5},{2,0},{3,7},{4,6},{5,1},{6,4},{7,3},{8,10},{9,13},{10,... | collective-permute-start | bytes 983048 | tf_op jit(solution)/shard_map/ppermute | solution.py:63
  69.5 1.2 collective-permute-done.40
  71.2 1.6 %collective-permute-start.41 = (bf16[1280,128]{1,0:T(8,128)(2,1)S(1)}, bf16[1280,128]{1,0:T(8,128)(2,1)S(1)}, u32[]{:S(2)}, u32[]{:S(2)}) collective-permute-start(bf16[1280,128]{1,0:T(8,128)(2,1)S(1)} %pad_maximum_fusion.2.refs_0_), channel_id=1, source_target_pairs={{0,8},{1,5},{2,10},{3,7},{4,12},{5,1},{6,14},{7,3},{8,0},{9,13},{1... | collective-permute-start | bytes 983048 | tf_op jit(solution)/shard_map/ppermute | solution.py:63
  72.7 2.3 %collective-permute-done.10.refs_1_ = bf16[1280,128]{1,0:T(8,128)(2,1)S(1)} collective-permute-done((bf16[1280,128]{1,0:T(8,128)(2,1)S(1)}, bf16[1280,128]{1,0:T(8,128)(2,1)S(1)}, u32[]{:S(2)}, u32[]{:S(2)}) %collective-permute-start.10) | collective-permute-done | bytes 327712 | tf_op jit(solution)/shard_map/ppermute | solution.py:63
  75.6 2.7 %collective-permute-done.41.refs_1_ = bf16[1280,128]{1,0:T(8,128)(2,1)S(1)} collective-permute-done((bf16[1280,128]{1,0:T(8,128)(2,1)S(1)}, bf16[1280,128]{1,0:T(8,128)(2,1)S(1)}, u32[]{:S(2)}, u32[]{:S(2)}) %collective-permute-start.41) | collective-permute-done | bytes 327712 | tf_op jit(solution)/shard_map/ppermute | solution.py:63
  78.3 1.8 %shard_map.138 = (bf16[4608,128]{1,0:T(8,128)(2,1)S(1)}, bf16[256,128]{1,0:T(8,128)(2,1)S(1)}, f32[256,128]{1,0:T(8,128)S(1)}, f32[256,1]{1,0:T(8,128)S(1)}, f32[144,128]{1,0:T(8,128)S(1)}) custom-call(bf16[1280,128]{1,0:T(8,128)(2,1)S(1)} %pad_maximum_fusion.1.refs_0_, bf16[1280,128]{1,0:T(8,128)(2,1)S(1)} %collective-permute-done.10.refs_1_, ...), custom_call_target="tpu_custom_call" | custom-call | flops 301989888 | bytes 2359296 | tf_op jit(solution)/shard_map/pallas_call | solution.py:403
  81.6 2.3 %shard_map.139 = (bf16[1152,128]{1,0:T(8,128)(2,1)S(1)}, f32[1152,128]{1,0:T(8,128)S(1)}) custom-call(bf16[256,128]{1,0:T(8,128)(2,1)S(1)} %get-tuple-element.78.low_ref.refs_10_, bf16[256,128]{1,0:T(8,128)(2,1)S(1)} %collective-permute-done.19.peer_low_ref, bf16[256,4608]{1,0:T(8,128)(2,1)S(1)} %copy-done, ...), custom_call_target="tpu_custom_call" | custom-call | flops 603979776 | bytes 4718592 | tf_op jit(solution)/shard_map/pallas_call | solution.py:448
  83.9 1.0 collective-permute-start.21
  84.9 1.6 %shard_map.146 = (bf16[4608,128]{1,0:T(8,128)(2,1)S(1)}, bf16[256,128]{1,0:T(8,128)(2,1)S(1)}, f32[256,128]{1,0:T(8,128)S(1)}, f32[256,1]{1,0:T(8,128)S(1)}, f32[144,128]{1,0:T(8,128)S(1)}) custom-call(bf16[1280,128]{1,0:T(8,128)(2,1)S(1)} %pad_maximum_fusion.2.refs_0_, bf16[1280,128]{1,0:T(8,128)(2,1)S(1)} %collective-permute-done.41.refs_1_, ...), custom_call_target="tpu_custom_call" | custom-call | flops 301989888 | bytes 2359296 | tf_op jit(solution)/shard_map/pallas_call | solution.py:403
  87.9 2.3 %shard_map.147 = (bf16[1152,128]{1,0:T(8,128)(2,1)S(1)}, f32[1152,128]{1,0:T(8,128)S(1)}) custom-call(bf16[256,128]{1,0:T(8,128)(2,1)S(1)} %get-tuple-element.103.low_ref.refs_11_, bf16[256,128]{1,0:T(8,128)(2,1)S(1)} %collective-permute-done.44.peer_low_ref, bf16[256,4608]{1,0:T(8,128)(2,1)S(1)} %copy-done, ...), custom_call_target="tpu_custom_call" | custom-call | flops 603979776 | bytes 4718592 | tf_op jit(solution)/shard_map/pallas_call | solution.py:448
  90.1 1.3 collective-permute-start.45
  91.5 1.2 collective-permute-start.22
  92.7 5.8 %collective-permute-done.45 = bf16[1152,128]{1,0:T(8,128)(2,1)S(1)} collective-permute-done((bf16[1152,128]{1,0:T(8,128)(2,1)S(1)}, bf16[1152,128]{1,0:T(8,128)(2,1)S(1)}, u32[]{:S(2)}, u32[]{:S(2)}) %collective-permute-start.45) | collective-permute-done | bytes 294944 | tf_op jit(solution)/shard_map/ppermute | solution.py:63
  98.6 1.2 collective-permute-start.46
  99.9 1.3 collective-permute-start.23
  101.2 3.0 %collective-permute-done.46 = bf16[576,128]{1,0:T(8,128)(2,1)S(1)} collective-permute-done((bf16[576,128]{1,0:T(8,128)(2,1)S(1)}, bf16[576,128]{1,0:T(8,128)(2,1)S(1)}, u32[]{:S(2)}, u32[]{:S(2)}) %collective-permute-start.46) | collective-permute-done | bytes 147488 | tf_op jit(solution)/shard_map/ppermute | solution.py:63
  104.3 1.7 %collective-permute-start.24 = (bf16[144,128]{1,0:T(8,128)(2,1)S(1)}, bf16[144,128]{1,0:T(8,128)(2,1)S(1)}, u32[]{:S(2)}, u32[]{:S(2)}) collective-permute-start(bf16[144,128]{1,0:T(8,128)(2,1)S(1)} %select_convert_fusion.5), channel_id=1, source_target_pairs={{0,16},{1,17},{2,18},{3,19},{4,20},{5,21},{6,22},{7,23},{8,24},{9,... | collective-permute-start | bytes 110600 | tf_op jit(solution)/shard_map/ppermute | solution.py:63
  106.1 1.4 collective-permute-start.47
  107.5 1.8 %collective-permute-done.24 = bf16[144,128]{1,0:T(8,128)(2,1)S(1)} collective-permute-done((bf16[144,128]{1,0:T(8,128)(2,1)S(1)}, bf16[144,128]{1,0:T(8,128)(2,1)S(1)}, u32[]{:S(2)}, u32[]{:S(2)}) %collective-permute-start.24) | collective-permute-done | bytes 36896 | tf_op jit(solution)/shard_map/ppermute | solution.py:63
  109.4 1.7 %collective-permute-start.25 = (bf16[144,128]{1,0:T(8,128)(2,1)S(1)}, bf16[144,128]{1,0:T(8,128)(2,1)S(1)}, u32[]{:S(2)}, u32[]{:S(2)}) collective-permute-start(bf16[144,128]{1,0:T(8,128)(2,1)S(1)} %add_convert_fusion.1), channel_id=1, source_target_pairs={{0,16},{1,17},{2,18},{3,19},{4,20},{5,21},{6,22},{7,23},{8,24},{9,... | collective-permute-start | bytes 110600 | tf_op jit(solution)/shard_map/ppermute | solution.py:63
  111.2 1.3 collective-permute-start.48
  112.5 2.2 %collective-permute-done.25 = bf16[144,128]{1,0:T(8,128)(2,1)S(1)} collective-permute-done((bf16[144,128]{1,0:T(8,128)(2,1)S(1)}, bf16[144,128]{1,0:T(8,128)(2,1)S(1)}, u32[]{:S(2)}, u32[]{:S(2)}) %collective-permute-start.25) | collective-permute-done | bytes 36896 | tf_op jit(solution)/shard_map/ppermute | solution.py:63
  114.7 1.4 collective-permute-done.48
  116.1 1.4 collective-permute-start.49
  117.5 2.8 %collective-permute-start.26 = (bf16[288,128]{1,0:T(8,128)(2,1)S(1)}, bf16[288,128]{1,0:T(8,128)(2,1)S(1)}, u32[]{:S(2)}, u32[]{:S(2)}) collective-permute-start(bf16[288,128]{1,0:T(8,128)(2,1)S(1)} %pad_maximum_fusion.15), channel_id=1, source_target_pairs={{0,8},{1,3},{2,10},{3,1},{4,12},{5,7},{6,14},{7,5},{8,0},{9,11},{1... | collective-permute-start | bytes 221192 | tf_op jit(solution)/shard_map/ppermute | solution.py:63
  121.2 1.6 %collective-permute-start.50 = (bf16[288,128]{1,0:T(8,128)(2,1)S(1)}, bf16[288,128]{1,0:T(8,128)(2,1)S(1)}, u32[]{:S(2)}, u32[]{:S(2)}) collective-permute-start(bf16[288,128]{1,0:T(8,128)(2,1)S(1)} %pad_maximum_fusion.16), channel_id=1, source_target_pairs={{0,4},{1,9},{2,6},{3,11},{4,0},{5,13},{6,2},{7,15},{8,12},{9,1},{1... | collective-permute-start | bytes 221192 | tf_op jit(solution)/shard_map/ppermute | solution.py:63
  124.4 1.2 collective-permute-done.50
  125.6 1.2 collective-permute-start.51
  126.9 3.4 %collective-permute-done.27 = bf16[576,128]{1,0:T(8,128)(2,1)S(1)} collective-permute-done((bf16[576,128]{1,0:T(8,128)(2,1)S(1)}, bf16[576,128]{1,0:T(8,128)(2,1)S(1)}, u32[]{:S(2)}, u32[]{:S(2)}) %collective-permute-start.27) | collective-permute-done | bytes 147488 | tf_op jit(solution)/shard_map/ppermute | solution.py:63
  131.0 3.8 %collective-permute-start.52 = (bf16[1152,128]{1,0:T(8,128)(2,1)S(1)}, bf16[1152,128]{1,0:T(8,128)(2,1)S(1)}, u32[]{:S(2)}, u32[]{:S(2)}) collective-permute-start(bf16[1152,128]{1,0:T(8,128)(2,1)S(1)} %pad_maximum_fusion.5.refs_4_), channel_id=1, source_target_pairs={{0,8},{1,5},{2,10},{3,7},{4,12},{5,1},{6,14},{7,3},{8,0},{9,13},{1... | collective-permute-start | bytes 884744 | tf_op jit(solution)/shard_map/ppermute | solution.py:63
  135.4 1.7 %collective-permute-done.28.refs_1_ = bf16[1152,128]{1,0:T(8,128)(2,1)S(1)} collective-permute-done((bf16[1152,128]{1,0:T(8,128)(2,1)S(1)}, bf16[1152,128]{1,0:T(8,128)(2,1)S(1)}, u32[]{:S(2)}, u32[]{:S(2)}) %collective-permute-start.28) | collective-permute-done | bytes 294944 | tf_op jit(solution)/shard_map/ppermute | solution.py:63
  137.1 2.5 %collective-permute-done.52.refs_5_ = bf16[1152,128]{1,0:T(8,128)(2,1)S(1)} collective-permute-done((bf16[1152,128]{1,0:T(8,128)(2,1)S(1)}, bf16[1152,128]{1,0:T(8,128)(2,1)S(1)}, u32[]{:S(2)}, u32[]{:S(2)}) %collective-permute-start.52) | collective-permute-done | bytes 294944 | tf_op jit(solution)/shard_map/ppermute | solution.py:63
  139.6 1.6 %collective-permute-done.54.refs_7_ = bf16[1152,128]{1,0:T(8,128)(2,1)S(1)} collective-permute-done((bf16[1152,128]{1,0:T(8,128)(2,1)S(1)}, bf16[1152,128]{1,0:T(8,128)(2,1)S(1)}, u32[]{:S(2)}, u32[]{:S(2)}) %collective-permute-start.54) | collective-permute-done | bytes 294944 | tf_op jit(solution)/shard_map/ppermute | solution.py:63
  141.2 5.7 %shard_map.148 = (bf16[4608,256]{1,0:T(8,128)(2,1)}, f32[1,256]{1,0:T(1,128)}, bf16[256,4608]{1,0:T(8,128)(2,1)}) custom-call(bf16[1152,128]{1,0:T(8,128)(2,1)S(1)} %pad_maximum_fusion.4.refs_0_, bf16[1152,128]{1,0:T(8,128)(2,1)S(1)} %collective-permute-done.28.refs_1_, bf16[1152,128]{1,0:T(8,128)(2,1)S(1)} %collective-permute-done.29.refs_2_, ...), custom_call_target="tpu_custom_call" | custom-call | flops 1811939328 | bytes 14155776 | tf_op jit(solution)/shard_map/pallas_call | solution.py:513
  (134 shorter events, 17.6 us)
Async XLA Ops:
  1.6 0.9 copy-start.3
  2.5 0.7 copy-start.6
  5.2 16.4 %collective-permute-start.13 = (bf16[144,256]{1,0:T(8,128)(2,1)S(1)}, bf16[144,256]{1,0:T(8,128)(2,1)S(1)}, u32[]{:S(2)}, u32[]{:S(2)}) collective-permute-start(bf16[144,256]{1,0:T(8,128)(2,1)S(1)} %slice_select_fusion), channel_id=1, source_target_pairs={{0,16},{1,17},{2,18},{3,19},{4,20},{5,21},{6,22},{7,23},{8,24},{9,... | collective-permute-start | bytes 221192 | tf_op jit(solution)/shard_map/ppermute | solution.py:63
  9.3 6.4 %collective-permute-start = (bf16[1040,128]{1,0:T(8,128)(2,1)S(1)}, bf16[1040,128]{1,0:T(8,128)(2,1)S(1)}, u32[]{:S(2)}, u32[]{:S(2)}) collective-permute-start(bf16[1040,128]{1,0:T(8,128)(2,1)S(1)} %get-tuple-element.62), channel_id=1, source_target_pairs={{0,2},{1,5},{2,0},{3,7},{4,6},{5,1},{6,4},{7,3},{8,10},{9,13},{10,... | collective-permute-start | bytes 798728 | tf_op jit(solution)/shard_map/ppermute | solution.py:63
  10.8 9.1 %collective-permute-start.31 = (bf16[1040,128]{1,0:T(8,128)(2,1)S(1)}, bf16[1040,128]{1,0:T(8,128)(2,1)S(1)}, u32[]{:S(2)}, u32[]{:S(2)}) collective-permute-start(bf16[1040,128]{1,0:T(8,128)(2,1)S(1)} %get-tuple-element.83), channel_id=1, source_target_pairs={{0,2},{1,5},{2,0},{3,7},{4,6},{5,1},{6,4},{7,3},{8,10},{9,13},{10,... | collective-permute-start | bytes 798728 | tf_op jit(solution)/shard_map/ppermute | solution.py:63
  11.3 70.3 %collective-permute-start.20 = (bf16[256,4608]{1,0:T(8,128)(2,1)}, bf16[256,4608]{1,0:T(8,128)(2,1)}, u32[]{:S(2)}, u32[]{:S(2)}) collective-permute-start(bf16[256,4608]{1,0:T(8,128)(2,1)} %refs_16_.1), channel_id=1, source_target_pairs={{0,1},{1,0},{2,3},{3,2},{4,5},{5,4},{6,7},{7,6},{8,9},{9,8},{10,11... | collective-permute-start | bytes 7077896 | tf_op jit(solution)/shard_map/ppermute | solution.py:63
  15.8 7.5 %collective-permute-start.1 = (bf16[528,128]{1,0:T(8,128)(2,1)S(1)}, bf16[528,128]{1,0:T(8,128)(2,1)S(1)}, u32[]{:S(2)}, u32[]{:S(2)}) collective-permute-start(bf16[528,128]{1,0:T(8,128)(2,1)S(1)} %get-tuple-element.65), channel_id=1, source_target_pairs={{0,4},{1,3},{2,6},{3,1},{4,0},{5,7},{6,2},{7,5},{8,12},{9,11},{10,... | collective-permute-start | bytes 405512 | tf_op jit(solution)/shard_map/ppermute | solution.py:63
  20.0 5.1 %collective-permute-start.32 = (bf16[528,128]{1,0:T(8,128)(2,1)S(1)}, bf16[528,128]{1,0:T(8,128)(2,1)S(1)}, u32[]{:S(2)}, u32[]{:S(2)}) collective-permute-start(bf16[528,128]{1,0:T(8,128)(2,1)S(1)} %get-tuple-element.86), channel_id=1, source_target_pairs={{0,4},{1,3},{2,6},{3,1},{4,0},{5,7},{6,2},{7,5},{8,12},{9,11},{10,... | collective-permute-start | bytes 405512 | tf_op jit(solution)/shard_map/ppermute | solution.py:63
  21.6 12.1 %collective-permute-start.14 = (bf16[288,256]{1,0:T(8,128)(2,1)S(1)}, bf16[288,256]{1,0:T(8,128)(2,1)S(1)}, u32[]{:S(2)}, u32[]{:S(2)}) collective-permute-start(bf16[288,256]{1,0:T(8,128)(2,1)S(1)} %pad_maximum_fusion.8), channel_id=1, source_target_pairs={{0,8},{1,3},{2,10},{3,1},{4,12},{5,7},{6,14},{7,5},{8,0},{9,11},{1... | collective-permute-start | bytes 442376 | tf_op jit(solution)/shard_map/ppermute | solution.py:63
  23.3 24.9 %copy-start.2 = (bf16[1024,288]{0,1:T(8,128)(2,1)S(1)}, bf16[1024,288]{0,1:T(8,128)(2,1)}, u32[]{:S(2)}) copy-start(bf16[1024,288]{0,1:T(8,128)(2,1)} %param.16) | copy-start | bytes 1769476
  23.3 7.2 %collective-permute-start.2 = (bf16[528,128]{1,0:T(8,128)(2,1)S(1)}, bf16[528,128]{1,0:T(8,128)(2,1)S(1)}, u32[]{:S(2)}, u32[]{:S(2)}) collective-permute-start(bf16[528,128]{1,0:T(8,128)(2,1)S(1)} %get-tuple-element.68), channel_id=1, source_target_pairs={{0,8},{1,9},{2,10},{3,11},{4,12},{5,13},{6,14},{7,15},{8,0},{9,1},... | collective-permute-start | bytes 405512 | tf_op jit(solution)/shard_map/ppermute | solution.py:63
  25.1 7.1 %collective-permute-start.33 = (bf16[528,128]{1,0:T(8,128)(2,1)S(1)}, bf16[528,128]{1,0:T(8,128)(2,1)S(1)}, u32[]{:S(2)}, u32[]{:S(2)}) collective-permute-start(bf16[528,128]{1,0:T(8,128)(2,1)S(1)} %get-tuple-element.89), channel_id=1, source_target_pairs={{0,8},{1,9},{2,10},{3,11},{4,12},{5,13},{6,14},{7,15},{8,0},{9,1},... | collective-permute-start | bytes 405512 | tf_op jit(solution)/shard_map/ppermute | solution.py:63
  30.6 6.1 %collective-permute-start.3 = (bf16[528,128]{1,0:T(8,128)(2,1)S(1)}, bf16[528,128]{1,0:T(8,128)(2,1)S(1)}, u32[]{:S(2)}, u32[]{:S(2)}) collective-permute-start(bf16[528,128]{1,0:T(8,128)(2,1)S(1)} %get-tuple-element.71), channel_id=1, source_target_pairs={{0,16},{1,17},{2,18},{3,19},{4,20},{5,21},{6,22},{7,23},{8,24},{9,... | collective-permute-start | bytes 405512 | tf_op jit(solution)/shard_map/ppermute | solution.py:63
  32.3 7.2 %collective-permute-start.34 = (bf16[528,128]{1,0:T(8,128)(2,1)S(1)}, bf16[528,128]{1,0:T(8,128)(2,1)S(1)}, u32[]{:S(2)}, u32[]{:S(2)}) collective-permute-start(bf16[528,128]{1,0:T(8,128)(2,1)S(1)} %get-tuple-element.92), channel_id=1, source_target_pairs={{0,16},{1,17},{2,18},{3,19},{4,20},{5,21},{6,22},{7,23},{8,24},{9,... | collective-permute-start | bytes 405512 | tf_op jit(solution)/shard_map/ppermute | solution.py:63
  37.1 4.9 %collective-permute-start.4 = (bf16[256,128]{1,0:T(8,128)(2,1)S(1)}, bf16[256,128]{1,0:T(8,128)(2,1)S(1)}, u32[]{:S(2)}, u32[]{:S(2)}) collective-permute-start(bf16[256,128]{1,0:T(8,128)(2,1)S(1)} %get-tuple-element.73), channel_id=1, source_target_pairs={{0,4},{1,3},{2,6},{3,1},{4,0},{5,7},{6,2},{7,5},{8,12},{9,11},{10,... | collective-permute-start | bytes 196616 | tf_op jit(solution)/shard_map/ppermute | solution.py:63
  38.9 13.2 %copy-start.4 = (f32[288]{0:T(512)S(1)}, f32[288]{0:T(512)}, u32[]{:S(2)}) copy-start(f32[288]{0:T(512)} %gain_ref.5) | copy-start | bytes 3460
  38.9 9.7 %collective-permute-start.15 = (bf16[576,256]{1,0:T(8,128)(2,1)S(1)}, bf16[576,256]{1,0:T(8,128)(2,1)S(1)}, u32[]{:S(2)}, u32[]{:S(2)}) collective-permute-start(bf16[576,256]{1,0:T(8,128)(2,1)S(1)} %pad_maximum_fusion.3), channel_id=1, source_target_pairs={{0,4},{1,9},{2,6},{3,11},{4,0},{5,13},{6,2},{7,15},{8,12},{9,1},{1... | collective-permute-start | bytes 884744 | tf_op jit(solution)/shard_map/ppermute | solution.py:63
  40.4 6.3 %collective-permute-start.35 = (bf16[256,128]{1,0:T(8,128)(2,1)S(1)}, bf16[256,128]{1,0:T(8,128)(2,1)S(1)}, u32[]{:S(2)}, u32[]{:S(2)}) collective-permute-start(bf16[256,128]{1,0:T(8,128)(2,1)S(1)} %get-tuple-element.96), channel_id=1, source_target_pairs={{0,4},{1,3},{2,6},{3,1},{4,0},{5,7},{6,2},{7,5},{8,12},{9,11},{10,... | collective-permute-start | bytes 196616 | tf_op jit(solution)/shard_map/ppermute | solution.py:63
  42.0 6.2 %collective-permute-start.5 = (bf16[512,128]{1,0:T(8,128)(2,1)S(1)}, bf16[512,128]{1,0:T(8,128)(2,1)S(1)}, u32[]{:S(2)}, u32[]{:S(2)}) collective-permute-start(bf16[512,128]{1,0:T(8,128)(2,1)S(1)} %pad_maximum_fusion.11.own_ref), channel_id=1, source_target_pairs={{0,2},{1,5},{2,0},{3,7},{4,6},{5,1},{6,4},{7,3},{8,10},{9,13},{10,... | collective-permute-start | bytes 393224 | tf_op jit(solution)/shard_map/ppermute | solution.py:63
  46.7 5.0 %collective-permute-start.36 = (bf16[512,128]{1,0:T(8,128)(2,1)S(1)}, bf16[512,128]{1,0:T(8,128)(2,1)S(1)}, u32[]{:S(2)}, u32[]{:S(2)}) collective-permute-start(bf16[512,128]{1,0:T(8,128)(2,1)S(1)} %pad_maximum_fusion.12.own_ref), channel_id=1, source_target_pairs={{0,2},{1,5},{2,0},{3,7},{4,6},{5,1},{6,4},{7,3},{8,10},{9,13},{10,... | collective-permute-start | bytes 393224 | tf_op jit(solution)/shard_map/ppermute | solution.py:63
  48.6 3.6 %collective-permute-start.6 = (f32[144,128]{1,0:T(8,128)S(1)}, f32[144,128]{1,0:T(8,128)S(1)}, u32[]{:S(2)}, u32[]{:S(2)}) collective-permute-start(f32[144,128]{1,0:T(8,128)S(1)} %get-tuple-element.75), channel_id=1, source_target_pairs={{0,1},{1,0},{2,3},{3,2},{4,5},{5,4},{6,7},{7,6},{8,9},{9,8},{10,11... | collective-permute-start | bytes 221192 | tf_op jit(solution)/shard_map/ppermute | solution.py:63
  52.0 3.3 %collective-permute-start.37 = (f32[144,128]{1,0:T(8,128)S(1)}, f32[144,128]{1,0:T(8,128)S(1)}, u32[]{:S(2)}, u32[]{:S(2)}) collective-permute-start(f32[144,128]{1,0:T(8,128)S(1)} %get-tuple-element.98), channel_id=1, source_target_pairs={{0,1},{1,0},{2,3},{3,2},{4,5},{5,4},{6,7},{7,6},{8,9},{9,8},{10,11... | collective-permute-start | bytes 221192 | tf_op jit(solution)/shard_map/ppermute | solution.py:63
  52.3 5.0 %collective-permute-start.7 = (bf16[160,128]{1,0:T(8,128)(2,1)S(1)}, bf16[160,128]{1,0:T(8,128)(2,1)S(1)}, u32[]{:S(2)}, u32[]{:S(2)}) collective-permute-start(bf16[160,128]{1,0:T(8,128)(2,1)S(1)} %shard_map.136), channel_id=1, source_target_pairs={{0,16},{1,17},{2,18},{3,19},{4,20},{5,21},{6,22},{7,23},{8,24},{9,... | collective-permute-start | bytes 122888 | tf_op jit(solution)/shard_map/ppermute | solution.py:63
  53.0 17.7 %collective-permute-start.17 = (bf16[1152,256]{1,0:T(8,128)(2,1)S(1)}, bf16[1152,256]{1,0:T(8,128)(2,1)S(1)}, u32[]{:S(2)}, u32[]{:S(2)}) collective-permute-start(bf16[1152,256]{1,0:T(8,128)(2,1)S(1)} %pad_maximum_fusion.refs_0_), channel_id=1, source_target_pairs={{0,1},{1,0},{2,3},{3,2},{4,5},{5,4},{6,7},{7,6},{8,9},{9,8},{10,11... | collective-permute-start | bytes 1769480 | tf_op jit(solution)/shard_map/ppermute | solution.py:63
  53.3 12.9 %collective-permute-start.16 = (bf16[1152,256]{1,0:T(8,128)(2,1)S(1)}, bf16[1152,256]{1,0:T(8,128)(2,1)S(1)}, u32[]{:S(2)}, u32[]{:S(2)}) collective-permute-start(bf16[1152,256]{1,0:T(8,128)(2,1)S(1)} %pad_maximum_fusion.refs_0_), channel_id=1, source_target_pairs={{0,2},{1,5},{2,0},{3,7},{4,6},{5,1},{6,4},{7,3},{8,10},{9,13},{10,... | collective-permute-start | bytes 1769480 | tf_op jit(solution)/shard_map/ppermute | solution.py:63
  55.4 5.2 %collective-permute-start.38 = (bf16[160,128]{1,0:T(8,128)(2,1)S(1)}, bf16[160,128]{1,0:T(8,128)(2,1)S(1)}, u32[]{:S(2)}, u32[]{:S(2)}) collective-permute-start(bf16[160,128]{1,0:T(8,128)(2,1)S(1)} %shard_map.145), channel_id=1, source_target_pairs={{0,16},{1,17},{2,18},{3,19},{4,20},{5,21},{6,22},{7,23},{8,24},{9,... | collective-permute-start | bytes 122888 | tf_op jit(solution)/shard_map/ppermute | solution.py:63
  57.3 5.1 %collective-permute-start.8 = (bf16[320,128]{1,0:T(8,128)(2,1)S(1)}, bf16[320,128]{1,0:T(8,128)(2,1)S(1)}, u32[]{:S(2)}, u32[]{:S(2)}) collective-permute-start(bf16[320,128]{1,0:T(8,128)(2,1)S(1)} %pad_maximum_fusion.13), channel_id=1, source_target_pairs={{0,8},{1,3},{2,10},{3,1},{4,12},{5,7},{6,14},{7,5},{8,0},{9,11},{1... | collective-permute-start | bytes 245768 | tf_op jit(solution)/shard_map/ppermute | solution.py:63
  60.7 4.5 %collective-permute-start.39 = (bf16[320,128]{1,0:T(8,128)(2,1)S(1)}, bf16[320,128]{1,0:T(8,128)(2,1)S(1)}, u32[]{:S(2)}, u32[]{:S(2)}) collective-permute-start(bf16[320,128]{1,0:T(8,128)(2,1)S(1)} %pad_maximum_fusion.14), channel_id=1, source_target_pairs={{0,4},{1,9},{2,6},{3,11},{4,0},{5,13},{6,2},{7,15},{8,12},{9,1},{1... | collective-permute-start | bytes 245768 | tf_op jit(solution)/shard_map/ppermute | solution.py:63
  62.4 5.4 %collective-permute-start.9 = (bf16[640,128]{1,0:T(8,128)(2,1)S(1)}, bf16[640,128]{1,0:T(8,128)(2,1)S(1)}, u32[]{:S(2)}, u32[]{:S(2)}) collective-permute-start(bf16[640,128]{1,0:T(8,128)(2,1)S(1)} %pad_maximum_fusion.6), channel_id=1, source_target_pairs={{0,4},{1,9},{2,6},{3,11},{4,0},{5,13},{6,2},{7,15},{8,12},{9,1},{1... | collective-permute-start | bytes 491528 | tf_op jit(solution)/shard_map/ppermute | solution.py:63
  65.3 13.1 %copy-start.1 = (bf16[4608,256]{1,0:T(8,128)(2,1)S(1)}, bf16[4608,256]{1,0:T(8,128)(2,1)}, u32[]{:S(2)}) copy-start(bf16[4608,256]{1,0:T(8,128)(2,1)} %refs_5_.3) | copy-start | bytes 7077892
  65.3 13.0 %copy-start.5 = (f32[256]{0:T(256)S(1)}, f32[256]{0:T(256)}, u32[]{:S(2)}) copy-start(f32[256]{0:T(256)} %refs_6_.3) | copy-start | bytes 3076
  65.3 5.4 %collective-permute-start.40 = (bf16[640,128]{1,0:T(8,128)(2,1)S(1)}, bf16[640,128]{1,0:T(8,128)(2,1)S(1)}, u32[]{:S(2)}, u32[]{:S(2)}) collective-permute-start(bf16[640,128]{1,0:T(8,128)(2,1)S(1)} %pad_maximum_fusion.7), channel_id=1, source_target_pairs={{0,2},{1,3},{2,0},{3,1},{4,6},{5,7},{6,4},{7,5},{8,10},{9,11},{10,... | collective-permute-start | bytes 491528 | tf_op jit(solution)/shard_map/ppermute | solution.py:63
  66.2 4.6 %collective-permute-start.18 = (bf16[1152,256]{1,0:T(8,128)(2,1)S(1)}, bf16[1152,256]{1,0:T(8,128)(2,1)S(1)}, u32[]{:S(2)}, u32[]{:S(2)}) collective-permute-start(bf16[1152,256]{1,0:T(8,128)(2,1)S(1)} %collective-permute-done.16.refs_1_), channel_id=1, source_target_pairs={{0,1},{1,0},{2,3},{3,2},{4,5},{5,4},{6,7},{7,6},{8,9},{9,8},{10,11... | collective-permute-start | bytes 1769480 | tf_op jit(solution)/shard_map/ppermute | solution.py:63
  67.9 7.1 %collective-permute-start.10 = (bf16[1280,128]{1,0:T(8,128)(2,1)S(1)}, bf16[1280,128]{1,0:T(8,128)(2,1)S(1)}, u32[]{:S(2)}, u32[]{:S(2)}) collective-permute-start(bf16[1280,128]{1,0:T(8,128)(2,1)S(1)} %pad_maximum_fusion.1.refs_0_), channel_id=1, source_target_pairs={{0,2},{1,5},{2,0},{3,7},{4,6},{5,1},{6,4},{7,3},{8,10},{9,13},{10,... | collective-permute-start | bytes 983048 | tf_op jit(solution)/shard_map/ppermute | solution.py:63
  71.2 10.5 %copy-start = (bf16[256,4608]{1,0:T(8,128)(2,1)S(1)}, bf16[256,4608]{1,0:T(8,128)(2,1)}, u32[]{:S(2)}) copy-start(bf16[256,4608]{1,0:T(8,128)(2,1)} %refs_16_.1) | copy-start | bytes 7077892
  71.2 7.1 %collective-permute-start.41 = (bf16[1280,128]{1,0:T(8,128)(2,1)S(1)}, bf16[1280,128]{1,0:T(8,128)(2,1)S(1)}, u32[]{:S(2)}, u32[]{:S(2)}) collective-permute-start(bf16[1280,128]{1,0:T(8,128)(2,1)S(1)} %pad_maximum_fusion.2.refs_0_), channel_id=1, source_target_pairs={{0,8},{1,5},{2,10},{3,7},{4,12},{5,1},{6,14},{7,3},{8,0},{9,13},{1... | collective-permute-start | bytes 983048 | tf_op jit(solution)/shard_map/ppermute | solution.py:63
  72.7 5.6 %collective-permute-start.11 = (bf16[1280,128]{1,0:T(8,128)(2,1)S(1)}, bf16[1280,128]{1,0:T(8,128)(2,1)S(1)}, u32[]{:S(2)}, u32[]{:S(2)}) collective-permute-start(bf16[1280,128]{1,0:T(8,128)(2,1)S(1)} %pad_maximum_fusion.1.refs_0_), channel_id=1, source_target_pairs={{0,1},{1,0},{2,3},{3,2},{4,5},{5,4},{6,7},{7,6},{8,9},{9,8},{10,11... | collective-permute-start | bytes 983048 | tf_op jit(solution)/shard_map/ppermute | solution.py:63
  75.1 3.2 %collective-permute-start.12 = (bf16[1280,128]{1,0:T(8,128)(2,1)S(1)}, bf16[1280,128]{1,0:T(8,128)(2,1)S(1)}, u32[]{:S(2)}, u32[]{:S(2)}) collective-permute-start(bf16[1280,128]{1,0:T(8,128)(2,1)S(1)} %collective-permute-done.10.refs_1_), channel_id=1, source_target_pairs={{0,1},{1,0},{2,3},{3,2},{4,5},{5,4},{6,7},{7,6},{8,9},{9,8},{10,11... | collective-permute-start | bytes 983048 | tf_op jit(solution)/shard_map/ppermute | solution.py:63
  75.1 9.8 %collective-permute-start.42 = (bf16[1280,128]{1,0:T(8,128)(2,1)S(1)}, bf16[1280,128]{1,0:T(8,128)(2,1)S(1)}, u32[]{:S(2)}, u32[]{:S(2)}) collective-permute-start(bf16[1280,128]{1,0:T(8,128)(2,1)S(1)} %pad_maximum_fusion.2.refs_0_), channel_id=1, source_target_pairs={{0,1},{1,0},{2,3},{3,2},{4,5},{5,4},{6,7},{7,6},{8,9},{9,8},{10,11... | collective-permute-start | bytes 983048 | tf_op jit(solution)/shard_map/ppermute | solution.py:63
  78.3 6.6 %collective-permute-start.43 = (bf16[1280,128]{1,0:T(8,128)(2,1)S(1)}, bf16[1280,128]{1,0:T(8,128)(2,1)S(1)}, u32[]{:S(2)}, u32[]{:S(2)}) collective-permute-start(bf16[1280,128]{1,0:T(8,128)(2,1)S(1)} %collective-permute-done.41.refs_1_), channel_id=1, source_target_pairs={{0,1},{1,0},{2,3},{3,2},{4,5},{5,4},{6,7},{7,6},{8,9},{9,8},{10,11... | collective-permute-start | bytes 983048 | tf_op jit(solution)/shard_map/ppermute | solution.py:63
  80.2 1.5 collective-permute-start.19
  83.9 7.5 %collective-permute-start.21 = (bf16[1152,128]{1,0:T(8,128)(2,1)S(1)}, bf16[1152,128]{1,0:T(8,128)(2,1)S(1)}, u32[]{:S(2)}, u32[]{:S(2)}) collective-permute-start(bf16[1152,128]{1,0:T(8,128)(2,1)S(1)} %get-tuple-element.80), channel_id=1, source_target_pairs={{0,2},{1,5},{2,0},{3,7},{4,6},{5,1},{6,4},{7,3},{8,10},{9,13},{10,... | collective-permute-start | bytes 884744 | tf_op jit(solution)/shard_map/ppermute | solution.py:63
  86.5 1.3 collective-permute-start.44
  90.1 8.4 %collective-permute-start.45 = (bf16[1152,128]{1,0:T(8,128)(2,1)S(1)}, bf16[1152,128]{1,0:T(8,128)(2,1)S(1)}, u32[]{:S(2)}, u32[]{:S(2)}) collective-permute-start(bf16[1152,128]{1,0:T(8,128)(2,1)S(1)} %get-tuple-element.105), channel_id=1, source_target_pairs={{0,8},{1,5},{2,10},{3,7},{4,12},{5,1},{6,14},{7,3},{8,0},{9,13},{1... | collective-permute-start | bytes 884744 | tf_op jit(solution)/shard_map/ppermute | solution.py:63
  91.5 8.2 %collective-permute-start.22 = (bf16[576,128]{1,0:T(8,128)(2,1)S(1)}, bf16[576,128]{1,0:T(8,128)(2,1)S(1)}, u32[]{:S(2)}, u32[]{:S(2)}) collective-permute-start(bf16[576,128]{1,0:T(8,128)(2,1)S(1)} %select_convert_fusion.1), channel_id=1, source_target_pairs={{0,4},{1,9},{2,6},{3,11},{4,0},{5,13},{6,2},{7,15},{8,12},{9,1},{1... | collective-permute-start | bytes 442376 | tf_op jit(solution)/shard_map/ppermute | solution.py:63
  98.6 5.6 %collective-permute-start.46 = (bf16[576,128]{1,0:T(8,128)(2,1)S(1)}, bf16[576,128]{1,0:T(8,128)(2,1)S(1)}, u32[]{:S(2)}, u32[]{:S(2)}) collective-permute-start(bf16[576,128]{1,0:T(8,128)(2,1)S(1)} %select_convert_fusion), channel_id=1, source_target_pairs={{0,2},{1,3},{2,0},{3,1},{4,6},{5,7},{6,4},{7,5},{8,10},{9,11},{10,... | collective-permute-start | bytes 442376 | tf_op jit(solution)/shard_map/ppermute | solution.py:63
  99.9 4.4 %collective-permute-start.23 = (bf16[288,128]{1,0:T(8,128)(2,1)S(1)}, bf16[288,128]{1,0:T(8,128)(2,1)S(1)}, u32[]{:S(2)}, u32[]{:S(2)}) collective-permute-start(bf16[288,128]{1,0:T(8,128)(2,1)S(1)} %select_convert_fusion.3), channel_id=1, source_target_pairs={{0,8},{1,3},{2,10},{3,1},{4,12},{5,7},{6,14},{7,5},{8,0},{9,11},{1... | collective-permute-start | bytes 221192 | tf_op jit(solution)/shard_map/ppermute | solution.py:63
  104.3 5.0 %collective-permute-start.24 = (bf16[144,128]{1,0:T(8,128)(2,1)S(1)}, bf16[144,128]{1,0:T(8,128)(2,1)S(1)}, u32[]{:S(2)}, u32[]{:S(2)}) collective-permute-start(bf16[144,128]{1,0:T(8,128)(2,1)S(1)} %select_convert_fusion.5), channel_id=1, source_target_pairs={{0,16},{1,17},{2,18},{3,19},{4,20},{5,21},{6,22},{7,23},{8,24},{9,... | collective-permute-start | bytes 110600 | tf_op jit(solution)/shard_map/ppermute | solution.py:63
  106.1 5.0 %collective-permute-start.47 = (bf16[288,128]{1,0:T(8,128)(2,1)S(1)}, bf16[288,128]{1,0:T(8,128)(2,1)S(1)}, u32[]{:S(2)}, u32[]{:S(2)}) collective-permute-start(bf16[288,128]{1,0:T(8,128)(2,1)S(1)} %select_convert_fusion.2), channel_id=1, source_target_pairs={{0,4},{1,9},{2,6},{3,11},{4,0},{5,13},{6,2},{7,15},{8,12},{9,1},{1... | collective-permute-start | bytes 221192 | tf_op jit(solution)/shard_map/ppermute | solution.py:63
  109.4 5.3 %collective-permute-start.25 = (bf16[144,128]{1,0:T(8,128)(2,1)S(1)}, bf16[144,128]{1,0:T(8,128)(2,1)S(1)}, u32[]{:S(2)}, u32[]{:S(2)}) collective-permute-start(bf16[144,128]{1,0:T(8,128)(2,1)S(1)} %add_convert_fusion.1), channel_id=1, source_target_pairs={{0,16},{1,17},{2,18},{3,19},{4,20},{5,21},{6,22},{7,23},{8,24},{9,... | collective-permute-start | bytes 110600 | tf_op jit(solution)/shard_map/ppermute | solution.py:63
  111.2 4.9 %collective-permute-start.48 = (bf16[144,128]{1,0:T(8,128)(2,1)S(1)}, bf16[144,128]{1,0:T(8,128)(2,1)S(1)}, u32[]{:S(2)}, u32[]{:S(2)}) collective-permute-start(bf16[144,128]{1,0:T(8,128)(2,1)S(1)} %select_convert_fusion.4), channel_id=1, source_target_pairs={{0,16},{1,17},{2,18},{3,19},{4,20},{5,21},{6,22},{7,23},{8,24},{9,... | collective-permute-start | bytes 110600 | tf_op jit(solution)/shard_map/ppermute | solution.py:63
  116.1 5.0 %collective-permute-start.49 = (bf16[144,128]{1,0:T(8,128)(2,1)S(1)}, bf16[144,128]{1,0:T(8,128)(2,1)S(1)}, u32[]{:S(2)}, u32[]{:S(2)}) collective-permute-start(bf16[144,128]{1,0:T(8,128)(2,1)S(1)} %add_convert_fusion), channel_id=1, source_target_pairs={{0,16},{1,17},{2,18},{3,19},{4,20},{5,21},{6,22},{7,23},{8,24},{9,... | collective-permute-start | bytes 110600 | tf_op jit(solution)/shard_map/ppermute | solution.py:63
  117.5 5.9 %collective-permute-start.26 = (bf16[288,128]{1,0:T(8,128)(2,1)S(1)}, bf16[288,128]{1,0:T(8,128)(2,1)S(1)}, u32[]{:S(2)}, u32[]{:S(2)}) collective-permute-start(bf16[288,128]{1,0:T(8,128)(2,1)S(1)} %pad_maximum_fusion.15), channel_id=1, source_target_pairs={{0,8},{1,3},{2,10},{3,1},{4,12},{5,7},{6,14},{7,5},{8,0},{9,11},{1... | collective-permute-start | bytes 221192 | tf_op jit(solution)/shard_map/ppermute | solution.py:63
  121.2 4.4 %collective-permute-start.50 = (bf16[288,128]{1,0:T(8,128)(2,1)S(1)}, bf16[288,128]{1,0:T(8,128)(2,1)S(1)}, u32[]{:S(2)}, u32[]{:S(2)}) collective-permute-start(bf16[288,128]{1,0:T(8,128)(2,1)S(1)} %pad_maximum_fusion.16), channel_id=1, source_target_pairs={{0,4},{1,9},{2,6},{3,11},{4,0},{5,13},{6,2},{7,15},{8,12},{9,1},{1... | collective-permute-start | bytes 221192 | tf_op jit(solution)/shard_map/ppermute | solution.py:63
  123.5 6.7 %collective-permute-start.27 = (bf16[576,128]{1,0:T(8,128)(2,1)S(1)}, bf16[576,128]{1,0:T(8,128)(2,1)S(1)}, u32[]{:S(2)}, u32[]{:S(2)}) collective-permute-start(bf16[576,128]{1,0:T(8,128)(2,1)S(1)} %pad_maximum_fusion.9), channel_id=1, source_target_pairs={{0,4},{1,9},{2,6},{3,11},{4,0},{5,13},{6,2},{7,15},{8,12},{9,1},{1... | collective-permute-start | bytes 442376 | tf_op jit(solution)/shard_map/ppermute | solution.py:63
  125.6 5.3 %collective-permute-start.51 = (bf16[576,128]{1,0:T(8,128)(2,1)S(1)}, bf16[576,128]{1,0:T(8,128)(2,1)S(1)}, u32[]{:S(2)}, u32[]{:S(2)}) collective-permute-start(bf16[576,128]{1,0:T(8,128)(2,1)S(1)} %pad_maximum_fusion.10), channel_id=1, source_target_pairs={{0,2},{1,3},{2,0},{3,1},{4,6},{5,7},{6,4},{7,5},{8,10},{9,11},{10,... | collective-permute-start | bytes 442376 | tf_op jit(solution)/shard_map/ppermute | solution.py:63
  130.3 6.8 %collective-permute-start.28 = (bf16[1152,128]{1,0:T(8,128)(2,1)S(1)}, bf16[1152,128]{1,0:T(8,128)(2,1)S(1)}, u32[]{:S(2)}, u32[]{:S(2)}) collective-permute-start(bf16[1152,128]{1,0:T(8,128)(2,1)S(1)} %pad_maximum_fusion.4.refs_0_), channel_id=1, source_target_pairs={{0,2},{1,5},{2,0},{3,7},{4,6},{5,1},{6,4},{7,3},{8,10},{9,13},{10,... | collective-permute-start | bytes 884744 | tf_op jit(solution)/shard_map/ppermute | solution.py:63
  131.0 8.5 %collective-permute-start.52 = (bf16[1152,128]{1,0:T(8,128)(2,1)S(1)}, bf16[1152,128]{1,0:T(8,128)(2,1)S(1)}, u32[]{:S(2)}, u32[]{:S(2)}) collective-permute-start(bf16[1152,128]{1,0:T(8,128)(2,1)S(1)} %pad_maximum_fusion.5.refs_4_), channel_id=1, source_target_pairs={{0,8},{1,5},{2,10},{3,7},{4,12},{5,1},{6,14},{7,3},{8,0},{9,13},{1... | collective-permute-start | bytes 884744 | tf_op jit(solution)/shard_map/ppermute | solution.py:63
  134.9 4.7 %collective-permute-start.29 = (bf16[1152,128]{1,0:T(8,128)(2,1)S(1)}, bf16[1152,128]{1,0:T(8,128)(2,1)S(1)}, u32[]{:S(2)}, u32[]{:S(2)}) collective-permute-start(bf16[1152,128]{1,0:T(8,128)(2,1)S(1)} %pad_maximum_fusion.4.refs_0_), channel_id=1, source_target_pairs={{0,1},{1,0},{2,3},{3,2},{4,5},{5,4},{6,7},{7,6},{8,9},{9,8},{10,11... | collective-permute-start | bytes 884744 | tf_op jit(solution)/shard_map/ppermute | solution.py:63
  134.9 4.7 %collective-permute-start.53 = (bf16[1152,128]{1,0:T(8,128)(2,1)S(1)}, bf16[1152,128]{1,0:T(8,128)(2,1)S(1)}, u32[]{:S(2)}, u32[]{:S(2)}) collective-permute-start(bf16[1152,128]{1,0:T(8,128)(2,1)S(1)} %pad_maximum_fusion.5.refs_4_), channel_id=1, source_target_pairs={{0,1},{1,0},{2,3},{3,2},{4,5},{5,4},{6,7},{7,6},{8,9},{9,8},{10,11... | collective-permute-start | bytes 884744 | tf_op jit(solution)/shard_map/ppermute | solution.py:63
  137.1 2.5 %collective-permute-start.30 = (bf16[1152,128]{1,0:T(8,128)(2,1)S(1)}, bf16[1152,128]{1,0:T(8,128)(2,1)S(1)}, u32[]{:S(2)}, u32[]{:S(2)}) collective-permute-start(bf16[1152,128]{1,0:T(8,128)(2,1)S(1)} %collective-permute-done.28.refs_1_), channel_id=1, source_target_pairs={{0,1},{1,0},{2,3},{3,2},{4,5},{5,4},{6,7},{7,6},{8,9},{9,8},{10,11... | collective-permute-start | bytes 884744 | tf_op jit(solution)/shard_map/ppermute | solution.py:63
  139.6 1.6 %collective-permute-start.54 = (bf16[1152,128]{1,0:T(8,128)(2,1)S(1)}, bf16[1152,128]{1,0:T(8,128)(2,1)S(1)}, u32[]{:S(2)}, u32[]{:S(2)}) collective-permute-start(bf16[1152,128]{1,0:T(8,128)(2,1)S(1)} %collective-permute-done.52.refs_5_), channel_id=1, source_target_pairs={{0,1},{1,0},{2,3},{3,2},{4,5},{5,4},{6,7},{7,6},{8,9},{9,8},{10,11... | collective-permute-start | bytes 884744 | tf_op jit(solution)/shard_map/ppermute | solution.py:63

commit v5 on v4

--- a/solution.py
+++ b/solution.py
@@ -564,13 +564,14 @@
     core_bit = ladder.bit(core)
     paired = len(cores) == 1 and residual_t.shape[0] % 32 == 0 and group_bits >= 1
 
-    mine, gain = residual_t, post_gain[:, None]
-    for step in cores:
-        half = mine.shape[0] // 2
-        up = ladder.bit(step) == 1
-        mine = jnp.where(up, mine[half:], mine[:half])
-        gain = jnp.where(up, gain[half:], gain[:half])
-    block = mine.shape[0]
+    def share(value):
+        for step in cores:
+            half = value.shape[0] // 2
+            value = jnp.where(ladder.bit(step) == 1, value[half:], value[:half])
+        return value
+
+    gain = share(post_gain[:, None])
+    block = gain.shape[0]
 
     def canonical(pieces, steps, stride):
         own, far, own_peer, far_peer = pieces
@@ -627,7 +628,8 @@
             keeps.append(keep)
             squares.append(square[:, cut])
 
-    sends[0], mine = lax.optimization_barrier((sends[0], mine))
+    sends[0], sends[1], later = lax.optimization_barrier((sends[0], sends[1], residual_t))
+    mine = share(later)
     steps = cores[1:] + routes[0]
     residual_own = ladder.gather(mine, steps[1:])
     residual_far = ladder.swap(residual_own, steps[0])

time: 147 us -> 146 us (level)
  transfers between devices with their start and end apart: 55 -> 55, of which waited for: 30 -> 31; matrix products, arithmetic and copies ran while one was open for 3% -> 3% of each run, Pallas kernels for 7% -> 7%
where the time goes in v5:
time: 146 us
  starting transfers between devices  62.6 us (43%)
  waiting for transfers between devices  57.3 us (39%)
  Pallas kernels  18.4 us (13%)
  other arithmetic  3.89 us (3%)
  local copies, waits for them, and re-layouts  2.47 us (2%)
    ppermute x55, starting transfers between devices, swap(): return lax.ppermute(value, AXES, self.pairs(step))  62.6 us
    ppermute x55, waiting for transfers between devices, swap(): return lax.ppermute(value, AXES, self.pairs(step))  57.3 us
    pallas_call x1, Pallas kernels, gradients(): pl.pallas_call(functools.partial(final_kernel, ladder, core, steps), out_...  5.64 us
    pallas_call x2, Pallas kernels, decode(): pl.pallas_call(functools.partial(decode_kernel, ladder, core, step), out_...  4.53 us
    pallas_call x2, Pallas kernels, encode(): pl.pallas_call(functools.partial(encode_kernel, ladder, core, steps, plac...  3.45 us
  transfers between devices with their start and end apart: 55, of which 31 were waited for; matrix products, arithmetic and copies ran while one was open for 3% of the time, Pallas kernels for 7%

profile of v5, /device:TPU:0, one launch (start us, length us, event | category | flops | bytes accessed | tf_op | source)
XLA Modules:
  0.0 146.0 jit_solution(15761759376380384958)
XLA Ops:
  2.2 2.0 %shard_map.130 = (bf16[1040,128]{1,0:T(8,128)(2,1)S(1)}, bf16[1040,128]{1,0:T(8,128)(2,1)S(1)}, f32[1024,128]{1,0:T(8,128)S(1)}, f32[1024,128]{1,0:T(8,128)S(1)}...) custom-call(bf16[288,256]{1,0:T(8,128)(2,1)S(1)} %bitcast.5, f32[288]{0:T(512)S(1)} %copy-done.7, bf16[288,1024]{1,0:T(8,128)(2,1)} %refs_0_.1, ...), custom_call_target="tpu_custom_call" | custom-call | flops 301989888 | bytes 1179648 | tf_op jit(solution)/shard_map/pallas_call | solution.py:187
  4.3 4.1 %collective-permute-start.13 = (bf16[144,256]{1,0:T(8,128)(2,1)S(1)}, bf16[144,256]{1,0:T(8,128)(2,1)S(1)}, u32[]{:S(2)}, u32[]{:S(2)}) collective-permute-start(bf16[144,256]{1,0:T(8,128)(2,1)S(1)} %slice_select_fusion), channel_id=1, source_target_pairs={{0,16},{1,17},{2,18},{3,19},{4,20},{5,21},{6,22},{7,23},{8,24},{9,... | collective-permute-start | bytes 221192 | tf_op jit(solution)/shard_map/ppermute | solution.py:63
  8.4 1.5 %collective-permute-start = (bf16[1040,128]{1,0:T(8,128)(2,1)S(1)}, bf16[1040,128]{1,0:T(8,128)(2,1)S(1)}, u32[]{:S(2)}, u32[]{:S(2)}) collective-permute-start(bf16[1040,128]{1,0:T(8,128)(2,1)S(1)} %get-tuple-element.64), channel_id=1, source_target_pairs={{0,2},{1,5},{2,0},{3,7},{4,6},{5,1},{6,4},{7,3},{8,10},{9,13},{10,... | collective-permute-start | bytes 798728 | tf_op jit(solution)/shard_map/ppermute | solution.py:63
  10.4 2.2 %multiply_reduce_fusion = f32[256]{0:T(256)S(1)} fusion(bf16[256,4608]{1,0:T(8,128)(2,1)} %refs_16_.1), kind=kLoop, calls=%fused_computation | loop fusion | flops 3538688 | bytes 2360320 | tf_op jit(solution)/shard_map/reduce_sum | solution.py:601
  13.0 1.8 %collective-permute-done.got_ref = bf16[1040,128]{1,0:T(8,128)(2,1)S(1)} collective-permute-done((bf16[1040,128]{1,0:T(8,128)(2,1)S(1)}, bf16[1040,128]{1,0:T(8,128)(2,1)S(1)}, u32[]{:S(2)}, u32[]{:S(2)}) %collective-permute-start) | collective-permute-done | bytes 266272 | tf_op jit(solution)/shard_map/ppermute | solution.py:63
  14.9 1.6 %collective-permute-start.1 = (bf16[528,128]{1,0:T(8,128)(2,1)S(1)}, bf16[528,128]{1,0:T(8,128)(2,1)S(1)}, u32[]{:S(2)}, u32[]{:S(2)}) collective-permute-start(bf16[528,128]{1,0:T(8,128)(2,1)S(1)} %get-tuple-element.67), channel_id=1, source_target_pairs={{0,4},{1,3},{2,6},{3,1},{4,0},{5,7},{6,2},{7,5},{8,12},{9,11},{10,... | collective-permute-start | bytes 405512 | tf_op jit(solution)/shard_map/ppermute | solution.py:63
  16.5 2.6 %collective-permute-done.31.got_ref = bf16[1040,128]{1,0:T(8,128)(2,1)S(1)} collective-permute-done((bf16[1040,128]{1,0:T(8,128)(2,1)S(1)}, bf16[1040,128]{1,0:T(8,128)(2,1)S(1)}, u32[]{:S(2)}, u32[]{:S(2)}) %collective-permute-start.31) | collective-permute-done | bytes 266272 | tf_op jit(solution)/shard_map/ppermute | solution.py:63
  19.1 1.6 %collective-permute-start.32 = (bf16[528,128]{1,0:T(8,128)(2,1)S(1)}, bf16[528,128]{1,0:T(8,128)(2,1)S(1)}, u32[]{:S(2)}, u32[]{:S(2)}) collective-permute-start(bf16[528,128]{1,0:T(8,128)(2,1)S(1)} %get-tuple-element.88), channel_id=1, source_target_pairs={{0,4},{1,3},{2,6},{3,1},{4,0},{5,7},{6,2},{7,5},{8,12},{9,11},{10,... | collective-permute-start | bytes 405512 | tf_op jit(solution)/shard_map/ppermute | solution.py:63
  20.7 1.6 %collective-permute-start.14 = (bf16[288,256]{1,0:T(8,128)(2,1)S(1)}, bf16[288,256]{1,0:T(8,128)(2,1)S(1)}, u32[]{:S(2)}, u32[]{:S(2)}) collective-permute-start(bf16[288,256]{1,0:T(8,128)(2,1)S(1)} %pad_maximum_fusion.8), channel_id=1, source_target_pairs={{0,8},{1,3},{2,10},{3,1},{4,12},{5,7},{6,14},{7,5},{8,0},{9,11},{1... | collective-permute-start | bytes 442376 | tf_op jit(solution)/shard_map/ppermute | solution.py:63
  22.9 1.2 collective-permute-done.32.got_ref
  24.2 1.6 %collective-permute-start.33 = (bf16[528,128]{1,0:T(8,128)(2,1)S(1)}, bf16[528,128]{1,0:T(8,128)(2,1)S(1)}, u32[]{:S(2)}, u32[]{:S(2)}) collective-permute-start(bf16[528,128]{1,0:T(8,128)(2,1)S(1)} %get-tuple-element.91), channel_id=1, source_target_pairs={{0,8},{1,9},{2,10},{3,11},{4,12},{5,13},{6,14},{7,15},{8,0},{9,1},... | collective-permute-start | bytes 405512 | tf_op jit(solution)/shard_map/ppermute | solution.py:63
  26.7 2.9 %collective-permute-done.2.got_ref = bf16[528,128]{1,0:T(8,128)(2,1)S(1)} collective-permute-done((bf16[528,128]{1,0:T(8,128)(2,1)S(1)}, bf16[528,128]{1,0:T(8,128)(2,1)S(1)}, u32[]{:S(2)}, u32[]{:S(2)}) %collective-permute-start.2) | collective-permute-done | bytes 135200 | tf_op jit(solution)/shard_map/ppermute | solution.py:63
  29.8 1.6 %collective-permute-done.33.got_ref = bf16[528,128]{1,0:T(8,128)(2,1)S(1)} collective-permute-done((bf16[528,128]{1,0:T(8,128)(2,1)S(1)}, bf16[528,128]{1,0:T(8,128)(2,1)S(1)}, u32[]{:S(2)}, u32[]{:S(2)}) %collective-permute-start.33) | collective-permute-done | bytes 135200 | tf_op jit(solution)/shard_map/ppermute | solution.py:63
  31.4 1.4 collective-permute-start.34
  32.8 2.9 %collective-permute-done.3.got_ref = bf16[528,128]{1,0:T(8,128)(2,1)S(1)} collective-permute-done((bf16[528,128]{1,0:T(8,128)(2,1)S(1)}, bf16[528,128]{1,0:T(8,128)(2,1)S(1)}, u32[]{:S(2)}, u32[]{:S(2)}) %collective-permute-start.3) | collective-permute-done | bytes 135200 | tf_op jit(solution)/shard_map/ppermute | solution.py:63
  36.2 1.8 %collective-permute-start.4 = (bf16[256,128]{1,0:T(8,128)(2,1)S(1)}, bf16[256,128]{1,0:T(8,128)(2,1)S(1)}, u32[]{:S(2)}, u32[]{:S(2)}) collective-permute-start(bf16[256,128]{1,0:T(8,128)(2,1)S(1)} %get-tuple-element.75), channel_id=1, source_target_pairs={{0,4},{1,3},{2,6},{3,1},{4,0},{5,7},{6,2},{7,5},{8,12},{9,11},{10,... | collective-permute-start | bytes 196616 | tf_op jit(solution)/shard_map/ppermute | solution.py:63
  39.4 1.7 %collective-permute-start.35 = (bf16[256,128]{1,0:T(8,128)(2,1)S(1)}, bf16[256,128]{1,0:T(8,128)(2,1)S(1)}, u32[]{:S(2)}, u32[]{:S(2)}) collective-permute-start(bf16[256,128]{1,0:T(8,128)(2,1)S(1)} %get-tuple-element.98), channel_id=1, source_target_pairs={{0,4},{1,3},{2,6},{3,1},{4,0},{5,7},{6,2},{7,5},{8,12},{9,11},{10,... | collective-permute-start | bytes 196616 | tf_op jit(solution)/shard_map/ppermute | solution.py:63
  41.1 1.7 %collective-permute-start.5 = (bf16[512,128]{1,0:T(8,128)(2,1)S(1)}, bf16[512,128]{1,0:T(8,128)(2,1)S(1)}, u32[]{:S(2)}, u32[]{:S(2)}) collective-permute-start(bf16[512,128]{1,0:T(8,128)(2,1)S(1)} %pad_maximum_fusion.11.own_ref), channel_id=1, source_target_pairs={{0,2},{1,5},{2,0},{3,7},{4,6},{5,1},{6,4},{7,3},{8,10},{9,13},{10,... | collective-permute-start | bytes 393224 | tf_op jit(solution)/shard_map/ppermute | solution.py:63
  42.8 3.0 %collective-permute-done.35 = bf16[256,128]{1,0:T(8,128)(2,1)S(1)} collective-permute-done((bf16[256,128]{1,0:T(8,128)(2,1)S(1)}, bf16[256,128]{1,0:T(8,128)(2,1)S(1)}, u32[]{:S(2)}, u32[]{:S(2)}) %collective-permute-start.35) | collective-permute-done | bytes 65568 | tf_op jit(solution)/shard_map/ppermute | solution.py:63
  45.8 1.5 %collective-permute-start.36 = (bf16[512,128]{1,0:T(8,128)(2,1)S(1)}, bf16[512,128]{1,0:T(8,128)(2,1)S(1)}, u32[]{:S(2)}, u32[]{:S(2)}) collective-permute-start(bf16[512,128]{1,0:T(8,128)(2,1)S(1)} %pad_maximum_fusion.12.own_ref), channel_id=1, source_target_pairs={{0,2},{1,5},{2,0},{3,7},{4,6},{5,1},{6,4},{7,3},{8,10},{9,13},{10,... | collective-permute-start | bytes 393224 | tf_op jit(solution)/shard_map/ppermute | solution.py:63
  47.9 2.9 %collective-permute-done.36.got_ref = bf16[512,128]{1,0:T(8,128)(2,1)S(1)} collective-permute-done((bf16[512,128]{1,0:T(8,128)(2,1)S(1)}, bf16[512,128]{1,0:T(8,128)(2,1)S(1)}, u32[]{:S(2)}, u32[]{:S(2)}) %collective-permute-start.36) | collective-permute-done | bytes 131104 | tf_op jit(solution)/shard_map/ppermute | solution.py:63
  52.4 2.0 %collective-permute-start.16 = (bf16[1152,256]{1,0:T(8,128)(2,1)S(1)}, bf16[1152,256]{1,0:T(8,128)(2,1)S(1)}, u32[]{:S(2)}, u32[]{:S(2)}) collective-permute-start(bf16[1152,256]{1,0:T(8,128)(2,1)S(1)} %pad_maximum_fusion.refs_0_), channel_id=1, source_target_pairs={{0,2},{1,5},{2,0},{3,7},{4,6},{5,1},{6,4},{7,3},{8,10},{9,13},{10,... | collective-permute-start | bytes 1769480 | tf_op jit(solution)/shard_map/ppermute | solution.py:63
  54.5 1.8 %collective-permute-start.38 = (bf16[160,128]{1,0:T(8,128)(2,1)S(1)}, bf16[160,128]{1,0:T(8,128)(2,1)S(1)}, u32[]{:S(2)}, u32[]{:S(2)}) collective-permute-start(bf16[160,128]{1,0:T(8,128)(2,1)S(1)} %shard_map.145), channel_id=1, source_target_pairs={{0,16},{1,17},{2,18},{3,19},{4,20},{5,21},{6,22},{7,23},{8,24},{9,... | collective-permute-start | bytes 122888 | tf_op jit(solution)/shard_map/ppermute | solution.py:63
  56.4 2.4 %collective-permute-start.8 = (bf16[320,128]{1,0:T(8,128)(2,1)S(1)}, bf16[320,128]{1,0:T(8,128)(2,1)S(1)}, u32[]{:S(2)}, u32[]{:S(2)}) collective-permute-start(bf16[320,128]{1,0:T(8,128)(2,1)S(1)} %pad_maximum_fusion.13), channel_id=1, source_target_pairs={{0,8},{1,3},{2,10},{3,1},{4,12},{5,7},{6,14},{7,5},{8,0},{9,11},{1... | collective-permute-start | bytes 245768 | tf_op jit(solution)/shard_map/ppermute | solution.py:63
  58.7 1.0 collective-permute-done.38
  59.8 1.3 collective-permute-start.39
  61.5 2.1 %collective-permute-start.9 = (bf16[640,128]{1,0:T(8,128)(2,1)S(1)}, bf16[640,128]{1,0:T(8,128)(2,1)S(1)}, u32[]{:S(2)}, u32[]{:S(2)}) collective-permute-start(bf16[640,128]{1,0:T(8,128)(2,1)S(1)} %pad_maximum_fusion.6), channel_id=1, source_target_pairs={{0,4},{1,9},{2,6},{3,11},{4,0},{5,13},{6,2},{7,15},{8,12},{9,1},{1... | collective-permute-start | bytes 491528 | tf_op jit(solution)/shard_map/ppermute | solution.py:63
  64.4 1.0 collective-permute-start.40
  65.4 1.5 %collective-permute-done.9 = bf16[640,128]{1,0:T(8,128)(2,1)S(1)} collective-permute-done((bf16[640,128]{1,0:T(8,128)(2,1)S(1)}, bf16[640,128]{1,0:T(8,128)(2,1)S(1)}, u32[]{:S(2)}, u32[]{:S(2)}) %collective-permute-start.9) | collective-permute-done | bytes 163872 | tf_op jit(solution)/shard_map/ppermute | solution.py:63
  67.0 1.6 %collective-permute-start.10 = (bf16[1280,128]{1,0:T(8,128)(2,1)S(1)}, bf16[1280,128]{1,0:T(8,128)(2,1)S(1)}, u32[]{:S(2)}, u32[]{:S(2)}) collective-permute-start(bf16[1280,128]{1,0:T(8,128)(2,1)S(1)} %pad_maximum_fusion.1.refs_0_), channel_id=1, source_target_pairs={{0,2},{1,5},{2,0},{3,7},{4,6},{5,1},{6,4},{7,3},{8,10},{9,13},{10,... | collective-permute-start | bytes 983048 | tf_op jit(solution)/shard_map/ppermute | solution.py:63
  68.6 1.1 collective-permute-done.40
  70.2 1.6 %collective-permute-start.41 = (bf16[1280,128]{1,0:T(8,128)(2,1)S(1)}, bf16[1280,128]{1,0:T(8,128)(2,1)S(1)}, u32[]{:S(2)}, u32[]{:S(2)}) collective-permute-start(bf16[1280,128]{1,0:T(8,128)(2,1)S(1)} %pad_maximum_fusion.2.refs_0_), channel_id=1, source_target_pairs={{0,8},{1,5},{2,10},{3,7},{4,12},{5,1},{6,14},{7,3},{8,0},{9,13},{1... | collective-permute-start | bytes 983048 | tf_op jit(solution)/shard_map/ppermute | solution.py:63
  71.8 2.3 %collective-permute-done.10.refs_1_ = bf16[1280,128]{1,0:T(8,128)(2,1)S(1)} collective-permute-done((bf16[1280,128]{1,0:T(8,128)(2,1)S(1)}, bf16[1280,128]{1,0:T(8,128)(2,1)S(1)}, u32[]{:S(2)}, u32[]{:S(2)}) %collective-permute-start.10) | collective-permute-done | bytes 327712 | tf_op jit(solution)/shard_map/ppermute | solution.py:63
  74.7 2.7 %collective-permute-done.41.refs_1_ = bf16[1280,128]{1,0:T(8,128)(2,1)S(1)} collective-permute-done((bf16[1280,128]{1,0:T(8,128)(2,1)S(1)}, bf16[1280,128]{1,0:T(8,128)(2,1)S(1)}, u32[]{:S(2)}, u32[]{:S(2)}) %collective-permute-start.41) | collective-permute-done | bytes 327712 | tf_op jit(solution)/shard_map/ppermute | solution.py:63
  77.4 1.8 %shard_map.138 = (bf16[4608,128]{1,0:T(8,128)(2,1)S(1)}, bf16[256,128]{1,0:T(8,128)(2,1)S(1)}, f32[256,128]{1,0:T(8,128)S(1)}, f32[256,1]{1,0:T(8,128)S(1)}, f32[144,128]{1,0:T(8,128)S(1)}) custom-call(bf16[1280,128]{1,0:T(8,128)(2,1)S(1)} %pad_maximum_fusion.1.refs_0_, bf16[1280,128]{1,0:T(8,128)(2,1)S(1)} %collective-permute-done.10.refs_1_, ...), custom_call_target="tpu_custom_call" | custom-call | flops 301989888 | bytes 2359296 | tf_op jit(solution)/shard_map/pallas_call | solution.py:403
  80.7 2.3 %shard_map.139 = (bf16[1152,128]{1,0:T(8,128)(2,1)S(1)}, f32[1152,128]{1,0:T(8,128)S(1)}) custom-call(bf16[256,128]{1,0:T(8,128)(2,1)S(1)} %get-tuple-element.80.low_ref.refs_10_, bf16[256,128]{1,0:T(8,128)(2,1)S(1)} %collective-permute-done.19.peer_low_ref, bf16[256,4608]{1,0:T(8,128)(2,1)S(1)} %copy-done, ...), custom_call_target="tpu_custom_call" | custom-call | flops 603979776 | bytes 4718592 | tf_op jit(solution)/shard_map/pallas_call | solution.py:448
  83.0 1.0 collective-permute-start.21
  84.0 1.6 %shard_map.146 = (bf16[4608,128]{1,0:T(8,128)(2,1)S(1)}, bf16[256,128]{1,0:T(8,128)(2,1)S(1)}, f32[256,128]{1,0:T(8,128)S(1)}, f32[256,1]{1,0:T(8,128)S(1)}, f32[144,128]{1,0:T(8,128)S(1)}) custom-call(bf16[1280,128]{1,0:T(8,128)(2,1)S(1)} %pad_maximum_fusion.2.refs_0_, bf16[1280,128]{1,0:T(8,128)(2,1)S(1)} %collective-permute-done.41.refs_1_, ...), custom_call_target="tpu_custom_call" | custom-call | flops 301989888 | bytes 2359296 | tf_op jit(solution)/shard_map/pallas_call | solution.py:403
  86.1 0.9 collective-permute-done.44.peer_low_ref
  87.0 2.3 %shard_map.147 = (bf16[1152,128]{1,0:T(8,128)(2,1)S(1)}, f32[1152,128]{1,0:T(8,128)S(1)}) custom-call(bf16[256,128]{1,0:T(8,128)(2,1)S(1)} %get-tuple-element.105.low_ref.refs_11_, bf16[256,128]{1,0:T(8,128)(2,1)S(1)} %collective-permute-done.44.peer_low_ref, bf16[256,4608]{1,0:T(8,128)(2,1)S(1)} %copy-done, ...), custom_call_target="tpu_custom_call" | custom-call | flops 603979776 | bytes 4718592 | tf_op jit(solution)/shard_map/pallas_call | solution.py:448
  89.3 1.3 collective-permute-start.45
  90.7 1.2 collective-permute-start.22
  91.9 5.8 %collective-permute-done.45 = bf16[1152,128]{1,0:T(8,128)(2,1)S(1)} collective-permute-done((bf16[1152,128]{1,0:T(8,128)(2,1)S(1)}, bf16[1152,128]{1,0:T(8,128)(2,1)S(1)}, u32[]{:S(2)}, u32[]{:S(2)}) %collective-permute-start.45) | collective-permute-done | bytes 294944 | tf_op jit(solution)/shard_map/ppermute | solution.py:63
  97.7 1.1 collective-permute-start.46
  98.9 1.4 collective-permute-start.23
  100.3 3.0 %collective-permute-done.46 = bf16[576,128]{1,0:T(8,128)(2,1)S(1)} collective-permute-done((bf16[576,128]{1,0:T(8,128)(2,1)S(1)}, bf16[576,128]{1,0:T(8,128)(2,1)S(1)}, u32[]{:S(2)}, u32[]{:S(2)}) %collective-permute-start.46) | collective-permute-done | bytes 147488 | tf_op jit(solution)/shard_map/ppermute | solution.py:63
  103.4 1.8 %collective-permute-start.24 = (bf16[144,128]{1,0:T(8,128)(2,1)S(1)}, bf16[144,128]{1,0:T(8,128)(2,1)S(1)}, u32[]{:S(2)}, u32[]{:S(2)}) collective-permute-start(bf16[144,128]{1,0:T(8,128)(2,1)S(1)} %select_convert_fusion.5), channel_id=1, source_target_pairs={{0,16},{1,17},{2,18},{3,19},{4,20},{5,21},{6,22},{7,23},{8,24},{9,... | collective-permute-start | bytes 110600 | tf_op jit(solution)/shard_map/ppermute | solution.py:63
  105.2 1.4 collective-permute-start.47
  106.5 1.9 %collective-permute-done.24 = bf16[144,128]{1,0:T(8,128)(2,1)S(1)} collective-permute-done((bf16[144,128]{1,0:T(8,128)(2,1)S(1)}, bf16[144,128]{1,0:T(8,128)(2,1)S(1)}, u32[]{:S(2)}, u32[]{:S(2)}) %collective-permute-start.24) | collective-permute-done | bytes 36896 | tf_op jit(solution)/shard_map/ppermute | solution.py:63
  108.4 1.8 %collective-permute-start.25 = (bf16[144,128]{1,0:T(8,128)(2,1)S(1)}, bf16[144,128]{1,0:T(8,128)(2,1)S(1)}, u32[]{:S(2)}, u32[]{:S(2)}) collective-permute-start(bf16[144,128]{1,0:T(8,128)(2,1)S(1)} %add_convert_fusion.1), channel_id=1, source_target_pairs={{0,16},{1,17},{2,18},{3,19},{4,20},{5,21},{6,22},{7,23},{8,24},{9,... | collective-permute-start | bytes 110600 | tf_op jit(solution)/shard_map/ppermute | solution.py:63
  110.3 1.3 collective-permute-start.48
  111.5 2.2 %collective-permute-done.25 = bf16[144,128]{1,0:T(8,128)(2,1)S(1)} collective-permute-done((bf16[144,128]{1,0:T(8,128)(2,1)S(1)}, bf16[144,128]{1,0:T(8,128)(2,1)S(1)}, u32[]{:S(2)}, u32[]{:S(2)}) %collective-permute-start.25) | collective-permute-done | bytes 36896 | tf_op jit(solution)/shard_map/ppermute | solution.py:63
  113.8 1.4 collective-permute-done.48
  115.2 1.4 collective-permute-start.49
  116.6 2.8 %collective-permute-start.26 = (bf16[288,128]{1,0:T(8,128)(2,1)S(1)}, bf16[288,128]{1,0:T(8,128)(2,1)S(1)}, u32[]{:S(2)}, u32[]{:S(2)}) collective-permute-start(bf16[288,128]{1,0:T(8,128)(2,1)S(1)} %pad_maximum_fusion.15), channel_id=1, source_target_pairs={{0,8},{1,3},{2,10},{3,1},{4,12},{5,7},{6,14},{7,5},{8,0},{9,11},{1... | collective-permute-start | bytes 221192 | tf_op jit(solution)/shard_map/ppermute | solution.py:63
  120.3 1.5 %collective-permute-start.50 = (bf16[288,128]{1,0:T(8,128)(2,1)S(1)}, bf16[288,128]{1,0:T(8,128)(2,1)S(1)}, u32[]{:S(2)}, u32[]{:S(2)}) collective-permute-start(bf16[288,128]{1,0:T(8,128)(2,1)S(1)} %pad_maximum_fusion.16), channel_id=1, source_target_pairs={{0,4},{1,9},{2,6},{3,11},{4,0},{5,13},{6,2},{7,15},{8,12},{9,1},{1... | collective-permute-start | bytes 221192 | tf_op jit(solution)/shard_map/ppermute | solution.py:63
  123.4 1.3 collective-permute-done.50
  124.7 1.1 collective-permute-start.51
  125.9 3.4 %collective-permute-done.27 = bf16[576,128]{1,0:T(8,128)(2,1)S(1)} collective-permute-done((bf16[576,128]{1,0:T(8,128)(2,1)S(1)}, bf16[576,128]{1,0:T(8,128)(2,1)S(1)}, u32[]{:S(2)}, u32[]{:S(2)}) %collective-permute-start.27) | collective-permute-done | bytes 147488 | tf_op jit(solution)/shard_map/ppermute | solution.py:63
  130.0 3.9 %collective-permute-start.52 = (bf16[1152,128]{1,0:T(8,128)(2,1)S(1)}, bf16[1152,128]{1,0:T(8,128)(2,1)S(1)}, u32[]{:S(2)}, u32[]{:S(2)}) collective-permute-start(bf16[1152,128]{1,0:T(8,128)(2,1)S(1)} %pad_maximum_fusion.5.refs_4_), channel_id=1, source_target_pairs={{0,8},{1,5},{2,10},{3,7},{4,12},{5,1},{6,14},{7,3},{8,0},{9,13},{1... | collective-permute-start | bytes 884744 | tf_op jit(solution)/shard_map/ppermute | solution.py:63
  134.5 1.7 %collective-permute-done.28.refs_1_ = bf16[1152,128]{1,0:T(8,128)(2,1)S(1)} collective-permute-done((bf16[1152,128]{1,0:T(8,128)(2,1)S(1)}, bf16[1152,128]{1,0:T(8,128)(2,1)S(1)}, u32[]{:S(2)}, u32[]{:S(2)}) %collective-permute-start.28) | collective-permute-done | bytes 294944 | tf_op jit(solution)/shard_map/ppermute | solution.py:63
  136.2 2.5 %collective-permute-done.52.refs_5_ = bf16[1152,128]{1,0:T(8,128)(2,1)S(1)} collective-permute-done((bf16[1152,128]{1,0:T(8,128)(2,1)S(1)}, bf16[1152,128]{1,0:T(8,128)(2,1)S(1)}, u32[]{:S(2)}, u32[]{:S(2)}) %collective-permute-start.52) | collective-permute-done | bytes 294944 | tf_op jit(solution)/shard_map/ppermute | solution.py:63
  138.7 1.6 %collective-permute-done.54.refs_7_ = bf16[1152,128]{1,0:T(8,128)(2,1)S(1)} collective-permute-done((bf16[1152,128]{1,0:T(8,128)(2,1)S(1)}, bf16[1152,128]{1,0:T(8,128)(2,1)S(1)}, u32[]{:S(2)}, u32[]{:S(2)}) %collective-permute-start.54) | collective-permute-done | bytes 294944 | tf_op jit(solution)/shard_map/ppermute | solution.py:63
  140.2 5.6 %shard_map.148 = (bf16[4608,256]{1,0:T(8,128)(2,1)}, f32[1,256]{1,0:T(1,128)}, bf16[256,4608]{1,0:T(8,128)(2,1)}) custom-call(bf16[1152,128]{1,0:T(8,128)(2,1)S(1)} %pad_maximum_fusion.4.refs_0_, bf16[1152,128]{1,0:T(8,128)(2,1)S(1)} %collective-permute-done.28.refs_1_, bf16[1152,128]{1,0:T(8,128)(2,1)S(1)} %collective-permute-done.29.refs_2_, ...), custom_call_target="tpu_custom_call" | custom-call | flops 1811939328 | bytes 14155776 | tf_op jit(solution)/shard_map/pallas_call | solution.py:513
  (136 shorter events, 16.6 us)
Async XLA Ops:
  0.6 0.9 copy-start.3
  1.6 0.7 copy-start.7
  4.3 16.4 %copy-start.4 = (bf16[256,288]{0,1:T(8,128)(2,1)S(1)}, bf16[256,288]{0,1:T(8,128)(2,1)}, u32[]{:S(2)}) copy-start(bf16[256,288]{0,1:T(8,128)(2,1)} %param.11) | copy-start | bytes 442372
  4.3 16.4 %collective-permute-start.13 = (bf16[144,256]{1,0:T(8,128)(2,1)S(1)}, bf16[144,256]{1,0:T(8,128)(2,1)S(1)}, u32[]{:S(2)}, u32[]{:S(2)}) collective-permute-start(bf16[144,256]{1,0:T(8,128)(2,1)S(1)} %slice_select_fusion), channel_id=1, source_target_pairs={{0,16},{1,17},{2,18},{3,19},{4,20},{5,21},{6,22},{7,23},{8,24},{9,... | collective-permute-start | bytes 221192 | tf_op jit(solution)/shard_map/ppermute | solution.py:63
  8.4 6.4 %collective-permute-start = (bf16[1040,128]{1,0:T(8,128)(2,1)S(1)}, bf16[1040,128]{1,0:T(8,128)(2,1)S(1)}, u32[]{:S(2)}, u32[]{:S(2)}) collective-permute-start(bf16[1040,128]{1,0:T(8,128)(2,1)S(1)} %get-tuple-element.64), channel_id=1, source_target_pairs={{0,2},{1,5},{2,0},{3,7},{4,6},{5,1},{6,4},{7,3},{8,10},{9,13},{10,... | collective-permute-start | bytes 798728 | tf_op jit(solution)/shard_map/ppermute | solution.py:63
  9.9 9.1 %collective-permute-start.31 = (bf16[1040,128]{1,0:T(8,128)(2,1)S(1)}, bf16[1040,128]{1,0:T(8,128)(2,1)S(1)}, u32[]{:S(2)}, u32[]{:S(2)}) collective-permute-start(bf16[1040,128]{1,0:T(8,128)(2,1)S(1)} %get-tuple-element.85), channel_id=1, source_target_pairs={{0,2},{1,5},{2,0},{3,7},{4,6},{5,1},{6,4},{7,3},{8,10},{9,13},{10,... | collective-permute-start | bytes 798728 | tf_op jit(solution)/shard_map/ppermute | solution.py:63
  10.4 70.3 %collective-permute-start.20 = (bf16[256,4608]{1,0:T(8,128)(2,1)}, bf16[256,4608]{1,0:T(8,128)(2,1)}, u32[]{:S(2)}, u32[]{:S(2)}) collective-permute-start(bf16[256,4608]{1,0:T(8,128)(2,1)} %refs_16_.1), channel_id=1, source_target_pairs={{0,1},{1,0},{2,3},{3,2},{4,5},{5,4},{6,7},{7,6},{8,9},{9,8},{10,11... | collective-permute-start | bytes 7077896 | tf_op jit(solution)/shard_map/ppermute | solution.py:63
  14.9 7.5 %collective-permute-start.1 = (bf16[528,128]{1,0:T(8,128)(2,1)S(1)}, bf16[528,128]{1,0:T(8,128)(2,1)S(1)}, u32[]{:S(2)}, u32[]{:S(2)}) collective-permute-start(bf16[528,128]{1,0:T(8,128)(2,1)S(1)} %get-tuple-element.67), channel_id=1, source_target_pairs={{0,4},{1,3},{2,6},{3,1},{4,0},{5,7},{6,2},{7,5},{8,12},{9,11},{10,... | collective-permute-start | bytes 405512 | tf_op jit(solution)/shard_map/ppermute | solution.py:63
  19.1 5.1 %collective-permute-start.32 = (bf16[528,128]{1,0:T(8,128)(2,1)S(1)}, bf16[528,128]{1,0:T(8,128)(2,1)S(1)}, u32[]{:S(2)}, u32[]{:S(2)}) collective-permute-start(bf16[528,128]{1,0:T(8,128)(2,1)S(1)} %get-tuple-element.88), channel_id=1, source_target_pairs={{0,4},{1,3},{2,6},{3,1},{4,0},{5,7},{6,2},{7,5},{8,12},{9,11},{10,... | collective-permute-start | bytes 405512 | tf_op jit(solution)/shard_map/ppermute | solution.py:63
  20.7 12.0 %collective-permute-start.14 = (bf16[288,256]{1,0:T(8,128)(2,1)S(1)}, bf16[288,256]{1,0:T(8,128)(2,1)S(1)}, u32[]{:S(2)}, u32[]{:S(2)}) collective-permute-start(bf16[288,256]{1,0:T(8,128)(2,1)S(1)} %pad_maximum_fusion.8), channel_id=1, source_target_pairs={{0,8},{1,3},{2,10},{3,1},{4,12},{5,7},{6,14},{7,5},{8,0},{9,11},{1... | collective-permute-start | bytes 442376 | tf_op jit(solution)/shard_map/ppermute | solution.py:63
  22.4 24.9 %copy-start.2 = (bf16[1024,288]{0,1:T(8,128)(2,1)S(1)}, bf16[1024,288]{0,1:T(8,128)(2,1)}, u32[]{:S(2)}) copy-start(bf16[1024,288]{0,1:T(8,128)(2,1)} %param.16) | copy-start | bytes 1769476
  22.4 7.2 %collective-permute-start.2 = (bf16[528,128]{1,0:T(8,128)(2,1)S(1)}, bf16[528,128]{1,0:T(8,128)(2,1)S(1)}, u32[]{:S(2)}, u32[]{:S(2)}) collective-permute-start(bf16[528,128]{1,0:T(8,128)(2,1)S(1)} %get-tuple-element.70), channel_id=1, source_target_pairs={{0,8},{1,9},{2,10},{3,11},{4,12},{5,13},{6,14},{7,15},{8,0},{9,1},... | collective-permute-start | bytes 405512 | tf_op jit(solution)/shard_map/ppermute | solution.py:63
  24.2 7.1 %collective-permute-start.33 = (bf16[528,128]{1,0:T(8,128)(2,1)S(1)}, bf16[528,128]{1,0:T(8,128)(2,1)S(1)}, u32[]{:S(2)}, u32[]{:S(2)}) collective-permute-start(bf16[528,128]{1,0:T(8,128)(2,1)S(1)} %get-tuple-element.91), channel_id=1, source_target_pairs={{0,8},{1,9},{2,10},{3,11},{4,12},{5,13},{6,14},{7,15},{8,0},{9,1},... | collective-permute-start | bytes 405512 | tf_op jit(solution)/shard_map/ppermute | solution.py:63
  29.7 6.1 %collective-permute-start.3 = (bf16[528,128]{1,0:T(8,128)(2,1)S(1)}, bf16[528,128]{1,0:T(8,128)(2,1)S(1)}, u32[]{:S(2)}, u32[]{:S(2)}) collective-permute-start(bf16[528,128]{1,0:T(8,128)(2,1)S(1)} %get-tuple-element.73), channel_id=1, source_target_pairs={{0,16},{1,17},{2,18},{3,19},{4,20},{5,21},{6,22},{7,23},{8,24},{9,... | collective-permute-start | bytes 405512 | tf_op jit(solution)/shard_map/ppermute | solution.py:63
  31.4 7.2 %collective-permute-start.34 = (bf16[528,128]{1,0:T(8,128)(2,1)S(1)}, bf16[528,128]{1,0:T(8,128)(2,1)S(1)}, u32[]{:S(2)}, u32[]{:S(2)}) collective-permute-start(bf16[528,128]{1,0:T(8,128)(2,1)S(1)} %get-tuple-element.94), channel_id=1, source_target_pairs={{0,16},{1,17},{2,18},{3,19},{4,20},{5,21},{6,22},{7,23},{8,24},{9,... | collective-permute-start | bytes 405512 | tf_op jit(solution)/shard_map/ppermute | solution.py:63
  36.2 4.9 %collective-permute-start.4 = (bf16[256,128]{1,0:T(8,128)(2,1)S(1)}, bf16[256,128]{1,0:T(8,128)(2,1)S(1)}, u32[]{:S(2)}, u32[]{:S(2)}) collective-permute-start(bf16[256,128]{1,0:T(8,128)(2,1)S(1)} %get-tuple-element.75), channel_id=1, source_target_pairs={{0,4},{1,3},{2,6},{3,1},{4,0},{5,7},{6,2},{7,5},{8,12},{9,11},{10,... | collective-permute-start | bytes 196616 | tf_op jit(solution)/shard_map/ppermute | solution.py:63
  38.0 13.3 %copy-start.5 = (f32[288]{0:T(512)S(1)}, f32[288]{0:T(512)}, u32[]{:S(2)}) copy-start(f32[288]{0:T(512)} %gain_ref.5) | copy-start | bytes 3460
  38.0 9.8 %collective-permute-start.15 = (bf16[576,256]{1,0:T(8,128)(2,1)S(1)}, bf16[576,256]{1,0:T(8,128)(2,1)S(1)}, u32[]{:S(2)}, u32[]{:S(2)}) collective-permute-start(bf16[576,256]{1,0:T(8,128)(2,1)S(1)} %pad_maximum_fusion.3), channel_id=1, source_target_pairs={{0,4},{1,9},{2,6},{3,11},{4,0},{5,13},{6,2},{7,15},{8,12},{9,1},{1... | collective-permute-start | bytes 884744 | tf_op jit(solution)/shard_map/ppermute | solution.py:63
  39.4 6.3 %collective-permute-start.35 = (bf16[256,128]{1,0:T(8,128)(2,1)S(1)}, bf16[256,128]{1,0:T(8,128)(2,1)S(1)}, u32[]{:S(2)}, u32[]{:S(2)}) collective-permute-start(bf16[256,128]{1,0:T(8,128)(2,1)S(1)} %get-tuple-element.98), channel_id=1, source_target_pairs={{0,4},{1,3},{2,6},{3,1},{4,0},{5,7},{6,2},{7,5},{8,12},{9,11},{10,... | collective-permute-start | bytes 196616 | tf_op jit(solution)/shard_map/ppermute | solution.py:63
  41.1 6.2 %collective-permute-start.5 = (bf16[512,128]{1,0:T(8,128)(2,1)S(1)}, bf16[512,128]{1,0:T(8,128)(2,1)S(1)}, u32[]{:S(2)}, u32[]{:S(2)}) collective-permute-start(bf16[512,128]{1,0:T(8,128)(2,1)S(1)} %pad_maximum_fusion.11.own_ref), channel_id=1, source_target_pairs={{0,2},{1,5},{2,0},{3,7},{4,6},{5,1},{6,4},{7,3},{8,10},{9,13},{10,... | collective-permute-start | bytes 393224 | tf_op jit(solution)/shard_map/ppermute | solution.py:63
  45.8 5.0 %collective-permute-start.36 = (bf16[512,128]{1,0:T(8,128)(2,1)S(1)}, bf16[512,128]{1,0:T(8,128)(2,1)S(1)}, u32[]{:S(2)}, u32[]{:S(2)}) collective-permute-start(bf16[512,128]{1,0:T(8,128)(2,1)S(1)} %pad_maximum_fusion.12.own_ref), channel_id=1, source_target_pairs={{0,2},{1,5},{2,0},{3,7},{4,6},{5,1},{6,4},{7,3},{8,10},{9,13},{10,... | collective-permute-start | bytes 393224 | tf_op jit(solution)/shard_map/ppermute | solution.py:63
  47.7 3.6 %collective-permute-start.6 = (f32[144,128]{1,0:T(8,128)S(1)}, f32[144,128]{1,0:T(8,128)S(1)}, u32[]{:S(2)}, u32[]{:S(2)}) collective-permute-start(f32[144,128]{1,0:T(8,128)S(1)} %get-tuple-element.77), channel_id=1, source_target_pairs={{0,1},{1,0},{2,3},{3,2},{4,5},{5,4},{6,7},{7,6},{8,9},{9,8},{10,11... | collective-permute-start | bytes 221192 | tf_op jit(solution)/shard_map/ppermute | solution.py:63
  51.1 3.3 %collective-permute-start.37 = (f32[144,128]{1,0:T(8,128)S(1)}, f32[144,128]{1,0:T(8,128)S(1)}, u32[]{:S(2)}, u32[]{:S(2)}) collective-permute-start(f32[144,128]{1,0:T(8,128)S(1)} %get-tuple-element.100), channel_id=1, source_target_pairs={{0,1},{1,0},{2,3},{3,2},{4,5},{5,4},{6,7},{7,6},{8,9},{9,8},{10,11... | collective-permute-start | bytes 221192 | tf_op jit(solution)/shard_map/ppermute | solution.py:63
  51.4 5.0 %collective-permute-start.7 = (bf16[160,128]{1,0:T(8,128)(2,1)S(1)}, bf16[160,128]{1,0:T(8,128)(2,1)S(1)}, u32[]{:S(2)}, u32[]{:S(2)}) collective-permute-start(bf16[160,128]{1,0:T(8,128)(2,1)S(1)} %shard_map.136), channel_id=1, source_target_pairs={{0,16},{1,17},{2,18},{3,19},{4,20},{5,21},{6,22},{7,23},{8,24},{9,... | collective-permute-start | bytes 122888 | tf_op jit(solution)/shard_map/ppermute | solution.py:63
  52.1 17.7 %collective-permute-start.17 = (bf16[1152,256]{1,0:T(8,128)(2,1)S(1)}, bf16[1152,256]{1,0:T(8,128)(2,1)S(1)}, u32[]{:S(2)}, u32[]{:S(2)}) collective-permute-start(bf16[1152,256]{1,0:T(8,128)(2,1)S(1)} %pad_maximum_fusion.refs_0_), channel_id=1, source_target_pairs={{0,1},{1,0},{2,3},{3,2},{4,5},{5,4},{6,7},{7,6},{8,9},{9,8},{10,11... | collective-permute-start | bytes 1769480 | tf_op jit(solution)/shard_map/ppermute | solution.py:63
  52.4 13.0 %collective-permute-start.16 = (bf16[1152,256]{1,0:T(8,128)(2,1)S(1)}, bf16[1152,256]{1,0:T(8,128)(2,1)S(1)}, u32[]{:S(2)}, u32[]{:S(2)}) collective-permute-start(bf16[1152,256]{1,0:T(8,128)(2,1)S(1)} %pad_maximum_fusion.refs_0_), channel_id=1, source_target_pairs={{0,2},{1,5},{2,0},{3,7},{4,6},{5,1},{6,4},{7,3},{8,10},{9,13},{10,... | collective-permute-start | bytes 1769480 | tf_op jit(solution)/shard_map/ppermute | solution.py:63
  54.5 5.2 %collective-permute-start.38 = (bf16[160,128]{1,0:T(8,128)(2,1)S(1)}, bf16[160,128]{1,0:T(8,128)(2,1)S(1)}, u32[]{:S(2)}, u32[]{:S(2)}) collective-permute-start(bf16[160,128]{1,0:T(8,128)(2,1)S(1)} %shard_map.145), channel_id=1, source_target_pairs={{0,16},{1,17},{2,18},{3,19},{4,20},{5,21},{6,22},{7,23},{8,24},{9,... | collective-permute-start | bytes 122888 | tf_op jit(solution)/shard_map/ppermute | solution.py:63
  56.4 5.1 %collective-permute-start.8 = (bf16[320,128]{1,0:T(8,128)(2,1)S(1)}, bf16[320,128]{1,0:T(8,128)(2,1)S(1)}, u32[]{:S(2)}, u32[]{:S(2)}) collective-permute-start(bf16[320,128]{1,0:T(8,128)(2,1)S(1)} %pad_maximum_fusion.13), channel_id=1, source_target_pairs={{0,8},{1,3},{2,10},{3,1},{4,12},{5,7},{6,14},{7,5},{8,0},{9,11},{1... | collective-permute-start | bytes 245768 | tf_op jit(solution)/shard_map/ppermute | solution.py:63
  59.8 4.5 %collective-permute-start.39 = (bf16[320,128]{1,0:T(8,128)(2,1)S(1)}, bf16[320,128]{1,0:T(8,128)(2,1)S(1)}, u32[]{:S(2)}, u32[]{:S(2)}) collective-permute-start(bf16[320,128]{1,0:T(8,128)(2,1)S(1)} %pad_maximum_fusion.14), channel_id=1, source_target_pairs={{0,4},{1,9},{2,6},{3,11},{4,0},{5,13},{6,2},{7,15},{8,12},{9,1},{1... | collective-permute-start | bytes 245768 | tf_op jit(solution)/shard_map/ppermute | solution.py:63
  61.5 5.4 %collective-permute-start.9 = (bf16[640,128]{1,0:T(8,128)(2,1)S(1)}, bf16[640,128]{1,0:T(8,128)(2,1)S(1)}, u32[]{:S(2)}, u32[]{:S(2)}) collective-permute-start(bf16[640,128]{1,0:T(8,128)(2,1)S(1)} %pad_maximum_fusion.6), channel_id=1, source_target_pairs={{0,4},{1,9},{2,6},{3,11},{4,0},{5,13},{6,2},{7,15},{8,12},{9,1},{1... | collective-permute-start | bytes 491528 | tf_op jit(solution)/shard_map/ppermute | solution.py:63
  64.3 13.1 %copy-start.1 = (bf16[4608,256]{1,0:T(8,128)(2,1)S(1)}, bf16[4608,256]{1,0:T(8,128)(2,1)}, u32[]{:S(2)}) copy-start(bf16[4608,256]{1,0:T(8,128)(2,1)} %refs_5_.3) | copy-start | bytes 7077892
  64.4 13.0 %copy-start.6 = (f32[256]{0:T(256)S(1)}, f32[256]{0:T(256)}, u32[]{:S(2)}) copy-start(f32[256]{0:T(256)} %refs_6_.3) | copy-start | bytes 3076
  64.4 5.4 %collective-permute-start.40 = (bf16[640,128]{1,0:T(8,128)(2,1)S(1)}, bf16[640,128]{1,0:T(8,128)(2,1)S(1)}, u32[]{:S(2)}, u32[]{:S(2)}) collective-permute-start(bf16[640,128]{1,0:T(8,128)(2,1)S(1)} %pad_maximum_fusion.7), channel_id=1, source_target_pairs={{0,2},{1,3},{2,0},{3,1},{4,6},{5,7},{6,4},{7,5},{8,10},{9,11},{10,... | collective-permute-start | bytes 491528 | tf_op jit(solution)/shard_map/ppermute | solution.py:63
  65.4 4.5 %collective-permute-start.18 = (bf16[1152,256]{1,0:T(8,128)(2,1)S(1)}, bf16[1152,256]{1,0:T(8,128)(2,1)S(1)}, u32[]{:S(2)}, u32[]{:S(2)}) collective-permute-start(bf16[1152,256]{1,0:T(8,128)(2,1)S(1)} %collective-permute-done.16.refs_1_), channel_id=1, source_target_pairs={{0,1},{1,0},{2,3},{3,2},{4,5},{5,4},{6,7},{7,6},{8,9},{9,8},{10,11... | collective-permute-start | bytes 1769480 | tf_op jit(solution)/shard_map/ppermute | solution.py:63
  67.0 7.1 %collective-permute-start.10 = (bf16[1280,128]{1,0:T(8,128)(2,1)S(1)}, bf16[1280,128]{1,0:T(8,128)(2,1)S(1)}, u32[]{:S(2)}, u32[]{:S(2)}) collective-permute-start(bf16[1280,128]{1,0:T(8,128)(2,1)S(1)} %pad_maximum_fusion.1.refs_0_), channel_id=1, source_target_pairs={{0,2},{1,5},{2,0},{3,7},{4,6},{5,1},{6,4},{7,3},{8,10},{9,13},{10,... | collective-permute-start | bytes 983048 | tf_op jit(solution)/shard_map/ppermute | solution.py:63
  70.2 10.5 %copy-start = (bf16[256,4608]{1,0:T(8,128)(2,1)S(1)}, bf16[256,4608]{1,0:T(8,128)(2,1)}, u32[]{:S(2)}) copy-start(bf16[256,4608]{1,0:T(8,128)(2,1)} %refs_16_.1) | copy-start | bytes 7077892
  70.2 7.1 %collective-permute-start.41 = (bf16[1280,128]{1,0:T(8,128)(2,1)S(1)}, bf16[1280,128]{1,0:T(8,128)(2,1)S(1)}, u32[]{:S(2)}, u32[]{:S(2)}) collective-permute-start(bf16[1280,128]{1,0:T(8,128)(2,1)S(1)} %pad_maximum_fusion.2.refs_0_), channel_id=1, source_target_pairs={{0,8},{1,5},{2,10},{3,7},{4,12},{5,1},{6,14},{7,3},{8,0},{9,13},{1... | collective-permute-start | bytes 983048 | tf_op jit(solution)/shard_map/ppermute | solution.py:63
  71.8 5.6 %collective-permute-start.11 = (bf16[1280,128]{1,0:T(8,128)(2,1)S(1)}, bf16[1280,128]{1,0:T(8,128)(2,1)S(1)}, u32[]{:S(2)}, u32[]{:S(2)}) collective-permute-start(bf16[1280,128]{1,0:T(8,128)(2,1)S(1)} %pad_maximum_fusion.1.refs_0_), channel_id=1, source_target_pairs={{0,1},{1,0},{2,3},{3,2},{4,5},{5,4},{6,7},{7,6},{8,9},{9,8},{10,11... | collective-permute-start | bytes 983048 | tf_op jit(solution)/shard_map/ppermute | solution.py:63
  74.1 3.2 %collective-permute-start.12 = (bf16[1280,128]{1,0:T(8,128)(2,1)S(1)}, bf16[1280,128]{1,0:T(8,128)(2,1)S(1)}, u32[]{:S(2)}, u32[]{:S(2)}) collective-permute-start(bf16[1280,128]{1,0:T(8,128)(2,1)S(1)} %collective-permute-done.10.refs_1_), channel_id=1, source_target_pairs={{0,1},{1,0},{2,3},{3,2},{4,5},{5,4},{6,7},{7,6},{8,9},{9,8},{10,11... | collective-permute-start | bytes 983048 | tf_op jit(solution)/shard_map/ppermute | solution.py:63
  74.1 9.9 %collective-permute-start.42 = (bf16[1280,128]{1,0:T(8,128)(2,1)S(1)}, bf16[1280,128]{1,0:T(8,128)(2,1)S(1)}, u32[]{:S(2)}, u32[]{:S(2)}) collective-permute-start(bf16[1280,128]{1,0:T(8,128)(2,1)S(1)} %pad_maximum_fusion.2.refs_0_), channel_id=1, source_target_pairs={{0,1},{1,0},{2,3},{3,2},{4,5},{5,4},{6,7},{7,6},{8,9},{9,8},{10,11... | collective-permute-start | bytes 983048 | tf_op jit(solution)/shard_map/ppermute | solution.py:63
  77.4 6.7 %collective-permute-start.43 = (bf16[1280,128]{1,0:T(8,128)(2,1)S(1)}, bf16[1280,128]{1,0:T(8,128)(2,1)S(1)}, u32[]{:S(2)}, u32[]{:S(2)}) collective-permute-start(bf16[1280,128]{1,0:T(8,128)(2,1)S(1)} %collective-permute-done.41.refs_1_), channel_id=1, source_target_pairs={{0,1},{1,0},{2,3},{3,2},{4,5},{5,4},{6,7},{7,6},{8,9},{9,8},{10,11... | collective-permute-start | bytes 983048 | tf_op jit(solution)/shard_map/ppermute | solution.py:63
  79.2 1.5 %collective-permute-start.19 = (bf16[256,128]{1,0:T(8,128)(2,1)S(1)}, bf16[256,128]{1,0:T(8,128)(2,1)S(1)}, u32[]{:S(2)}, u32[]{:S(2)}) collective-permute-start(bf16[256,128]{1,0:T(8,128)(2,1)S(1)} %get-tuple-element.80.low_ref.refs_10_), channel_id=1, source_target_pairs={{0,1},{1,0},{2,3},{3,2},{4,5},{5,4},{6,7},{7,6},{8,9},{9,8},{10,11... | collective-permute-start | bytes 196616 | tf_op jit(solution)/shard_map/ppermute | solution.py:63
  83.0 7.6 %collective-permute-start.21 = (bf16[1152,128]{1,0:T(8,128)(2,1)S(1)}, bf16[1152,128]{1,0:T(8,128)(2,1)S(1)}, u32[]{:S(2)}, u32[]{:S(2)}) collective-permute-start(bf16[1152,128]{1,0:T(8,128)(2,1)S(1)} %get-tuple-element.82), channel_id=1, source_target_pairs={{0,2},{1,5},{2,0},{3,7},{4,6},{5,1},{6,4},{7,3},{8,10},{9,13},{10,... | collective-permute-start | bytes 884744 | tf_op jit(solution)/shard_map/ppermute | solution.py:63
  85.7 1.3 collective-permute-start.44
  89.3 8.4 %collective-permute-start.45 = (bf16[1152,128]{1,0:T(8,128)(2,1)S(1)}, bf16[1152,128]{1,0:T(8,128)(2,1)S(1)}, u32[]{:S(2)}, u32[]{:S(2)}) collective-permute-start(bf16[1152,128]{1,0:T(8,128)(2,1)S(1)} %get-tuple-element.107), channel_id=1, source_target_pairs={{0,8},{1,5},{2,10},{3,7},{4,12},{5,1},{6,14},{7,3},{8,0},{9,13},{1... | collective-permute-start | bytes 884744 | tf_op jit(solution)/shard_map/ppermute | solution.py:63
  90.7 8.2 %collective-permute-start.22 = (bf16[576,128]{1,0:T(8,128)(2,1)S(1)}, bf16[576,128]{1,0:T(8,128)(2,1)S(1)}, u32[]{:S(2)}, u32[]{:S(2)}) collective-permute-start(bf16[576,128]{1,0:T(8,128)(2,1)S(1)} %select_convert_fusion.1), channel_id=1, source_target_pairs={{0,4},{1,9},{2,6},{3,11},{4,0},{5,13},{6,2},{7,15},{8,12},{9,1},{1... | collective-permute-start | bytes 442376 | tf_op jit(solution)/shard_map/ppermute | solution.py:63
  97.7 5.5 %collective-permute-start.46 = (bf16[576,128]{1,0:T(8,128)(2,1)S(1)}, bf16[576,128]{1,0:T(8,128)(2,1)S(1)}, u32[]{:S(2)}, u32[]{:S(2)}) collective-permute-start(bf16[576,128]{1,0:T(8,128)(2,1)S(1)} %select_convert_fusion), channel_id=1, source_target_pairs={{0,2},{1,3},{2,0},{3,1},{4,6},{5,7},{6,4},{7,5},{8,10},{9,11},{10,... | collective-permute-start | bytes 442376 | tf_op jit(solution)/shard_map/ppermute | solution.py:63
  98.9 4.4 %collective-permute-start.23 = (bf16[288,128]{1,0:T(8,128)(2,1)S(1)}, bf16[288,128]{1,0:T(8,128)(2,1)S(1)}, u32[]{:S(2)}, u32[]{:S(2)}) collective-permute-start(bf16[288,128]{1,0:T(8,128)(2,1)S(1)} %select_convert_fusion.3), channel_id=1, source_target_pairs={{0,8},{1,3},{2,10},{3,1},{4,12},{5,7},{6,14},{7,5},{8,0},{9,11},{1... | collective-permute-start | bytes 221192 | tf_op jit(solution)/shard_map/ppermute | solution.py:63
  103.4 5.0 %collective-permute-start.24 = (bf16[144,128]{1,0:T(8,128)(2,1)S(1)}, bf16[144,128]{1,0:T(8,128)(2,1)S(1)}, u32[]{:S(2)}, u32[]{:S(2)}) collective-permute-start(bf16[144,128]{1,0:T(8,128)(2,1)S(1)} %select_convert_fusion.5), channel_id=1, source_target_pairs={{0,16},{1,17},{2,18},{3,19},{4,20},{5,21},{6,22},{7,23},{8,24},{9,... | collective-permute-start | bytes 110600 | tf_op jit(solution)/shard_map/ppermute | solution.py:63
  105.2 5.0 %collective-permute-start.47 = (bf16[288,128]{1,0:T(8,128)(2,1)S(1)}, bf16[288,128]{1,0:T(8,128)(2,1)S(1)}, u32[]{:S(2)}, u32[]{:S(2)}) collective-permute-start(bf16[288,128]{1,0:T(8,128)(2,1)S(1)} %select_convert_fusion.2), channel_id=1, source_target_pairs={{0,4},{1,9},{2,6},{3,11},{4,0},{5,13},{6,2},{7,15},{8,12},{9,1},{1... | collective-permute-start | bytes 221192 | tf_op jit(solution)/shard_map/ppermute | solution.py:63
  108.4 5.3 %collective-permute-start.25 = (bf16[144,128]{1,0:T(8,128)(2,1)S(1)}, bf16[144,128]{1,0:T(8,128)(2,1)S(1)}, u32[]{:S(2)}, u32[]{:S(2)}) collective-permute-start(bf16[144,128]{1,0:T(8,128)(2,1)S(1)} %add_convert_fusion.1), channel_id=1, source_target_pairs={{0,16},{1,17},{2,18},{3,19},{4,20},{5,21},{6,22},{7,23},{8,24},{9,... | collective-permute-start | bytes 110600 | tf_op jit(solution)/shard_map/ppermute | solution.py:63
  110.3 4.9 %collective-permute-start.48 = (bf16[144,128]{1,0:T(8,128)(2,1)S(1)}, bf16[144,128]{1,0:T(8,128)(2,1)S(1)}, u32[]{:S(2)}, u32[]{:S(2)}) collective-permute-start(bf16[144,128]{1,0:T(8,128)(2,1)S(1)} %select_convert_fusion.4), channel_id=1, source_target_pairs={{0,16},{1,17},{2,18},{3,19},{4,20},{5,21},{6,22},{7,23},{8,24},{9,... | collective-permute-start | bytes 110600 | tf_op jit(solution)/shard_map/ppermute | solution.py:63
  115.2 5.0 %collective-permute-start.49 = (bf16[144,128]{1,0:T(8,128)(2,1)S(1)}, bf16[144,128]{1,0:T(8,128)(2,1)S(1)}, u32[]{:S(2)}, u32[]{:S(2)}) collective-permute-start(bf16[144,128]{1,0:T(8,128)(2,1)S(1)} %add_convert_fusion), channel_id=1, source_target_pairs={{0,16},{1,17},{2,18},{3,19},{4,20},{5,21},{6,22},{7,23},{8,24},{9,... | collective-permute-start | bytes 110600 | tf_op jit(solution)/shard_map/ppermute | solution.py:63
  116.6 5.9 %collective-permute-start.26 = (bf16[288,128]{1,0:T(8,128)(2,1)S(1)}, bf16[288,128]{1,0:T(8,128)(2,1)S(1)}, u32[]{:S(2)}, u32[]{:S(2)}) collective-permute-start(bf16[288,128]{1,0:T(8,128)(2,1)S(1)} %pad_maximum_fusion.15), channel_id=1, source_target_pairs={{0,8},{1,3},{2,10},{3,1},{4,12},{5,7},{6,14},{7,5},{8,0},{9,11},{1... | collective-permute-start | bytes 221192 | tf_op jit(solution)/shard_map/ppermute | solution.py:63
  120.3 4.4 %collective-permute-start.50 = (bf16[288,128]{1,0:T(8,128)(2,1)S(1)}, bf16[288,128]{1,0:T(8,128)(2,1)S(1)}, u32[]{:S(2)}, u32[]{:S(2)}) collective-permute-start(bf16[288,128]{1,0:T(8,128)(2,1)S(1)} %pad_maximum_fusion.16), channel_id=1, source_target_pairs={{0,4},{1,9},{2,6},{3,11},{4,0},{5,13},{6,2},{7,15},{8,12},{9,1},{1... | collective-permute-start | bytes 221192 | tf_op jit(solution)/shard_map/ppermute | solution.py:63
  122.6 6.7 %collective-permute-start.27 = (bf16[576,128]{1,0:T(8,128)(2,1)S(1)}, bf16[576,128]{1,0:T(8,128)(2,1)S(1)}, u32[]{:S(2)}, u32[]{:S(2)}) collective-permute-start(bf16[576,128]{1,0:T(8,128)(2,1)S(1)} %pad_maximum_fusion.9), channel_id=1, source_target_pairs={{0,4},{1,9},{2,6},{3,11},{4,0},{5,13},{6,2},{7,15},{8,12},{9,1},{1... | collective-permute-start | bytes 442376 | tf_op jit(solution)/shard_map/ppermute | solution.py:63
  124.7 5.2 %collective-permute-start.51 = (bf16[576,128]{1,0:T(8,128)(2,1)S(1)}, bf16[576,128]{1,0:T(8,128)(2,1)S(1)}, u32[]{:S(2)}, u32[]{:S(2)}) collective-permute-start(bf16[576,128]{1,0:T(8,128)(2,1)S(1)} %pad_maximum_fusion.10), channel_id=1, source_target_pairs={{0,2},{1,3},{2,0},{3,1},{4,6},{5,7},{6,4},{7,5},{8,10},{9,11},{10,... | collective-permute-start | bytes 442376 | tf_op jit(solution)/shard_map/ppermute | solution.py:63
  129.4 6.8 %collective-permute-start.28 = (bf16[1152,128]{1,0:T(8,128)(2,1)S(1)}, bf16[1152,128]{1,0:T(8,128)(2,1)S(1)}, u32[]{:S(2)}, u32[]{:S(2)}) collective-permute-start(bf16[1152,128]{1,0:T(8,128)(2,1)S(1)} %pad_maximum_fusion.4.refs_0_), channel_id=1, source_target_pairs={{0,2},{1,5},{2,0},{3,7},{4,6},{5,1},{6,4},{7,3},{8,10},{9,13},{10,... | collective-permute-start | bytes 884744 | tf_op jit(solution)/shard_map/ppermute | solution.py:63
  130.0 8.6 %collective-permute-start.52 = (bf16[1152,128]{1,0:T(8,128)(2,1)S(1)}, bf16[1152,128]{1,0:T(8,128)(2,1)S(1)}, u32[]{:S(2)}, u32[]{:S(2)}) collective-permute-start(bf16[1152,128]{1,0:T(8,128)(2,1)S(1)} %pad_maximum_fusion.5.refs_4_), channel_id=1, source_target_pairs={{0,8},{1,5},{2,10},{3,7},{4,12},{5,1},{6,14},{7,3},{8,0},{9,13},{1... | collective-permute-start | bytes 884744 | tf_op jit(solution)/shard_map/ppermute | solution.py:63
  133.9 4.7 %collective-permute-start.29 = (bf16[1152,128]{1,0:T(8,128)(2,1)S(1)}, bf16[1152,128]{1,0:T(8,128)(2,1)S(1)}, u32[]{:S(2)}, u32[]{:S(2)}) collective-permute-start(bf16[1152,128]{1,0:T(8,128)(2,1)S(1)} %pad_maximum_fusion.4.refs_0_), channel_id=1, source_target_pairs={{0,1},{1,0},{2,3},{3,2},{4,5},{5,4},{6,7},{7,6},{8,9},{9,8},{10,11... | collective-permute-start | bytes 884744 | tf_op jit(solution)/shard_map/ppermute | solution.py:63
  133.9 4.7 %collective-permute-start.53 = (bf16[1152,128]{1,0:T(8,128)(2,1)S(1)}, bf16[1152,128]{1,0:T(8,128)(2,1)S(1)}, u32[]{:S(2)}, u32[]{:S(2)}) collective-permute-start(bf16[1152,128]{1,0:T(8,128)(2,1)S(1)} %pad_maximum_fusion.5.refs_4_), channel_id=1, source_target_pairs={{0,1},{1,0},{2,3},{3,2},{4,5},{5,4},{6,7},{7,6},{8,9},{9,8},{10,11... | collective-permute-start | bytes 884744 | tf_op jit(solution)/shard_map/ppermute | solution.py:63
  136.2 2.5 %collective-permute-start.30 = (bf16[1152,128]{1,0:T(8,128)(2,1)S(1)}, bf16[1152,128]{1,0:T(8,128)(2,1)S(1)}, u32[]{:S(2)}, u32[]{:S(2)}) collective-permute-start(bf16[1152,128]{1,0:T(8,128)(2,1)S(1)} %collective-permute-done.28.refs_1_), channel_id=1, source_target_pairs={{0,1},{1,0},{2,3},{3,2},{4,5},{5,4},{6,7},{7,6},{8,9},{9,8},{10,11... | collective-permute-start | bytes 884744 | tf_op jit(solution)/shard_map/ppermute | solution.py:63
  138.6 1.6 %collective-permute-start.54 = (bf16[1152,128]{1,0:T(8,128)(2,1)S(1)}, bf16[1152,128]{1,0:T(8,128)(2,1)S(1)}, u32[]{:S(2)}, u32[]{:S(2)}) collective-permute-start(bf16[1152,128]{1,0:T(8,128)(2,1)S(1)} %collective-permute-done.52.refs_5_), channel_id=1, source_target_pairs={{0,1},{1,0},{2,3},{3,2},{4,5},{5,4},{6,7},{7,6},{8,9},{9,8},{10,11... | collective-permute-start | bytes 884744 | tf_op jit(solution)/shard_map/ppermute | solution.py:63

commit v6 on v5

--- a/solution.py
+++ b/solution.py
@@ -630,7 +630,8 @@
 
     sends[0], sends[1], later = lax.optimization_barrier((sends[0], sends[1], residual_t))
     mine = share(later)
-    steps = cores[1:] + routes[0]
+    spread = ladder.route((0, 1, 2), (1, 0, 2))
+    steps = cores[1:] + spread
     residual_own = ladder.gather(mine, steps[1:])
     residual_far = ladder.swap(residual_own, steps[0])
     old = ()
@@ -647,7 +648,7 @@
 
     residuals = (residual_own, residual_far, ladder.swap(residual_own, core), ladder.swap(residual_far, core))
     if paired:
-        residual_all = assemble(ladder, core, steps[0], ladder.order(cores + routes[0]), block, residuals)
+        residual_all = assemble(ladder, core, steps[0], ladder.order(cores + spread), block, residuals)
     else:
         residual_all = canonical(residuals, steps, block)
         residual_all = [residual_all[:, cut] for cut in cuts]

time: 146 us -> 146 us (level)
  starting transfers between devices: 62.6 us -> 59.2 us
  waiting for transfers between devices: 57.3 us -> 60.3 us
    ppermute x55, starting transfers between devices: 62.6 us -> 59.2 us  [swap(): return lax.ppermute(value, AXES, self.pairs(step))]
    ppermute x55, waiting for transfers between devices: 57.3 us -> 60.3 us  [swap(): return lax.ppermute(value, AXES, self.pairs(step))]
  transfers between devices with their start and end apart: 55 -> 55, of which waited for: 31 -> 30; matrix products, arithmetic and copies ran while one was open for 3% -> 3% of each run, Pallas kernels for 7% -> 7%
where the time goes in v6:
time: 146 us
  waiting for transfers between devices  60.3 us (41%)
  starting transfers between devices  59.2 us (41%)
  Pallas kernels  18.3 us (13%)
  other arithmetic  3.89 us (3%)
  local copies, waits for them, and re-layouts  2.47 us (2%)
    ppermute x55, waiting for transfers between devices, swap(): return lax.ppermute(value, AXES, self.pairs(step))  60.3 us
    ppermute x55, starting transfers between devices, swap(): return lax.ppermute(value, AXES, self.pairs(step))  59.2 us
    pallas_call x1, Pallas kernels, gradients(): pl.pallas_call(functools.partial(final_kernel, ladder, core, steps), out_...  5.64 us
    pallas_call x2, Pallas kernels, decode(): pl.pallas_call(functools.partial(decode_kernel, ladder, core, step), out_...  4.53 us
    pallas_call x2, Pallas kernels, encode(): pl.pallas_call(functools.partial(encode_kernel, ladder, core, steps, plac...  3.45 us
  transfers between devices with their start and end apart: 55, of which 30 were waited for; matrix products, arithmetic and copies ran while one was open for 3% of the time, Pallas kernels for 7%

profile of v6, /device:TPU:0, one launch (start us, length us, event | category | flops | bytes accessed | tf_op | source)
XLA Modules:
  0.0 145.7 jit_solution(14495502902937104588)
XLA Ops:
  0.6 0.9 copy-done.3
  2.2 2.0 %shard_map.130 = (bf16[1040,128]{1,0:T(8,128)(2,1)S(1)}, bf16[1040,128]{1,0:T(8,128)(2,1)S(1)}, f32[1024,128]{1,0:T(8,128)S(1)}, f32[1024,128]{1,0:T(8,128)S(1)}...) custom-call(bf16[288,256]{1,0:T(8,128)(2,1)S(1)} %bitcast.5, f32[288]{0:T(512)S(1)} %copy-done.7, bf16[288,1024]{1,0:T(8,128)(2,1)} %refs_0_.1, ...), custom_call_target="tpu_custom_call" | custom-call | flops 301989888 | bytes 1179648 | tf_op jit(solution)/shard_map/pallas_call | solution.py:187
  4.3 4.1 %collective-permute-start.13 = (bf16[144,256]{1,0:T(8,128)(2,1)S(1)}, bf16[144,256]{1,0:T(8,128)(2,1)S(1)}, u32[]{:S(2)}, u32[]{:S(2)}) collective-permute-start(bf16[144,256]{1,0:T(8,128)(2,1)S(1)} %slice_select_fusion), channel_id=1, source_target_pairs={{0,16},{1,17},{2,18},{3,19},{4,20},{5,21},{6,22},{7,23},{8,24},{9,... | collective-permute-start | bytes 221192 | tf_op jit(solution)/shard_map/ppermute | solution.py:63
  8.4 1.5 %collective-permute-start = (bf16[1040,128]{1,0:T(8,128)(2,1)S(1)}, bf16[1040,128]{1,0:T(8,128)(2,1)S(1)}, u32[]{:S(2)}, u32[]{:S(2)}) collective-permute-start(bf16[1040,128]{1,0:T(8,128)(2,1)S(1)} %get-tuple-element.64), channel_id=1, source_target_pairs={{0,2},{1,5},{2,0},{3,7},{4,6},{5,1},{6,4},{7,3},{8,10},{9,13},{10,... | collective-permute-start | bytes 798728 | tf_op jit(solution)/shard_map/ppermute | solution.py:63
  10.4 2.2 %multiply_reduce_fusion = f32[256]{0:T(256)S(1)} fusion(bf16[256,4608]{1,0:T(8,128)(2,1)} %refs_16_.1), kind=kLoop, calls=%fused_computation | loop fusion | flops 3538688 | bytes 2360320 | tf_op jit(solution)/shard_map/reduce_sum | solution.py:601
  13.0 1.8 %collective-permute-done.got_ref = bf16[1040,128]{1,0:T(8,128)(2,1)S(1)} collective-permute-done((bf16[1040,128]{1,0:T(8,128)(2,1)S(1)}, bf16[1040,128]{1,0:T(8,128)(2,1)S(1)}, u32[]{:S(2)}, u32[]{:S(2)}) %collective-permute-start) | collective-permute-done | bytes 266272 | tf_op jit(solution)/shard_map/ppermute | solution.py:63
  14.9 1.6 %collective-permute-start.1 = (bf16[528,128]{1,0:T(8,128)(2,1)S(1)}, bf16[528,128]{1,0:T(8,128)(2,1)S(1)}, u32[]{:S(2)}, u32[]{:S(2)}) collective-permute-start(bf16[528,128]{1,0:T(8,128)(2,1)S(1)} %get-tuple-element.67), channel_id=1, source_target_pairs={{0,4},{1,3},{2,6},{3,1},{4,0},{5,7},{6,2},{7,5},{8,12},{9,11},{10,... | collective-permute-start | bytes 405512 | tf_op jit(solution)/shard_map/ppermute | solution.py:63
  16.5 2.6 %collective-permute-done.31.got_ref = bf16[1040,128]{1,0:T(8,128)(2,1)S(1)} collective-permute-done((bf16[1040,128]{1,0:T(8,128)(2,1)S(1)}, bf16[1040,128]{1,0:T(8,128)(2,1)S(1)}, u32[]{:S(2)}, u32[]{:S(2)}) %collective-permute-start.31) | collective-permute-done | bytes 266272 | tf_op jit(solution)/shard_map/ppermute | solution.py:63
  19.1 1.6 %collective-permute-start.32 = (bf16[528,128]{1,0:T(8,128)(2,1)S(1)}, bf16[528,128]{1,0:T(8,128)(2,1)S(1)}, u32[]{:S(2)}, u32[]{:S(2)}) collective-permute-start(bf16[528,128]{1,0:T(8,128)(2,1)S(1)} %get-tuple-element.88), channel_id=1, source_target_pairs={{0,4},{1,3},{2,6},{3,1},{4,0},{5,7},{6,2},{7,5},{8,12},{9,11},{10,... | collective-permute-start | bytes 405512 | tf_op jit(solution)/shard_map/ppermute | solution.py:63
  20.7 1.6 %collective-permute-start.14 = (bf16[288,256]{1,0:T(8,128)(2,1)S(1)}, bf16[288,256]{1,0:T(8,128)(2,1)S(1)}, u32[]{:S(2)}, u32[]{:S(2)}) collective-permute-start(bf16[288,256]{1,0:T(8,128)(2,1)S(1)} %pad_maximum_fusion.8), channel_id=1, source_target_pairs={{0,8},{1,9},{2,10},{3,11},{4,12},{5,13},{6,14},{7,15},{8,0},{9,1},... | collective-permute-start | bytes 442376 | tf_op jit(solution)/shard_map/ppermute | solution.py:63
  22.9 1.2 collective-permute-done.32.got_ref
  24.2 1.6 %collective-permute-start.33 = (bf16[528,128]{1,0:T(8,128)(2,1)S(1)}, bf16[528,128]{1,0:T(8,128)(2,1)S(1)}, u32[]{:S(2)}, u32[]{:S(2)}) collective-permute-start(bf16[528,128]{1,0:T(8,128)(2,1)S(1)} %get-tuple-element.91), channel_id=1, source_target_pairs={{0,8},{1,9},{2,10},{3,11},{4,12},{5,13},{6,14},{7,15},{8,0},{9,1},... | collective-permute-start | bytes 405512 | tf_op jit(solution)/shard_map/ppermute | solution.py:63
  25.9 0.8 fusion
  26.7 3.0 %collective-permute-done.2.got_ref = bf16[528,128]{1,0:T(8,128)(2,1)S(1)} collective-permute-done((bf16[528,128]{1,0:T(8,128)(2,1)S(1)}, bf16[528,128]{1,0:T(8,128)(2,1)S(1)}, u32[]{:S(2)}, u32[]{:S(2)}) %collective-permute-start.2) | collective-permute-done | bytes 135200 | tf_op jit(solution)/shard_map/ppermute | solution.py:63
  29.8 1.7 %collective-permute-done.33.got_ref = bf16[528,128]{1,0:T(8,128)(2,1)S(1)} collective-permute-done((bf16[528,128]{1,0:T(8,128)(2,1)S(1)}, bf16[528,128]{1,0:T(8,128)(2,1)S(1)}, u32[]{:S(2)}, u32[]{:S(2)}) %collective-permute-start.33) | collective-permute-done | bytes 135200 | tf_op jit(solution)/shard_map/ppermute | solution.py:63
  31.5 1.3 collective-permute-start.34
  32.9 2.8 %collective-permute-done.3.got_ref = bf16[528,128]{1,0:T(8,128)(2,1)S(1)} collective-permute-done((bf16[528,128]{1,0:T(8,128)(2,1)S(1)}, bf16[528,128]{1,0:T(8,128)(2,1)S(1)}, u32[]{:S(2)}, u32[]{:S(2)}) %collective-permute-start.3) | collective-permute-done | bytes 135200 | tf_op jit(solution)/shard_map/ppermute | solution.py:63
  36.1 2.7 %collective-permute-start.4 = (bf16[256,128]{1,0:T(8,128)(2,1)S(1)}, bf16[256,128]{1,0:T(8,128)(2,1)S(1)}, u32[]{:S(2)}, u32[]{:S(2)}) collective-permute-start(bf16[256,128]{1,0:T(8,128)(2,1)S(1)} %get-tuple-element.75), channel_id=1, source_target_pairs={{0,4},{1,3},{2,6},{3,1},{4,0},{5,7},{6,2},{7,5},{8,12},{9,11},{10,... | collective-permute-start | bytes 196616 | tf_op jit(solution)/shard_map/ppermute | solution.py:63
  39.0 1.4 collective-permute-done.34.got_ref
  40.4 0.9 shard_map.143
  41.2 0.9 collective-permute-start.35
  42.2 1.5 %collective-permute-start.5 = (bf16[512,128]{1,0:T(8,128)(2,1)S(1)}, bf16[512,128]{1,0:T(8,128)(2,1)S(1)}, u32[]{:S(2)}, u32[]{:S(2)}) collective-permute-start(bf16[512,128]{1,0:T(8,128)(2,1)S(1)} %pad_maximum_fusion.11.own_ref), channel_id=1, source_target_pairs={{0,2},{1,5},{2,0},{3,7},{4,6},{5,1},{6,4},{7,3},{8,10},{9,13},{10,... | collective-permute-start | bytes 393224 | tf_op jit(solution)/shard_map/ppermute | solution.py:63
  43.7 2.7 %collective-permute-done.35 = bf16[256,128]{1,0:T(8,128)(2,1)S(1)} collective-permute-done((bf16[256,128]{1,0:T(8,128)(2,1)S(1)}, bf16[256,128]{1,0:T(8,128)(2,1)S(1)}, u32[]{:S(2)}, u32[]{:S(2)}) %collective-permute-start.35) | collective-permute-done | bytes 65568 | tf_op jit(solution)/shard_map/ppermute | solution.py:63
  46.4 1.5 %collective-permute-start.36 = (bf16[512,128]{1,0:T(8,128)(2,1)S(1)}, bf16[512,128]{1,0:T(8,128)(2,1)S(1)}, u32[]{:S(2)}, u32[]{:S(2)}) collective-permute-start(bf16[512,128]{1,0:T(8,128)(2,1)S(1)} %pad_maximum_fusion.12.own_ref), channel_id=1, source_target_pairs={{0,2},{1,5},{2,0},{3,7},{4,6},{5,1},{6,4},{7,3},{8,10},{9,13},{10,... | collective-permute-start | bytes 393224 | tf_op jit(solution)/shard_map/ppermute | solution.py:63
  48.4 3.0 %collective-permute-done.36.got_ref = bf16[512,128]{1,0:T(8,128)(2,1)S(1)} collective-permute-done((bf16[512,128]{1,0:T(8,128)(2,1)S(1)}, bf16[512,128]{1,0:T(8,128)(2,1)S(1)}, u32[]{:S(2)}, u32[]{:S(2)}) %collective-permute-start.36) | collective-permute-done | bytes 131104 | tf_op jit(solution)/shard_map/ppermute | solution.py:63
  52.0 1.0 collective-permute-start.7
  53.2 0.9 collective-permute-start.16
  54.2 2.6 %collective-permute-start.38 = (bf16[160,128]{1,0:T(8,128)(2,1)S(1)}, bf16[160,128]{1,0:T(8,128)(2,1)S(1)}, u32[]{:S(2)}, u32[]{:S(2)}) collective-permute-start(bf16[160,128]{1,0:T(8,128)(2,1)S(1)} %shard_map.145), channel_id=1, source_target_pairs={{0,16},{1,17},{2,18},{3,19},{4,20},{5,21},{6,22},{7,23},{8,24},{9,... | collective-permute-start | bytes 122888 | tf_op jit(solution)/shard_map/ppermute | solution.py:63
  57.0 1.8 %collective-permute-start.8 = (bf16[320,128]{1,0:T(8,128)(2,1)S(1)}, bf16[320,128]{1,0:T(8,128)(2,1)S(1)}, u32[]{:S(2)}, u32[]{:S(2)}) collective-permute-start(bf16[320,128]{1,0:T(8,128)(2,1)S(1)} %pad_maximum_fusion.13), channel_id=1, source_target_pairs={{0,8},{1,3},{2,10},{3,1},{4,12},{5,7},{6,14},{7,5},{8,0},{9,11},{1... | collective-permute-start | bytes 245768 | tf_op jit(solution)/shard_map/ppermute | solution.py:63
  59.2 1.5 %collective-permute-start.39 = (bf16[320,128]{1,0:T(8,128)(2,1)S(1)}, bf16[320,128]{1,0:T(8,128)(2,1)S(1)}, u32[]{:S(2)}, u32[]{:S(2)}) collective-permute-start(bf16[320,128]{1,0:T(8,128)(2,1)S(1)} %pad_maximum_fusion.14), channel_id=1, source_target_pairs={{0,4},{1,9},{2,6},{3,11},{4,0},{5,13},{6,2},{7,15},{8,12},{9,1},{1... | collective-permute-start | bytes 245768 | tf_op jit(solution)/shard_map/ppermute | solution.py:63
  61.5 3.1 %collective-permute-start.9 = (bf16[640,128]{1,0:T(8,128)(2,1)S(1)}, bf16[640,128]{1,0:T(8,128)(2,1)S(1)}, u32[]{:S(2)}, u32[]{:S(2)}) collective-permute-start(bf16[640,128]{1,0:T(8,128)(2,1)S(1)} %pad_maximum_fusion.6), channel_id=1, source_target_pairs={{0,4},{1,9},{2,6},{3,11},{4,0},{5,13},{6,2},{7,15},{8,12},{9,1},{1... | collective-permute-start | bytes 491528 | tf_op jit(solution)/shard_map/ppermute | solution.py:63
  64.8 1.9 %collective-permute-start.40 = (bf16[640,128]{1,0:T(8,128)(2,1)S(1)}, bf16[640,128]{1,0:T(8,128)(2,1)S(1)}, u32[]{:S(2)}, u32[]{:S(2)}) collective-permute-start(bf16[640,128]{1,0:T(8,128)(2,1)S(1)} %pad_maximum_fusion.7), channel_id=1, source_target_pairs={{0,2},{1,3},{2,0},{3,1},{4,6},{5,7},{6,4},{7,5},{8,10},{9,11},{10,... | collective-permute-start | bytes 491528 | tf_op jit(solution)/shard_map/ppermute | solution.py:63
  66.7 1.3 collective-permute-done.9
  68.1 2.5 %collective-permute-start.10 = (bf16[1280,128]{1,0:T(8,128)(2,1)S(1)}, bf16[1280,128]{1,0:T(8,128)(2,1)S(1)}, u32[]{:S(2)}, u32[]{:S(2)}) collective-permute-start(bf16[1280,128]{1,0:T(8,128)(2,1)S(1)} %pad_maximum_fusion.1.refs_0_), channel_id=1, source_target_pairs={{0,2},{1,5},{2,0},{3,7},{4,6},{5,1},{6,4},{7,3},{8,10},{9,13},{10,... | collective-permute-start | bytes 983048 | tf_op jit(solution)/shard_map/ppermute | solution.py:63
  71.0 1.8 %collective-permute-start.41 = (bf16[1280,128]{1,0:T(8,128)(2,1)S(1)}, bf16[1280,128]{1,0:T(8,128)(2,1)S(1)}, u32[]{:S(2)}, u32[]{:S(2)}) collective-permute-start(bf16[1280,128]{1,0:T(8,128)(2,1)S(1)} %pad_maximum_fusion.2.refs_0_), channel_id=1, source_target_pairs={{0,8},{1,5},{2,10},{3,7},{4,12},{5,1},{6,14},{7,3},{8,0},{9,13},{1... | collective-permute-start | bytes 983048 | tf_op jit(solution)/shard_map/ppermute | solution.py:63
  72.9 2.7 %collective-permute-done.10.refs_1_ = bf16[1280,128]{1,0:T(8,128)(2,1)S(1)} collective-permute-done((bf16[1280,128]{1,0:T(8,128)(2,1)S(1)}, bf16[1280,128]{1,0:T(8,128)(2,1)S(1)}, u32[]{:S(2)}, u32[]{:S(2)}) %collective-permute-start.10) | collective-permute-done | bytes 327712 | tf_op jit(solution)/shard_map/ppermute | solution.py:63
  76.1 2.1 %collective-permute-done.41.refs_1_ = bf16[1280,128]{1,0:T(8,128)(2,1)S(1)} collective-permute-done((bf16[1280,128]{1,0:T(8,128)(2,1)S(1)}, bf16[1280,128]{1,0:T(8,128)(2,1)S(1)}, u32[]{:S(2)}, u32[]{:S(2)}) %collective-permute-start.41) | collective-permute-done | bytes 327712 | tf_op jit(solution)/shard_map/ppermute | solution.py:63
  78.2 1.8 %shard_map.138 = (bf16[4608,128]{1,0:T(8,128)(2,1)S(1)}, bf16[256,128]{1,0:T(8,128)(2,1)S(1)}, f32[256,128]{1,0:T(8,128)S(1)}, f32[256,1]{1,0:T(8,128)S(1)}, f32[144,128]{1,0:T(8,128)S(1)}) custom-call(bf16[1280,128]{1,0:T(8,128)(2,1)S(1)} %pad_maximum_fusion.1.refs_0_, bf16[1280,128]{1,0:T(8,128)(2,1)S(1)} %collective-permute-done.10.refs_1_, ...), custom_call_target="tpu_custom_call" | custom-call | flops 301989888 | bytes 2359296 | tf_op jit(solution)/shard_map/pallas_call | solution.py:403
  80.6 0.9 collective-permute-done.19.peer_low_ref
  81.5 2.3 %shard_map.139 = (bf16[1152,128]{1,0:T(8,128)(2,1)S(1)}, f32[1152,128]{1,0:T(8,128)S(1)}) custom-call(bf16[256,128]{1,0:T(8,128)(2,1)S(1)} %get-tuple-element.80.low_ref.refs_10_, bf16[256,128]{1,0:T(8,128)(2,1)S(1)} %collective-permute-done.19.peer_low_ref, bf16[256,4608]{1,0:T(8,128)(2,1)S(1)} %copy-done, ...), custom_call_target="tpu_custom_call" | custom-call | flops 603979776 | bytes 4718592 | tf_op jit(solution)/shard_map/pallas_call | solution.py:448
  83.8 1.5 %collective-permute-start.21 = (bf16[1152,128]{1,0:T(8,128)(2,1)S(1)}, bf16[1152,128]{1,0:T(8,128)(2,1)S(1)}, u32[]{:S(2)}, u32[]{:S(2)}) collective-permute-start(bf16[1152,128]{1,0:T(8,128)(2,1)S(1)} %get-tuple-element.82), channel_id=1, source_target_pairs={{0,2},{1,5},{2,0},{3,7},{4,6},{5,1},{6,4},{7,3},{8,10},{9,13},{10,... | collective-permute-start | bytes 884744 | tf_op jit(solution)/shard_map/ppermute | solution.py:63
  85.3 1.6 %shard_map.146 = (bf16[4608,128]{1,0:T(8,128)(2,1)S(1)}, bf16[256,128]{1,0:T(8,128)(2,1)S(1)}, f32[256,128]{1,0:T(8,128)S(1)}, f32[256,1]{1,0:T(8,128)S(1)}, f32[144,128]{1,0:T(8,128)S(1)}) custom-call(bf16[1280,128]{1,0:T(8,128)(2,1)S(1)} %pad_maximum_fusion.2.refs_0_, bf16[1280,128]{1,0:T(8,128)(2,1)S(1)} %collective-permute-done.41.refs_1_, ...), custom_call_target="tpu_custom_call" | custom-call | flops 301989888 | bytes 2359296 | tf_op jit(solution)/shard_map/pallas_call | solution.py:403
  86.9 1.2 collective-permute-start.44
  88.1 0.9 collective-permute-done.44.peer_low_ref
  89.0 2.3 %shard_map.147 = (bf16[1152,128]{1,0:T(8,128)(2,1)S(1)}, f32[1152,128]{1,0:T(8,128)S(1)}) custom-call(bf16[256,128]{1,0:T(8,128)(2,1)S(1)} %get-tuple-element.105.low_ref.refs_11_, bf16[256,128]{1,0:T(8,128)(2,1)S(1)} %collective-permute-done.44.peer_low_ref, bf16[256,4608]{1,0:T(8,128)(2,1)S(1)} %copy-done, ...), custom_call_target="tpu_custom_call" | custom-call | flops 603979776 | bytes 4718592 | tf_op jit(solution)/shard_map/pallas_call | solution.py:448
  91.7 1.6 %collective-permute-start.22 = (bf16[576,128]{1,0:T(8,128)(2,1)S(1)}, bf16[576,128]{1,0:T(8,128)(2,1)S(1)}, u32[]{:S(2)}, u32[]{:S(2)}) collective-permute-start(bf16[576,128]{1,0:T(8,128)(2,1)S(1)} %select_convert_fusion.1), channel_id=1, source_target_pairs={{0,4},{1,9},{2,6},{3,11},{4,0},{5,13},{6,2},{7,15},{8,12},{9,1},{1... | collective-permute-start | bytes 442376 | tf_op jit(solution)/shard_map/ppermute | solution.py:63
  93.2 6.5 %collective-permute-done.45 = bf16[1152,128]{1,0:T(8,128)(2,1)S(1)} collective-permute-done((bf16[1152,128]{1,0:T(8,128)(2,1)S(1)}, bf16[1152,128]{1,0:T(8,128)(2,1)S(1)}, u32[]{:S(2)}, u32[]{:S(2)}) %collective-permute-start.45) | collective-permute-done | bytes 294944 | tf_op jit(solution)/shard_map/ppermute | solution.py:63
  100.6 1.0 collective-permute-start.23
  101.6 4.3 %collective-permute-done.46 = bf16[576,128]{1,0:T(8,128)(2,1)S(1)} collective-permute-done((bf16[576,128]{1,0:T(8,128)(2,1)S(1)}, bf16[576,128]{1,0:T(8,128)(2,1)S(1)}, u32[]{:S(2)}, u32[]{:S(2)}) %collective-permute-start.46) | collective-permute-done | bytes 147488 | tf_op jit(solution)/shard_map/ppermute | solution.py:63
  106.1 1.0 collective-permute-start.47
  107.1 3.8 %collective-permute-done.24 = bf16[144,128]{1,0:T(8,128)(2,1)S(1)} collective-permute-done((bf16[144,128]{1,0:T(8,128)(2,1)S(1)}, bf16[144,128]{1,0:T(8,128)(2,1)S(1)}, u32[]{:S(2)}, u32[]{:S(2)}) %collective-permute-start.24) | collective-permute-done | bytes 36896 | tf_op jit(solution)/shard_map/ppermute | solution.py:63
  111.4 2.6 %collective-permute-start.48 = (bf16[144,128]{1,0:T(8,128)(2,1)S(1)}, bf16[144,128]{1,0:T(8,128)(2,1)S(1)}, u32[]{:S(2)}, u32[]{:S(2)}) collective-permute-start(bf16[144,128]{1,0:T(8,128)(2,1)S(1)} %select_convert_fusion.4), channel_id=1, source_target_pairs={{0,16},{1,17},{2,18},{3,19},{4,20},{5,21},{6,22},{7,23},{8,24},{9,... | collective-permute-start | bytes 110600 | tf_op jit(solution)/shard_map/ppermute | solution.py:63
  114.0 1.8 %collective-permute-done.25 = bf16[144,128]{1,0:T(8,128)(2,1)S(1)} collective-permute-done((bf16[144,128]{1,0:T(8,128)(2,1)S(1)}, bf16[144,128]{1,0:T(8,128)(2,1)S(1)}, u32[]{:S(2)}, u32[]{:S(2)}) %collective-permute-start.25) | collective-permute-done | bytes 36896 | tf_op jit(solution)/shard_map/ppermute | solution.py:63
  116.4 2.6 %collective-permute-start.49 = (bf16[144,128]{1,0:T(8,128)(2,1)S(1)}, bf16[144,128]{1,0:T(8,128)(2,1)S(1)}, u32[]{:S(2)}, u32[]{:S(2)}) collective-permute-start(bf16[144,128]{1,0:T(8,128)(2,1)S(1)} %add_convert_fusion), channel_id=1, source_target_pairs={{0,16},{1,17},{2,18},{3,19},{4,20},{5,21},{6,22},{7,23},{8,24},{9,... | collective-permute-start | bytes 110600 | tf_op jit(solution)/shard_map/ppermute | solution.py:63
  119.2 2.1 %collective-permute-done.49 = bf16[144,128]{1,0:T(8,128)(2,1)S(1)} collective-permute-done((bf16[144,128]{1,0:T(8,128)(2,1)S(1)}, bf16[144,128]{1,0:T(8,128)(2,1)S(1)}, u32[]{:S(2)}, u32[]{:S(2)}) %collective-permute-start.49) | collective-permute-done | bytes 36896 | tf_op jit(solution)/shard_map/ppermute | solution.py:63
  121.3 0.9 collective-permute-start.50
  122.2 1.5 %collective-permute-done.26 = bf16[288,128]{1,0:T(8,128)(2,1)S(1)} collective-permute-done((bf16[288,128]{1,0:T(8,128)(2,1)S(1)}, bf16[288,128]{1,0:T(8,128)(2,1)S(1)}, u32[]{:S(2)}, u32[]{:S(2)}) %collective-permute-start.26) | collective-permute-done | bytes 73760 | tf_op jit(solution)/shard_map/ppermute | solution.py:63
  123.8 1.2 collective-permute-start.27
  125.8 1.2 collective-permute-start.51
  127.0 3.6 %collective-permute-done.27 = bf16[576,128]{1,0:T(8,128)(2,1)S(1)} collective-permute-done((bf16[576,128]{1,0:T(8,128)(2,1)S(1)}, bf16[576,128]{1,0:T(8,128)(2,1)S(1)}, u32[]{:S(2)}, u32[]{:S(2)}) %collective-permute-start.27) | collective-permute-done | bytes 147488 | tf_op jit(solution)/shard_map/ppermute | solution.py:63
  131.5 1.7 %collective-permute-start.52 = (bf16[1152,128]{1,0:T(8,128)(2,1)S(1)}, bf16[1152,128]{1,0:T(8,128)(2,1)S(1)}, u32[]{:S(2)}, u32[]{:S(2)}) collective-permute-start(bf16[1152,128]{1,0:T(8,128)(2,1)S(1)} %pad_maximum_fusion.5.refs_4_), channel_id=1, source_target_pairs={{0,8},{1,5},{2,10},{3,7},{4,12},{5,1},{6,14},{7,3},{8,0},{9,13},{1... | collective-permute-start | bytes 884744 | tf_op jit(solution)/shard_map/ppermute | solution.py:63
  133.7 3.8 %collective-permute-done.28.refs_1_ = bf16[1152,128]{1,0:T(8,128)(2,1)S(1)} collective-permute-done((bf16[1152,128]{1,0:T(8,128)(2,1)S(1)}, bf16[1152,128]{1,0:T(8,128)(2,1)S(1)}, u32[]{:S(2)}, u32[]{:S(2)}) %collective-permute-start.28) | collective-permute-done | bytes 294944 | tf_op jit(solution)/shard_map/ppermute | solution.py:63
  139.1 0.8 collective-permute-done.54.refs_7_
  139.9 5.6 %shard_map.148 = (bf16[4608,256]{1,0:T(8,128)(2,1)}, f32[1,256]{1,0:T(1,128)}, bf16[256,4608]{1,0:T(8,128)(2,1)}) custom-call(bf16[1152,128]{1,0:T(8,128)(2,1)S(1)} %pad_maximum_fusion.4.refs_0_, bf16[1152,128]{1,0:T(8,128)(2,1)S(1)} %collective-permute-done.28.refs_1_, bf16[1152,128]{1,0:T(8,128)(2,1)S(1)} %collective-permute-done.29.refs_2_, ...), custom_call_target="tpu_custom_call" | custom-call | flops 1811939328 | bytes 14155776 | tf_op jit(solution)/shard_map/pallas_call | solution.py:513
  (136 shorter events, 14.1 us)
Async XLA Ops:
  0.6 0.9 copy-start.3
  1.6 0.7 copy-start.7
  4.3 16.4 %copy-start.4 = (bf16[256,288]{0,1:T(8,128)(2,1)S(1)}, bf16[256,288]{0,1:T(8,128)(2,1)}, u32[]{:S(2)}) copy-start(bf16[256,288]{0,1:T(8,128)(2,1)} %param.11) | copy-start | bytes 442372
  4.3 16.4 %collective-permute-start.13 = (bf16[144,256]{1,0:T(8,128)(2,1)S(1)}, bf16[144,256]{1,0:T(8,128)(2,1)S(1)}, u32[]{:S(2)}, u32[]{:S(2)}) collective-permute-start(bf16[144,256]{1,0:T(8,128)(2,1)S(1)} %slice_select_fusion), channel_id=1, source_target_pairs={{0,16},{1,17},{2,18},{3,19},{4,20},{5,21},{6,22},{7,23},{8,24},{9,... | collective-permute-start | bytes 221192 | tf_op jit(solution)/shard_map/ppermute | solution.py:63
  8.4 6.4 %collective-permute-start = (bf16[1040,128]{1,0:T(8,128)(2,1)S(1)}, bf16[1040,128]{1,0:T(8,128)(2,1)S(1)}, u32[]{:S(2)}, u32[]{:S(2)}) collective-permute-start(bf16[1040,128]{1,0:T(8,128)(2,1)S(1)} %get-tuple-element.64), channel_id=1, source_target_pairs={{0,2},{1,5},{2,0},{3,7},{4,6},{5,1},{6,4},{7,3},{8,10},{9,13},{10,... | collective-permute-start | bytes 798728 | tf_op jit(solution)/shard_map/ppermute | solution.py:63
  9.9 9.1 %collective-permute-start.31 = (bf16[1040,128]{1,0:T(8,128)(2,1)S(1)}, bf16[1040,128]{1,0:T(8,128)(2,1)S(1)}, u32[]{:S(2)}, u32[]{:S(2)}) collective-permute-start(bf16[1040,128]{1,0:T(8,128)(2,1)S(1)} %get-tuple-element.85), channel_id=1, source_target_pairs={{0,2},{1,5},{2,0},{3,7},{4,6},{5,1},{6,4},{7,3},{8,10},{9,13},{10,... | collective-permute-start | bytes 798728 | tf_op jit(solution)/shard_map/ppermute | solution.py:63
  10.4 71.1 %collective-permute-start.20 = (bf16[256,4608]{1,0:T(8,128)(2,1)}, bf16[256,4608]{1,0:T(8,128)(2,1)}, u32[]{:S(2)}, u32[]{:S(2)}) collective-permute-start(bf16[256,4608]{1,0:T(8,128)(2,1)} %refs_16_.1), channel_id=1, source_target_pairs={{0,1},{1,0},{2,3},{3,2},{4,5},{5,4},{6,7},{7,6},{8,9},{9,8},{10,11... | collective-permute-start | bytes 7077896 | tf_op jit(solution)/shard_map/ppermute | solution.py:63
  14.9 7.5 %collective-permute-start.1 = (bf16[528,128]{1,0:T(8,128)(2,1)S(1)}, bf16[528,128]{1,0:T(8,128)(2,1)S(1)}, u32[]{:S(2)}, u32[]{:S(2)}) collective-permute-start(bf16[528,128]{1,0:T(8,128)(2,1)S(1)} %get-tuple-element.67), channel_id=1, source_target_pairs={{0,4},{1,3},{2,6},{3,1},{4,0},{5,7},{6,2},{7,5},{8,12},{9,11},{10,... | collective-permute-start | bytes 405512 | tf_op jit(solution)/shard_map/ppermute | solution.py:63
  19.1 5.1 %collective-permute-start.32 = (bf16[528,128]{1,0:T(8,128)(2,1)S(1)}, bf16[528,128]{1,0:T(8,128)(2,1)S(1)}, u32[]{:S(2)}, u32[]{:S(2)}) collective-permute-start(bf16[528,128]{1,0:T(8,128)(2,1)S(1)} %get-tuple-element.88), channel_id=1, source_target_pairs={{0,4},{1,3},{2,6},{3,1},{4,0},{5,7},{6,2},{7,5},{8,12},{9,11},{10,... | collective-permute-start | bytes 405512 | tf_op jit(solution)/shard_map/ppermute | solution.py:63
  20.7 12.1 %collective-permute-start.14 = (bf16[288,256]{1,0:T(8,128)(2,1)S(1)}, bf16[288,256]{1,0:T(8,128)(2,1)S(1)}, u32[]{:S(2)}, u32[]{:S(2)}) collective-permute-start(bf16[288,256]{1,0:T(8,128)(2,1)S(1)} %pad_maximum_fusion.8), channel_id=1, source_target_pairs={{0,8},{1,9},{2,10},{3,11},{4,12},{5,13},{6,14},{7,15},{8,0},{9,1},... | collective-permute-start | bytes 442376 | tf_op jit(solution)/shard_map/ppermute | solution.py:63
  22.4 25.5 %copy-start.2 = (bf16[1024,288]{0,1:T(8,128)(2,1)S(1)}, bf16[1024,288]{0,1:T(8,128)(2,1)}, u32[]{:S(2)}) copy-start(bf16[1024,288]{0,1:T(8,128)(2,1)} %param.16) | copy-start | bytes 1769476
  22.4 7.2 %collective-permute-start.2 = (bf16[528,128]{1,0:T(8,128)(2,1)S(1)}, bf16[528,128]{1,0:T(8,128)(2,1)S(1)}, u32[]{:S(2)}, u32[]{:S(2)}) collective-permute-start(bf16[528,128]{1,0:T(8,128)(2,1)S(1)} %get-tuple-element.70), channel_id=1, source_target_pairs={{0,8},{1,9},{2,10},{3,11},{4,12},{5,13},{6,14},{7,15},{8,0},{9,1},... | collective-permute-start | bytes 405512 | tf_op jit(solution)/shard_map/ppermute | solution.py:63
  24.2 7.2 %collective-permute-start.33 = (bf16[528,128]{1,0:T(8,128)(2,1)S(1)}, bf16[528,128]{1,0:T(8,128)(2,1)S(1)}, u32[]{:S(2)}, u32[]{:S(2)}) collective-permute-start(bf16[528,128]{1,0:T(8,128)(2,1)S(1)} %get-tuple-element.91), channel_id=1, source_target_pairs={{0,8},{1,9},{2,10},{3,11},{4,12},{5,13},{6,14},{7,15},{8,0},{9,1},... | collective-permute-start | bytes 405512 | tf_op jit(solution)/shard_map/ppermute | solution.py:63
  29.7 6.0 %collective-permute-start.3 = (bf16[528,128]{1,0:T(8,128)(2,1)S(1)}, bf16[528,128]{1,0:T(8,128)(2,1)S(1)}, u32[]{:S(2)}, u32[]{:S(2)}) collective-permute-start(bf16[528,128]{1,0:T(8,128)(2,1)S(1)} %get-tuple-element.73), channel_id=1, source_target_pairs={{0,16},{1,17},{2,18},{3,19},{4,20},{5,21},{6,22},{7,23},{8,24},{9,... | collective-permute-start | bytes 405512 | tf_op jit(solution)/shard_map/ppermute | solution.py:63
  31.5 8.9 %collective-permute-start.34 = (bf16[528,128]{1,0:T(8,128)(2,1)S(1)}, bf16[528,128]{1,0:T(8,128)(2,1)S(1)}, u32[]{:S(2)}, u32[]{:S(2)}) collective-permute-start(bf16[528,128]{1,0:T(8,128)(2,1)S(1)} %get-tuple-element.94), channel_id=1, source_target_pairs={{0,16},{1,17},{2,18},{3,19},{4,20},{5,21},{6,22},{7,23},{8,24},{9,... | collective-permute-start | bytes 405512 | tf_op jit(solution)/shard_map/ppermute | solution.py:63
  36.1 6.1 %collective-permute-start.4 = (bf16[256,128]{1,0:T(8,128)(2,1)S(1)}, bf16[256,128]{1,0:T(8,128)(2,1)S(1)}, u32[]{:S(2)}, u32[]{:S(2)}) collective-permute-start(bf16[256,128]{1,0:T(8,128)(2,1)S(1)} %get-tuple-element.75), channel_id=1, source_target_pairs={{0,4},{1,3},{2,6},{3,1},{4,0},{5,7},{6,2},{7,5},{8,12},{9,11},{10,... | collective-permute-start | bytes 196616 | tf_op jit(solution)/shard_map/ppermute | solution.py:63
  38.9 13.0 %copy-start.5 = (f32[288]{0:T(512)S(1)}, f32[288]{0:T(512)}, u32[]{:S(2)}) copy-start(f32[288]{0:T(512)} %gain_ref.5) | copy-start | bytes 3460
  38.9 9.4 %collective-permute-start.15 = (bf16[576,256]{1,0:T(8,128)(2,1)S(1)}, bf16[576,256]{1,0:T(8,128)(2,1)S(1)}, u32[]{:S(2)}, u32[]{:S(2)}) collective-permute-start(bf16[576,256]{1,0:T(8,128)(2,1)S(1)} %pad_maximum_fusion.3), channel_id=1, source_target_pairs={{0,4},{1,3},{2,6},{3,1},{4,0},{5,7},{6,2},{7,5},{8,12},{9,11},{10,... | collective-permute-start | bytes 884744 | tf_op jit(solution)/shard_map/ppermute | solution.py:63
  41.2 5.1 %collective-permute-start.35 = (bf16[256,128]{1,0:T(8,128)(2,1)S(1)}, bf16[256,128]{1,0:T(8,128)(2,1)S(1)}, u32[]{:S(2)}, u32[]{:S(2)}) collective-permute-start(bf16[256,128]{1,0:T(8,128)(2,1)S(1)} %get-tuple-element.98), channel_id=1, source_target_pairs={{0,4},{1,3},{2,6},{3,1},{4,0},{5,7},{6,2},{7,5},{8,12},{9,11},{10,... | collective-permute-start | bytes 196616 | tf_op jit(solution)/shard_map/ppermute | solution.py:63
  42.2 5.7 %collective-permute-start.5 = (bf16[512,128]{1,0:T(8,128)(2,1)S(1)}, bf16[512,128]{1,0:T(8,128)(2,1)S(1)}, u32[]{:S(2)}, u32[]{:S(2)}) collective-permute-start(bf16[512,128]{1,0:T(8,128)(2,1)S(1)} %pad_maximum_fusion.11.own_ref), channel_id=1, source_target_pairs={{0,2},{1,5},{2,0},{3,7},{4,6},{5,1},{6,4},{7,3},{8,10},{9,13},{10,... | collective-permute-start | bytes 393224 | tf_op jit(solution)/shard_map/ppermute | solution.py:63
  46.4 5.0 %collective-permute-start.36 = (bf16[512,128]{1,0:T(8,128)(2,1)S(1)}, bf16[512,128]{1,0:T(8,128)(2,1)S(1)}, u32[]{:S(2)}, u32[]{:S(2)}) collective-permute-start(bf16[512,128]{1,0:T(8,128)(2,1)S(1)} %pad_maximum_fusion.12.own_ref), channel_id=1, source_target_pairs={{0,2},{1,5},{2,0},{3,7},{4,6},{5,1},{6,4},{7,3},{8,10},{9,13},{10,... | collective-permute-start | bytes 393224 | tf_op jit(solution)/shard_map/ppermute | solution.py:63
  48.2 3.6 %collective-permute-start.6 = (f32[144,128]{1,0:T(8,128)S(1)}, f32[144,128]{1,0:T(8,128)S(1)}, u32[]{:S(2)}, u32[]{:S(2)}) collective-permute-start(f32[144,128]{1,0:T(8,128)S(1)} %get-tuple-element.77), channel_id=1, source_target_pairs={{0,1},{1,0},{2,3},{3,2},{4,5},{5,4},{6,7},{7,6},{8,9},{9,8},{10,11... | collective-permute-start | bytes 221192 | tf_op jit(solution)/shard_map/ppermute | solution.py:63
  51.7 2.4 %collective-permute-start.37 = (f32[144,128]{1,0:T(8,128)S(1)}, f32[144,128]{1,0:T(8,128)S(1)}, u32[]{:S(2)}, u32[]{:S(2)}) collective-permute-start(f32[144,128]{1,0:T(8,128)S(1)} %get-tuple-element.100), channel_id=1, source_target_pairs={{0,1},{1,0},{2,3},{3,2},{4,5},{5,4},{6,7},{7,6},{8,9},{9,8},{10,11... | collective-permute-start | bytes 221192 | tf_op jit(solution)/shard_map/ppermute | solution.py:63
  52.0 5.0 %collective-permute-start.7 = (bf16[160,128]{1,0:T(8,128)(2,1)S(1)}, bf16[160,128]{1,0:T(8,128)(2,1)S(1)}, u32[]{:S(2)}, u32[]{:S(2)}) collective-permute-start(bf16[160,128]{1,0:T(8,128)(2,1)S(1)} %shard_map.136), channel_id=1, source_target_pairs={{0,16},{1,17},{2,18},{3,19},{4,20},{5,21},{6,22},{7,23},{8,24},{9,... | collective-permute-start | bytes 122888 | tf_op jit(solution)/shard_map/ppermute | solution.py:63
  53.0 17.7 %collective-permute-start.17 = (bf16[1152,256]{1,0:T(8,128)(2,1)S(1)}, bf16[1152,256]{1,0:T(8,128)(2,1)S(1)}, u32[]{:S(2)}, u32[]{:S(2)}) collective-permute-start(bf16[1152,256]{1,0:T(8,128)(2,1)S(1)} %pad_maximum_fusion.refs_0_), channel_id=1, source_target_pairs={{0,1},{1,0},{2,3},{3,2},{4,5},{5,4},{6,7},{7,6},{8,9},{9,8},{10,11... | collective-permute-start | bytes 1769480 | tf_op jit(solution)/shard_map/ppermute | solution.py:63
  53.2 13.4 %collective-permute-start.16 = (bf16[1152,256]{1,0:T(8,128)(2,1)S(1)}, bf16[1152,256]{1,0:T(8,128)(2,1)S(1)}, u32[]{:S(2)}, u32[]{:S(2)}) collective-permute-start(bf16[1152,256]{1,0:T(8,128)(2,1)S(1)} %pad_maximum_fusion.refs_0_), channel_id=1, source_target_pairs={{0,2},{1,5},{2,0},{3,7},{4,6},{5,1},{6,4},{7,3},{8,10},{9,13},{10,... | collective-permute-start | bytes 1769480 | tf_op jit(solution)/shard_map/ppermute | solution.py:63
  54.2 5.0 %collective-permute-start.38 = (bf16[160,128]{1,0:T(8,128)(2,1)S(1)}, bf16[160,128]{1,0:T(8,128)(2,1)S(1)}, u32[]{:S(2)}, u32[]{:S(2)}) collective-permute-start(bf16[160,128]{1,0:T(8,128)(2,1)S(1)} %shard_map.145), channel_id=1, source_target_pairs={{0,16},{1,17},{2,18},{3,19},{4,20},{5,21},{6,22},{7,23},{8,24},{9,... | collective-permute-start | bytes 122888 | tf_op jit(solution)/shard_map/ppermute | solution.py:63
  57.0 4.5 %collective-permute-start.8 = (bf16[320,128]{1,0:T(8,128)(2,1)S(1)}, bf16[320,128]{1,0:T(8,128)(2,1)S(1)}, u32[]{:S(2)}, u32[]{:S(2)}) collective-permute-start(bf16[320,128]{1,0:T(8,128)(2,1)S(1)} %pad_maximum_fusion.13), channel_id=1, source_target_pairs={{0,8},{1,3},{2,10},{3,1},{4,12},{5,7},{6,14},{7,5},{8,0},{9,11},{1... | collective-permute-start | bytes 245768 | tf_op jit(solution)/shard_map/ppermute | solution.py:63
  59.2 5.4 %collective-permute-start.39 = (bf16[320,128]{1,0:T(8,128)(2,1)S(1)}, bf16[320,128]{1,0:T(8,128)(2,1)S(1)}, u32[]{:S(2)}, u32[]{:S(2)}) collective-permute-start(bf16[320,128]{1,0:T(8,128)(2,1)S(1)} %pad_maximum_fusion.14), channel_id=1, source_target_pairs={{0,4},{1,9},{2,6},{3,11},{4,0},{5,13},{6,2},{7,15},{8,12},{9,1},{1... | collective-permute-start | bytes 245768 | tf_op jit(solution)/shard_map/ppermute | solution.py:63
  61.5 6.4 %collective-permute-start.9 = (bf16[640,128]{1,0:T(8,128)(2,1)S(1)}, bf16[640,128]{1,0:T(8,128)(2,1)S(1)}, u32[]{:S(2)}, u32[]{:S(2)}) collective-permute-start(bf16[640,128]{1,0:T(8,128)(2,1)S(1)} %pad_maximum_fusion.6), channel_id=1, source_target_pairs={{0,4},{1,9},{2,6},{3,11},{4,0},{5,13},{6,2},{7,15},{8,12},{9,1},{1... | collective-permute-start | bytes 491528 | tf_op jit(solution)/shard_map/ppermute | solution.py:63
  64.7 13.5 %copy-start.1 = (bf16[4608,256]{1,0:T(8,128)(2,1)S(1)}, bf16[4608,256]{1,0:T(8,128)(2,1)}, u32[]{:S(2)}) copy-start(bf16[4608,256]{1,0:T(8,128)(2,1)} %refs_5_.3) | copy-start | bytes 7077892
  64.7 13.5 %copy-start.6 = (f32[256]{0:T(256)S(1)}, f32[256]{0:T(256)}, u32[]{:S(2)}) copy-start(f32[256]{0:T(256)} %refs_6_.3) | copy-start | bytes 3076
  64.8 5.8 %collective-permute-start.40 = (bf16[640,128]{1,0:T(8,128)(2,1)S(1)}, bf16[640,128]{1,0:T(8,128)(2,1)S(1)}, u32[]{:S(2)}, u32[]{:S(2)}) collective-permute-start(bf16[640,128]{1,0:T(8,128)(2,1)S(1)} %pad_maximum_fusion.7), channel_id=1, source_target_pairs={{0,2},{1,3},{2,0},{3,1},{4,6},{5,7},{6,4},{7,5},{8,10},{9,11},{10,... | collective-permute-start | bytes 491528 | tf_op jit(solution)/shard_map/ppermute | solution.py:63
  66.7 4.0 %collective-permute-start.18 = (bf16[1152,256]{1,0:T(8,128)(2,1)S(1)}, bf16[1152,256]{1,0:T(8,128)(2,1)S(1)}, u32[]{:S(2)}, u32[]{:S(2)}) collective-permute-start(bf16[1152,256]{1,0:T(8,128)(2,1)S(1)} %collective-permute-done.16.refs_1_), channel_id=1, source_target_pairs={{0,1},{1,0},{2,3},{3,2},{4,5},{5,4},{6,7},{7,6},{8,9},{9,8},{10,11... | collective-permute-start | bytes 1769480 | tf_op jit(solution)/shard_map/ppermute | solution.py:63
  68.1 7.5 %collective-permute-start.10 = (bf16[1280,128]{1,0:T(8,128)(2,1)S(1)}, bf16[1280,128]{1,0:T(8,128)(2,1)S(1)}, u32[]{:S(2)}, u32[]{:S(2)}) collective-permute-start(bf16[1280,128]{1,0:T(8,128)(2,1)S(1)} %pad_maximum_fusion.1.refs_0_), channel_id=1, source_target_pairs={{0,2},{1,5},{2,0},{3,7},{4,6},{5,1},{6,4},{7,3},{8,10},{9,13},{10,... | collective-permute-start | bytes 983048 | tf_op jit(solution)/shard_map/ppermute | solution.py:63
  71.0 10.5 %copy-start = (bf16[256,4608]{1,0:T(8,128)(2,1)S(1)}, bf16[256,4608]{1,0:T(8,128)(2,1)}, u32[]{:S(2)}) copy-start(bf16[256,4608]{1,0:T(8,128)(2,1)} %refs_16_.1) | copy-start | bytes 7077892
  71.0 7.1 %collective-permute-start.41 = (bf16[1280,128]{1,0:T(8,128)(2,1)S(1)}, bf16[1280,128]{1,0:T(8,128)(2,1)S(1)}, u32[]{:S(2)}, u32[]{:S(2)}) collective-permute-start(bf16[1280,128]{1,0:T(8,128)(2,1)S(1)} %pad_maximum_fusion.2.refs_0_), channel_id=1, source_target_pairs={{0,8},{1,5},{2,10},{3,7},{4,12},{5,1},{6,14},{7,3},{8,0},{9,13},{1... | collective-permute-start | bytes 983048 | tf_op jit(solution)/shard_map/ppermute | solution.py:63
  72.9 5.3 %collective-permute-start.11 = (bf16[1280,128]{1,0:T(8,128)(2,1)S(1)}, bf16[1280,128]{1,0:T(8,128)(2,1)S(1)}, u32[]{:S(2)}, u32[]{:S(2)}) collective-permute-start(bf16[1280,128]{1,0:T(8,128)(2,1)S(1)} %pad_maximum_fusion.1.refs_0_), channel_id=1, source_target_pairs={{0,1},{1,0},{2,3},{3,2},{4,5},{5,4},{6,7},{7,6},{8,9},{9,8},{10,11... | collective-permute-start | bytes 983048 | tf_op jit(solution)/shard_map/ppermute | solution.py:63
  75.6 2.6 %collective-permute-start.12 = (bf16[1280,128]{1,0:T(8,128)(2,1)S(1)}, bf16[1280,128]{1,0:T(8,128)(2,1)S(1)}, u32[]{:S(2)}, u32[]{:S(2)}) collective-permute-start(bf16[1280,128]{1,0:T(8,128)(2,1)S(1)} %collective-permute-done.10.refs_1_), channel_id=1, source_target_pairs={{0,1},{1,0},{2,3},{3,2},{4,5},{5,4},{6,7},{7,6},{8,9},{9,8},{10,11... | collective-permute-start | bytes 983048 | tf_op jit(solution)/shard_map/ppermute | solution.py:63
  75.6 9.7 %collective-permute-start.42 = (bf16[1280,128]{1,0:T(8,128)(2,1)S(1)}, bf16[1280,128]{1,0:T(8,128)(2,1)S(1)}, u32[]{:S(2)}, u32[]{:S(2)}) collective-permute-start(bf16[1280,128]{1,0:T(8,128)(2,1)S(1)} %pad_maximum_fusion.2.refs_0_), channel_id=1, source_target_pairs={{0,1},{1,0},{2,3},{3,2},{4,5},{5,4},{6,7},{7,6},{8,9},{9,8},{10,11... | collective-permute-start | bytes 983048 | tf_op jit(solution)/shard_map/ppermute | solution.py:63
  78.2 7.1 %collective-permute-start.43 = (bf16[1280,128]{1,0:T(8,128)(2,1)S(1)}, bf16[1280,128]{1,0:T(8,128)(2,1)S(1)}, u32[]{:S(2)}, u32[]{:S(2)}) collective-permute-start(bf16[1280,128]{1,0:T(8,128)(2,1)S(1)} %collective-permute-done.41.refs_1_), channel_id=1, source_target_pairs={{0,1},{1,0},{2,3},{3,2},{4,5},{5,4},{6,7},{7,6},{8,9},{9,8},{10,11... | collective-permute-start | bytes 983048 | tf_op jit(solution)/shard_map/ppermute | solution.py:63
  80.0 1.5 %collective-permute-start.19 = (bf16[256,128]{1,0:T(8,128)(2,1)S(1)}, bf16[256,128]{1,0:T(8,128)(2,1)S(1)}, u32[]{:S(2)}, u32[]{:S(2)}) collective-permute-start(bf16[256,128]{1,0:T(8,128)(2,1)S(1)} %get-tuple-element.80.low_ref.refs_10_), channel_id=1, source_target_pairs={{0,1},{1,0},{2,3},{3,2},{4,5},{5,4},{6,7},{7,6},{8,9},{9,8},{10,11... | collective-permute-start | bytes 196616 | tf_op jit(solution)/shard_map/ppermute | solution.py:63
  83.8 7.8 %collective-permute-start.21 = (bf16[1152,128]{1,0:T(8,128)(2,1)S(1)}, bf16[1152,128]{1,0:T(8,128)(2,1)S(1)}, u32[]{:S(2)}, u32[]{:S(2)}) collective-permute-start(bf16[1152,128]{1,0:T(8,128)(2,1)S(1)} %get-tuple-element.82), channel_id=1, source_target_pairs={{0,2},{1,5},{2,0},{3,7},{4,6},{5,1},{6,4},{7,3},{8,10},{9,13},{10,... | collective-permute-start | bytes 884744 | tf_op jit(solution)/shard_map/ppermute | solution.py:63
  86.9 2.1 %collective-permute-start.44 = (bf16[256,128]{1,0:T(8,128)(2,1)S(1)}, bf16[256,128]{1,0:T(8,128)(2,1)S(1)}, u32[]{:S(2)}, u32[]{:S(2)}) collective-permute-start(bf16[256,128]{1,0:T(8,128)(2,1)S(1)} %get-tuple-element.105.low_ref.refs_11_), channel_id=1, source_target_pairs={{0,1},{1,0},{2,3},{3,2},{4,5},{5,4},{6,7},{7,6},{8,9},{9,8},{10,11... | collective-permute-start | bytes 196616 | tf_op jit(solution)/shard_map/ppermute | solution.py:63
  91.3 8.4 %collective-permute-start.45 = (bf16[1152,128]{1,0:T(8,128)(2,1)S(1)}, bf16[1152,128]{1,0:T(8,128)(2,1)S(1)}, u32[]{:S(2)}, u32[]{:S(2)}) collective-permute-start(bf16[1152,128]{1,0:T(8,128)(2,1)S(1)} %get-tuple-element.107), channel_id=1, source_target_pairs={{0,8},{1,5},{2,10},{3,7},{4,12},{5,1},{6,14},{7,3},{8,0},{9,13},{1... | collective-permute-start | bytes 884744 | tf_op jit(solution)/shard_map/ppermute | solution.py:63
  91.7 8.9 %collective-permute-start.22 = (bf16[576,128]{1,0:T(8,128)(2,1)S(1)}, bf16[576,128]{1,0:T(8,128)(2,1)S(1)}, u32[]{:S(2)}, u32[]{:S(2)}) collective-permute-start(bf16[576,128]{1,0:T(8,128)(2,1)S(1)} %select_convert_fusion.1), channel_id=1, source_target_pairs={{0,4},{1,9},{2,6},{3,11},{4,0},{5,13},{6,2},{7,15},{8,12},{9,1},{1... | collective-permute-start | bytes 442376 | tf_op jit(solution)/shard_map/ppermute | solution.py:63
  99.7 6.1 %collective-permute-start.46 = (bf16[576,128]{1,0:T(8,128)(2,1)S(1)}, bf16[576,128]{1,0:T(8,128)(2,1)S(1)}, u32[]{:S(2)}, u32[]{:S(2)}) collective-permute-start(bf16[576,128]{1,0:T(8,128)(2,1)S(1)} %select_convert_fusion), channel_id=1, source_target_pairs={{0,2},{1,3},{2,0},{3,1},{4,6},{5,7},{6,4},{7,5},{8,10},{9,11},{10,... | collective-permute-start | bytes 442376 | tf_op jit(solution)/shard_map/ppermute | solution.py:63
  100.6 5.3 %collective-permute-start.23 = (bf16[288,128]{1,0:T(8,128)(2,1)S(1)}, bf16[288,128]{1,0:T(8,128)(2,1)S(1)}, u32[]{:S(2)}, u32[]{:S(2)}) collective-permute-start(bf16[288,128]{1,0:T(8,128)(2,1)S(1)} %select_convert_fusion.3), channel_id=1, source_target_pairs={{0,8},{1,3},{2,10},{3,1},{4,12},{5,7},{6,14},{7,5},{8,0},{9,11},{1... | collective-permute-start | bytes 221192 | tf_op jit(solution)/shard_map/ppermute | solution.py:63
  106.0 4.9 %collective-permute-start.24 = (bf16[144,128]{1,0:T(8,128)(2,1)S(1)}, bf16[144,128]{1,0:T(8,128)(2,1)S(1)}, u32[]{:S(2)}, u32[]{:S(2)}) collective-permute-start(bf16[144,128]{1,0:T(8,128)(2,1)S(1)} %select_convert_fusion.5), channel_id=1, source_target_pairs={{0,16},{1,17},{2,18},{3,19},{4,20},{5,21},{6,22},{7,23},{8,24},{9,... | collective-permute-start | bytes 110600 | tf_op jit(solution)/shard_map/ppermute | solution.py:63
  106.1 5.3 %collective-permute-start.47 = (bf16[288,128]{1,0:T(8,128)(2,1)S(1)}, bf16[288,128]{1,0:T(8,128)(2,1)S(1)}, u32[]{:S(2)}, u32[]{:S(2)}) collective-permute-start(bf16[288,128]{1,0:T(8,128)(2,1)S(1)} %select_convert_fusion.2), channel_id=1, source_target_pairs={{0,4},{1,9},{2,6},{3,11},{4,0},{5,13},{6,2},{7,15},{8,12},{9,1},{1... | collective-permute-start | bytes 221192 | tf_op jit(solution)/shard_map/ppermute | solution.py:63
  110.9 4.9 %collective-permute-start.25 = (bf16[144,128]{1,0:T(8,128)(2,1)S(1)}, bf16[144,128]{1,0:T(8,128)(2,1)S(1)}, u32[]{:S(2)}, u32[]{:S(2)}) collective-permute-start(bf16[144,128]{1,0:T(8,128)(2,1)S(1)} %add_convert_fusion.1), channel_id=1, source_target_pairs={{0,16},{1,17},{2,18},{3,19},{4,20},{5,21},{6,22},{7,23},{8,24},{9,... | collective-permute-start | bytes 110600 | tf_op jit(solution)/shard_map/ppermute | solution.py:63
  111.4 4.9 %collective-permute-start.48 = (bf16[144,128]{1,0:T(8,128)(2,1)S(1)}, bf16[144,128]{1,0:T(8,128)(2,1)S(1)}, u32[]{:S(2)}, u32[]{:S(2)}) collective-permute-start(bf16[144,128]{1,0:T(8,128)(2,1)S(1)} %select_convert_fusion.4), channel_id=1, source_target_pairs={{0,16},{1,17},{2,18},{3,19},{4,20},{5,21},{6,22},{7,23},{8,24},{9,... | collective-permute-start | bytes 110600 | tf_op jit(solution)/shard_map/ppermute | solution.py:63
  116.4 4.9 %collective-permute-start.49 = (bf16[144,128]{1,0:T(8,128)(2,1)S(1)}, bf16[144,128]{1,0:T(8,128)(2,1)S(1)}, u32[]{:S(2)}, u32[]{:S(2)}) collective-permute-start(bf16[144,128]{1,0:T(8,128)(2,1)S(1)} %add_convert_fusion), channel_id=1, source_target_pairs={{0,16},{1,17},{2,18},{3,19},{4,20},{5,21},{6,22},{7,23},{8,24},{9,... | collective-permute-start | bytes 110600 | tf_op jit(solution)/shard_map/ppermute | solution.py:63
  119.0 4.7 %collective-permute-start.26 = (bf16[288,128]{1,0:T(8,128)(2,1)S(1)}, bf16[288,128]{1,0:T(8,128)(2,1)S(1)}, u32[]{:S(2)}, u32[]{:S(2)}) collective-permute-start(bf16[288,128]{1,0:T(8,128)(2,1)S(1)} %pad_maximum_fusion.15), channel_id=1, source_target_pairs={{0,8},{1,3},{2,10},{3,1},{4,12},{5,7},{6,14},{7,5},{8,0},{9,11},{1... | collective-permute-start | bytes 221192 | tf_op jit(solution)/shard_map/ppermute | solution.py:63
  121.3 4.4 %collective-permute-start.50 = (bf16[288,128]{1,0:T(8,128)(2,1)S(1)}, bf16[288,128]{1,0:T(8,128)(2,1)S(1)}, u32[]{:S(2)}, u32[]{:S(2)}) collective-permute-start(bf16[288,128]{1,0:T(8,128)(2,1)S(1)} %pad_maximum_fusion.16), channel_id=1, source_target_pairs={{0,4},{1,9},{2,6},{3,11},{4,0},{5,13},{6,2},{7,15},{8,12},{9,1},{1... | collective-permute-start | bytes 221192 | tf_op jit(solution)/shard_map/ppermute | solution.py:63
  123.8 6.8 %collective-permute-start.27 = (bf16[576,128]{1,0:T(8,128)(2,1)S(1)}, bf16[576,128]{1,0:T(8,128)(2,1)S(1)}, u32[]{:S(2)}, u32[]{:S(2)}) collective-permute-start(bf16[576,128]{1,0:T(8,128)(2,1)S(1)} %pad_maximum_fusion.9), channel_id=1, source_target_pairs={{0,4},{1,9},{2,6},{3,11},{4,0},{5,13},{6,2},{7,15},{8,12},{9,1},{1... | collective-permute-start | bytes 442376 | tf_op jit(solution)/shard_map/ppermute | solution.py:63
  125.8 5.6 %collective-permute-start.51 = (bf16[576,128]{1,0:T(8,128)(2,1)S(1)}, bf16[576,128]{1,0:T(8,128)(2,1)S(1)}, u32[]{:S(2)}, u32[]{:S(2)}) collective-permute-start(bf16[576,128]{1,0:T(8,128)(2,1)S(1)} %pad_maximum_fusion.10), channel_id=1, source_target_pairs={{0,2},{1,3},{2,0},{3,1},{4,6},{5,7},{6,4},{7,5},{8,10},{9,11},{10,... | collective-permute-start | bytes 442376 | tf_op jit(solution)/shard_map/ppermute | solution.py:63
  130.7 6.8 %collective-permute-start.28 = (bf16[1152,128]{1,0:T(8,128)(2,1)S(1)}, bf16[1152,128]{1,0:T(8,128)(2,1)S(1)}, u32[]{:S(2)}, u32[]{:S(2)}) collective-permute-start(bf16[1152,128]{1,0:T(8,128)(2,1)S(1)} %pad_maximum_fusion.4.refs_0_), channel_id=1, source_target_pairs={{0,2},{1,5},{2,0},{3,7},{4,6},{5,1},{6,4},{7,3},{8,10},{9,13},{10,... | collective-permute-start | bytes 884744 | tf_op jit(solution)/shard_map/ppermute | solution.py:63
  131.5 6.8 %collective-permute-start.52 = (bf16[1152,128]{1,0:T(8,128)(2,1)S(1)}, bf16[1152,128]{1,0:T(8,128)(2,1)S(1)}, u32[]{:S(2)}, u32[]{:S(2)}) collective-permute-start(bf16[1152,128]{1,0:T(8,128)(2,1)S(1)} %pad_maximum_fusion.5.refs_4_), channel_id=1, source_target_pairs={{0,8},{1,5},{2,10},{3,7},{4,12},{5,1},{6,14},{7,3},{8,0},{9,13},{1... | collective-permute-start | bytes 884744 | tf_op jit(solution)/shard_map/ppermute | solution.py:63
  133.2 5.1 %collective-permute-start.29 = (bf16[1152,128]{1,0:T(8,128)(2,1)S(1)}, bf16[1152,128]{1,0:T(8,128)(2,1)S(1)}, u32[]{:S(2)}, u32[]{:S(2)}) collective-permute-start(bf16[1152,128]{1,0:T(8,128)(2,1)S(1)} %pad_maximum_fusion.4.refs_0_), channel_id=1, source_target_pairs={{0,1},{1,0},{2,3},{3,2},{4,5},{5,4},{6,7},{7,6},{8,9},{9,8},{10,11... | collective-permute-start | bytes 884744 | tf_op jit(solution)/shard_map/ppermute | solution.py:63
  133.2 5.1 %collective-permute-start.53 = (bf16[1152,128]{1,0:T(8,128)(2,1)S(1)}, bf16[1152,128]{1,0:T(8,128)(2,1)S(1)}, u32[]{:S(2)}, u32[]{:S(2)}) collective-permute-start(bf16[1152,128]{1,0:T(8,128)(2,1)S(1)} %pad_maximum_fusion.5.refs_4_), channel_id=1, source_target_pairs={{0,1},{1,0},{2,3},{3,2},{4,5},{5,4},{6,7},{7,6},{8,9},{9,8},{10,11... | collective-permute-start | bytes 884744 | tf_op jit(solution)/shard_map/ppermute | solution.py:63
  137.5 1.6 %collective-permute-start.30 = (bf16[1152,128]{1,0:T(8,128)(2,1)S(1)}, bf16[1152,128]{1,0:T(8,128)(2,1)S(1)}, u32[]{:S(2)}, u32[]{:S(2)}) collective-permute-start(bf16[1152,128]{1,0:T(8,128)(2,1)S(1)} %collective-permute-done.28.refs_1_), channel_id=1, source_target_pairs={{0,1},{1,0},{2,3},{3,2},{4,5},{5,4},{6,7},{7,6},{8,9},{9,8},{10,11... | collective-permute-start | bytes 884744 | tf_op jit(solution)/shard_map/ppermute | solution.py:63
  138.3 1.6 %collective-permute-start.54 = (bf16[1152,128]{1,0:T(8,128)(2,1)S(1)}, bf16[1152,128]{1,0:T(8,128)(2,1)S(1)}, u32[]{:S(2)}, u32[]{:S(2)}) collective-permute-start(bf16[1152,128]{1,0:T(8,128)(2,1)S(1)} %collective-permute-done.52.refs_5_), channel_id=1, source_target_pairs={{0,1},{1,0},{2,3},{3,2},{4,5},{5,4},{6,7},{7,6},{8,9},{9,8},{10,11... | collective-permute-start | bytes 884744 | tf_op jit(solution)/shard_map/ppermute | solution.py:63
